TPU v7x, 32 devices: a whole 2x2x4 slice. The times are simulated.
32 devices in a mesh: row: 2 (over core), nar: 4 (over y, x), wid: 4 (over z).
Axes of the slice: x: 2, y: 2, z: 4, core: 2. Of those that a mesh axis runs over, the one named last changes fastest.
Arguments:
- hidden_in: bfloat16 [2, 2048, 2048], P('row', ('nar', 'wid')), may hold values from -6 to 6
- doc_lengths: int32 [2, 8], P('row'), may hold values from 1 to 1024, 2048 in all within a row
- w_query: bfloat16 [2048, 2048], P('nar', 'wid'), may hold values from -0.125 to 0.125
- w_key: bfloat16 [2048, 512], P('nar'), may hold values from -0.125 to 0.125
- w_value: bfloat16 [2048, 512], P('nar'), may hold values from -0.125 to 0.125
- w_output: bfloat16 [2048, 2048], P('wid', 'nar'), may hold values from -1 to 1
- w_gate: bfloat16 [2048, 8192], P('nar', 'wid'), may hold values from -0.125 to 0.125
- w_up: bfloat16 [2048, 8192], P('nar', 'wid'), may hold values from -0.125 to 0.125
- w_down: bfloat16 [8192, 2048], P('wid', 'nar'), may hold values from -0.0625 to 0.0625
- gain_attn: float32 [2048], replicated, may hold values from 0.5 to 1.5
- gain_ffn: float32 [2048], replicated, may hold values from 0.5 to 1.5
- grad_out: bfloat16 [2, 2048, 2048], P('row', ('nar', 'wid')), may hold values from -9 to 9
Outputs:
- hidden_out: bfloat16 [2, 2048, 2048], P('row', ('nar', 'wid'))
- grad_in: bfloat16 [2, 2048, 2048], P('row', ('nar', 'wid'))
- grad_query: float32 [2048, 2048], P(('row', 'nar'), 'wid')
- grad_key: float32 [2048, 512], P(('row', 'nar'))
- grad_value: float32 [2048, 512], P(('row', 'nar'))
- grad_output: float32 [2048, 2048], P('wid', ('row', 'nar'))
- grad_gate: float32 [2048, 8192], P(('row', 'nar'), 'wid')
- grad_up: float32 [2048, 8192], P(('row', 'nar'), 'wid')
- grad_down: float32 [8192, 2048], P('wid', ('row', 'nar'))
- grad_gain_attn: float32 [2048], P(('row', 'nar'))
- grad_gain_ffn: float32 [2048], P(('row', 'nar'))
Inputs may be any that keep to these rules, and one draw needn't show every extreme that they name: `doc_lengths`: each row's 8 lengths add up to 2048, and the longest is exactly 1024.
All inputs are finite; a program needn't handle non-finite values.
Results may differ from a plain program's by a relative error of at most 0.024.
Values may be sent and summed in bfloat16 or wider, within the bound.
A program may use at most 192 MiB of HBM per device.

v0:
```python
import math

import jax
import jax.numpy as jnp
from jax import lax
from jax.sharding import PartitionSpec as P

H = 32
KV = 8
HD = 64


norm_eps = 1e-05
masked_score = -1e30


def inverse_freq():
    listed = []
    for pair_index in range(HD // 2):
        base_freq = 500000.0 ** (-2.0 * pair_index / HD)
        wavelength = 2.0 * math.pi / base_freq
        smoothing = (8192.0 / wavelength - 1.0) / 3.0
        blended = (1.0 - smoothing) * base_freq / 32.0 + smoothing * base_freq
        if wavelength < 2048.0:
            listed.append(base_freq)
        elif wavelength > 8192.0:
            listed.append(base_freq / 32.0)
        else:
            listed.append(blended)
    return jnp.asarray(listed, dtype=jnp.float32)


def rotate(values, cosine_table, sine_table):
    half_dim = HD // 2
    first_half = values[..., :half_dim]
    second_half = values[..., half_dim:]
    return jnp.concatenate(
        [
            first_half * cosine_table - second_half * sine_table,
            second_half * cosine_table + first_half * sine_table,
        ],
        axis=-1,
    )


def rotate_back(grads_in, cosine_table, sine_table):
    half_dim = HD // 2
    first_half = grads_in[..., :half_dim]
    second_half = grads_in[..., half_dim:]
    return jnp.concatenate(
        [
            first_half * cosine_table + second_half * sine_table,
            second_half * cosine_table - first_half * sine_table,
        ],
        axis=-1,
    )


def doc_layout(lengths_row, token_ids):
    ends_at = jnp.cumsum(lengths_row, dtype=jnp.int32)
    starts_at = ends_at - lengths_row
    inside = (token_ids[:, None] >= starts_at[None, :]) & (token_ids[:, None] < ends_at[None, :])
    doc_start = jnp.sum(jnp.where(inside, starts_at[None, :], 0), axis=1, dtype=jnp.int32)
    return (doc_start, token_ids - doc_start)


def norm_forward(values, gain_vector):
    root_inv = lax.rsqrt(jnp.mean(values * values, axis=-1, keepdims=True) + norm_eps)
    return (root_inv, (values * root_inv * gain_vector).astype(jnp.bfloat16))


def norm_backward(values, root_inv, gain_vector, grad_normed):
    weighted = grad_normed * gain_vector
    inner_sum = jnp.mean(weighted * values, axis=-1, keepdims=True)
    grad_values = root_inv * weighted - values * (root_inv * root_inv * root_inv) * inner_sum
    gain_term = jnp.sum(grad_normed * values * root_inv, axis=0)
    return (grad_values, gain_term)


def contract_last(left_side, right_side):
    return lax.dot_general(
        left_side, right_side, (((1,), (1,)), ((), ())), preferred_element_type=jnp.float32
    )


def contract_first(left_side, right_side):
    return lax.dot_general(
        left_side, right_side, (((0,), (0,)), ((), ())), preferred_element_type=jnp.float32
    )


def local(
    hidden_in,
    doc_lengths,
    w_query,
    w_key,
    w_value,
    w_output,
    w_gate,
    w_up,
    w_down,
    gain_attn,
    gain_ffn,
    grad_out,
):
    wid_count = lax.axis_size("wid")
    nar_count = lax.axis_size("nar")
    wid_index = lax.axis_index("wid")
    nar_index = lax.axis_index("nar")
    local_tokens = hidden_in.shape[1]
    block_tokens = local_tokens * wid_count
    seq_length = block_tokens * nar_count
    query_heads = w_query.shape[1] // HD
    group_size = H // KV
    kv_local = max(query_heads // group_size, 1)
    heads_per_kv = query_heads // kv_local
    kv_first = wid_index * query_heads // group_size
    query_block = min(512, block_tokens)
    block_count = block_tokens // query_block
    item_count = block_count * query_heads
    attn_scale = HD ** (-0.5)
    query_full, key_full, value_full, output_full, gate_full, up_full, down_full = (
        lax.all_gather(w_query, "nar", axis=0, tiled=True),
        lax.all_gather(w_key, "nar", axis=0, tiled=True),
        lax.all_gather(w_value, "nar", axis=0, tiled=True),
        lax.all_gather(w_output, "nar", axis=1, tiled=True),
        lax.all_gather(w_gate, "nar", axis=0, tiled=True),
        lax.all_gather(w_up, "nar", axis=0, tiled=True),
        lax.all_gather(w_down, "nar", axis=1, tiled=True),
    )
    key_local = lax.dynamic_slice_in_dim(key_full, kv_first * HD, kv_local * HD, 1)
    value_local = lax.dynamic_slice_in_dim(value_full, kv_first * HD, kv_local * HD, 1)
    token_ids = nar_index * block_tokens + jnp.arange(block_tokens, dtype=jnp.int32)
    doc_start, places = doc_layout(doc_lengths[0], token_ids)
    angles = places.astype(jnp.float32)[:, None] * inverse_freq()[None, :]
    cosine_table = jnp.cos(angles)[:, None, :]
    sine_table = jnp.sin(angles)[:, None, :]
    key_ids = jnp.arange(seq_length, dtype=jnp.int32)
    residual = hidden_in[0].astype(jnp.float32)
    root_attn, normed_attn = norm_forward(residual, gain_attn)
    normed_rows = lax.all_gather(normed_attn, "wid", axis=0, tiled=True)
    query_pre = jnp.dot(normed_rows, query_full, preferred_element_type=jnp.float32)
    key_pre = jnp.dot(normed_rows, key_local, preferred_element_type=jnp.float32)
    value_rows = jnp.dot(normed_rows, value_local, preferred_element_type=jnp.float32).astype(
        jnp.bfloat16
    )
    query_rot = (
        rotate(query_pre.reshape(block_tokens, query_heads, HD), cosine_table, sine_table)
        .astype(jnp.bfloat16)
        .reshape(block_tokens, query_heads * HD)
    )
    key_rot = (
        rotate(key_pre.reshape(block_tokens, kv_local, HD), cosine_table, sine_table)
        .astype(jnp.bfloat16)
        .reshape(block_tokens, kv_local * HD)
    )
    key_seq, value_seq = (
        lax.all_gather(key_rot, "nar", axis=0, tiled=True),
        lax.all_gather(value_rows, "nar", axis=0, tiled=True),
    )

    def item_inputs(item_index):
        block_index = item_index // query_heads
        head_index = item_index % query_heads
        kv_index = head_index // heads_per_kv
        row_first = block_index * query_block
        query_part = lax.dynamic_slice(query_rot, (row_first, head_index * HD), (query_block, HD))
        key_head = lax.dynamic_slice_in_dim(key_seq, kv_index * HD, HD, 1)
        value_head = lax.dynamic_slice_in_dim(value_seq, kv_index * HD, HD, 1)
        query_ids = lax.dynamic_slice_in_dim(token_ids, row_first, query_block, 0)
        query_starts = lax.dynamic_slice_in_dim(doc_start, row_first, query_block, 0)
        allowed = (key_ids[None, :] <= query_ids[:, None]) & (
            key_ids[None, :] >= query_starts[:, None]
        )
        scores = contract_last(query_part, key_head) * attn_scale
        return (
            row_first,
            head_index,
            kv_index,
            query_part,
            key_head,
            value_head,
            jnp.where(allowed, scores, masked_score),
        )

    def attend(item_index):
        row_first, head_index, kv_index, query_part, key_head, value_head, scores = item_inputs(
            item_index
        )
        row_max = jnp.max(scores, axis=1, keepdims=True)
        exp_scores = jnp.exp(scores - row_max)
        row_total = jnp.sum(exp_scores, axis=1, keepdims=True)
        probability = (exp_scores / row_total).astype(jnp.bfloat16)
        attended = jnp.dot(probability, value_head, preferred_element_type=jnp.float32)
        return (attended, (row_max + jnp.log(row_total))[:, 0])

    attended_items, logsum_items = lax.map(attend, jnp.arange(item_count, dtype=jnp.int32))
    attended_rows = (
        attended_items.reshape(block_count, query_heads, query_block, HD)
        .transpose(0, 2, 1, 3)
        .reshape(block_tokens, query_heads * HD)
        .astype(jnp.bfloat16)
    )
    rows_here = attended_rows
    branch_attn = lax.psum_scatter(
        jnp.dot(rows_here, output_full, preferred_element_type=jnp.float32),
        "wid",
        scatter_dimension=0,
        tiled=True,
    )
    middle = residual + branch_attn
    root_ffn, normed_ffn = norm_forward(middle, gain_ffn)
    ffn_rows = lax.all_gather(normed_ffn, "wid", axis=0, tiled=True)
    gate_proj = jnp.dot(ffn_rows, gate_full, preferred_element_type=jnp.float32)
    up_proj = jnp.dot(ffn_rows, up_full, preferred_element_type=jnp.float32)
    gate_sigmoid = jax.nn.sigmoid(gate_proj)
    gate_silu = gate_proj * gate_sigmoid
    activated = (gate_silu * up_proj).astype(jnp.bfloat16)
    rows_here = activated
    branch_ffn = lax.psum_scatter(
        jnp.dot(rows_here, down_full, preferred_element_type=jnp.float32).astype(jnp.bfloat16),
        "wid",
        scatter_dimension=0,
        tiled=True,
    ).astype(jnp.float32)
    hidden_out = (middle + branch_ffn).astype(jnp.bfloat16)[None]
    grad_top = grad_out[0]
    grad_rows = lax.all_gather(grad_top, "wid", axis=0, tiled=True)
    grad_activated = contract_last(grad_rows, down_full)
    down_weight_grad = contract_first(activated, grad_rows)
    silu_slope = gate_sigmoid * (1.0 + gate_proj * (1.0 - gate_sigmoid))
    grad_gate_b = (grad_activated * up_proj * silu_slope).astype(jnp.bfloat16)
    grad_up_b = (grad_activated * gate_silu).astype(jnp.bfloat16)
    gate_weight_grad = contract_first(ffn_rows, grad_gate_b)
    up_weight_grad = contract_first(ffn_rows, grad_up_b)
    grad_normed_ffn = lax.psum_scatter(
        contract_last(grad_gate_b, gate_full) + contract_last(grad_up_b, up_full),
        "wid",
        scatter_dimension=0,
        tiled=True,
    )
    grad_middle, gain_ffn_term = norm_backward(middle, root_ffn, gain_ffn, grad_normed_ffn)
    grad_middle = grad_middle + grad_top.astype(jnp.float32)
    grad_branch = grad_middle.astype(jnp.bfloat16)
    branch_rows = lax.all_gather(grad_branch, "wid", axis=0, tiled=True)
    grad_attended = contract_last(branch_rows, output_full).astype(jnp.bfloat16)
    output_weight_grad = contract_first(attended_rows, branch_rows)

    def attend_back(carried, item_index):
        key_grad, value_grad = carried
        row_first, head_index, kv_index, query_part, key_head, value_head, scores = item_inputs(
            item_index
        )
        logsum = lax.dynamic_index_in_dim(logsum_items, item_index, 0, keepdims=False)
        probability = jnp.exp(scores - logsum[:, None])
        grad_part = lax.dynamic_slice(
            grad_attended, (row_first, head_index * HD), (query_block, HD)
        )
        grad_prob = contract_last(grad_part, value_head)
        inner_sum = jnp.sum(probability * grad_prob, axis=1, keepdims=True)
        grad_scores = (probability * (grad_prob - inner_sum)).astype(jnp.bfloat16)
        query_grad = jnp.dot(grad_scores, key_head, preferred_element_type=jnp.float32) * attn_scale
        key_part = contract_first(grad_scores, query_part) * attn_scale
        value_part = contract_first(probability.astype(jnp.bfloat16), grad_part)
        key_old = lax.dynamic_slice_in_dim(key_grad, kv_index * HD, HD, 1)
        key_grad = lax.dynamic_update_slice_in_dim(key_grad, key_old + key_part, kv_index * HD, 1)
        value_old = lax.dynamic_slice_in_dim(value_grad, kv_index * HD, HD, 1)
        value_grad = lax.dynamic_update_slice_in_dim(
            value_grad, value_old + value_part, kv_index * HD, 1
        )
        return ((key_grad, value_grad), query_grad)

    zero_grads = jnp.zeros((seq_length, kv_local * HD), jnp.float32)
    (key_grad_seq, value_grad_seq), query_grad_items = lax.scan(
        attend_back, (zero_grads, zero_grads), jnp.arange(item_count, dtype=jnp.int32)
    )
    key_grad_block, value_grad_block = (
        lax.psum_scatter(
            key_grad_seq.astype(jnp.bfloat16), "nar", scatter_dimension=0, tiled=True
        ).astype(jnp.float32),
        lax.psum_scatter(
            value_grad_seq.astype(jnp.bfloat16), "nar", scatter_dimension=0, tiled=True
        ).astype(jnp.float32),
    )
    query_grad_rows = (
        query_grad_items.reshape(block_count, query_heads, query_block, HD)
        .transpose(0, 2, 1, 3)
        .reshape(block_tokens, query_heads, HD)
    )
    query_grad_b = (
        rotate_back(query_grad_rows, cosine_table, sine_table)
        .astype(jnp.bfloat16)
        .reshape(block_tokens, query_heads * HD)
    )
    key_grad_b = (
        rotate_back(key_grad_block.reshape(block_tokens, kv_local, HD), cosine_table, sine_table)
        .astype(jnp.bfloat16)
        .reshape(block_tokens, kv_local * HD)
    )
    value_grad_b = value_grad_block.astype(jnp.bfloat16)
    query_weight_grad = contract_first(normed_rows, query_grad_b)
    key_weight_grad = contract_first(normed_rows, key_grad_b)
    value_weight_grad = contract_first(normed_rows, value_grad_b)
    grad_normed_attn = lax.psum_scatter(
        (
            contract_last(query_grad_b, query_full)
            + contract_last(key_grad_b, key_local)
            + contract_last(value_grad_b, value_local)
        ).astype(jnp.bfloat16),
        "wid",
        scatter_dimension=0,
        tiled=True,
    ).astype(jnp.float32)
    grad_residual, gain_attn_term = norm_backward(residual, root_attn, gain_attn, grad_normed_attn)
    grad_in = (grad_residual + grad_middle).astype(jnp.bfloat16)[None]
    summed = (
        lax.psum_scatter(
            query_weight_grad.astype(jnp.bfloat16), ("row", "nar"), scatter_dimension=0, tiled=True
        ).astype(jnp.float32),
        lax.psum_scatter(
            key_weight_grad.astype(jnp.bfloat16), ("row", "nar"), scatter_dimension=0, tiled=True
        ).astype(jnp.float32),
        lax.psum_scatter(
            value_weight_grad.astype(jnp.bfloat16), ("row", "nar"), scatter_dimension=0, tiled=True
        ).astype(jnp.float32),
        lax.psum_scatter(
            output_weight_grad.astype(jnp.bfloat16), ("row", "nar"), scatter_dimension=1, tiled=True
        ).astype(jnp.float32),
        lax.psum_scatter(
            gate_weight_grad.astype(jnp.bfloat16), ("row", "nar"), scatter_dimension=0, tiled=True
        ).astype(jnp.float32),
        lax.psum_scatter(
            up_weight_grad.astype(jnp.bfloat16), ("row", "nar"), scatter_dimension=0, tiled=True
        ).astype(jnp.float32),
        lax.psum_scatter(
            down_weight_grad.astype(jnp.bfloat16), ("row", "nar"), scatter_dimension=1, tiled=True
        ).astype(jnp.float32),
        lax.psum_scatter(
            gain_attn_term.astype(jnp.bfloat16), ("row", "nar"), scatter_dimension=0, tiled=True
        ).astype(jnp.float32),
        lax.psum_scatter(
            gain_ffn_term.astype(jnp.bfloat16), ("row", "nar"), scatter_dimension=0, tiled=True
        ).astype(jnp.float32),
    )
    (
        grad_query,
        key_sum,
        value_sum,
        grad_output,
        grad_gate,
        grad_up,
        grad_down,
        gain_attn_sum,
        gain_ffn_sum,
    ) = summed
    key_all, value_all, gain_attn_all, gain_ffn_all = (
        lax.all_gather(key_sum.astype(jnp.bfloat16), "wid", axis=1, tiled=True).astype(
            key_sum.dtype
        ),
        lax.all_gather(value_sum.astype(jnp.bfloat16), "wid", axis=1, tiled=True).astype(
            value_sum.dtype
        ),
        lax.all_gather(gain_attn_sum.astype(jnp.bfloat16), "wid", axis=0, tiled=True).astype(
            gain_attn_sum.dtype
        ),
        lax.all_gather(gain_ffn_sum.astype(jnp.bfloat16), "wid", axis=0, tiled=True).astype(
            gain_ffn_sum.dtype
        ),
    )
    shard_rows = key_sum.shape[0]
    repeats = wid_count * kv_local // KV
    grad_key = key_all.reshape(shard_rows, KV, repeats, HD).sum(axis=2).reshape(shard_rows, KV * HD)
    grad_value = (
        value_all.reshape(shard_rows, KV, repeats, HD).sum(axis=2).reshape(shard_rows, KV * HD)
    )
    grad_gain_attn = gain_attn_all.reshape(wid_count, shard_rows).sum(axis=0)
    grad_gain_ffn = gain_ffn_all.reshape(wid_count, shard_rows).sum(axis=0)
    return (
        hidden_out,
        grad_in,
        grad_query,
        grad_key,
        grad_value,
        grad_output,
        grad_gate,
        grad_up,
        grad_down,
        grad_gain_attn,
        grad_gain_ffn,
    )


def solution(mesh):
    in_specs = (
        P("row", ("nar", "wid"), None),
        P("row", None),
        P("nar", "wid"),
        P("nar", None),
        P("nar", None),
        P("wid", "nar"),
        P("nar", "wid"),
        P("nar", "wid"),
        P("wid", "nar"),
        P(),
        P(),
        P("row", ("nar", "wid"), None),
    )
    out_specs = (
        P("row", ("nar", "wid"), None),
        P("row", ("nar", "wid"), None),
        P(("row", "nar"), "wid"),
        P(("row", "nar"), None),
        P(("row", "nar"), None),
        P("wid", ("row", "nar")),
        P(("row", "nar"), "wid"),
        P(("row", "nar"), "wid"),
        P("wid", ("row", "nar")),
        P(("row", "nar")),
        P(("row", "nar")),
    )
    return jax.shard_map(local, mesh=mesh, in_specs=in_specs, out_specs=out_specs, check_vma=False)
```

profile of v0, /device:TPU:0, one launch (start us, length us, event | category | flops | bytes accessed | tf_op | source)
XLA Modules:
  0.0 1567.6 jit_solution(5654025398106240852)
XLA Ops:
  15.8 44.3 %all-gather.15.cloned.1.call-done = bf16[512,2048]{1,0:T(8,128)(2,1)} async-done(((bf16[128,2048]{1,0:T(8,128)(2,1)}), bf16[512,2048]{1,0:T(8,128)(2,1)}) %all-gather.15.cloned.1.call-update) | async-done | bytes 2097168 | tf_op jit(solution)/shard_map/all_gather | solution.py:141
  60.1 35.9 %all-gather.19.cloned.1.call-done = bf16[2048,512]{1,0:T(8,128)(2,1)} async-done(((bf16[512,512]{1,0:T(8,128)(2,1)}), bf16[2048,512]{1,0:T(8,128)(2,1)}) %all-gather.19.cloned.1.call-update) | async-done | bytes 2097168 | tf_op jit(solution)/shard_map/all_gather | solution.py:124
  99.0 11.9 all_gather.54
  111.2 22.4 %all-gather.21.cloned.1.call-done = bf16[2048,512]{1,0:T(8,128)(2,1)} async-done(((bf16[512,512]{1,0:T(8,128)(2,1)}), bf16[2048,512]{1,0:T(8,128)(2,1)}) %all-gather.21.cloned.1.call-update) | async-done | bytes 2097168 | tf_op jit(solution)/shard_map/all_gather | solution.py:125
  135.6 10.3 all_gather.56
  145.9 24.6 %all-gather.17.cloned.1.call-done = bf16[2048,512]{1,0:T(8,128)(2,1)} async-done(((bf16[512,512]{1,0:T(8,128)(2,1)}), bf16[2048,512]{1,0:T(8,128)(2,1)}) %all-gather.17.cloned.1.call-update) | async-done | bytes 2097168 | tf_op jit(solution)/shard_map/all_gather | solution.py:123
  174.4 75.7 %while.36 = (s32[]{:T(128)}, bf16[8,512,64]{1,2,0:T(8,128)(2,1)S(1)}, f32[8,512]{1,0:T(8,128)S(1)}, s32[512]{0:T(512)S(1)}, s32[8]{0:T(128)S(1)}, /*index=5*/bf1...) while((s32[]{:T(128)}, ...), condition=%wide.region_6.7_spmd.clone.clone.clone, body=%wide.region_3.6_spmd.clone.clone.sunk.clone | while | flops 279969824 | bytes 30697980 | solution.py:197
  180.6 3.3 fusion.147
  199.6 3.3 fusion.147
  209.0 3.3 fusion.147
  218.5 3.3 fusion.147
  250.2 5.2 fusion.69
  256.3 76.2 %reduce-scatter.14.cloned.1.call-done = f32[128,2048]{1,0:T(8,128)} async-done(((f32[512,2048]{1,0:T(8,128)}), f32[128,2048]{1,0:T(8,128)}) %reduce-scatter.14.cloned.1.call-update) | async-done | bytes 1048592 | tf_op jit(solution)/shard_map/reduce_scatter | solution.py:205
  337.5 84.9 %all-gather.27.cloned.1.call-done = bf16[2048,2048]{1,0:T(8,128)(2,1)} async-done(((bf16[512,2048]{1,0:T(8,128)(2,1)}), bf16[2048,2048]{1,0:T(8,128)(2,1)}) %all-gather.27.cloned.1.call-update) | async-done | bytes 8388624 | tf_op jit(solution)/shard_map/all_gather | solution.py:127
  422.4 47.8 %all-gather.25.cloned.1.call-done = bf16[512,2048]{1,0:T(8,128)(2,1)} async-done(((bf16[128,2048]{1,0:T(8,128)(2,1)}), bf16[512,2048]{1,0:T(8,128)(2,1)}) %all-gather.25.cloned.1.call-update) | async-done | bytes 2097168 | tf_op jit(solution)/shard_map/all_gather | solution.py:213
  470.2 10.5 fusion.70
  480.7 77.7 %all-gather.29.cloned.1.call-done = bf16[2048,2048]{1,0:T(8,128)(2,1)} async-done(((bf16[512,2048]{1,0:T(8,128)(2,1)}), bf16[2048,2048]{1,0:T(8,128)(2,1)}) %all-gather.29.cloned.1.call-update) | async-done | bytes 8388624 | tf_op jit(solution)/shard_map/all_gather | solution.py:128
  558.4 10.5 fusion.71
  568.8 36.6 %all-gather.35.cloned.1.call-done = bf16[1,512,2048]{2,1,0:T(8,128)(2,1)} async-done(((bf16[1,128,2048]{2,1,0:T(8,128)(2,1)}), bf16[1,512,2048]{2,1,0:T(8,128)(2,1)}) %all-gather.35.cloned.1.call-update) | async-done | bytes 2097168 | tf_op jit(solution)/shard_map/all_gather | solution.py:228
  605.5 88.0 %all-gather.31.cloned.1.call-done = bf16[2048,2048]{1,0:T(8,128)(2,1)} async-done(((bf16[2048,512]{1,0:T(8,128)(2,1)}), bf16[2048,2048]{1,0:T(8,128)(2,1)}) %all-gather.31.cloned.1.call-update) | async-done | bytes 8388624 | tf_op jit(solution)/shard_map/all_gather | solution.py:129
  693.5 13.6 multiply_convert_fusion.1
  707.1 8.7 fusion.72
  715.9 6.2 convolution_add_fusion.1
  722.1 9.8 convolution_convert_fusion.5
  732.0 67.0 %reduce-scatter.18.cloned.1.call-done = f32[128,2048]{1,0:T(8,128)} async-done(((f32[512,2048]{1,0:T(8,128)}), f32[128,2048]{1,0:T(8,128)}) %reduce-scatter.18.cloned.1.call-update) | async-done | bytes 1048592 | tf_op jit(solution)/shard_map/reduce_scatter | solution.py:236
  800.6 45.4 %reduce-scatter.16.cloned.1.call-done = bf16[128,2048]{1,0:T(8,128)(2,1)} async-done(((bf16[512,2048]{1,0:T(8,128)(2,1)}), bf16[128,2048]{1,0:T(8,128)(2,1)}) %reduce-scatter.16.cloned.1.call-update) | async-done | bytes 524304 | tf_op jit(solution)/shard_map/reduce_scatter | solution.py:220
  849.1 44.9 %all-gather.33.cloned.1.call-done = bf16[512,2048]{1,0:T(8,128)(2,1)} async-done(((bf16[128,2048]{1,0:T(8,128)(2,1)}), bf16[512,2048]{1,0:T(8,128)(2,1)}) %all-gather.33.cloned.1.call-update) | async-done | bytes 2097168 | tf_op jit(solution)/shard_map/all_gather | solution.py:245
  894.0 4.3 convolution_convert_fusion.8
  898.5 137.0 %while.37 = (s32[]{:T(128)}, f32[2048,128]{0,1:T(8,128)S(1)}, f32[2048,128]{0,1:T(8,128)S(1)}, f32[8,512,64]{1,2,0:T(8,128)}, s32[8]{0:T(128)S(1)}, /*index=5*/s...) while((s32[]{:T(128)}, f32[2048,128]{0,1:T(8,128)S(1)}, ...), condition=%wide.region_14.15_spmd.clone.clone.clone, body=%wide.region_12.14_spmd.clone.clone.sunk.clone | while | flops 684097536 | bytes 52577344 | solution.py:274
  901.3 3.7 fusion.156
  906.4 4.4 multiply_reduce_fusion.6
  918.4 3.7 fusion.156
  923.5 4.4 multiply_reduce_fusion.6
  935.6 3.7 fusion.156
  940.6 4.4 multiply_reduce_fusion.6
  952.7 3.7 fusion.156
  957.7 4.4 multiply_reduce_fusion.6
  969.8 3.7 fusion.156
  974.8 4.4 multiply_reduce_fusion.6
  986.9 3.7 fusion.156
  991.9 4.4 multiply_reduce_fusion.6
  1004.0 3.7 fusion.156
  1009.0 4.4 multiply_reduce_fusion.6
  1021.1 3.7 fusion.156
  1026.1 4.4 multiply_reduce_fusion.6
  1037.5 10.1 convolution_convert_fusion.2
  1049.1 8.3 convolution_convert_fusion.1
  1059.0 8.8 convolution_convert_fusion
  1071.2 17.7 %reduce-scatter.22.cloned.1.call-done = bf16[512,128]{0,1:T(8,128)(2,1)} async-done(((bf16[2048,128]{0,1:T(8,128)(2,1)}), bf16[512,128]{0,1:T(8,128)(2,1)}) %reduce-scatter.22.cloned.1.call-update) | async-done | bytes 131088 | tf_op jit(solution)/shard_map/reduce_scatter | solution.py:281
  1096.6 4.7 convolution_convert_fusion.3
  1106.9 3.5 add_convert_fusion
  1112.3 51.5 %reduce-scatter.34.cloned.1.call-done = bf16[256,2048]{1,0:T(8,128)(2,1)} async-done(((bf16[2048,2048]{1,0:T(8,128)(2,1)}), bf16[256,2048]{1,0:T(8,128)(2,1)}) %reduce-scatter.34.cloned.1.call-update) | async-done | bytes 1048592 | tf_op jit(solution)/shard_map/reduce_scatter | solution.py:329
  1166.5 72.1 %reduce-scatter.36.cloned.1.call-done = bf16[256,2048]{1,0:T(8,128)(2,1)} async-done(((bf16[2048,2048]{1,0:T(8,128)(2,1)}), bf16[256,2048]{1,0:T(8,128)(2,1)}) %reduce-scatter.36.cloned.1.call-update) | async-done | bytes 1048592 | tf_op jit(solution)/shard_map/reduce_scatter | solution.py:332
  1241.4 72.0 %reduce-scatter.38.cloned.1.call-done = bf16[2048,256]{1,0:T(8,128)(2,1)} async-done(((bf16[2048,2048]{1,0:T(8,128)(2,1)}), bf16[2048,256]{1,0:T(8,128)(2,1)}) %reduce-scatter.38.cloned.1.call-update) | async-done | bytes 1048592 | tf_op jit(solution)/shard_map/reduce_scatter | solution.py:335
  1316.1 34.9 %reduce-scatter.28.cloned.1.call-done = bf16[256,128]{1,0:T(8,128)(2,1)} async-done(((bf16[2048,128]{1,0:T(8,128)(2,1)}), bf16[256,128]{1,0:T(8,128)(2,1)}) %reduce-scatter.28.cloned.1.call-update) | async-done | bytes 65552 | tf_op jit(solution)/shard_map/reduce_scatter | solution.py:320
  1351.0 13.1 all_gather.64
  1364.9 23.8 %reduce-scatter.30.cloned.1.call-done = bf16[256,128]{1,0:T(8,128)(2,1)} async-done(((bf16[2048,128]{1,0:T(8,128)(2,1)}), bf16[256,128]{1,0:T(8,128)(2,1)}) %reduce-scatter.30.cloned.1.call-update) | async-done | bytes 65552 | tf_op jit(solution)/shard_map/reduce_scatter | solution.py:323
  1388.8 13.1 all_gather.65
  1402.7 30.5 %reduce-scatter.26.cloned.1.call-done = bf16[256,512]{1,0:T(8,128)(2,1)} async-done(((bf16[2048,512]{1,0:T(8,128)(2,1)}), bf16[256,512]{1,0:T(8,128)(2,1)}) %reduce-scatter.26.cloned.1.call-update) | async-done | bytes 262160 | tf_op jit(solution)/shard_map/reduce_scatter | solution.py:317
  1435.0 42.6 %reduce-scatter.32.cloned.1.call-done = bf16[512,256]{1,0:T(8,128)(2,1)} async-done(((bf16[512,2048]{1,0:T(8,128)(2,1)}), bf16[512,256]{1,0:T(8,128)(2,1)}) %reduce-scatter.32.cloned.1.call-update) | async-done | bytes 262160 | tf_op jit(solution)/shard_map/reduce_scatter | solution.py:326
  1479.4 44.0 %reduce-scatter.24.cloned.1.call-done = bf16[128,2048]{1,0:T(8,128)(2,1)} async-done(((bf16[512,2048]{1,0:T(8,128)(2,1)}), bf16[128,2048]{1,0:T(8,128)(2,1)}) %reduce-scatter.24.cloned.1.call-update) | async-done | bytes 524304 | tf_op jit(solution)/shard_map/reduce_scatter | solution.py:304
  1524.8 14.7 all-reduce.2
  1539.6 9.1 all-gather.2
  1549.4 8.0 all-gather.1
  (308 shorter events, 161.0 us)
Async XLA Ops:
  7.2 53.0 %all-gather.15.cloned.1.call-start = ((), (), s32[]{:S(2)}) async-start(), calls=%async_computation.13 | async-start | bytes 2621440 | tf_op jit(solution)/shard_map/all_gather | solution.py:141
  9.5 5.6 copy-start.27
  9.5 5.9 copy-start.22
  11.6 84.4 %all-gather.19.cloned.1.call-start = ((), (), s32[]{:S(2)}) async-start(), calls=%async_computation.15 | async-start | bytes 2621440 | tf_op jit(solution)/shard_map/all_gather | solution.py:124
  12.4 121.2 %all-gather.21.cloned.1.call-start = ((), (), s32[]{:S(2)}) async-start(), calls=%async_computation.16 | async-start | bytes 2621440 | tf_op jit(solution)/shard_map/all_gather | solution.py:125
  13.1 157.4 %all-gather.17.cloned.1.call-start = ((), (), s32[]{:S(2)}) async-start(), calls=%async_computation.14 | async-start | bytes 2621440 | tf_op jit(solution)/shard_map/all_gather | solution.py:123
  13.7 236.5 %all-gather.23.cloned.1.call-start = ((), (), s32[]{:S(2)}) async-start(), calls=%async_computation.17 | async-start | bytes 2621440 | tf_op jit(solution)/shard_map/all_gather | solution.py:126
  14.3 318.2 %reduce-scatter.14.cloned.1.call-start = ((), (), s32[]{:S(2)}) async-start(), calls=%async_computation.18 | async-start | bytes 5242880 | tf_op jit(solution)/shard_map/reduce_scatter | solution.py:205
  15.8 157.6 %copy-start.13 = (f32[512,32]{0,1:T(8,128)}, f32[512,32]{0,1:T(8,128)S(1)}, u32[]{:S(2)}) copy-start(f32[512,32]{0,1:T(8,128)S(1)} %get-tuple-element.573) | copy-start | bytes 196612
  15.8 157.6 %copy-start.15 = (f32[512,32]{0,1:T(8,128)}, f32[512,32]{0,1:T(8,128)S(1)}, u32[]{:S(2)}) copy-start(f32[512,32]{0,1:T(8,128)S(1)} %get-tuple-element.574) | copy-start | bytes 196612
  60.1 73.5 %copy-start.2 = (bf16[512,2048]{1,0:T(8,128)(2,1)S(1)}, bf16[512,2048]{1,0:T(8,128)(2,1)}, u32[]{:S(2)}) copy-start(bf16[512,2048]{1,0:T(8,128)(2,1)} %all-gather.15.cloned.1.call-done) | copy-start | bytes 6291460
  178.6 2.0 copy-start.1
  188.1 2.0 copy-start.1
  197.5 2.0 copy-start.1
  207.0 2.0 copy-start.1
  216.4 2.0 copy-start.1
  225.9 2.0 copy-start.1
  235.4 2.0 copy-start.1
  244.8 2.0 copy-start.1
  250.2 5.3 copy-start.8
  250.2 5.3 copy-start.11
  255.5 77.0 %copy-start.4 = (bf16[1,128,2048]{2,1,0:T(8,128)(2,1)S(1)}, bf16[1,128,2048]{2,1,0:T(8,128)(2,1)}, u32[]{:S(2)}) copy-start(bf16[1,128,2048]{2,1,0:T(8,128)(2,1)} %param.17) | copy-start | bytes 1572868
  255.5 78.5 %copy-start.18 = (f32[2048]{0:T(1024)S(1)}, f32[2048]{0:T(1024)}, u32[]{:S(2)}) copy-start(f32[2048]{0:T(1024)} %param.27) | copy-start | bytes 24580
  255.5 166.9 %all-gather.27.cloned.1.call-start = ((), (), s32[]{:S(2)}) async-start(), calls=%async_computation.20 | async-start | bytes 10485760 | tf_op jit(solution)/shard_map/all_gather | solution.py:127
  256.2 213.9 %all-gather.25.cloned.1.call-start = ((), (), s32[]{:S(2)}) async-start(), calls=%async_computation.19 | async-start | bytes 2621440 | tf_op jit(solution)/shard_map/all_gather | solution.py:213
  334.9 223.4 %all-gather.29.cloned.1.call-start = ((), (), s32[]{:S(2)}) async-start(), calls=%async_computation.21 | async-start | bytes 10485760 | tf_op jit(solution)/shard_map/all_gather | solution.py:128
  335.6 269.8 %all-gather.35.cloned.1.call-start = ((), (), s32[]{:S(2)}) async-start(), calls=%async_computation.36 | async-start | bytes 2621440 | tf_op jit(solution)/shard_map/all_gather | solution.py:228
  336.2 357.2 %all-gather.31.cloned.1.call-start = ((), (), s32[]{:S(2)}) async-start(), calls=%async_computation.22 | async-start | bytes 10485760 | tf_op jit(solution)/shard_map/all_gather | solution.py:129
  337.0 462.1 %reduce-scatter.18.cloned.1.call-start = ((), (), s32[]{:S(2)}) async-start(), calls=%async_computation.24 | async-start | bytes 5242880 | tf_op jit(solution)/shard_map/reduce_scatter | solution.py:236
  707.1 8.7 copy-start.30
  707.1 8.7 copy-start.29
  707.1 8.8 copy-start.24
  722.1 124.0 %reduce-scatter.16.cloned.1.call-start = ((), (), s32[]{:S(2)}) async-start(), calls=%async_computation.23 | async-start | bytes 2621440 | tf_op jit(solution)/shard_map/reduce_scatter | solution.py:220
  732.0 162.1 %all-gather.33.cloned.1.call-start = ((), (), s32[]{:S(2)}) async-start(), calls=%async_computation.25 | async-start | bytes 2621440 | tf_op jit(solution)/shard_map/all_gather | solution.py:245
  799.0 47.0 %copy-start.7 = (f32[128,2048]{1,0:T(8,128)S(1)}, f32[128,2048]{1,0:T(8,128)}, u32[]{:S(2)}) copy-start(f32[128,2048]{1,0:T(8,128)} %reduce-scatter.18.cloned.1.call-done) | copy-start | bytes 3145732
  849.0 218.9 %reduce-scatter.20.cloned.1.call-start = ((), (), s32[]{:S(2)}) async-start(), calls=%async_computation.26 | async-start | bytes 655360 | tf_op jit(solution)/shard_map/reduce_scatter | solution.py:278
  906.3 4.5 copy-start
  923.4 4.5 copy-start
  940.6 4.5 copy-start
  957.7 4.5 copy-start
  974.8 4.5 copy-start
  991.9 4.5 copy-start
  1009.0 4.5 copy-start
  1026.1 4.5 copy-start
  1036.5 52.5 %reduce-scatter.22.cloned.1.call-start = ((), (), s32[]{:S(2)}) async-start(), calls=%async_computation.27 | async-start | bytes 655360 | tf_op jit(solution)/shard_map/reduce_scatter | solution.py:281
  1037.4 126.4 %reduce-scatter.34.cloned.1.call-start = ((), (), s32[]{:S(2)}) async-start(), calls=%async_computation.33 | async-start | bytes 9437184 | tf_op jit(solution)/shard_map/reduce_scatter | solution.py:329
  1047.5 1.6 copy-start.25
  1047.6 191.0 %reduce-scatter.36.cloned.1.call-start = ((), (), s32[]{:S(2)}) async-start(), calls=%async_computation.34 | async-start | bytes 9437184 | tf_op jit(solution)/shard_map/reduce_scatter | solution.py:332
  1057.4 1.6 copy-start.26
  1057.5 255.9 %reduce-scatter.38.cloned.1.call-start = ((), (), s32[]{:S(2)}) async-start(), calls=%async_computation.35 | async-start | bytes 9437184 | tf_op jit(solution)/shard_map/reduce_scatter | solution.py:335
  1067.8 1.2 copy-start.16
  1067.8 1.7 copy-start.3
  1067.8 283.1 %reduce-scatter.28.cloned.1.call-start = ((), (), s32[]{:S(2)}) async-start(), calls=%async_computation.30 | async-start | bytes 589824 | tf_op jit(solution)/shard_map/reduce_scatter | solution.py:320
  1071.1 317.7 %reduce-scatter.30.cloned.1.call-start = ((), (), s32[]{:S(2)}) async-start(), calls=%async_computation.31 | async-start | bytes 589824 | tf_op jit(solution)/shard_map/reduce_scatter | solution.py:323
  1091.4 341.8 %reduce-scatter.26.cloned.1.call-start = ((), (), s32[]{:S(2)}) async-start(), calls=%async_computation.29 | async-start | bytes 2359296 | tf_op jit(solution)/shard_map/reduce_scatter | solution.py:317
  1095.6 382.1 %reduce-scatter.32.cloned.1.call-start = ((), (), s32[]{:S(2)}) async-start(), calls=%async_computation.32 | async-start | bytes 2359296 | tf_op jit(solution)/shard_map/reduce_scatter | solution.py:326
  1101.3 2.0 copy-start.9
  1101.3 422.1 %reduce-scatter.24.cloned.1.call-start = ((), (), s32[]{:S(2)}) async-start(), calls=%async_computation.28 | async-start | bytes 2621440 | tf_op jit(solution)/shard_map/reduce_scatter | solution.py:304
  1104.6 2.3 copy-start.17
  1316.1 207.4 %copy-start.5 = (bf16[1,128,2048]{2,1,0:T(8,128)(2,1)S(1)}, bf16[1,128,2048]{2,1,0:T(8,128)(2,1)}, u32[]{:S(2)}) copy-start(bf16[1,128,2048]{2,1,0:T(8,128)(2,1)} %param.17) | copy-start | bytes 1572868
  1316.1 207.4 %copy-start.19 = (f32[2048]{0:T(1024)S(1)}, f32[2048]{0:T(1024)}, u32[]{:S(2)}) copy-start(f32[2048]{0:T(1024)} %param.26) | copy-start | bytes 24580
  1316.1 207.4 %copy-start.21 = (f32[128]{0:T(128)S(1)}, f32[128]{0:T(128)}, u32[]{:S(2)}) copy-start(f32[128]{0:T(128)} %copy-done.20) | copy-start | bytes 1540
  1364.1 193.9 %copy-start.6 = (f32[128,2048]{1,0:T(8,128)S(1)}, f32[128,2048]{1,0:T(8,128)}, u32[]{:S(2)}) copy-start(f32[128,2048]{1,0:T(8,128)} %get-tuple-element.554) | copy-start | bytes 3145732
  1364.1 193.9 %copy-start.23 = (f32[128]{0:T(128)S(1)}, f32[128]{0:T(128)}, u32[]{:S(2)}) copy-start(f32[128]{0:T(128)} %get-tuple-element.575) | copy-start | bytes 1540
  (5 other events, 4.4 us)
Sparse Core Ops, SparseCore 0:
  11.7 48.3 all-gather.14
  62.0 33.9 all-gather.18
  97.8 35.7 all-gather.20
  135.3 35.1 all-gather.16
  172.2 35.0 all-gather.22
  255.6 76.8 reduce-scatter.13
  334.3 87.9 all-gather.26
  424.5 45.6 all-gather.24
  472.0 86.2 all-gather.28
  559.8 45.6 all-gather.34
  607.3 86.1 all-gather.30
  722.2 76.7 reduce-scatter.17
  801.9 44.1 reduce-scatter.15
  849.2 44.8 all-gather.32
  1036.6 23.9 reduce-scatter.19
  1063.8 25.0 reduce-scatter.21
  1092.2 71.4 reduce-scatter.33
  1167.1 71.4 reduce-scatter.35
  1242.1 71.2 reduce-scatter.37
  1316.9 34.0 reduce-scatter.27
  1354.7 34.0 reduce-scatter.29
  1392.1 41.1 reduce-scatter.25
  1436.5 41.0 reduce-scatter.31
  1479.8 43.5 reduce-scatter.23
where the time goes:
time: 1580 us; the launch traced here: 1570 us
  waiting for transfers between devices  1090 us (69%)
  matrix products  263 us (17%)
  blocking collectives  80.2 us (5%)
  other arithmetic  44.3 us (3%)
  loops' own time  43.3 us (3%)
  local copies, waits for them, and re-layouts  29.6 us (2%)
  between operations  15.9 us (1%)
    dot_general x31, matrix products, contract_last(): lax.dot_general(left_side, right_side, (((1,), (1,)), ((), ())), preferre...  117 us
    all_gather x1, waiting for transfers between devices, local(): lax.all_gather(w_down, 'nar', axis=1, tiled=True)  88 us
    all_gather x1, waiting for transfers between devices, local(): lax.all_gather(w_gate, 'nar', axis=0, tiled=True)  84.9 us
    all_gather x1, waiting for transfers between devices, local(): lax.all_gather(w_up, 'nar', axis=0, tiled=True)  77.7 us
    reduce_scatter x1, waiting for transfers between devices, local(): lax.psum_scatter(jnp.dot(rows_here, output_full, preferred_element_type=j...  76.2 us
    reduce_scatter x1, waiting for transfers between devices, local(): lax.psum_scatter(up_weight_grad.astype(jnp.bfloat16), ('row', 'nar'), sca...  72.1 us
    reduce_scatter x1, waiting for transfers between devices, local(): lax.psum_scatter(down_weight_grad.astype(jnp.bfloat16), ('row', 'nar'), s...  72 us
    reduce_scatter x1, waiting for transfers between devices, local(): lax.psum_scatter(contract_last(grad_gate_b, gate_full) + contract_last(gr...  67 us
  transfers between devices with their start and end apart: 24, of which 22 were waited for; matrix products, arithmetic and copies ran while one was open for 10% of the time, Pallas kernels for 0%

commit v1 on v0

--- a/solution.py
+++ b/solution.py
@@ -3,6 +3,8 @@
 import jax
 import jax.numpy as jnp
 from jax import lax
+from jax.experimental import pallas as pl
+from jax.experimental.pallas import tpu as pltpu
 from jax.sharding import PartitionSpec as P
 
 H = 32
@@ -390,6 +392,1271 @@
     )
 
 
+MESH = pl.DeviceIdType.MESH
+bf16 = jnp.bfloat16
+f32 = jnp.float32
+VMEM_LIMIT = 60 * 2**20
+
+
+def spot():
+    return lax.axis_index("row"), lax.axis_index("nar"), lax.axis_index("wid")
+
+
+def greet(partners):
+    barrier = pltpu.get_barrier_semaphore()
+    total = 0
+    for there, device in partners:
+        @pl.when(there)
+        def _():
+            pl.semaphore_signal(barrier, inc=1, device_id=device, device_id_type=MESH)
+
+        total = total + there.astype(jnp.int32)
+    pl.semaphore_wait(barrier, total)
+
+
+def line_partners(r, n, w, wid_count):
+    return [
+        (w < wid_count - 1, (r, n, jnp.minimum(w + 1, wid_count - 1))),
+        (w > 0, (r, n, jnp.maximum(w - 1, 0))),
+        (w >= 0, (1 - r, n, w)),
+    ]
+
+
+def each_rows(count, step, body):
+    def run(i, carry):
+        body(pl.ds(pl.multiple_of(i * step, step), step))
+        return carry
+
+    lax.fori_loop(0, count // step, run, 0)
+
+
+class Gather:
+    def __init__(self, buf, sems, me, wid_count):
+        self.buf, (self.up_s, self.dn_s, self.pt_s, self.got) = buf, sems
+        self.r, self.n, self.w = me
+        self.last = wid_count - 1
+        self.up = (self.r, self.n, jnp.minimum(self.w + 1, self.last))
+        self.dn = (self.r, self.n, jnp.maximum(self.w - 1, 0))
+        self.pt = (1 - self.r, self.n, self.w)
+
+    def copy(self, j, sem, device, row=None):
+        row = self.r if row is None else row
+        return pltpu.make_async_remote_copy(
+            self.buf.at[row, j],
+            self.buf.at[row, j],
+            sem.at[j],
+            self.got.at[row, j],
+            device_id=device,
+            device_id_type=MESH,
+        )
+
+    def pass_on(self, j, go_up, go_dn):
+        if go_up:
+            @pl.when(self.w < self.last)
+            def _():
+                self.copy(j, self.up_s, self.up).start()
+
+        if go_dn:
+            @pl.when(self.w > 0)
+            def _():
+                self.copy(j, self.dn_s, self.dn).start()
+
+        self.copy(j, self.pt_s, self.pt).start()
+
+    def own(self):
+        self.pass_on(self.w, True, True)
+
+    def arrive(self, row, j):
+        self.copy(j, self.pt_s, self.pt, row).wait_recv()
+
+    def step(self, k):
+        below, above = self.w - k, self.w + k
+
+        @pl.when(below >= 0)
+        def _():
+            self.arrive(self.r, below)
+            self.pass_on(below, True, False)
+
+        @pl.when(above <= self.last)
+        def _():
+            self.arrive(self.r, above)
+            self.pass_on(above, False, True)
+
+    def rest(self):
+        for j in range(self.last + 1):
+            self.arrive(1 - self.r, j)
+
+    def sent(self):
+        for j in range(self.last + 1):
+            @pl.when((j <= self.w) & (self.w < self.last))
+            def _():
+                self.copy(j, self.up_s, self.up).wait_send()
+
+            @pl.when((j >= self.w) & (self.w > 0))
+            def _():
+                self.copy(j, self.dn_s, self.dn).wait_send()
+
+            self.copy(j, self.pt_s, self.pt).wait_send()
+
+
+def gather_scratch(shard, width):
+    return [pltpu.VMEM((2, 4, shard, width), bf16)] + gather_sems()
+
+
+def gather_sems():
+    return [pltpu.SemaphoreType.DMA((4,))] * 3 + [pltpu.SemaphoreType.DMA((2, 4))]
+
+
+class Scatter:
+    def __init__(self, mine, theirs, bufs, sems, me, wid_count):
+        self.mine, self.theirs = mine, theirs
+        self.from_pt, self.from_up, self.from_dn = bufs
+        self.pt_s, self.pt_g, self.up_s, self.up_g, self.dn_s, self.dn_g = sems
+        self.r, self.n, self.w = me
+        self.last = wid_count - 1
+        self.up = (self.r, self.n, jnp.minimum(self.w + 1, self.last))
+        self.dn = (self.r, self.n, jnp.maximum(self.w - 1, 0))
+        self.pt = (1 - self.r, self.n, self.w)
+
+    def order(self, i):
+        low, high = (3, 0, 2, 1)[i], (0, 3, 1, 2)[i]
+        return jnp.where(self.w < 2, low, high)
+
+    def pair(self, s):
+        return pltpu.make_async_remote_copy(
+            self.theirs.at[s], self.from_pt.at[s], self.pt_s.at[s], self.pt_g.at[s],
+            device_id=self.pt, device_id_type=MESH,
+        )
+
+    def climb(self, s):
+        return pltpu.make_async_remote_copy(
+            self.mine.at[s], self.from_dn.at[s], self.up_s.at[s], self.up_g.at[s],
+            device_id=self.up, device_id_type=MESH,
+        )
+
+    def fall(self, s):
+        return pltpu.make_async_remote_copy(
+            self.mine.at[s], self.from_up.at[s], self.dn_s.at[s], self.dn_g.at[s],
+            device_id=self.dn, device_id_type=MESH,
+        )
+
+    def add(self, s, others):
+        def body(rows):
+            total = self.mine[s, rows, :].astype(f32)
+            for other in others:
+                total = total + other[s, rows, :].astype(f32)
+            self.mine[s, rows, :] = total.astype(bf16)
+
+        each_rows(self.mine.shape[1], 16, body)
+
+    def step(self, s):
+        self.pair(s).wait_recv()
+
+        @pl.when((s > self.w) & (self.w > 0))
+        def _():
+            self.climb(s).wait_recv()
+            self.add(s, (self.from_pt, self.from_dn))
+
+        @pl.when((s < self.w) & (self.w < self.last))
+        def _():
+            self.fall(s).wait_recv()
+            self.add(s, (self.from_pt, self.from_up))
+
+        @pl.when(((s > self.w) & (self.w == 0)) | ((s < self.w) & (self.w == self.last)))
+        def _():
+            self.add(s, (self.from_pt,))
+
+        @pl.when(s > self.w)
+        def _():
+            self.climb(s).start()
+
+        @pl.when(s < self.w)
+        def _():
+            self.fall(s).start()
+
+    def total(self, out):
+        w = self.w
+
+        def first(rows):
+            out[rows, :] = self.mine[w, rows, :].astype(f32) + self.from_pt[w, rows, :].astype(f32)
+
+        each_rows(out.shape[0], 16, first)
+
+        @pl.when(w > 0)
+        def _():
+            self.climb(w).wait_recv()
+
+            def more(rows):
+                out[rows, :] += self.from_dn[w, rows, :].astype(f32)
+
+            each_rows(out.shape[0], 16, more)
+
+        @pl.when(w < self.last)
+        def _():
+            self.fall(w).wait_recv()
+
+            def more(rows):
+                out[rows, :] += self.from_up[w, rows, :].astype(f32)
+
+            each_rows(out.shape[0], 16, more)
+
+    def sent(self):
+        for s in range(self.last + 1):
+            self.pair(s).wait_send()
+
+            @pl.when(s > self.w)
+            def _():
+                self.climb(s).wait_send()
+
+            @pl.when(s < self.w)
+            def _():
+                self.fall(s).wait_send()
+
+
+def scatter_bufs(shard, width):
+    return [pltpu.VMEM((4, shard, width), bf16)] * 3
+
+
+def scatter_sems():
+    return [pltpu.SemaphoreType.DMA((4,))] * 6
+
+
+def vmem():
+    return pl.BlockSpec(memory_space=pltpu.VMEM)
+
+
+def hbm():
+    return pl.BlockSpec(memory_space=pl.ANY)
+
+
+def comm_call(kernel, name, cid, out_shape, in_specs, out_specs, scratch, args, flops=0, sent=0):
+    return pl.pallas_call(
+        kernel,
+        out_shape=out_shape,
+        in_specs=in_specs,
+        out_specs=out_specs,
+        scratch_shapes=scratch,
+        compiler_params=pltpu.CompilerParams(
+            collective_id=cid, has_side_effects=True, vmem_limit_bytes=VMEM_LIMIT
+        ),
+        cost_estimate=pl.CostEstimate(flops=flops, bytes_accessed=sent, transcendentals=0),
+        name=name,
+    )(*args)
+
+
+def norm_rows(x, gain):
+    root = lax.rsqrt(jnp.mean(x * x, axis=-1, keepdims=True) + norm_eps)
+    return x * root * gain
+
+
+def turn(x, cosine, sine):
+    lane = lax.broadcasted_iota(jnp.int32, x.shape, 1)
+    swapped = jnp.where(lane % 64 < 32, pltpu.roll(x, 96, 1), pltpu.roll(x, 32, 1))
+    return x * cosine + swapped * sine
+
+
+def enter_kernel(hidden, gain, tab, rows_out, tabs_out, buf, up_s, dn_s, pt_s, got, tabs, tab_s, tab_g, out_s):
+    me = spot()
+    r, n, w = me
+    greet(line_partners(r, n, w, 4))
+    gather = Gather(buf, (up_s, dn_s, pt_s, got), me, 4)
+    tab_copy = pltpu.make_async_remote_copy(
+        tab, tabs.at[r], tab_s, tab_g, device_id=(1 - r, n, w), device_id_type=MESH
+    )
+
+    def body(rows):
+        buf[r, w, rows, :] = norm_rows(hidden[rows, :].astype(f32), gain[...]).astype(bf16)
+
+    each_rows(hidden.shape[0], 16, body)
+    gather.own()
+    tab_copy.start()
+
+    def keep(rows):
+        tabs[r, rows, :] = tab[rows, :]
+
+    each_rows(tab.shape[0], 16, keep)
+    for k in (1, 2, 3):
+        gather.step(k)
+    gather.rest()
+    out = pltpu.make_async_copy(buf, rows_out, out_s.at[0])
+    out.start()
+    tab_copy.wait_recv()
+    out_tab = pltpu.make_async_copy(tabs, tabs_out, out_s.at[1])
+    out_tab.start()
+    gather.sent()
+    tab_copy.wait_send()
+    out.wait()
+    out_tab.wait()
+
+
+def enter(hidden, gain, tab):
+    shard, width = hidden.shape
+    return comm_call(
+        enter_kernel, "enter", 1,
+        (
+            jax.ShapeDtypeStruct((2, 4, shard, width), bf16),
+            jax.ShapeDtypeStruct((2,) + tab.shape, f32),
+        ),
+        [vmem()] * 3, [hbm()] * 2,
+        gather_scratch(shard, width)
+        + [
+            pltpu.VMEM((2,) + tab.shape, f32),
+            pltpu.SemaphoreType.DMA(()),
+            pltpu.SemaphoreType.DMA(()),
+            pltpu.SemaphoreType.DMA((2,)),
+        ],
+        (hidden, gain, tab), flops=10**10, sent=10**8,
+    )
+
+
+def nar_device(r, n, w, by):
+    return (r, jnp.clip(n + by, 0, 3), w)
+
+
+def project_kernel(x, p1, tabs, q_out, kv_out, kv, s_s, s_g, out_s):
+    r, n, w = spot()
+    greet(
+        [
+            (n >= 1, nar_device(r, n, w, -1)),
+            (n >= 2, nar_device(r, n, w, -2)),
+            (n <= 2, nar_device(r, n, w, 1)),
+            (n <= 1, nar_device(r, n, w, 2)),
+        ]
+    )
+
+    def copy(row, slot, by):
+        return pltpu.make_async_remote_copy(
+            kv.at[row, 2], kv.at[row, slot], s_s.at[row, slot], s_g.at[row, slot],
+            device_id=nar_device(r, n, w, by), device_id_type=MESH,
+        )
+
+    lane = lax.broadcasted_iota(jnp.int32, (256, 128), 1)
+    weight = p1[:, :, 0:384].reshape(2048, 384)
+    for row in range(2):
+        def tile(i, carry):
+            rows = pl.ds(pl.multiple_of(i * 256, 256), 256)
+            cosine, sine = tabs[row, rows, 0:128], tabs[row, rows, 128:256]
+            pre = jnp.dot(x[row, rows, :], weight, preferred_element_type=f32)
+            q_out[row, rows, 0:128] = turn(pre[:, 0:128], cosine, sine).astype(bf16)
+            q_out[row, rows, 128:256] = turn(pre[:, 128:256], cosine, sine).astype(bf16)
+            both = pre[:, 256:384]
+            kv[row, 2, rows, :] = jnp.where(lane < 64, turn(both, cosine, sine), both).astype(bf16)
+            return carry
+
+        lax.fori_loop(0, 2, tile, 0)
+
+        @pl.when(n <= 2)
+        def _():
+            copy(row, 1, 1).start()
+
+        @pl.when(n <= 1)
+        def _():
+            copy(row, 0, 2).start()
+
+        for slot, least in ((1, 1), (0, 2)):
+            @pl.when(n < least)
+            def _():
+                kv[row, slot] = jnp.zeros((512, 128), bf16)
+
+    for row in range(2):
+        for slot, least, by in ((1, 1, 1), (0, 2, 2)):
+            @pl.when(n >= least)
+            def _():
+                copy(row, slot, by).wait_recv()
+
+    out = pltpu.make_async_copy(kv, kv_out, out_s)
+    out.start()
+    for row in range(2):
+        @pl.when(n <= 2)
+        def _():
+            copy(row, 1, 1).wait_send()
+
+        @pl.when(n <= 1)
+        def _():
+            copy(row, 0, 2).wait_send()
+
+    out.wait()
+
+
+def project(x, p1, tabs):
+    return comm_call(
+        project_kernel, "project", 2,
+        (
+            jax.ShapeDtypeStruct((2, 512, 256), bf16),
+            jax.ShapeDtypeStruct((2, 3, 512, 128), bf16),
+        ),
+        [vmem()] * 3, [vmem(), hbm()],
+        [
+            pltpu.VMEM((2, 3, 512, 128), bf16),
+            pltpu.SemaphoreType.DMA((2, 3)),
+            pltpu.SemaphoreType.DMA((2, 3)),
+            pltpu.SemaphoreType.DMA(()),
+        ],
+        (x, p1, tabs), flops=10**10, sent=10**7,
+    )
+
+
+KEYS = 256
+QUERIES = 128
+
+
+def stack_low(x):
+    lane = lax.broadcasted_iota(jnp.int32, (QUERIES, 128), 1)
+    zero = jnp.zeros((QUERIES, 128), x.dtype)
+    parts = []
+    for pair in range(2):
+        block = x[:, pair * 128 : pair * 128 + 128]
+        parts.append(jnp.where(lane < 64, block, zero))
+        parts.append(jnp.where(lane < 64, pltpu.roll(block, 64, 1), zero))
+    return jnp.concatenate(parts, axis=0)
+
+
+def stack_high(x):
+    lane = lax.broadcasted_iota(jnp.int32, (QUERIES, 128), 1)
+    zero = jnp.zeros((QUERIES, 128), x.dtype)
+    parts = []
+    for pair in range(2):
+        block = x[:, pair * 128 : pair * 128 + 128]
+        parts.append(jnp.where(lane >= 64, pltpu.roll(block, 64, 1), zero))
+        parts.append(jnp.where(lane >= 64, block, zero))
+    return jnp.concatenate(parts, axis=0)
+
+
+def unstack(x, low):
+    lane = lax.broadcasted_iota(jnp.int32, (QUERIES, 128), 1)
+    out = []
+    for pair in range(2):
+        even = x[2 * pair * QUERIES : (2 * pair + 1) * QUERIES]
+        odd = x[(2 * pair + 1) * QUERIES : (2 * pair + 2) * QUERIES]
+        if low:
+            out.append(jnp.where(lane < 64, even, pltpu.roll(odd, 64, 1)))
+        else:
+            out.append(jnp.where(lane < 64, pltpu.roll(even, 64, 1), odd))
+    return jnp.concatenate(out, axis=1)
+
+
+def allowed_tile(starts, tile, first_query):
+    key = lax.broadcasted_iota(jnp.int32, (QUERIES, KEYS), 1) + tile * KEYS
+    query = lax.broadcasted_iota(jnp.int32, (QUERIES, KEYS), 0) + first_query
+    start = jnp.concatenate([starts] * (KEYS // 128), axis=1)
+    ok = (key <= query) & (key.astype(f32) >= start)
+    return jnp.concatenate([ok] * 4, axis=0)
+
+
+def key_tiles(low, row, block):
+    first_query = 1024 + block * QUERIES
+    return low[row * 4 + block] // KEYS, first_query // KEYS + 1, first_query
+
+
+def attend_kernel(low, q, kv, starts, out, lse):
+    row, block = pl.program_id(0), pl.program_id(1)
+    first, end, first_query = key_tiles(low, row, block)
+    query = stack_low(q[0].astype(f32)).astype(bf16)
+
+    def body(tile, carry):
+        top, total, acc = carry
+        both = kv[0, pl.ds(pl.multiple_of(tile * KEYS, KEYS), KEYS), :]
+        scores = contract_last(query, both) * 0.125
+        ok = allowed_tile(starts[0], tile, first_query)
+        scores = jnp.where(ok, scores, masked_score)
+        new_top = jnp.maximum(top, jnp.max(scores, axis=1, keepdims=True))
+        shrink = jnp.exp(top - new_top)
+        part = jnp.exp(scores - new_top)
+        total = total * shrink + jnp.sum(part, axis=1, keepdims=True)
+        acc = acc * shrink + jnp.dot(part.astype(bf16), both, preferred_element_type=f32)
+        return new_top, total, acc
+
+    top, total, acc = lax.fori_loop(
+        first, end, body,
+        (
+            jnp.full((4 * QUERIES, 1), masked_score, f32),
+            jnp.zeros((4 * QUERIES, 1), f32),
+            jnp.zeros((4 * QUERIES, 128), f32),
+        ),
+    )
+    out[0] = unstack(acc / total, False).astype(bf16)
+    lse[0, 0] = jnp.broadcast_to(top + jnp.log(total), (4 * QUERIES, 128))
+
+
+def attend_specs():
+    return [
+        pl.BlockSpec((1, QUERIES, 256), lambda i, j, low: (i, j, 0)),
+        pl.BlockSpec((1, 1536, 128), lambda i, j, low: (i, 0, 0)),
+        pl.BlockSpec((1, QUERIES, 128), lambda i, j, low: (i, j, 2)),
+    ]
+
+
+def attend(low, q, kv, tabs):
+    return pl.pallas_call(
+        attend_kernel,
+        out_shape=(
+            jax.ShapeDtypeStruct((2, 512, 256), bf16),
+            jax.ShapeDtypeStruct((2, 4, 4 * QUERIES, 128), f32),
+        ),
+        grid_spec=pltpu.PrefetchScalarGridSpec(
+            num_scalar_prefetch=1, grid=(2, 4),
+            in_specs=attend_specs(),
+            out_specs=[
+                pl.BlockSpec((1, QUERIES, 256), lambda i, j, low: (i, j, 0)),
+                pl.BlockSpec((1, 1, 4 * QUERIES, 128), lambda i, j, low: (i, j, 0, 0)),
+            ],
+        ),
+        compiler_params=pltpu.CompilerParams(vmem_limit_bytes=VMEM_LIMIT),
+        cost_estimate=pl.CostEstimate(flops=2 * 10**10, bytes_accessed=10**7, transcendentals=10**7),
+        name="attend",
+    )(low, q, kv, tabs)
+
+
+def attend_back_kernel(low, q, kv, starts, turns, att, grad, lse, dq_out, dkv_out, dkv):
+    row, block = pl.program_id(0), pl.program_id(1)
+    first, end, first_query = key_tiles(low, row, block)
+
+    @pl.when(block == 0)
+    def _():
+        dkv[...] = jnp.zeros_like(dkv)
+
+    query = stack_low(q[0].astype(f32)).astype(bf16)
+    grads = stack_high(grad[0].astype(f32))
+    inner = jnp.sum(grads * stack_high(att[0].astype(f32)), axis=1, keepdims=True)
+    grads = grads.astype(bf16)
+    logsum = jnp.concatenate([lse[0, 0]] * (KEYS // 128), axis=1)
+
+    def body(tile, dq):
+        rows = pl.ds(pl.multiple_of(tile * KEYS, KEYS), KEYS)
+        both = kv[0, rows, :]
+        ok = allowed_tile(starts[0], tile, first_query)
+        scores = contract_last(query, both) * 0.125
+        prob = jnp.where(ok, jnp.exp(scores - logsum), 0.0)
+        grad_prob = contract_last(grads, both)
+        grad_scores = (prob * (grad_prob - inner)).astype(bf16)
+        dkv[rows, :] += contract_first(grad_scores, query) * 0.125 + contract_first(
+            prob.astype(bf16), grads
+        )
+        return dq + jnp.dot(grad_scores, both, preferred_element_type=f32)
+
+    dq = lax.fori_loop(first, end, body, jnp.zeros((4 * QUERIES, 128), f32))
+    flat = unstack(dq, True) * 0.125
+    cosine, sine = turns[0, :, 0:128], -turns[0, :, 128:256]
+    dq_out[0, :, 0:128] = turn(flat[:, 0:128], cosine, sine).astype(bf16)
+    dq_out[0, :, 128:256] = turn(flat[:, 128:256], cosine, sine).astype(bf16)
+
+    @pl.when(block == 3)
+    def _():
+        dkv_out[0] = dkv[...]
+
+
+def attend_back(low, q, kv, tabs, att, grad, lse):
+    tile = pl.BlockSpec((1, QUERIES, 256), lambda i, j, low: (i, j, 0))
+    return pl.pallas_call(
+        attend_back_kernel,
+        out_shape=(
+            jax.ShapeDtypeStruct((2, 512, 256), bf16),
+            jax.ShapeDtypeStruct((2, 1536, 128), f32),
+        ),
+        grid_spec=pltpu.PrefetchScalarGridSpec(
+            num_scalar_prefetch=1, grid=(2, 4),
+            in_specs=attend_specs()
+            + [tile, tile, tile, pl.BlockSpec((1, 1, 4 * QUERIES, 128), lambda i, j, low: (i, j, 0, 0))],
+            out_specs=[tile, pl.BlockSpec((1, 1536, 128), lambda i, j, low: (i, 0, 0))],
+            scratch_shapes=[pltpu.VMEM((1536, 128), f32)],
+        ),
+        compiler_params=pltpu.CompilerParams(vmem_limit_bytes=VMEM_LIMIT),
+        cost_estimate=pl.CostEstimate(flops=4 * 10**10, bytes_accessed=10**7, transcendentals=10**7),
+        name="attend_back",
+    )(low, q, kv, tabs, tabs, att, grad, lse)
+
+
+def out_block(p1, nn, half):
+    return p1[nn, half * 256 : half * 256 + 256, 384:640]
+
+
+def middle_kernel(
+    att, p1, hidden, gain, grad_top, mid_out, ffn_out, grad_out,
+    theirs, mine, from_pt, from_up, from_dn, s0, s1, s2, s3, s4, s5,
+    gbuf, g0, g1, g2, g3, fbuf, h0, h1, h2, h3, out_s,
+):
+    me = spot()
+    r, n, w = me
+    greet(line_partners(r, n, w, 4))
+    scatter = Scatter(
+        mine, theirs, (from_pt, from_up, from_dn), (s0, s1, s2, s3, s4, s5), me, 4
+    )
+    tops = Gather(gbuf, (g0, g1, g2, g3), me, 4)
+    ffn = Gather(fbuf, (h0, h1, h2, h3), me, 4)
+
+    def keep(rows):
+        gbuf[r, w, rows, :] = grad_top[rows, :]
+
+    each_rows(grad_top.shape[0], 16, keep)
+    for i in range(4):
+        s = scatter.order(i)
+        rows = pl.ds(pl.multiple_of(s * 128, 128), 128)
+        left = jnp.concatenate([att[1 - r, rows, :], att[r, rows, :]], axis=0)
+        for nn in range(4):
+            for half in range(2):
+                part = jnp.dot(left, out_block(p1, nn, half), preferred_element_type=f32).astype(bf16)
+                columns = slice(nn * 512 + half * 256, nn * 512 + half * 256 + 256)
+                theirs[s, :, columns] = part[0:128]
+                mine[s, :, columns] = part[128:256]
+        scatter.pair(s).start()
+    for i in range(4):
+        scatter.step(scatter.order(i))
+        if i == 0:
+            tops.own()
+        else:
+            tops.step(i)
+    scatter.total(mid_out)
+
+    def body(rows):
+        middle = mid_out[rows, :] + hidden[rows, :].astype(f32)
+        mid_out[rows, :] = middle
+        fbuf[r, w, rows, :] = norm_rows(middle, gain[...]).astype(bf16)
+
+    each_rows(hidden.shape[0], 16, body)
+    ffn.own()
+    tops.rest()
+    out_g = pltpu.make_async_copy(gbuf, grad_out, out_s.at[0])
+    out_g.start()
+    for k in (1, 2, 3):
+        ffn.step(k)
+    ffn.rest()
+    out_f = pltpu.make_async_copy(fbuf, ffn_out, out_s.at[1])
+    out_f.start()
+    scatter.sent()
+    tops.sent()
+    ffn.sent()
+    out_g.wait()
+    out_f.wait()
+
+
+def middle_stage(att, p1, hidden, gain, grad_top):
+    shard, width = hidden.shape
+    rows = jax.ShapeDtypeStruct((2, 4, shard, width), bf16)
+    return comm_call(
+        middle_kernel, "middle", 3,
+        (jax.ShapeDtypeStruct((shard, width), f32), rows, rows),
+        [vmem()] * 5, [vmem(), hbm(), hbm()],
+        [pltpu.VMEM((4, shard, width), bf16)] * 2
+        + scatter_bufs(shard, width) + scatter_sems()
+        + gather_scratch(shard, width) + gather_scratch(shard, width)
+        + [pltpu.SemaphoreType.DMA((2,))],
+        (att, p1, hidden, gain, grad_top), flops=10**10, sent=2 * 10**8,
+    )
+
+
+def ffn_kernel(
+    x, tops, p2, gain, part_out, sum_out, gain_out, grads_out,
+    theirs, mine, from_pt, from_up, from_dn, s0, s1, s2, s3, s4, s5,
+    act, dgu, stage, wide, out_s, give_s, give_g, keep_s,
+):
+    me = spot()
+    r, n, w = me
+    greet(line_partners(r, n, w, 4))
+    scatter = Scatter(
+        mine, theirs, (from_pt, from_up, from_dn), (s0, s1, s2, s3, s4, s5), me, 4
+    )
+    gain_out[...] = jnp.zeros_like(gain_out)
+
+    def put(s, slot, row_slot, row):
+        return pltpu.make_async_copy(
+            stage.at[slot, row_slot], part_out.at[row, s], out_s.at[slot, row_slot]
+        )
+
+    for i in range(4):
+        s = scatter.order(i)
+        slot = i % 2
+        rows_t = pl.ds(pl.multiple_of((1 - r) * 512 + s * 128, 128), 128)
+        rows_m = pl.ds(pl.multiple_of(r * 512 + s * 128, 128), 128)
+        if i >= 2:
+            put(s, slot, 0, 1 - r).wait()
+            put(s, slot, 1, r).wait()
+
+        def hidden_tile(ft, carry):
+            columns = pl.ds(pl.multiple_of(ft * 256, 256), 256)
+            left = jnp.concatenate([x[rows_t, :], x[rows_m, :]], axis=0)
+            gate = jnp.dot(left, p2[:, 0, :, columns].reshape(2048, 256), preferred_element_type=f32)
+            up = jnp.dot(left, p2[:, 1, :, columns].reshape(2048, 256), preferred_element_type=f32)
+            sig = 1.0 / (1.0 + jnp.exp(-gate))
+            silu = gate * sig
+            active = (silu * up).astype(bf16)
+            act[rows_t, columns] = active[0:128]
+            act[rows_m, columns] = active[128:256]
+            f_rows = pl.ds(pl.multiple_of((ft % 2) * 256, 256), 256)
+            f_cols = pl.ds(pl.multiple_of((ft // 2) * 512, 512), 512)
+            right = jnp.concatenate([p2[nn, 2, f_rows, f_cols] for nn in range(4)], axis=1)
+            top = jnp.concatenate([tops[rows_t, :], tops[rows_m, :]], axis=0)
+            dact = contract_last(top, right)
+            dgate = (dact * up * (sig * (1.0 + gate * (1.0 - sig)))).astype(bf16)
+            dup = (dact * silu).astype(bf16)
+            dgu[rows_t, columns] = dgate[0:128]
+            dgu[rows_m, columns] = dgate[128:256]
+            later = pl.ds(pl.multiple_of(1024 + ft * 256, 256), 256)
+            dgu[rows_t, later] = dup[0:128]
+            dgu[rows_m, later] = dup[128:256]
+            return carry
+
+        lax.fori_loop(0, 4, hidden_tile, 0)
+
+        def model_tile(dt, carry):
+            nn, half = dt // 2, dt % 2
+            columns = pl.ds(pl.multiple_of(dt * 256, 256), 256)
+            inner = pl.ds(pl.multiple_of(half * 256, 256), 256)
+            other = pl.ds(pl.multiple_of(512 + half * 256, 256), 256)
+            left = jnp.concatenate([dgu[rows_t, :], dgu[rows_m, :]], axis=0)
+            right = jnp.concatenate([p2[nn, 0, inner, :], p2[nn, 1, inner, :]], axis=1)
+            part = contract_last(left, right)
+            seen = jnp.concatenate([x[rows_t, columns], x[rows_m, columns]], axis=0)
+            terms = part * seen.astype(f32)
+            gain_out[:, columns] += jnp.sum(terms.reshape(32, 8, 256), axis=0)
+            part = part.astype(bf16)
+            theirs[s, :, columns] = part[0:128]
+            mine[s, :, columns] = part[128:256]
+            left = jnp.concatenate([act[rows_t, :], act[rows_m, :]], axis=0)
+            right = jnp.concatenate([p2[nn, 2, :, inner], p2[nn, 2, :, other]], axis=0)
+            part = jnp.dot(left, right, preferred_element_type=f32).astype(bf16)
+            stage[slot, 0, :, columns] = part[0:128]
+            stage[slot, 1, :, columns] = part[128:256]
+            return carry
+
+        lax.fori_loop(0, 8, model_tile, 0)
+        scatter.pair(s).start()
+        put(s, slot, 0, 1 - r).start()
+        put(s, slot, 1, r).start()
+
+    def scale(rows):
+        gain_out[rows, :] = gain_out[rows, :] / gain[...]
+
+    each_rows(8, 8, scale)
+
+    def give(which, half):
+        return pltpu.make_async_remote_copy(
+            wide.at[which % 2, half],
+            grads_out.at[:, which, :, pl.ds(pl.multiple_of(r * 1024, 1024), 1024)],
+            give_s.at[which], give_g.at[which],
+            device_id=(1 - r, n, w), device_id_type=MESH,
+        )
+
+    def keep(which):
+        return pltpu.make_async_copy(
+            wide.at[which % 2, 1],
+            grads_out.at[:, which, :, pl.ds(pl.multiple_of(r * 1024, 1024), 1024)],
+            keep_s.at[which],
+        )
+
+    for which in range(3):
+        scatter.step(scatter.order(which))
+        if which == 2:
+            give(0, 0).wait_send()
+            keep(0).wait()
+        for half in range(2):
+            d_first = (jnp.where(half == 0, 1 - r, r)) * 1024
+
+            def weight_tile(i, carry):
+                d_rows = pl.ds(pl.multiple_of(d_first + i * 256, 256), 256)
+                source = x if which < 2 else tops
+                left = source[:, d_rows]
+                if which < 2:
+                    right = dgu[:, which * 1024 : which * 1024 + 1024]
+                else:
+                    right = act[...]
+                wide[which % 2, half, i] = contract_first(left, right).astype(bf16)
+                return carry
+
+            lax.fori_loop(0, 4, weight_tile, 0)
+            if half == 0:
+                give(which, 0).start()
+            else:
+                keep(which).start()
+    scatter.step(scatter.order(3))
+    scatter.total(sum_out)
+    scatter.sent()
+    for which in range(3):
+        give(which, 0).wait_recv()
+        if which > 0:
+            give(which, 0).wait_send()
+            keep(which).wait()
+    for slot in range(2):
+        put(0, slot, 0, 1 - r).wait()
+        put(0, slot, 1, r).wait()
+
+
+def ffn_stage(x, tops, p2, gain):
+    shard, width = 128, 2048
+    return comm_call(
+        ffn_kernel, "ffn", 4,
+        (
+            jax.ShapeDtypeStruct((2, 4, shard, width), bf16),
+            jax.ShapeDtypeStruct((shard, width), f32),
+            jax.ShapeDtypeStruct((8, width), f32),
+            jax.ShapeDtypeStruct((4, 3, 256, width), bf16),
+        ),
+        [vmem()] * 4, [hbm(), vmem(), vmem(), hbm()],
+        [pltpu.VMEM((4, shard, width), bf16)] * 2
+        + scatter_bufs(shard, width) + scatter_sems()
+        + [
+            pltpu.VMEM((1024, 1024), bf16),
+            pltpu.VMEM((1024, 2048), bf16),
+            pltpu.VMEM((2, 2, shard, width), bf16),
+            pltpu.VMEM((2, 2, 4, 256, 1024), bf16),
+            pltpu.SemaphoreType.DMA((2, 2)),
+            pltpu.SemaphoreType.DMA((3,)),
+            pltpu.SemaphoreType.DMA((3,)),
+            pltpu.SemaphoreType.DMA((3,)),
+        ],
+        (x, tops, p2, gain), flops=4 * 10**10, sent=10**8,
+    )
+
+
+def norm_back(values, gain, grad):
+    root = lax.rsqrt(jnp.mean(values * values, axis=-1, keepdims=True) + norm_eps)
+    weighted = grad * gain
+    inner = jnp.mean(weighted * values, axis=-1, keepdims=True)
+    return root * weighted - values * (root * root * root) * inner
+
+
+def branch_kernel(
+    total, mid, grad_top, gain, parts, p1, att, hid_out, gmid_out, datt_out, go_out,
+    mine, from_pt, from_up, from_dn, s0, s1, s2, s3, s4, s5,
+    buf, g0, g1, g2, g3, acc, wide, give_s, give_g, keep_s,
+):
+    me = spot()
+    r, n, w = me
+    greet(line_partners(r, n, w, 4))
+    scatter = Scatter(
+        mine, parts.at[1 - r], (from_pt, from_up, from_dn), (s0, s1, s2, s3, s4, s5), me, 4
+    )
+    gather = Gather(buf, (g0, g1, g2, g3), me, 4)
+
+    def body(rows):
+        grad = norm_back(mid[rows, :], gain[...], total[rows, :]) + grad_top[rows, :].astype(f32)
+        gmid_out[rows, :] = grad
+        buf[r, w, rows, :] = grad.astype(bf16)
+
+    each_rows(mid.shape[0], 16, body)
+    gather.own()
+    for i in range(4):
+        scatter.pair(scatter.order(i)).start()
+
+    for s in range(4):
+        def fill(rows):
+            mine[s, rows, :] = parts[r, s, rows, :]
+
+        each_rows(128, 16, fill)
+    for i in range(4):
+        scatter.step(scatter.order(i))
+        if i < 3:
+            gather.step(i + 1)
+    gather.rest()
+    for row in range(2):
+        for pair in range(2):
+            left = jnp.concatenate([buf[row, 2 * pair], buf[row, 2 * pair + 1]], axis=0)
+            right = jnp.concatenate(
+                [out_block(p1, nn, half) for nn in range(4) for half in range(2)], axis=1
+            )
+            datt_out[row, pair * 256 : pair * 256 + 256, :] = contract_last(left, right).astype(bf16)
+
+    give = pltpu.make_async_remote_copy(
+        wide.at[0], go_out.at[:, pl.ds(pl.multiple_of(r * 256, 256), 256)], give_s, give_g,
+        device_id=(1 - r, n, w), device_id_type=MESH,
+    )
+    keep = pltpu.make_async_copy(
+        wide.at[1], go_out.at[:, pl.ds(pl.multiple_of(r * 256, 256), 256)], keep_s
+    )
+    for half in range(2):
+        d_first = (jnp.where(half == 0, 1 - r, r)) * 1024
+
+        def weight_tile(i, carry):
+            columns = pl.ds(pl.multiple_of(d_first + i * 256, 256), 256)
+            left = buf[:, :, :, columns].reshape(1024, 256)
+            wide[half, pl.ds(pl.multiple_of(i * 256, 256), 256), :] = contract_first(
+                left, att[...]
+            ).astype(bf16)
+            return carry
+
+        lax.fori_loop(0, 4, weight_tile, 0)
+        if half == 0:
+            give.start()
+        else:
+            keep.start()
+    scatter.total(acc)
+
+    def last(rows):
+        hid_out[rows, :] = (acc[rows, :] + mid[rows, :]).astype(bf16)
+
+    each_rows(mid.shape[0], 16, last)
+    scatter.sent()
+    gather.sent()
+    give.wait()
+    keep.wait()
+
+
+def branch_stage(total, mid, grad_top, gain, parts, p1, att):
+    shard, width = mid.shape
+    return comm_call(
+        branch_kernel, "branch", 5,
+        (
+            jax.ShapeDtypeStruct((shard, width), bf16),
+            jax.ShapeDtypeStruct((shard, width), f32),
+            jax.ShapeDtypeStruct((2, 512, 256), bf16),
+            jax.ShapeDtypeStruct((1024, 512), bf16),
+        ),
+        [vmem()] * 7, [vmem(), vmem(), vmem(), hbm()],
+        [pltpu.VMEM((4, shard, width), bf16)]
+        + scatter_bufs(shard, width) + scatter_sems()
+        + gather_scratch(shard, width)
+        + [
+            pltpu.VMEM((shard, width), f32),
+            pltpu.VMEM((2, 1024, 256), bf16),
+            pltpu.SemaphoreType.DMA(()),
+            pltpu.SemaphoreType.DMA(()),
+            pltpu.SemaphoreType.DMA(()),
+        ],
+        (total, mid, grad_top, gain, parts, p1, att), flops=10**10, sent=10**8,
+    )
+
+
+def unproject_kernel(
+    dq, dkv, x, p1, tabs, gain, part_out, gain_out, gq_out, gkv_out,
+    send, recv, both, wide_q, wide_kv, s_s, s_g, q_s, q_g, kv_s, kv_g, keep_s,
+):
+    r, n, w = spot()
+    greet(
+        [
+            (n >= 1, nar_device(r, n, w, -1)),
+            (n >= 2, nar_device(r, n, w, -2)),
+            (n <= 2, nar_device(r, n, w, 1)),
+            (n <= 1, nar_device(r, n, w, 2)),
+            (n >= 0, (1 - r, n, w)),
+        ]
+    )
+
+    def copy(row, slot, by):
+        return pltpu.make_async_remote_copy(
+            send.at[row, slot], recv.at[row, slot], s_s.at[row, slot], s_g.at[row, slot],
+            device_id=nar_device(r, n, w, by), device_id_type=MESH,
+        )
+
+    for row in range(2):
+        for slot, by in ((1, -1), (0, -2)):
+            @pl.when(n >= -by)
+            def _():
+                send[row, slot] = dkv[row, slot].astype(bf16)
+                copy(row, slot, by).start()
+
+    partner = (1 - r, n, w)
+    give_q = pltpu.make_async_remote_copy(
+        wide_q.at[0], gq_out.at[:, pl.ds(pl.multiple_of(r * 256, 256), 256)], q_s, q_g,
+        device_id=partner, device_id_type=MESH,
+    )
+    keep_q = pltpu.make_async_copy(
+        wide_q.at[1], gq_out.at[:, pl.ds(pl.multiple_of(r * 256, 256), 256)], keep_s.at[0]
+    )
+    give_kv = pltpu.make_async_remote_copy(
+        wide_kv.at[0], gkv_out.at[:, pl.ds(pl.multiple_of(r * 128, 128), 128)], kv_s, kv_g,
+        device_id=partner, device_id_type=MESH,
+    )
+    keep_kv = pltpu.make_async_copy(
+        wide_kv.at[1], gkv_out.at[:, pl.ds(pl.multiple_of(r * 128, 128), 128)], keep_s.at[1]
+    )
+
+    for row in range(2):
+        both[row * 512 : row * 512 + 512, 0:256] = dq[row]
+
+    def weight(half, columns, wide):
+        d_first = (jnp.where(half == 0, 1 - r, r)) * 1024
+
+        def tile(i, carry):
+            d_cols = pl.ds(pl.multiple_of(d_first + i * 256, 256), 256)
+            wide[half, pl.ds(pl.multiple_of(i * 256, 256), 256), :] = contract_first(
+                x[:, d_cols], both[:, columns]
+            ).astype(bf16)
+            return carry
+
+        lax.fori_loop(0, 4, tile, 0)
+
+    weight(0, slice(0, 256), wide_q)
+    give_q.start()
+    weight(1, slice(0, 256), wide_q)
+    keep_q.start()
+    lane = lax.broadcasted_iota(jnp.int32, (128, 128), 1)
+    for row in range(2):
+        for slot, by in ((1, -1), (0, -2)):
+            @pl.when(n <= 3 + by)
+            def _():
+                copy(row, slot, by).wait_recv()
+
+        def tile(i, carry):
+            rows = pl.ds(pl.multiple_of(i * 128, 128), 128)
+            total = dkv[row, 2, rows, :]
+            zero = jnp.zeros_like(total)
+            total = total + jnp.where(n <= 2, recv[row, 1, rows, :].astype(f32), zero)
+            total = total + jnp.where(n <= 1, recv[row, 0, rows, :].astype(f32), zero)
+            turned = turn(total, tabs[row, rows, 0:128], -tabs[row, rows, 128:256])
+            both[pl.ds(pl.multiple_of(row * 512 + i * 128, 128), 128), 256:384] = jnp.where(
+                lane < 64, turned, total
+            ).astype(bf16)
+            return carry
+
+        lax.fori_loop(0, 4, tile, 0)
+    weight(0, slice(256, 384), wide_kv)
+    give_kv.start()
+    weight(1, slice(256, 384), wide_kv)
+    keep_kv.start()
+    gain_out[...] = jnp.zeros_like(gain_out)
+
+    def model_tile(dt, carry):
+        nn, half = dt // 2, dt % 2
+        columns = pl.ds(pl.multiple_of(dt * 256, 256), 256)
+        inner = pl.ds(pl.multiple_of(half * 256, 256), 256)
+        right = p1[nn, inner, 0:384]
+        for row in range(2):
+            for block in range(2):
+                first = row * 512 + block * 256
+                part = contract_last(both[first : first + 256, :], right)
+                terms = part * x[first : first + 256, columns].astype(f32)
+                gain_out[:, columns] += jnp.sum(terms.reshape(32, 8, 256), axis=0)
+                part_out[row, 2 * block, :, columns] = part[0:128].astype(bf16)
+                part_out[row, 2 * block + 1, :, columns] = part[128:256].astype(bf16)
+        return carry
+
+    lax.fori_loop(0, 8, model_tile, 0)
+    gain_out[...] = gain_out[...] / gain[...]
+    for row in range(2):
+        for slot, by in ((1, -1), (0, -2)):
+            @pl.when(n >= -by)
+            def _():
+                copy(row, slot, by).wait_send()
+
+    give_q.wait()
+    keep_q.wait()
+    give_kv.wait()
+    keep_kv.wait()
+
+
+def unproject(dq, dkv, x, p1, tabs, gain):
+    return comm_call(
+        unproject_kernel, "unproject", 6,
+        (
+            jax.ShapeDtypeStruct((2, 4, 128, 2048), bf16),
+            jax.ShapeDtypeStruct((8, 2048), f32),
+            jax.ShapeDtypeStruct((1024, 512), bf16),
+            jax.ShapeDtypeStruct((1024, 256), bf16),
+        ),
+        [vmem()] * 6, [vmem(), vmem(), hbm(), hbm()],
+        [
+            pltpu.VMEM((2, 2, 512, 128), bf16),
+            pltpu.VMEM((2, 2, 512, 128), bf16),
+            pltpu.VMEM((1024, 384), bf16),
+            pltpu.VMEM((2, 1024, 256), bf16),
+            pltpu.VMEM((2, 1024, 128), bf16),
+            pltpu.SemaphoreType.DMA((2, 2)),
+            pltpu.SemaphoreType.DMA((2, 2)),
+            pltpu.SemaphoreType.DMA(()),
+            pltpu.SemaphoreType.DMA(()),
+            pltpu.SemaphoreType.DMA(()),
+            pltpu.SemaphoreType.DMA(()),
+            pltpu.SemaphoreType.DMA((2,)),
+        ],
+        (dq, dkv, x, p1, tabs, gain), flops=10**10, sent=10**7,
+    )
+
+
+def leave_kernel(
+    parts, hidden, gain, gmid, gains, grad_out, ga_out,
+    mine, from_pt, from_up, from_dn, s0, s1, s2, s3, s4, s5,
+    acc, over_wid, summed, over_rest, w_s, w_g, t_s, t_g,
+):
+    me = spot()
+    r, n, w = me
+    partners = [(w != j, (r, n, jnp.int32(j))) for j in range(4)]
+    partners += [
+        ((r != a) | (n != b), (jnp.int32(a), jnp.int32(b), w)) for a in range(2) for b in range(4)
+    ]
+    greet(partners)
+    scatter = Scatter(
+        mine, parts.at[1 - r], (from_pt, from_up, from_dn), (s0, s1, s2, s3, s4, s5), me, 4
+    )
+    for i in range(4):
+        scatter.pair(scatter.order(i)).start()
+
+    def wid_copy(j, slot):
+        return pltpu.make_async_remote_copy(
+            gains, over_wid.at[slot], w_s.at[j], w_g.at[slot],
+            device_id=(r, n, jnp.int32(j)), device_id_type=MESH,
+        )
+
+    def rest_copy(a, b, slot):
+        return pltpu.make_async_remote_copy(
+            summed, over_rest.at[slot], t_s.at[a * 4 + b], t_g.at[slot],
+            device_id=(jnp.int32(a), jnp.int32(b), w), device_id_type=MESH,
+        )
+
+    for j in range(4):
+        @pl.when(w != j)
+        def _():
+            wid_copy(j, w).start()
+
+    for s in range(4):
+        def fill(rows):
+            mine[s, rows, :] = parts[r, s, rows, :]
+
+        each_rows(128, 16, fill)
+    scatter.step(scatter.order(0))
+    summed[...] = gains[...]
+    for j in range(4):
+        @pl.when(w != j)
+        def _():
+            wid_copy(j, j).wait_recv()
+            summed[...] += over_wid[j]
+
+    for a in range(2):
+        for b in range(4):
+            @pl.when((r != a) | (n != b))
+            def _():
+                rest_copy(a, b, r * 4 + n).start()
+
+    for i in (1, 2, 3):
+        scatter.step(scatter.order(i))
+    mine_block = r * 4 + n
+    ga_out[0:1] = summed[pl.ds(mine_block, 1), :]
+    ga_out[1:2] = summed[pl.ds(mine_block + 8, 1), :]
+    for a in range(2):
+        for b in range(4):
+            @pl.when((r != a) | (n != b))
+            def _():
+                slot = a * 4 + b
+                rest_copy(a, b, slot).wait_recv()
+                ga_out[0:1] += over_rest[slot, pl.ds(mine_block, 1), :]
+                ga_out[1:2] += over_rest[slot, pl.ds(mine_block + 8, 1), :]
+
+    scatter.total(acc)
+
+    def last(rows):
+        grad = norm_back(hidden[rows, :].astype(f32), gain[...], acc[rows, :])
+        grad_out[rows, :] = (grad + gmid[rows, :]).astype(bf16)
+
+    each_rows(hidden.shape[0], 16, last)
+    scatter.sent()
+    for j in range(4):
+        @pl.when(w != j)
+        def _():
+            wid_copy(j, w).wait_send()
+
+    for a in range(2):
+        for b in range(4):
+            @pl.when((r != a) | (n != b))
+            def _():
+                rest_copy(a, b, r * 4 + n).wait_send()
+
+
+def leave(parts, hidden, gain, gmid, gains):
+    shard, width = hidden.shape
+    return comm_call(
+        leave_kernel, "leave", 7,
+        (jax.ShapeDtypeStruct((shard, width), bf16), jax.ShapeDtypeStruct((8, 256), f32)),
+        [vmem()] * 5, [vmem()] * 2,
+        [pltpu.VMEM((4, shard, width), bf16)]
+        + scatter_bufs(shard, width) + scatter_sems()
+        + [
+            pltpu.VMEM((shard, width), f32),
+            pltpu.VMEM((4, 16, 256), f32),
+            pltpu.VMEM((16, 256), f32),
+            pltpu.VMEM((8, 16, 256), f32),
+            pltpu.SemaphoreType.DMA((4,)),
+            pltpu.SemaphoreType.DMA((4,)),
+            pltpu.SemaphoreType.DMA((8,)),
+            pltpu.SemaphoreType.DMA((8,)),
+        ],
+        (parts, hidden, gain, gmid, gains), flops=10**10, sent=10**8,
+    )
+
+
+def local_fast(
+    hidden_in, doc_lengths, w_query, w_key, w_value, w_output, w_gate, w_up, w_down,
+    gain_attn, gain_ffn, grad_out,
+):
+    r, n, w = spot()
+    hidden, grad_top = hidden_in[0], grad_out[0]
+    gain_a, gain_f = gain_attn[None], gain_ffn[None]
+    def half(weight, axis):
+        size = weight.shape[axis] // 2
+        return lax.dynamic_slice_in_dim(weight, r * size, size, axis)
+
+    head = (w * 2 + r) * HD
+    kv_pack = jnp.concatenate(
+        [lax.dynamic_slice_in_dim(w_key, head, HD, 1), lax.dynamic_slice_in_dim(w_value, head, HD, 1)],
+        axis=1,
+    )
+    out_half = half(w_output, 0)
+    p1_shard = jnp.concatenate(
+        [half(w_query, 1), kv_pack, jnp.concatenate([out_half[:, :256], out_half[:, 256:]], axis=0)],
+        axis=1,
+    )
+    down_half = half(w_down, 0)
+    p2_shard = jnp.stack(
+        [
+            half(w_gate, 1),
+            half(w_up, 1),
+            jnp.concatenate([down_half[:512], down_half[512:]], axis=1),
+        ]
+    )
+    p1 = lax.all_gather(p1_shard, "nar", axis=0)
+    p2 = lax.all_gather(p2_shard, "nar", axis=0)
+
+    token_ids = n * 512 + jnp.arange(512, dtype=jnp.int32)
+    doc_start, places = doc_layout(doc_lengths[0], token_ids)
+    angles = places.astype(f32)[:, None] * inverse_freq()[None, :]
+    cosine, sine = jnp.cos(angles), jnp.sin(angles)
+    start_here = (doc_start - (n - 2) * 512).astype(f32)
+    tab = jnp.concatenate(
+        [cosine] * 4 + [-sine, sine] * 2 + [jnp.broadcast_to(start_here[:, None], (512, 128))],
+        axis=1,
+    )
+
+    rows, tabs = enter(hidden, gain_a, tab)
+    rows3, rows2 = rows.reshape(2, 512, 2048), rows.reshape(1024, 2048)
+    q, kv = project(rows3, p1, tabs)
+    low = tabs[:, ::QUERIES, 256].astype(jnp.int32).reshape(8)
+    kv_flat = kv.reshape(2, 1536, 128)
+    att, lse = attend(low, q, kv_flat, tabs)
+    mid, ffn_rows, top_rows = middle_stage(att, p1, hidden, gain_f, grad_top)
+    parts, total, gain_f_part, grads = ffn_stage(
+        ffn_rows.reshape(1024, 2048), top_rows.reshape(1024, 2048), p2, gain_f
+    )
+    summed = lax.psum_scatter(
+        grads.reshape(4 * 768, 2048), "nar", scatter_dimension=0, tiled=True
+    ).reshape(3, 256, 2048)
+    hidden_out, gmid, datt, grad_o = branch_stage(
+        total, mid, grad_top, gain_f, parts, p1, att.reshape(1024, 256)
+    )
+    dq, dkv = attend_back(low, q, kv_flat, tabs, att, datt, lse)
+    dparts, gain_a_part, grad_q, grad_kv = unproject(
+        dq, dkv.reshape(2, 3, 512, 128), rows2, p1, tabs, gain_a
+    )
+    small = lax.psum_scatter(
+        jnp.concatenate([grad_q, grad_o, grad_kv], axis=1), "nar", scatter_dimension=0, tiled=True
+    )
+    gains = jnp.concatenate(
+        [gain_f_part.sum(axis=0).reshape(8, 256), gain_a_part.sum(axis=0).reshape(8, 256)], axis=0
+    )
+    grad_in, gain_sums = leave(dparts, hidden, gain_a, gmid, gains)
+    kv_all = lax.all_gather(small[:, 1024:1280], "wid", axis=1, tiled=True)
+    kv_all = kv_all.astype(f32).reshape(256, KV, 2, HD)
+    return (
+        hidden_out[None],
+        grad_in[None],
+        small[:, 0:512].astype(f32),
+        kv_all[:, :, 0].reshape(256, KV * HD),
+        kv_all[:, :, 1].reshape(256, KV * HD),
+        small[:, 512:1024].T.astype(f32),
+        summed[0].astype(f32),
+        summed[1].astype(f32),
+        summed[2].T.astype(f32),
+        gain_sums[1],
+        gain_sums[0],
+    )
+
+
 def solution(mesh):
     in_specs = (
         P("row", ("nar", "wid"), None),
@@ -418,4 +1685,11 @@
         P(("row", "nar")),
         P(("row", "nar")),
     )
-    return jax.shard_map(local, mesh=mesh, in_specs=in_specs, out_specs=out_specs, check_vma=False)
+    sizes = dict(mesh.shape)
+    fits = sizes == {"row": 2, "nar": 4, "wid": 4}
+
+    def body(*args):
+        small = args[0].shape == (1, 128, 2048)
+        return (local_fast if fits and small else local)(*args)
+
+    return jax.shard_map(body, mesh=mesh, in_specs=in_specs, out_specs=out_specs, check_vma=False)

time: 1580 us -> 621 us (0.39)
  waiting for transfers between devices: 1090 us -> 74.2 us
  Pallas kernels: 0 us -> 462 us
  matrix products: 263 us -> 0 us
  blocking collectives: 80.2 us -> 16.1 us
  loops' own time: 43.3 us -> 0 us
  other arithmetic: 44.3 us -> 14.7 us
    all_gather x11 -> x2, waiting for transfers between devices: 507 us -> 0.02 us  [the longest x1 0.02 us: local_fast(): p2 = lax.all_gather(p2_shard, 'nar', axis=0)]
    reduce_scatter x13 -> x2, waiting for transfers between devices: 578 us -> 74.1 us  [the longest x1 74.1 us: local_fast(): lax.psum_scatter(grads.reshape(4 * 768, 2048), 'nar', scatter_dimension=0...]
    pallas_call x0 -> x9, Pallas kernels: none -> 462 us  [the longest x7 435 us: comm_call(): pl.pallas_call(kernel, out_shape=out_shape, in_specs=in_specs, out_specs=...]
    dot_general x77 -> x0, matrix products: 263 us -> none  [the longest x31 117 us: contract_last(): lax.dot_general(left_side, right_side, (((1,), (1,)), ((), ())), preferre...]
    all_gather x6 -> x1, blocking collectives: 65.5 us -> 16.1 us  [local_fast(): kv_all = lax.all_gather(small[:, 1024:1280], 'wid', axis=1, tiled=True)]
    another operation x2 -> x0, loops' own time: 43.3 us -> none  [the longest x1 27 us: local(): lax.scan(attend_back, (zero_grads, zero_grads), jnp.arange(item_count, dt...]
    convert_element_type x21 -> x4, other arithmetic: 24.6 us -> 6.58 us  [the longest x1 4.43 us: local_fast(): summed[2].T.astype(f32)]
    reshape x0 -> x4, local copies, waits for them, and re-layouts: none -> 17 us  [the longest x1 16.8 us: local_fast(): grads.reshape(4 * 768, 2048)]
  transfers between devices with their start and end apart: 24 -> 4, of which waited for: 22 -> 1; matrix products, arithmetic and copies ran while one was open for 10% -> 5% of each run, Pallas kernels for 0% -> 39%
where the time goes in v1:
time: 621 us; the launch traced here: 620 us
  Pallas kernels  462 us (74%)
  waiting for transfers between devices  74.2 us (12%)
  local copies, waits for them, and re-layouts  38.9 us (6%)
  blocking collectives  16.1 us (3%)
  other arithmetic  14.7 us (2%)
  between operations  14 us (2%)
    pallas_call x7, Pallas kernels, comm_call(): pl.pallas_call(kernel, out_shape=out_shape, in_specs=in_specs, out_specs=...  435 us
    reduce_scatter x1, waiting for transfers between devices, local_fast(): lax.psum_scatter(grads.reshape(4 * 768, 2048), 'nar', scatter_dimension=0...  74.1 us
    reshape x1, local copies, waits for them, and re-layouts, local_fast(): grads.reshape(4 * 768, 2048)  16.8 us
    all_gather x1, blocking collectives, local_fast(): kv_all = lax.all_gather(small[:, 1024:1280], 'wid', axis=1, tiled=True)  16.1 us
    pallas_call x1, Pallas kernels, attend_back(): pl.pallas_call(attend_back_kernel, out_shape=(jax.ShapeDtypeStruct((2, 51...  15.8 us
    unnamed x29, local copies, waits for them, and re-layouts  14.7 us
  transfers between devices with their start and end apart: 4, of which 1 were waited for; matrix products, arithmetic and copies ran while one was open for 5% of the time, Pallas kernels for 39%

profile of v1, /device:TPU:0, one launch (start us, length us, event | category | flops | bytes accessed | tf_op | source)
XLA Modules:
  0.0 620.3 jit_solution(14672254630102511839)
XLA Ops:
  7.2 0.0 copy-start
  7.2 0.0 copy-start.6
  7.2 0.0 all-gather.5.cloned.1.call-start
  7.3 1.0 copy-done
  8.2 1.0 constant_dynamic-slice_fusion
  9.2 1.1 constant_dynamic-slice_fusion.2
  10.4 1.0 maximum_maximum_fusion
  11.4 0.0 all-gather.5.cloned.1.call-update
  11.4 0.0 all-gather.7.cloned.1.call-start
  11.4 0.0 copy-done.6
  11.5 0.0 copy-start.3
  11.5 0.0 copy-start.4
  11.5 0.1 constant_dynamic-slice_fusion.5
  11.6 0.1 maximum_bitcast_fusion
  11.7 1.3 copy-done.3
  13.1 0.6 copy-done.4
  13.7 0.2 dynamic-slice_bitcast_fusion
  13.9 2.0 pad_maximum_fusion
  15.8 0.0 all-gather.7.cloned.1.call-update
  15.9 0.0 reduce-scatter.3.cloned.1.call-start
  15.9 0.6 copy-done.10
  16.5 0.2 reduce-window.4
  16.7 0.1 select_reduce_fusion
  16.8 0.0 copy-done.9
  16.8 1.0 multiply_sine_fusion
  17.8 0.1 broadcast_in_dim.22
  17.9 1.5 concatenate.18.tab
  19.4 47.1 %enter.1 = (bf16[2,4,128,2048]{3,2,1,0:T(8,128)(2,1)}, f32[2,512,384]{2,1,0:T(8,128)}) custom-call(bf16[128,2048]{1,0:T(8,128)(2,1)} %bitcast.55, f32[1,2048]{1,0:T(1,128)} %bitcast.61, f32[512,384]{1,0:T(8,128)} %concatenate.18.tab), custom_call_target="tpu_custom_call" | custom-call | flops 10000000000 | bytes 100000000 | tf_op jit(solution)/shard_map/enter/pallas_call | solution.py:633
  66.5 1.1 slice.48
  67.6 0.1 convert_reduce_fusion
  67.7 0.6 convert_element_type.46.low
  68.4 26.4 %project.1 = (bf16[2,512,256]{2,1,0:T(8,128)(2,1)}, bf16[2,3,512,128]{3,2,1,0:T(8,128)(2,1)}) custom-call(bf16[2,512,2048]{2,1,0:T(8,128)(2,1)} %bitcast.65, bf16[4,512,640]{2,1,0:T(8,128)(2,1)} %bitcast.49, f32[2,512,384]{2,1,0:T(8,128)} %get-tuple-element.36.tabs.starts.turns), custom_call_target="tpu_custom_call" | custom-call | flops 10000000000 | bytes 10000000 | tf_op jit(solution)/shard_map/project/pallas_call | solution.py:633
  94.8 11.4 %attend.1 = (bf16[2,512,256]{2,1,0:T(8,128)(2,1)}, f32[2,4,512,128]{3,2,1,0:T(8,128)}) custom-call(s32[8]{0:T(128)} %convert_element_type.46.low, bf16[2,512,256]{2,1,0:T(8,128)(2,1)} %get-tuple-element.38.q, bf16[2,1536,128]{2,1,0:T(8,128)(2,1)} %bitcast.70, f32[2,512,384]{2,1,0:T(8,128)} %get-tuple-element.36.tabs.starts.turns), custom_call_target="tpu_custom_call" | custom-call | flops 20000000000 | bytes 10000000 | tf_op jit(solution)/shard_map/attend/pallas_call | solution.py:890
  106.2 104.9 %middle.1 = (f32[128,2048]{1,0:T(8,128)}, bf16[2,4,128,2048]{3,2,1,0:T(8,128)(2,1)}, bf16[2,4,128,2048]{3,2,1,0:T(8,128)(2,1)}) custom-call(bf16[2,512,256]{2,1,0:T(8,128)(2,1)} %get-tuple-element.40.att, bf16[4,512,640]{2,1,0:T(8,128)(2,1)} %bitcast.50, bf16[128,2048]{1,0:T(8,128)(2,1)} %bitcast.56, f32[1,2048]{1,0:T(1,128)} %bitcast.58, ...), custom_call_target="tpu_custom_call" | custom-call | flops 10000000000 | bytes 200000000 | tf_op jit(solution)/shard_map/middle/pallas_call | solution.py:633
  211.1 0.0 all-gather.7.cloned.1.call-done
  211.1 85.8 %ffn.1 = (bf16[2,4,128,2048]{3,2,1,0:T(8,128)(2,1)}, f32[128,2048]{1,0:T(8,128)}, f32[8,2048]{1,0:T(8,128)}, bf16[4,3,256,2048]{3,2,1,0:T(8,128)(2,1)}) custom-call(bf16[1024,2048]{1,0:T(8,128)(2,1)} %bitcast.67, bf16[1024,2048]{1,0:T(8,128)(2,1)} %bitcast.68, bf16[4,3,512,1024]{3,2,1,0:T(8,128)(2,1)} %bitcast.48, f32[1,2048]{1,0:T(1,128)} %bitcast.59), custom_call_target="tpu_custom_call" | custom-call | flops 40000000000 | bytes 100000000 | tf_op jit(solution)/shard_map/ffn/pallas_call | solution.py:633
  296.9 78.8 %branch.1 = (bf16[128,2048]{1,0:T(8,128)(2,1)}, f32[128,2048]{1,0:T(8,128)}, bf16[2,512,256]{2,1,0:T(8,128)(2,1)}, bf16[1024,512]{1,0:T(8,128)(2,1)}) custom-call(f32[128,2048]{1,0:T(8,128)} %get-tuple-element.43.total, f32[128,2048]{1,0:T(8,128)} %get-tuple-element.44.mid, bf16[128,2048]{1,0:T(8,128)(2,1)} %bitcast.54, f32[1,2048]{1,0:T(1,128)} %bitcast.60, ...), custom_call_target="tpu_custom_call" | custom-call | flops 10000000000 | bytes 100000000 | tf_op jit(solution)/shard_map/branch/pallas_call | solution.py:633
  375.7 15.8 %attend_back.1 = (bf16[2,512,256]{2,1,0:T(8,128)(2,1)}, f32[2,1536,128]{2,1,0:T(8,128)}) custom-call(s32[8]{0:T(128)} %convert_element_type.46.low, bf16[2,512,256]{2,1,0:T(8,128)(2,1)} %get-tuple-element.38.q, bf16[2,1536,128]{2,1,0:T(8,128)(2,1)} %bitcast.71, f32[2,512,384]{2,1,0:T(8,128)} %get-tuple-element.36.tabs.starts.turns, ...), custom_call_target="tpu_custom_call" | custom-call | flops 40000000000 | bytes 10000000 | tf_op jit(solution)/shard_map/attend_back/pallas_call | solution.py:950
  391.5 40.9 %unproject.1 = (bf16[2,4,128,2048]{3,2,1,0:T(8,128)(2,1)}, f32[8,2048]{1,0:T(8,128)}, bf16[1024,512]{1,0:T(8,128)(2,1)}, bf16[1024,256]{1,0:T(8,128)(2,1)}) custom-call(bf16[2,512,256]{2,1,0:T(8,128)(2,1)} %get-tuple-element.49.dq, f32[2,3,512,128]{3,2,1,0:T(8,128)} %bitcast.69, bf16[1024,2048]{1,0:T(8,128)(2,1)} %bitcast.66, bf16[4,512,640]{2,1,0:T(8,128)(2,1)} %bitcast.52, ...), custom_call_target="tpu_custom_call" | custom-call | flops 10000000000 | bytes 10000000 | tf_op jit(solution)/shard_map/unproject/pallas_call | solution.py:633
  432.4 0.0 copy-done.2
  432.4 3.0 pad_maximum_fusion.1
  435.5 0.0 reduce-scatter.3.cloned.1.call-update
  435.5 0.0 reduce-scatter.5.cloned.1.call-start
  435.6 16.8 %copy.51 = bf16[3072,2048]{0,1:T(8,128)(2,1)} copy(bf16[3072,2048]{1,0:T(8,128)(2,1)} %bitcast.39) | data formatting | bytes 25165824 | tf_op jit(solution)/shard_map/reshape | solution.py:1627
  452.3 0.0 reduce-scatter.5.cloned.1.call-update
  452.4 0.8 copy-done.8
  453.2 0.0 copy-done.7
  453.3 0.6 pad_maximum_fusion.2.gains
  453.9 51.2 %leave.1 = (bf16[128,2048]{1,0:T(8,128)(2,1)}, f32[8,256]{1,0:T(8,128)}) custom-call(bf16[2,4,128,2048]{3,2,1,0:T(8,128)(2,1)} %get-tuple-element.51.parts, bf16[128,2048]{1,0:T(8,128)(2,1)} %bitcast.57, f32[1,2048]{1,0:T(1,128)} %bitcast.63, f32[128,2048]{1,0:T(8,128)} %get-tuple-element.52.gmid, f32[16,256]{1,0:T(8,128)} %pad_maximum_fusion.2.gains), custom_call_target="tpu_custom_call" | custom-call | flops 10000000000 | bytes 100000000 | tf_op jit(solution)/shard_map/leave/pallas_call | solution.py:633
  505.1 1.3 fusion.3
  506.5 2.0 convert_bitcast_fusion.1
  508.5 1.0 copy.54
  509.5 0.0 slice-done
  509.5 16.1 %all_gather.19 = bf16[256,1024]{1,0:T(8,128)(2,1)S(1)} all-gather(bf16[256,256]{1,0:T(8,128)(2,1)S(1)} %slice-done), channel_id=1, replica_groups=mesh['row'=2,'nar'=4,'wid'=4] {'wid'}, dimensions={1}, use_global_device_ids=true | all-gather | bytes 655360 | tf_op jit(solution)/shard_map/all_gather | solution.py:1643
  525.6 0.2 copy.50
  525.8 0.1 fusion.2
  525.9 1.0 copy.53
  526.9 1.0 copy.52
  527.9 74.1 %reduce-scatter.5.cloned.1.call-done = bf16[768,2048]{0,1:T(8,128)(2,1)} async-done(((bf16[3072,2048]{0,1:T(8,128)(2,1)}), bf16[768,2048]{0,1:T(8,128)(2,1)}) %reduce-scatter.5.cloned.1.call-update) | async-done | bytes 3145744 | tf_op jit(solution)/shard_map/reduce_scatter | solution.py:1626
  602.0 4.4 convert_bitcast_fusion
  606.4 2.9 copy.56
  609.3 1.8 copy.55
  611.1 0.8 copy.59
  611.9 1.9 copy.60
  (20 shorter events, 0.1 us)
Async XLA Ops:
  7.2 1.1 copy-start
  7.2 4.3 copy-start.6
  7.2 61.2 %all-gather.5.cloned.1.call-start = ((), (), s32[]{:S(2)}) async-start(), calls=%async_computation.4 | async-start | bytes 3276800 | tf_op jit(solution)/shard_map/all_gather | solution.py:1603
  11.4 199.7 %all-gather.7.cloned.1.call-start = ((), (), s32[]{:S(2)}) async-start(), calls=%async_computation.5 | async-start | bytes 15728640 | tf_op jit(solution)/shard_map/all_gather | solution.py:1604
  11.5 1.6 copy-start.3
  11.5 2.2 copy-start.4
  15.8 0.7 copy-start.10
  15.8 0.9 copy-start.9
  15.9 490.6 %reduce-scatter.3.cloned.1.call-start = ((), (), s32[]{:S(2)}) async-start(), calls=%async_computation.2 | async-start | bytes 3276800 | tf_op jit(solution)/shard_map/reduce_scatter | solution.py:1636
  391.5 40.9 %copy-start.2 = (bf16[1024,512]{1,0:T(8,128)(2,1)S(1)}, bf16[1024,512]{1,0:T(8,128)(2,1)}, u32[]{:S(2)}) copy-start(bf16[1024,512]{1,0:T(8,128)(2,1)} %get-tuple-element.57) | copy-start | bytes 3145732
  435.5 166.4 %reduce-scatter.5.cloned.1.call-start = ((), (), s32[]{:S(2)}) async-start(), calls=%async_computation.3 | async-start | bytes 15728640 | tf_op jit(solution)/shard_map/reduce_scatter | solution.py:1626
  452.3 0.8 copy-start.8
  452.3 0.9 copy-start.7
  506.5 3.0 slice-start
  609.3 1.8 copy-start.5
  609.3 4.5 copy-start.1
Sparse Core Ops, SparseCore 0:
  11.5 42.2 all-gather.4
  55.6 132.6 all-gather.6
  435.6 42.9 reduce-scatter.2
  481.6 120.2 reduce-scatter.4

commit v2 on v1

--- a/solution.py
+++ b/solution.py
@@ -713,8 +713,26 @@
     return (r, jnp.clip(n + by, 0, 3), w)
 
 
-def project_kernel(x, p1, tabs, q_out, kv_out, kv, s_s, s_g, out_s):
+def load_pieces(pieces, target, sems, n):
+    own, by_x, by_y, far_a, far_b = pieces
+    rows = own.shape[0] // 2
+    copies = [
+        pltpu.make_async_copy(own, target.at[n], sems.at[0]),
+        pltpu.make_async_copy(by_x, target.at[n ^ 1], sems.at[1]),
+        pltpu.make_async_copy(by_y, target.at[n ^ 2], sems.at[2]),
+        pltpu.make_async_copy(far_a, target.at[n ^ 3, pl.ds(0, rows)], sems.at[3]),
+        pltpu.make_async_copy(far_b, target.at[n ^ 3, pl.ds(rows, rows)], sems.at[4]),
+    ]
+    for copy in copies:
+        copy.start()
+    return copies
+
+
+def project_kernel(
+    x, a0, a1, a2, a3, a4, tabs, q_out, kv_out, p1_out, kv, s_s, s_g, out_s, p1, in_s, p1_s
+):
     r, n, w = spot()
+    loads = load_pieces((a0, a1, a2, a3, a4), p1, in_s, n)
     greet(
         [
             (n >= 1, nar_device(r, n, w, -1)),
@@ -730,6 +748,10 @@
             device_id=nar_device(r, n, w, by), device_id_type=MESH,
         )
 
+    for load in loads:
+        load.wait()
+    p1_copy = pltpu.make_async_copy(p1, p1_out, p1_s)
+    p1_copy.start()
     lane = lax.broadcasted_iota(jnp.int32, (256, 128), 1)
     weight = p1[:, :, 0:384].reshape(2048, 384)
     for row in range(2):
@@ -776,23 +798,28 @@
             copy(row, 0, 2).wait_send()
 
     out.wait()
-
-
-def project(x, p1, tabs):
+    p1_copy.wait()
+
+
+def project(x, pieces, tabs):
     return comm_call(
         project_kernel, "project", 2,
         (
             jax.ShapeDtypeStruct((2, 512, 256), bf16),
             jax.ShapeDtypeStruct((2, 3, 512, 128), bf16),
+            jax.ShapeDtypeStruct((4, 512, 640), bf16),
         ),
-        [vmem()] * 3, [vmem(), hbm()],
+        [vmem()] + [hbm()] * 5 + [vmem()], [vmem(), hbm(), hbm()],
         [
             pltpu.VMEM((2, 3, 512, 128), bf16),
             pltpu.SemaphoreType.DMA((2, 3)),
             pltpu.SemaphoreType.DMA((2, 3)),
             pltpu.SemaphoreType.DMA(()),
+            pltpu.VMEM((4, 512, 640), bf16),
+            pltpu.SemaphoreType.DMA((5,)),
+            pltpu.SemaphoreType.DMA(()),
         ],
-        (x, p1, tabs), flops=10**10, sent=10**7,
+        (x, *pieces, tabs), flops=10**10, sent=10**7,
     )
 
 
@@ -1044,18 +1071,73 @@
     )
 
 
+class Spread:
+    def __init__(self, outs, sems, me):
+        self.a_send, self.a_keep, self.b_send, self.b_keep = outs
+        self.r, self.n, self.w = me
+        self.give_s, self.give_g, self.keep_s = sems
+
+    def copies(self, wide, row, place, give):
+        for k in range(4):
+            block = wide.at[self.n ^ k]
+            for part in range(2):
+                source = block.at[pl.ds(part * 128, 128)]
+                if part == 0:
+                    target = (self.a_send if k & 1 else self.a_keep).at[k >> 1]
+                else:
+                    target = (self.b_send if k >= 2 else self.b_keep).at[k & 1]
+                target = place(target)
+                at = k * 2 + part
+                if give:
+                    yield pltpu.make_async_remote_copy(
+                        source, target, self.give_s.at[row, at], self.give_g.at[row, at],
+                        device_id=(1 - self.r, self.n, self.w), device_id_type=MESH,
+                    )
+                else:
+                    yield pltpu.make_async_copy(source, target, self.keep_s.at[row, at])
+
+    def start(self, *args):
+        for copy in self.copies(*args):
+            copy.start()
+
+    def wait_send(self, *args):
+        for copy in self.copies(*args):
+            copy.wait_send()
+
+    def wait_recv(self, *args):
+        for copy in self.copies(*args):
+            copy.wait_recv()
+
+    def wait(self, *args):
+        for copy in self.copies(*args):
+            copy.wait()
+
+
+def spread_sems(count):
+    return [pltpu.SemaphoreType.DMA((count, 8))] * 3
+
+
 def ffn_kernel(
-    x, tops, p2, gain, part_out, sum_out, gain_out, grads_out,
-    theirs, mine, from_pt, from_up, from_dn, s0, s1, s2, s3, s4, s5,
-    act, dgu, stage, wide, out_s, give_s, give_g, keep_s,
+    x, tops, *refs
 ):
+    pieces, refs = refs[:15], refs[15:]
+    (
+        gain, part_out, sum_out, gain_out, o0, o1, o2, o3,
+        theirs, mine, from_pt, from_up, from_dn, s0, s1, s2, s3, s4, s5,
+        act, dgu, stage, wide, out_s, give_s, give_g, keep_s, p2, in_s,
+    ) = refs
     me = spot()
     r, n, w = me
+    loads = []
+    for j in range(3):
+        loads += load_pieces(pieces[5 * j : 5 * j + 5], p2.at[j], in_s.at[j], n)
     greet(line_partners(r, n, w, 4))
     scatter = Scatter(
         mine, theirs, (from_pt, from_up, from_dn), (s0, s1, s2, s3, s4, s5), me, 4
     )
     gain_out[...] = jnp.zeros_like(gain_out)
+    for load in loads:
+        load.wait()
 
     def put(s, slot, row_slot, row):
         return pltpu.make_async_copy(
@@ -1074,8 +1156,8 @@
         def hidden_tile(ft, carry):
             columns = pl.ds(pl.multiple_of(ft * 256, 256), 256)
             left = jnp.concatenate([x[rows_t, :], x[rows_m, :]], axis=0)
-            gate = jnp.dot(left, p2[:, 0, :, columns].reshape(2048, 256), preferred_element_type=f32)
-            up = jnp.dot(left, p2[:, 1, :, columns].reshape(2048, 256), preferred_element_type=f32)
+            gate = jnp.dot(left, p2[0, :, :, columns].reshape(2048, 256), preferred_element_type=f32)
+            up = jnp.dot(left, p2[1, :, :, columns].reshape(2048, 256), preferred_element_type=f32)
             sig = 1.0 / (1.0 + jnp.exp(-gate))
             silu = gate * sig
             active = (silu * up).astype(bf16)
@@ -1083,7 +1165,7 @@
             act[rows_m, columns] = active[128:256]
             f_rows = pl.ds(pl.multiple_of((ft % 2) * 256, 256), 256)
             f_cols = pl.ds(pl.multiple_of((ft // 2) * 512, 512), 512)
-            right = jnp.concatenate([p2[nn, 2, f_rows, f_cols] for nn in range(4)], axis=1)
+            right = jnp.concatenate([p2[2, nn, f_rows, f_cols] for nn in range(4)], axis=1)
             top = jnp.concatenate([tops[rows_t, :], tops[rows_m, :]], axis=0)
             dact = contract_last(top, right)
             dgate = (dact * up * (sig * (1.0 + gate * (1.0 - sig)))).astype(bf16)
@@ -1103,7 +1185,7 @@
             inner = pl.ds(pl.multiple_of(half * 256, 256), 256)
             other = pl.ds(pl.multiple_of(512 + half * 256, 256), 256)
             left = jnp.concatenate([dgu[rows_t, :], dgu[rows_m, :]], axis=0)
-            right = jnp.concatenate([p2[nn, 0, inner, :], p2[nn, 1, inner, :]], axis=1)
+            right = jnp.concatenate([p2[0, nn, inner, :], p2[1, nn, inner, :]], axis=1)
             part = contract_last(left, right)
             seen = jnp.concatenate([x[rows_t, columns], x[rows_m, columns]], axis=0)
             terms = part * seen.astype(f32)
@@ -1112,7 +1194,7 @@
             theirs[s, :, columns] = part[0:128]
             mine[s, :, columns] = part[128:256]
             left = jnp.concatenate([act[rows_t, :], act[rows_m, :]], axis=0)
-            right = jnp.concatenate([p2[nn, 2, :, inner], p2[nn, 2, :, other]], axis=0)
+            right = jnp.concatenate([p2[2, nn, :, inner], p2[2, nn, :, other]], axis=0)
             part = jnp.dot(left, right, preferred_element_type=f32).astype(bf16)
             stage[slot, 0, :, columns] = part[0:128]
             stage[slot, 1, :, columns] = part[128:256]
@@ -1128,26 +1210,20 @@
 
     each_rows(8, 8, scale)
 
-    def give(which, half):
-        return pltpu.make_async_remote_copy(
-            wide.at[which % 2, half],
-            grads_out.at[:, which, :, pl.ds(pl.multiple_of(r * 1024, 1024), 1024)],
-            give_s.at[which], give_g.at[which],
-            device_id=(1 - r, n, w), device_id_type=MESH,
-        )
-
-    def keep(which):
-        return pltpu.make_async_copy(
-            wide.at[which % 2, 1],
-            grads_out.at[:, which, :, pl.ds(pl.multiple_of(r * 1024, 1024), 1024)],
-            keep_s.at[which],
-        )
+    spread = Spread((o0, o1, o2, o3), (give_s, give_g, keep_s), me)
+    columns_here = pl.ds(pl.multiple_of(r * 1024, 1024), 1024)
+
+    def moved(which, half):
+        def place(target):
+            return target.at[which, :, columns_here]
+
+        return wide.at[which % 2, half], which, place, half == 0
 
     for which in range(3):
         scatter.step(scatter.order(which))
         if which == 2:
-            give(0, 0).wait_send()
-            keep(0).wait()
+            spread.wait_send(*moved(0, 0))
+            spread.wait(*moved(0, 1))
         for half in range(2):
             d_first = (jnp.where(half == 0, 1 - r, r)) * 1024
 
@@ -1163,24 +1239,25 @@
                 return carry
 
             lax.fori_loop(0, 4, weight_tile, 0)
-            if half == 0:
-                give(which, 0).start()
-            else:
-                keep(which).start()
+            spread.start(*moved(which, half))
     scatter.step(scatter.order(3))
     scatter.total(sum_out)
     scatter.sent()
     for which in range(3):
-        give(which, 0).wait_recv()
+        spread.wait_recv(*moved(which, 0))
         if which > 0:
-            give(which, 0).wait_send()
-            keep(which).wait()
+            spread.wait_send(*moved(which, 0))
+            spread.wait(*moved(which, 1))
     for slot in range(2):
         put(0, slot, 0, 1 - r).wait()
         put(0, slot, 1, r).wait()
 
 
-def ffn_stage(x, tops, p2, gain):
+def spread_shapes(*dims):
+    return (jax.ShapeDtypeStruct((2,) + dims, bf16),) * 4
+
+
+def ffn_stage(x, tops, pieces, gain):
     shard, width = 128, 2048
     return comm_call(
         ffn_kernel, "ffn", 4,
@@ -1188,9 +1265,9 @@
             jax.ShapeDtypeStruct((2, 4, shard, width), bf16),
             jax.ShapeDtypeStruct((shard, width), f32),
             jax.ShapeDtypeStruct((8, width), f32),
-            jax.ShapeDtypeStruct((4, 3, 256, width), bf16),
-        ),
-        [vmem()] * 4, [hbm(), vmem(), vmem(), hbm()],
+        )
+        + spread_shapes(3, 128, width),
+        [vmem()] * 2 + [hbm()] * 15 + [vmem()], [hbm(), vmem(), vmem()] + [hbm()] * 4,
         [pltpu.VMEM((4, shard, width), bf16)] * 2
         + scatter_bufs(shard, width) + scatter_sems()
         + [
@@ -1199,11 +1276,10 @@
             pltpu.VMEM((2, 2, shard, width), bf16),
             pltpu.VMEM((2, 2, 4, 256, 1024), bf16),
             pltpu.SemaphoreType.DMA((2, 2)),
-            pltpu.SemaphoreType.DMA((3,)),
-            pltpu.SemaphoreType.DMA((3,)),
-            pltpu.SemaphoreType.DMA((3,)),
-        ],
-        (x, tops, p2, gain), flops=4 * 10**10, sent=10**8,
+        ]
+        + spread_sems(3)
+        + [pltpu.VMEM((3, 4, 512, 1024), bf16), pltpu.SemaphoreType.DMA((3, 5))],
+        (x, tops, *pieces, gain), flops=4 * 10**10, sent=10**8,
     )
 
 
@@ -1215,7 +1291,7 @@
 
 
 def branch_kernel(
-    total, mid, grad_top, gain, parts, p1, att, hid_out, gmid_out, datt_out, go_out,
+    total, mid, grad_top, gain, parts, p1, att, hid_out, gmid_out, datt_out, o0, o1, o2, o3,
     mine, from_pt, from_up, from_dn, s0, s1, s2, s3, s4, s5,
     buf, g0, g1, g2, g3, acc, wide, give_s, give_g, keep_s,
 ):
@@ -1255,29 +1331,25 @@
             )
             datt_out[row, pair * 256 : pair * 256 + 256, :] = contract_last(left, right).astype(bf16)
 
-    give = pltpu.make_async_remote_copy(
-        wide.at[0], go_out.at[:, pl.ds(pl.multiple_of(r * 256, 256), 256)], give_s, give_g,
-        device_id=(1 - r, n, w), device_id_type=MESH,
-    )
-    keep = pltpu.make_async_copy(
-        wide.at[1], go_out.at[:, pl.ds(pl.multiple_of(r * 256, 256), 256)], keep_s
-    )
+    spread = Spread((o0, o1, o2, o3), (give_s, give_g, keep_s), me)
+
+    def moved(half):
+        def place(target):
+            return target.at[:, pl.ds(pl.multiple_of(r * 256, 256), 256)]
+
+        return wide.at[half], 0, place, half == 0
+
     for half in range(2):
         d_first = (jnp.where(half == 0, 1 - r, r)) * 1024
 
         def weight_tile(i, carry):
             columns = pl.ds(pl.multiple_of(d_first + i * 256, 256), 256)
             left = buf[:, :, :, columns].reshape(1024, 256)
-            wide[half, pl.ds(pl.multiple_of(i * 256, 256), 256), :] = contract_first(
-                left, att[...]
-            ).astype(bf16)
+            wide[half, i] = contract_first(left, att[...]).astype(bf16)
             return carry
 
         lax.fori_loop(0, 4, weight_tile, 0)
-        if half == 0:
-            give.start()
-        else:
-            keep.start()
+        spread.start(*moved(half))
     scatter.total(acc)
 
     def last(rows):
@@ -1286,8 +1358,8 @@
     each_rows(mid.shape[0], 16, last)
     scatter.sent()
     gather.sent()
-    give.wait()
-    keep.wait()
+    spread.wait(*moved(0))
+    spread.wait(*moved(1))
 
 
 def branch_stage(total, mid, grad_top, gain, parts, p1, att):
@@ -1298,26 +1370,24 @@
             jax.ShapeDtypeStruct((shard, width), bf16),
             jax.ShapeDtypeStruct((shard, width), f32),
             jax.ShapeDtypeStruct((2, 512, 256), bf16),
-            jax.ShapeDtypeStruct((1024, 512), bf16),
-        ),
-        [vmem()] * 7, [vmem(), vmem(), vmem(), hbm()],
+        )
+        + spread_shapes(128, 512),
+        [vmem()] * 7, [vmem(), vmem(), vmem()] + [hbm()] * 4,
         [pltpu.VMEM((4, shard, width), bf16)]
         + scatter_bufs(shard, width) + scatter_sems()
         + gather_scratch(shard, width)
         + [
             pltpu.VMEM((shard, width), f32),
-            pltpu.VMEM((2, 1024, 256), bf16),
-            pltpu.SemaphoreType.DMA(()),
-            pltpu.SemaphoreType.DMA(()),
-            pltpu.SemaphoreType.DMA(()),
-        ],
+            pltpu.VMEM((2, 4, 256, 256), bf16),
+        ]
+        + spread_sems(1),
         (total, mid, grad_top, gain, parts, p1, att), flops=10**10, sent=10**8,
     )
 
 
 def unproject_kernel(
-    dq, dkv, x, p1, tabs, gain, part_out, gain_out, gq_out, gkv_out,
-    send, recv, both, wide_q, wide_kv, s_s, s_g, q_s, q_g, kv_s, kv_g, keep_s,
+    dq, dkv, x, p1, tabs, gain, part_out, gain_out, o0, o1, o2, o3,
+    send, recv, both, wide_q, wide_kv, s_s, s_g, give_s, give_g, keep_s,
 ):
     r, n, w = spot()
     greet(
@@ -1343,21 +1413,19 @@
                 send[row, slot] = dkv[row, slot].astype(bf16)
                 copy(row, slot, by).start()
 
-    partner = (1 - r, n, w)
-    give_q = pltpu.make_async_remote_copy(
-        wide_q.at[0], gq_out.at[:, pl.ds(pl.multiple_of(r * 256, 256), 256)], q_s, q_g,
-        device_id=partner, device_id_type=MESH,
-    )
-    keep_q = pltpu.make_async_copy(
-        wide_q.at[1], gq_out.at[:, pl.ds(pl.multiple_of(r * 256, 256), 256)], keep_s.at[0]
-    )
-    give_kv = pltpu.make_async_remote_copy(
-        wide_kv.at[0], gkv_out.at[:, pl.ds(pl.multiple_of(r * 128, 128), 128)], kv_s, kv_g,
-        device_id=partner, device_id_type=MESH,
-    )
-    keep_kv = pltpu.make_async_copy(
-        wide_kv.at[1], gkv_out.at[:, pl.ds(pl.multiple_of(r * 128, 128), 128)], keep_s.at[1]
-    )
+    spread = Spread((o0, o1, o2, o3), (give_s, give_g, keep_s), (r, n, w))
+
+    def moved_q(half):
+        def place(target):
+            return target.at[:, pl.ds(pl.multiple_of(r * 256, 256), 256)]
+
+        return wide_q.at[half], 0, place, half == 0
+
+    def moved_kv(half):
+        def place(target):
+            return target.at[:, pl.ds(pl.multiple_of(512 + r * 128, 128), 128)]
+
+        return wide_kv.at[half], 1, place, half == 0
 
     for row in range(2):
         both[row * 512 : row * 512 + 512, 0:256] = dq[row]
@@ -1367,17 +1435,14 @@
 
         def tile(i, carry):
             d_cols = pl.ds(pl.multiple_of(d_first + i * 256, 256), 256)
-            wide[half, pl.ds(pl.multiple_of(i * 256, 256), 256), :] = contract_first(
-                x[:, d_cols], both[:, columns]
-            ).astype(bf16)
+            wide[half, i] = contract_first(x[:, d_cols], both[:, columns]).astype(bf16)
             return carry
 
         lax.fori_loop(0, 4, tile, 0)
 
-    weight(0, slice(0, 256), wide_q)
-    give_q.start()
-    weight(1, slice(0, 256), wide_q)
-    keep_q.start()
+    for half in range(2):
+        weight(half, slice(0, 256), wide_q)
+        spread.start(*moved_q(half))
     lane = lax.broadcasted_iota(jnp.int32, (128, 128), 1)
     for row in range(2):
         for slot, by in ((1, -1), (0, -2)):
@@ -1398,10 +1463,9 @@
             return carry
 
         lax.fori_loop(0, 4, tile, 0)
-    weight(0, slice(256, 384), wide_kv)
-    give_kv.start()
-    weight(1, slice(256, 384), wide_kv)
-    keep_kv.start()
+    for half in range(2):
+        weight(half, slice(256, 384), wide_kv)
+        spread.start(*moved_kv(half))
     gain_out[...] = jnp.zeros_like(gain_out)
 
     def model_tile(dt, carry):
@@ -1427,10 +1491,9 @@
             def _():
                 copy(row, slot, by).wait_send()
 
-    give_q.wait()
-    keep_q.wait()
-    give_kv.wait()
-    keep_kv.wait()
+    for half in range(2):
+        spread.wait(*moved_q(half))
+        spread.wait(*moved_kv(half))
 
 
 def unproject(dq, dkv, x, p1, tabs, gain):
@@ -1439,24 +1502,19 @@
         (
             jax.ShapeDtypeStruct((2, 4, 128, 2048), bf16),
             jax.ShapeDtypeStruct((8, 2048), f32),
-            jax.ShapeDtypeStruct((1024, 512), bf16),
-            jax.ShapeDtypeStruct((1024, 256), bf16),
-        ),
-        [vmem()] * 6, [vmem(), vmem(), hbm(), hbm()],
+        )
+        + spread_shapes(128, 768),
+        [vmem()] * 6, [vmem(), vmem()] + [hbm()] * 4,
         [
             pltpu.VMEM((2, 2, 512, 128), bf16),
             pltpu.VMEM((2, 2, 512, 128), bf16),
             pltpu.VMEM((1024, 384), bf16),
-            pltpu.VMEM((2, 1024, 256), bf16),
-            pltpu.VMEM((2, 1024, 128), bf16),
+            pltpu.VMEM((2, 4, 256, 256), bf16),
+            pltpu.VMEM((2, 4, 256, 128), bf16),
             pltpu.SemaphoreType.DMA((2, 2)),
             pltpu.SemaphoreType.DMA((2, 2)),
-            pltpu.SemaphoreType.DMA(()),
-            pltpu.SemaphoreType.DMA(()),
-            pltpu.SemaphoreType.DMA(()),
-            pltpu.SemaphoreType.DMA(()),
-            pltpu.SemaphoreType.DMA((2,)),
-        ],
+        ]
+        + spread_sems(2),
         (dq, dkv, x, p1, tabs, gain), flops=10**10, sent=10**7,
     )
 
@@ -1571,6 +1629,27 @@
     )
 
 
+def swap_nar(x, bit):
+    return lax.ppermute(x, "nar", [(i, i ^ bit) for i in range(4)])
+
+
+def nar_gather(shard):
+    rows = shard.shape[0] // 2
+    by_x, by_y = swap_nar(shard, 1), swap_nar(shard, 2)
+    return shard, by_x, by_y, swap_nar(by_x[:rows], 2), swap_nar(by_y[rows:], 1)
+
+
+def nar_scatter(a_send, a_keep, b_send, b_keep):
+    def halves(send, keep, first, then):
+        total = (keep.astype(f32) + swap_nar(send, first).astype(f32))
+        over = swap_nar(total[1].astype(bf16), then)
+        return total[0] + over.astype(f32)
+
+    return jnp.concatenate(
+        [halves(a_send, a_keep, 1, 2), halves(b_send, b_keep, 2, 1)], axis=-2
+    )
+
+
 def local_fast(
     hidden_in, doc_lengths, w_query, w_key, w_value, w_output, w_gate, w_up, w_down,
     gain_attn, gain_ffn, grad_out,
@@ -1593,15 +1672,10 @@
         axis=1,
     )
     down_half = half(w_down, 0)
-    p2_shard = jnp.stack(
-        [
-            half(w_gate, 1),
-            half(w_up, 1),
-            jnp.concatenate([down_half[:512], down_half[512:]], axis=1),
-        ]
-    )
-    p1 = lax.all_gather(p1_shard, "nar", axis=0)
-    p2 = lax.all_gather(p2_shard, "nar", axis=0)
+    p1_pieces = nar_gather(p1_shard)
+    gate_pieces = nar_gather(half(w_gate, 1))
+    up_pieces = nar_gather(half(w_up, 1))
+    down_pieces = nar_gather(jnp.concatenate([down_half[:512], down_half[512:]], axis=1))
 
     token_ids = n * 512 + jnp.arange(512, dtype=jnp.int32)
     doc_start, places = doc_layout(doc_lengths[0], token_ids)
@@ -1615,43 +1689,41 @@
 
     rows, tabs = enter(hidden, gain_a, tab)
     rows3, rows2 = rows.reshape(2, 512, 2048), rows.reshape(1024, 2048)
-    q, kv = project(rows3, p1, tabs)
+    q, kv, p1 = project(rows3, p1_pieces, tabs)
     low = tabs[:, ::QUERIES, 256].astype(jnp.int32).reshape(8)
     kv_flat = kv.reshape(2, 1536, 128)
     att, lse = attend(low, q, kv_flat, tabs)
     mid, ffn_rows, top_rows = middle_stage(att, p1, hidden, gain_f, grad_top)
-    parts, total, gain_f_part, grads = ffn_stage(
-        ffn_rows.reshape(1024, 2048), top_rows.reshape(1024, 2048), p2, gain_f
-    )
-    summed = lax.psum_scatter(
-        grads.reshape(4 * 768, 2048), "nar", scatter_dimension=0, tiled=True
-    ).reshape(3, 256, 2048)
-    hidden_out, gmid, datt, grad_o = branch_stage(
+    parts, total, gain_f_part, *grads = ffn_stage(
+        ffn_rows.reshape(1024, 2048), top_rows.reshape(1024, 2048),
+        gate_pieces + up_pieces + down_pieces, gain_f,
+    )
+    summed = nar_scatter(*grads)
+    hidden_out, gmid, datt, *grad_o = branch_stage(
         total, mid, grad_top, gain_f, parts, p1, att.reshape(1024, 256)
     )
+    summed_o = nar_scatter(*grad_o)
     dq, dkv = attend_back(low, q, kv_flat, tabs, att, datt, lse)
-    dparts, gain_a_part, grad_q, grad_kv = unproject(
+    dparts, gain_a_part, *grad_qkv = unproject(
         dq, dkv.reshape(2, 3, 512, 128), rows2, p1, tabs, gain_a
     )
-    small = lax.psum_scatter(
-        jnp.concatenate([grad_q, grad_o, grad_kv], axis=1), "nar", scatter_dimension=0, tiled=True
-    )
+    summed_qkv = nar_scatter(*grad_qkv)
     gains = jnp.concatenate(
         [gain_f_part.sum(axis=0).reshape(8, 256), gain_a_part.sum(axis=0).reshape(8, 256)], axis=0
     )
     grad_in, gain_sums = leave(dparts, hidden, gain_a, gmid, gains)
-    kv_all = lax.all_gather(small[:, 1024:1280], "wid", axis=1, tiled=True)
+    kv_all = lax.all_gather(summed_qkv[:, 512:768].astype(bf16), "wid", axis=1, tiled=True)
     kv_all = kv_all.astype(f32).reshape(256, KV, 2, HD)
     return (
         hidden_out[None],
         grad_in[None],
-        small[:, 0:512].astype(f32),
+        summed_qkv[:, 0:512],
         kv_all[:, :, 0].reshape(256, KV * HD),
         kv_all[:, :, 1].reshape(256, KV * HD),
-        small[:, 512:1024].T.astype(f32),
-        summed[0].astype(f32),
-        summed[1].astype(f32),
-        summed[2].T.astype(f32),
+        summed_o.T,
+        summed[0],
+        summed[1],
+        summed[2].T,
         gain_sums[1],
         gain_sums[0],
     )

time: 621 us -> 717 us (1.15)
  starting transfers between devices: 0.16 us -> 49.7 us
  waiting for transfers between devices: 74.2 us -> 104 us
  Pallas kernels: 462 us -> 490 us
  between operations: 14 us -> 1.24 us
  other arithmetic: 14.7 us -> 22.1 us
    ppermute x0 -> x28, waiting for transfers between devices: none -> 104 us  [swap_nar(): return lax.ppermute(x, 'nar', [(i, i ^ bit) for i in range(4)])]
    reduce_scatter x2 -> x0, waiting for transfers between devices: 74.1 us -> none  [the longest x1 74.1 us: local_fast(): lax.psum_scatter(grads.reshape(4 * 768, 2048), 'nar', scatter_dimension=0...]
    ppermute x0 -> x28, starting transfers between devices: none -> 49.7 us  [swap_nar(): return lax.ppermute(x, 'nar', [(i, i ^ bit) for i in range(4)])]
    pallas_call x7, Pallas kernels: 435 us -> 462 us  [comm_call(): pl.pallas_call(kernel, out_shape=out_shape, in_specs=in_specs, out_specs=...]
    reshape x1 -> x0, local copies, waits for them, and re-layouts: 16.8 us -> none  [local_fast(): grads.reshape(4 * 768, 2048)]
    add x0 -> x12, other arithmetic: none -> 13.3 us  [the longest x6 7.68 us: halves(): total = keep.astype(f32) + swap_nar(send, first).astype(f32)]
    slice x2 -> x8, local copies, waits for them, and re-layouts: 0.01 us -> 9.18 us  [the longest x4 4.95 us: nar_gather(): by_x[:rows]]
    unnamed x29 -> x50, local copies, waits for them, and re-layouts: 14.7 us -> 12.4 us
  transfers between devices with their start and end apart: 4 -> 28, of which waited for: 1 -> 9; matrix products, arithmetic and copies ran while one was open for 5% -> 5% of each run, Pallas kernels for 39% -> 38%
where the time goes in v2:
time: 717 us
  Pallas kernels  490 us (68%)
  waiting for transfers between devices  104 us (15%)
  starting transfers between devices  49.7 us (7%)
  local copies, waits for them, and re-layouts  34.2 us (5%)
  other arithmetic  22.1 us (3%)
  blocking collectives  16.1 us (2%)
    pallas_call x7, Pallas kernels, comm_call(): pl.pallas_call(kernel, out_shape=out_shape, in_specs=in_specs, out_specs=...  462 us
    ppermute x28, waiting for transfers between devices, swap_nar(): return lax.ppermute(x, 'nar', [(i, i ^ bit) for i in range(4)])  104 us
    ppermute x28, starting transfers between devices, swap_nar(): return lax.ppermute(x, 'nar', [(i, i ^ bit) for i in range(4)])  49.7 us
    all_gather x1, blocking collectives, local_fast(): lax.all_gather(summed_qkv[:, 512:768].astype(bf16), 'wid', axis=1, tiled=...  16.1 us
    pallas_call x1, Pallas kernels, attend_back(): pl.pallas_call(attend_back_kernel, out_shape=(jax.ShapeDtypeStruct((2, 51...  15.8 us
  transfers between devices with their start and end apart: 28, of which 9 were waited for; matrix products, arithmetic and copies ran while one was open for 5% of the time, Pallas kernels for 38%

profile of v2, /device:TPU:0, one launch (start us, length us, event | category | flops | bytes accessed | tf_op | source)
XLA Modules:
  0.0 716.5 jit_solution(8050629929414986180)
XLA Ops:
  0.7 1.1 constant_dynamic-slice_fusion.6
  2.8 1.1 constant_dynamic-slice_fusion.4
  4.9 3.0 collective-permute-start.1
  7.9 1.5 collective-permute-start
  10.2 1.2 copy-done.8
  13.8 1.5 concatenate.24.tab
  15.3 45.1 %enter.1 = (bf16[2,4,128,2048]{3,2,1,0:T(8,128)(2,1)}, f32[2,512,384]{2,1,0:T(8,128)}) custom-call(bf16[128,2048]{1,0:T(8,128)(2,1)} %bitcast.82, f32[1,2048]{1,0:T(1,128)} %bitcast.88, f32[512,384]{1,0:T(8,128)} %concatenate.24.tab), custom_call_target="tpu_custom_call" | custom-call | flops 10000000000 | bytes 100000000 | tf_op jit(solution)/shard_map/enter/pallas_call | solution.py:633
  60.4 1.1 slice.109
  61.5 1.0 slice.144
  62.5 1.6 collective-permute-start.3
  64.1 1.7 slice.143
  67.0 1.3 constant_dynamic-slice_fusion.7
  68.3 1.1 pad_maximum_fusion.1.refs_10_
  69.5 2.9 collective-permute-done.3.a4
  72.4 1.5 collective-permute-start.4
  73.9 2.2 collective-permute-done.2.a3
  76.6 35.5 %project.1 = (bf16[2,512,256]{2,1,0:T(8,128)(2,1)}, bf16[2,3,512,128]{3,2,1,0:T(8,128)(2,1)}, bf16[4,512,640]{2,1,0:T(8,128)(2,1)}) custom-call(bf16[2,512,2048]{2,1,0:T(8,128)(2,1)} %bitcast.92, bf16[512,640]{1,0:T(8,128)(2,1)} %maximum_maximum_fusion.a0, bf16[512,640]{1,0:T(8,128)(2,1)} %collective-permute-done.a1, ...), custom_call_target="tpu_custom_call" | custom-call | flops 10000000000 | bytes 10000000 | tf_op jit(solution)/shard_map/project/pallas_call | solution.py:633
  112.2 1.1 slice.148
  113.3 2.1 collective-permute-start.11
  115.4 11.4 %attend.1 = (bf16[2,512,256]{2,1,0:T(8,128)(2,1)}, f32[2,4,512,128]{3,2,1,0:T(8,128)}) custom-call(s32[8]{0:T(128)} %convert_element_type.104.low, bf16[2,512,256]{2,1,0:T(8,128)(2,1)} %get-tuple-element.47.q, bf16[2,1536,128]{2,1,0:T(8,128)(2,1)} %bitcast.97, f32[2,512,384]{2,1,0:T(8,128)} %get-tuple-element.45.tabs.starts.turns), custom_call_target="tpu_custom_call" | custom-call | flops 20000000000 | bytes 10000000 | tf_op jit(solution)/shard_map/attend/pallas_call | solution.py:917
  126.7 1.1 slice.147
  127.8 10.4 %collective-permute-start.10 = (bf16[256,1024]{1,0:T(8,128)(2,1)S(1)}, bf16[256,1024]{1,0:T(8,128)(2,1)}, u32[]{:S(2)}, u32[]{:S(2)}) collective-permute-start(bf16[256,1024]{1,0:T(8,128)(2,1)S(1)} %slice.147), channel_id=1, source_target_pairs={{0,8},{4,12},{8,0},{12,4},{1,9},{5,13},{9,1},{13,5},{2,10},{6,14},... | collective-permute-start | bytes 1572872 | tf_op jit(solution)/shard_map/ppermute | solution.py:1633
  138.2 1.1 slice.146
  139.4 1.1 slice.145
  140.5 1.1 slice.150
  141.6 2.1 collective-permute-start.15
  143.7 1.1 slice.149
  144.8 4.9 collective-permute-done.11.refs_9_
  149.7 3.3 collective-permute-start.14
  153.0 104.1 %middle.1 = (f32[128,2048]{1,0:T(8,128)}, bf16[2,4,128,2048]{3,2,1,0:T(8,128)(2,1)}, bf16[2,4,128,2048]{3,2,1,0:T(8,128)(2,1)}) custom-call(bf16[2,512,256]{2,1,0:T(8,128)(2,1)} %get-tuple-element.49.att, bf16[4,512,640]{2,1,0:T(8,128)(2,1)} %get-tuple-element.50.p1, bf16[128,2048]{1,0:T(8,128)(2,1)} %bitcast.83, f32[1,2048]{1,0:T(1,128)} %bitcast.85, ...), custom_call_target="tpu_custom_call" | custom-call | flops 10000000000 | bytes 200000000 | tf_op jit(solution)/shard_map/middle/pallas_call | solution.py:633
  258.0 86.7 %ffn.1 = (bf16[2,4,128,2048]{3,2,1,0:T(8,128)(2,1)}, f32[128,2048]{1,0:T(8,128)}, f32[8,2048]{1,0:T(8,128)}, bf16[2,3,128,2048]{3,2,1,0:T(8,128)(2,1)}, bf16[2,3...) custom-call(bf16[1024,2048]{1,0:T(8,128)(2,1)} %bitcast.94, ...), custom_call_target="tpu_custom_call" | custom-call | flops 40000000000 | bytes 100000000 | tf_op jit(solution)/shard_map/ffn/pallas_call | solution.py:633
  344.7 84.0 %branch.1 = (bf16[128,2048]{1,0:T(8,128)(2,1)}, f32[128,2048]{1,0:T(8,128)}, bf16[2,512,256]{2,1,0:T(8,128)(2,1)}, bf16[2,128,512]{2,1,0:T(8,128)(2,1)}, bf16[2,...) custom-call(f32[128,2048]{1,0:T(8,128)} %get-tuple-element.53.total, ...), custom_call_target="tpu_custom_call" | custom-call | flops 10000000000 | bytes 100000000 | tf_op jit(solution)/shard_map/branch/pallas_call | solution.py:633
  428.8 15.8 %attend_back.1 = (bf16[2,512,256]{2,1,0:T(8,128)(2,1)}, f32[2,1536,128]{2,1,0:T(8,128)}) custom-call(s32[8]{0:T(128)} %convert_element_type.104.low, bf16[2,512,256]{2,1,0:T(8,128)(2,1)} %get-tuple-element.47.q, bf16[2,1536,128]{2,1,0:T(8,128)(2,1)} %bitcast.98, f32[2,512,384]{2,1,0:T(8,128)} %get-tuple-element.45.tabs.starts.turns, ...), custom_call_target="tpu_custom_call" | custom-call | flops 40000000000 | bytes 10000000 | tf_op jit(solution)/shard_map/attend_back/pallas_call | solution.py:977
  444.6 31.6 %unproject.1 = (bf16[2,4,128,2048]{3,2,1,0:T(8,128)(2,1)}, f32[8,2048]{1,0:T(8,128)}, bf16[2,128,768]{2,1,0:T(8,128)(2,1)}, bf16[2,128,768]{2,1,0:T(8,128)(2,1)}...) custom-call(bf16[2,512,256]{2,1,0:T(8,128)(2,1)} %get-tuple-element.59.dq, f32[2,3,512,128]{3,2,1,0:T(8,128)} %bitcast.96, ...), custom_call_target="tpu_custom_call" | custom-call | flops 10000000000 | bytes 10000000 | tf_op jit(solution)/shard_map/unproject/pallas_call | solution.py:633
  477.2 5.7 collective-permute-start.20
  483.5 75.3 %leave.1 = (bf16[128,2048]{1,0:T(8,128)(2,1)}, f32[8,256]{1,0:T(8,128)}) custom-call(bf16[2,4,128,2048]{3,2,1,0:T(8,128)(2,1)} %get-tuple-element.61.parts, bf16[128,2048]{1,0:T(8,128)(2,1)} %bitcast.84, f32[1,2048]{1,0:T(1,128)} %bitcast.90, f32[128,2048]{1,0:T(8,128)} %get-tuple-element.62.gmid, f32[16,256]{1,0:T(8,128)} %pad_maximum_fusion.3.gains), custom_call_target="tpu_custom_call" | custom-call | flops 10000000000 | bytes 100000000 | tf_op jit(solution)/shard_map/leave/pallas_call | solution.py:633
  558.8 1.7 collective-permute-start.22
  560.5 1.8 collective-permute-start.16
  562.6 1.3 fusion.22
  564.0 1.6 collective-permute-start.26
  565.7 2.3 collective-permute-done.22
  568.1 1.6 collective-permute-start.21
  569.8 76.1 %collective-permute-done.21 = bf16[128,512]{1,0:T(8,128)(2,1)S(1)} collective-permute-done((bf16[128,512]{1,0:T(8,128)(2,1)S(1)}, bf16[128,512]{1,0:T(8,128)(2,1)S(1)}, u32[]{:S(2)}, u32[]{:S(2)}) %collective-permute-start.21) | collective-permute-done | bytes 131104 | tf_op jit(solution)/shard_map/ppermute | solution.py:1633
  645.9 1.7 collective-permute-start.23
  647.7 3.2 collective-permute-done.23
  652.0 1.2 convert_add_fusion.3
  653.2 1.7 collective-permute-start.17
  655.0 1.8 collective-permute-start.19
  656.9 2.1 collective-permute-done.17
  659.0 3.1 convert_add_fusion.1
  662.2 1.4 fusion.7
  663.5 1.6 collective-permute-start.25
  665.2 1.2 copy-done.4
  666.3 3.1 convert_add_fusion
  669.5 1.6 fusion.8
  671.1 1.5 copy-done.3
  672.6 1.7 collective-permute-start.27
  674.5 16.1 %all_gather.3 = bf16[256,1024]{1,0:T(8,128)(2,1)S(1)} all-gather(bf16[256,256]{1,0:T(8,128)(2,1)S(1)} %fusion.14), channel_id=1, replica_groups=mesh['row'=2,'nar'=4,'wid'=4] {'wid'}, dimensions={1}, use_global_device_ids=true | all-gather | bytes 655360 | tf_op jit(solution)/shard_map/all_gather | solution.py:1715
  693.7 3.4 collective-permute-done.25
  697.2 2.8 fusion.1
  699.9 6.3 collective-permute-done.27
  706.3 2.8 fusion
  709.0 2.8 fusion.6
  711.9 3.0 copy.41
  (109 shorter events, 16.2 us)
Async XLA Ops:
  0.6 8.8 %copy-start = (bf16[512,2048]{1,0:T(8,128)(2,1)S(1)}, bf16[512,2048]{1,0:T(8,128)(2,1)}, u32[]{:S(2)}) copy-start(bf16[512,2048]{1,0:T(8,128)(2,1)} %param.20) | copy-start | bytes 6291460
  3.9 8.4 %copy-start.21 = (s32[1,8]{1,0:T(1,128)S(1)}, s32[1,8]{1,0:T(1,128)}, u32[]{:S(2)}) copy-start(s32[1,8]{1,0:T(1,128)} %param.14) | copy-start | bytes 100
  3.9 8.7 %copy-start.16 = (f32[32]{0:T(128)S(1)}, f32[32]{0:T(128)}, u32[]{:S(2)}) copy-start(f32[32]{0:T(128)} %constant.36.clone) | copy-start | bytes 388
  4.9 56.6 %collective-permute-start.1 = (bf16[512,640]{1,0:T(8,128)(2,1)}, bf16[512,640]{1,0:T(8,128)(2,1)}, u32[]{:S(2)}, u32[]{:S(2)}) collective-permute-start(bf16[512,640]{1,0:T(8,128)(2,1)} %maximum_maximum_fusion.a0), channel_id=1, source_target_pairs={{0,8},{4,12},{8,0},{12,4},{1,9},{5,13},{9,1},{13,5},{2,10},{6,14},... | collective-permute-start | bytes 1966088 | tf_op jit(solution)/shard_map/ppermute | solution.py:1633
  7.9 56.1 %collective-permute-start = (bf16[512,640]{1,0:T(8,128)(2,1)}, bf16[512,640]{1,0:T(8,128)(2,1)}, u32[]{:S(2)}, u32[]{:S(2)}) collective-permute-start(bf16[512,640]{1,0:T(8,128)(2,1)} %maximum_maximum_fusion.a0), channel_id=1, source_target_pairs={{0,4},{4,0},{8,12},{12,8},{1,5},{5,1},{9,13},{13,9},{2,6},{6,2},{1... | collective-permute-start | bytes 1966088 | tf_op jit(solution)/shard_map/ppermute | solution.py:1633
  9.4 2.0 copy-start.8
  9.5 5.7 copy-start.6
  9.5 102.6 %collective-permute-start.9 = (bf16[512,1024]{1,0:T(8,128)(2,1)S(1)}, bf16[512,1024]{1,0:T(8,128)(2,1)}, u32[]{:S(2)}, u32[]{:S(2)}) collective-permute-start(bf16[512,1024]{1,0:T(8,128)(2,1)S(1)} %constant_dynamic-slice_fusion.2.refs_5_), channel_id=1, source_target_pairs={{0,8},{4,12},{8,0},{12,4},{1,9},{5,13},{9,1},{13,5},{2,10},{6,14},... | collective-permute-start | bytes 3145736 | tf_op jit(solution)/shard_map/ppermute | solution.py:1633
  10.1 103.2 %collective-permute-start.8 = (bf16[512,1024]{1,0:T(8,128)(2,1)S(1)}, bf16[512,1024]{1,0:T(8,128)(2,1)}, u32[]{:S(2)}, u32[]{:S(2)}) collective-permute-start(bf16[512,1024]{1,0:T(8,128)(2,1)S(1)} %constant_dynamic-slice_fusion.2.refs_5_), channel_id=1, source_target_pairs={{0,4},{4,0},{8,12},{12,8},{1,5},{5,1},{9,13},{13,9},{2,6},{6,2},{1... | collective-permute-start | bytes 3145736 | tf_op jit(solution)/shard_map/ppermute | solution.py:1633
  11.5 60.9 %copy-start.7 = (bf16[512,1024]{1,0:T(8,128)(2,1)}, bf16[512,1024]{1,0:T(8,128)(2,1)S(1)}, u32[]{:S(2)}) copy-start(bf16[512,1024]{1,0:T(8,128)(2,1)S(1)} %constant_dynamic-slice_fusion.3.refs_0_) | copy-start | bytes 3145732
  11.5 116.3 %collective-permute-start.5 = (bf16[512,1024]{1,0:T(8,128)(2,1)S(1)}, bf16[512,1024]{1,0:T(8,128)(2,1)}, u32[]{:S(2)}, u32[]{:S(2)}) collective-permute-start(bf16[512,1024]{1,0:T(8,128)(2,1)S(1)} %constant_dynamic-slice_fusion.3.refs_0_), channel_id=1, source_target_pairs={{0,8},{4,12},{8,0},{12,4},{1,9},{5,13},{9,1},{13,5},{2,10},{6,14},... | collective-permute-start | bytes 3145736 | tf_op jit(solution)/shard_map/ppermute | solution.py:1633
  62.5 9.9 %collective-permute-start.3 = (bf16[256,640]{1,0:T(8,128)(2,1)S(1)}, bf16[256,640]{1,0:T(8,128)(2,1)}, u32[]{:S(2)}, u32[]{:S(2)}) collective-permute-start(bf16[256,640]{1,0:T(8,128)(2,1)S(1)} %slice.144), channel_id=1, source_target_pairs={{0,4},{4,0},{8,12},{12,8},{1,5},{5,1},{9,13},{13,9},{2,6},{6,2},{1... | collective-permute-start | bytes 983048 | tf_op jit(solution)/shard_map/ppermute | solution.py:1633
  65.8 10.3 %collective-permute-start.2 = (bf16[256,640]{1,0:T(8,128)(2,1)}, bf16[256,640]{1,0:T(8,128)(2,1)}, u32[]{:S(2)}, u32[]{:S(2)}) collective-permute-start(bf16[256,640]{1,0:T(8,128)(2,1)} %slice.143), channel_id=1, source_target_pairs={{0,8},{4,12},{8,0},{12,4},{1,9},{5,13},{9,1},{13,5},{2,10},{6,14},... | collective-permute-start | bytes 983048 | tf_op jit(solution)/shard_map/ppermute | solution.py:1633
  72.4 66.9 %collective-permute-start.4 = (bf16[512,1024]{1,0:T(8,128)(2,1)S(1)}, bf16[512,1024]{1,0:T(8,128)(2,1)}, u32[]{:S(2)}, u32[]{:S(2)}) collective-permute-start(bf16[512,1024]{1,0:T(8,128)(2,1)S(1)} %constant_dynamic-slice_fusion.3.refs_0_), channel_id=1, source_target_pairs={{0,4},{4,0},{8,12},{12,8},{1,5},{5,1},{9,13},{13,9},{2,6},{6,2},{1... | collective-permute-start | bytes 3145736 | tf_op jit(solution)/shard_map/ppermute | solution.py:1633
  76.1 64.4 %collective-permute-start.13 = (bf16[512,1024]{1,0:T(8,128)(2,1)}, bf16[512,1024]{1,0:T(8,128)(2,1)}, u32[]{:S(2)}, u32[]{:S(2)}) collective-permute-start(bf16[512,1024]{1,0:T(8,128)(2,1)} %pad_maximum_fusion.1.refs_10_), channel_id=1, source_target_pairs={{0,8},{4,12},{8,0},{12,4},{1,9},{5,13},{9,1},{13,5},{2,10},{6,14},... | collective-permute-start | bytes 3145736 | tf_op jit(solution)/shard_map/ppermute | solution.py:1633
  112.1 29.5 %collective-permute-start.12 = (bf16[512,1024]{1,0:T(8,128)(2,1)}, bf16[512,1024]{1,0:T(8,128)(2,1)}, u32[]{:S(2)}, u32[]{:S(2)}) collective-permute-start(bf16[512,1024]{1,0:T(8,128)(2,1)} %pad_maximum_fusion.1.refs_10_), channel_id=1, source_target_pairs={{0,4},{4,0},{8,12},{12,8},{1,5},{5,1},{9,13},{13,9},{2,6},{6,2},{1... | collective-permute-start | bytes 3145736 | tf_op jit(solution)/shard_map/ppermute | solution.py:1633
  113.3 36.4 %collective-permute-start.11 = (bf16[256,1024]{1,0:T(8,128)(2,1)S(1)}, bf16[256,1024]{1,0:T(8,128)(2,1)S(1)}, u32[]{:S(2)}, u32[]{:S(2)}) collective-permute-start(bf16[256,1024]{1,0:T(8,128)(2,1)S(1)} %slice.148), channel_id=1, source_target_pairs={{0,4},{4,0},{8,12},{12,8},{1,5},{5,1},{9,13},{13,9},{2,6},{6,2},{1... | collective-permute-start | bytes 1572872 | tf_op jit(solution)/shard_map/ppermute | solution.py:1633
  127.8 129.3 %collective-permute-start.10 = (bf16[256,1024]{1,0:T(8,128)(2,1)S(1)}, bf16[256,1024]{1,0:T(8,128)(2,1)}, u32[]{:S(2)}, u32[]{:S(2)}) collective-permute-start(bf16[256,1024]{1,0:T(8,128)(2,1)S(1)} %slice.147), channel_id=1, source_target_pairs={{0,8},{4,12},{8,0},{12,4},{1,9},{5,13},{9,1},{13,5},{2,10},{6,14},... | collective-permute-start | bytes 1572872 | tf_op jit(solution)/shard_map/ppermute | solution.py:1633
  139.3 117.9 %collective-permute-start.7 = (bf16[256,1024]{1,0:T(8,128)(2,1)S(1)}, bf16[256,1024]{1,0:T(8,128)(2,1)}, u32[]{:S(2)}, u32[]{:S(2)}) collective-permute-start(bf16[256,1024]{1,0:T(8,128)(2,1)S(1)} %slice.146), channel_id=1, source_target_pairs={{0,4},{4,0},{8,12},{12,8},{1,5},{5,1},{9,13},{13,9},{2,6},{6,2},{1... | collective-permute-start | bytes 1572872 | tf_op jit(solution)/shard_map/ppermute | solution.py:1633
  140.4 116.7 %collective-permute-start.6 = (bf16[256,1024]{1,0:T(8,128)(2,1)S(1)}, bf16[256,1024]{1,0:T(8,128)(2,1)}, u32[]{:S(2)}, u32[]{:S(2)}) collective-permute-start(bf16[256,1024]{1,0:T(8,128)(2,1)S(1)} %slice.145), channel_id=1, source_target_pairs={{0,8},{4,12},{8,0},{12,4},{1,9},{5,13},{9,1},{13,5},{2,10},{6,14},... | collective-permute-start | bytes 1572872 | tf_op jit(solution)/shard_map/ppermute | solution.py:1633
  141.6 115.6 %collective-permute-start.15 = (bf16[256,1024]{1,0:T(8,128)(2,1)S(1)}, bf16[256,1024]{1,0:T(8,128)(2,1)}, u32[]{:S(2)}, u32[]{:S(2)}) collective-permute-start(bf16[256,1024]{1,0:T(8,128)(2,1)S(1)} %slice.150), channel_id=1, source_target_pairs={{0,4},{4,0},{8,12},{12,8},{1,5},{5,1},{9,13},{13,9},{2,6},{6,2},{1... | collective-permute-start | bytes 1572872 | tf_op jit(solution)/shard_map/ppermute | solution.py:1633
  149.7 107.5 %copy-start.17 = (bf16[256,1024]{1,0:T(8,128)(2,1)}, bf16[256,1024]{1,0:T(8,128)(2,1)S(1)}, u32[]{:S(2)}) copy-start(bf16[256,1024]{1,0:T(8,128)(2,1)S(1)} %collective-permute-done.11.refs_9_) | copy-start | bytes 1572868
  149.7 107.5 %collective-permute-start.14 = (bf16[256,1024]{1,0:T(8,128)(2,1)S(1)}, bf16[256,1024]{1,0:T(8,128)(2,1)S(1)}, u32[]{:S(2)}, u32[]{:S(2)}) collective-permute-start(bf16[256,1024]{1,0:T(8,128)(2,1)S(1)} %slice.149), channel_id=1, source_target_pairs={{0,8},{4,12},{8,0},{12,4},{1,9},{5,13},{9,1},{13,5},{2,10},{6,14},... | collective-permute-start | bytes 1572872 | tf_op jit(solution)/shard_map/ppermute | solution.py:1633
  257.2 0.8 copy-start.18
  444.6 32.5 %copy-start.15 = (f32[8,2048]{1,0:T(8,128)S(1)}, f32[8,2048]{1,0:T(8,128)}, u32[]{:S(2)}) copy-start(f32[8,2048]{1,0:T(8,128)} %get-tuple-element.63) | copy-start | bytes 196612
  444.6 32.5 %copy-start.20 = (bf16[2,128,512]{2,1,0:T(8,128)(2,1)S(1)}, bf16[2,128,512]{2,1,0:T(8,128)(2,1)}, u32[]{:S(2)}) copy-start(bf16[2,128,512]{2,1,0:T(8,128)(2,1)} %get-tuple-element.71) | copy-start | bytes 786436
  477.2 86.8 %collective-permute-start.20 = (bf16[2,128,512]{2,1,0:T(8,128)(2,1)S(1)}, bf16[2,128,512]{2,1,0:T(8,128)(2,1)S(1)}, u32[]{:S(2)}, u32[]{:S(2)}) collective-permute-start(bf16[2,128,512]{2,1,0:T(8,128)(2,1)S(1)} %copy-done.20), channel_id=1, source_target_pairs={{0,4},{4,0},{8,12},{12,8},{1,5},{5,1},{9,13},{13,9},{2,6},{6,2},{1... | collective-permute-start | bytes 786440 | tf_op jit(solution)/shard_map/ppermute | solution.py:1633
  482.8 176.2 %collective-permute-start.24 = (bf16[2,3,128,2048]{3,2,1,0:T(8,128)(2,1)}, bf16[2,3,128,2048]{3,2,1,0:T(8,128)(2,1)}, u32[]{:S(2)}, u32[]{:S(2)}) collective-permute-start(bf16[2,3,128,2048]{3,2,1,0:T(8,128)(2,1)} %get-tuple-element.75), channel_id=1, source_target_pairs={{0,4},{4,0},{8,12},{12,8},{1,5},{5,1},{9,13},{13,9},{2,6},{6,2},{1... | collective-permute-start | bytes 9437192 | tf_op jit(solution)/shard_map/ppermute | solution.py:1633
  483.5 75.3 %copy-start.19 = (bf16[2,128,512]{2,1,0:T(8,128)(2,1)S(1)}, bf16[2,128,512]{2,1,0:T(8,128)(2,1)}, u32[]{:S(2)}) copy-start(bf16[2,128,512]{2,1,0:T(8,128)(2,1)} %get-tuple-element.73) | copy-start | bytes 786436
  483.5 82.1 %copy-start.14 = (bf16[2,128,512]{2,1,0:T(8,128)(2,1)S(1)}, bf16[2,128,512]{2,1,0:T(8,128)(2,1)}, u32[]{:S(2)}) copy-start(bf16[2,128,512]{2,1,0:T(8,128)(2,1)} %get-tuple-element.70) | copy-start | bytes 786436
  483.5 86.2 %copy-start.13 = (bf16[2,128,512]{2,1,0:T(8,128)(2,1)S(1)}, bf16[2,128,512]{2,1,0:T(8,128)(2,1)}, u32[]{:S(2)}) copy-start(bf16[2,128,512]{2,1,0:T(8,128)(2,1)} %get-tuple-element.72) | copy-start | bytes 786436
  558.8 9.2 %collective-permute-start.22 = (bf16[2,128,512]{2,1,0:T(8,128)(2,1)S(1)}, bf16[2,128,512]{2,1,0:T(8,128)(2,1)S(1)}, u32[]{:S(2)}, u32[]{:S(2)}) collective-permute-start(bf16[2,128,512]{2,1,0:T(8,128)(2,1)S(1)} %copy-done.19), channel_id=1, source_target_pairs={{0,8},{4,12},{8,0},{12,4},{1,9},{5,13},{9,1},{13,5},{2,10},{6,14},... | collective-permute-start | bytes 786440 | tf_op jit(solution)/shard_map/ppermute | solution.py:1633
  560.5 91.4 %collective-permute-start.16 = (bf16[2,128,768]{2,1,0:T(8,128)(2,1)}, bf16[2,128,768]{2,1,0:T(8,128)(2,1)}, u32[]{:S(2)}, u32[]{:S(2)}) collective-permute-start(bf16[2,128,768]{2,1,0:T(8,128)(2,1)} %get-tuple-element.67), channel_id=1, source_target_pairs={{0,4},{4,0},{8,12},{12,8},{1,5},{5,1},{9,13},{13,9},{2,6},{6,2},{1... | collective-permute-start | bytes 1179656 | tf_op jit(solution)/shard_map/ppermute | solution.py:1633
  562.3 92.7 %collective-permute-start.18 = (bf16[2,128,768]{2,1,0:T(8,128)(2,1)}, bf16[2,128,768]{2,1,0:T(8,128)(2,1)S(1)}, u32[]{:S(2)}, u32[]{:S(2)}) collective-permute-start(bf16[2,128,768]{2,1,0:T(8,128)(2,1)} %get-tuple-element.69), channel_id=1, source_target_pairs={{0,8},{4,12},{8,0},{12,4},{1,9},{5,13},{9,1},{13,5},{2,10},{6,14},... | collective-permute-start | bytes 1179656 | tf_op jit(solution)/shard_map/ppermute | solution.py:1633
  564.0 101.2 %collective-permute-start.26 = (bf16[2,3,128,2048]{3,2,1,0:T(8,128)(2,1)}, bf16[2,3,128,2048]{3,2,1,0:T(8,128)(2,1)}, u32[]{:S(2)}, u32[]{:S(2)}) collective-permute-start(bf16[2,3,128,2048]{3,2,1,0:T(8,128)(2,1)} %get-tuple-element.77), channel_id=1, source_target_pairs={{0,8},{4,12},{8,0},{12,4},{1,9},{5,13},{9,1},{13,5},{2,10},{6,14},... | collective-permute-start | bytes 9437192 | tf_op jit(solution)/shard_map/ppermute | solution.py:1633
  565.7 86.2 %copy-start.12 = (bf16[2,128,768]{2,1,0:T(8,128)(2,1)S(1)}, bf16[2,128,768]{2,1,0:T(8,128)(2,1)}, u32[]{:S(2)}) copy-start(bf16[2,128,768]{2,1,0:T(8,128)(2,1)} %get-tuple-element.66) | copy-start | bytes 1179652
  568.1 77.9 %collective-permute-start.21 = (bf16[128,512]{1,0:T(8,128)(2,1)S(1)}, bf16[128,512]{1,0:T(8,128)(2,1)S(1)}, u32[]{:S(2)}, u32[]{:S(2)}) collective-permute-start(bf16[128,512]{1,0:T(8,128)(2,1)S(1)} %fusion.17), channel_id=1, source_target_pairs={{0,8},{4,12},{8,0},{12,4},{1,9},{5,13},{9,1},{13,5},{2,10},{6,14},... | collective-permute-start | bytes 393224 | tf_op jit(solution)/shard_map/ppermute | solution.py:1633
  569.8 85.1 %copy-start.11 = (bf16[2,128,768]{2,1,0:T(8,128)(2,1)S(1)}, bf16[2,128,768]{2,1,0:T(8,128)(2,1)}, u32[]{:S(2)}) copy-start(bf16[2,128,768]{2,1,0:T(8,128)(2,1)} %get-tuple-element.68) | copy-start | bytes 1179652
  645.9 5.0 collective-permute-start.23
  651.9 7.1 copy-start.5
  653.2 5.7 collective-permute-start.17
  655.0 19.3 %collective-permute-start.19 = (bf16[128,768]{1,0:T(8,128)(2,1)S(1)}, bf16[128,768]{1,0:T(8,128)(2,1)S(1)}, u32[]{:S(2)}, u32[]{:S(2)}) collective-permute-start(bf16[128,768]{1,0:T(8,128)(2,1)S(1)} %fusion.16), channel_id=1, source_target_pairs={{0,4},{4,0},{8,12},{12,8},{1,5},{5,1},{9,13},{13,9},{2,6},{6,2},{1... | collective-permute-start | bytes 589832 | tf_op jit(solution)/shard_map/ppermute | solution.py:1633
  662.1 7.3 %copy-start.2 = (f32[2,3,128,2048]{3,2,1,0:T(8,128)}, f32[2,3,128,2048]{3,2,1,0:T(8,128)S(1)}, u32[]{:S(2)}) copy-start(f32[2,3,128,2048]{3,2,1,0:T(8,128)S(1)} %convert_add_fusion.1) | copy-start | bytes 18874372
  662.1 4.2 copy-start.4
  663.5 33.6 %collective-permute-start.25 = (bf16[3,128,2048]{2,1,0:T(8,128)(2,1)}, bf16[3,128,2048]{2,1,0:T(8,128)(2,1)}, u32[]{:S(2)}, u32[]{:S(2)}) collective-permute-start(bf16[3,128,2048]{2,1,0:T(8,128)(2,1)} %fusion.7), channel_id=1, source_target_pairs={{0,8},{4,12},{8,0},{12,4},{1,9},{5,13},{9,1},{13,5},{2,10},{6,14},... | collective-permute-start | bytes 4718600 | tf_op jit(solution)/shard_map/ppermute | solution.py:1633
  669.5 3.1 copy-start.3
  672.6 33.6 %collective-permute-start.27 = (bf16[3,128,2048]{2,1,0:T(8,128)(2,1)}, bf16[3,128,2048]{2,1,0:T(8,128)(2,1)}, u32[]{:S(2)}, u32[]{:S(2)}) collective-permute-start(bf16[3,128,2048]{2,1,0:T(8,128)(2,1)} %fusion.8), channel_id=1, source_target_pairs={{0,4},{4,0},{8,12},{12,8},{1,5},{5,1},{9,13},{13,9},{2,6},{6,2},{1... | collective-permute-start | bytes 4718600 | tf_op jit(solution)/shard_map/ppermute | solution.py:1633
  711.9 3.1 copy-start.9
  711.9 4.6 copy-start.1
  711.9 3.8 copy-start.10

commit v3 on v2

--- a/solution.py
+++ b/solution.py
@@ -430,6 +430,24 @@
     lax.fori_loop(0, count // step, run, 0)
 
 
+def square_partners(r, n, w):
+    return [(n >= 0, over_x(r, n, w)), (n >= 0, over_y(r, n, w))]
+
+
+def over_x(r, n, w):
+    return (r, n + 1 - 2 * (n % 2), w)
+
+
+def over_y(r, n, w):
+    return (r, (n + 2) % 4, w)
+
+
+def push(source, target, s_s, s_g, device):
+    return pltpu.make_async_remote_copy(
+        source, target, s_s, s_g, device_id=device, device_id_type=MESH
+    )
+
+
 class Gather:
     def __init__(self, buf, sems, me, wid_count):
         self.buf, (self.up_s, self.dn_s, self.pt_s, self.got) = buf, sems
@@ -573,6 +591,15 @@
         @pl.when(s < self.w)
         def _():
             self.fall(s).start()
+
+    def advance(self, edge_steps, inner_steps):
+        for ends, steps in ((True, edge_steps), (False, inner_steps)):
+            at_end = (self.w == 0) | (self.w == self.last)
+
+            @pl.when(at_end if ends else jnp.logical_not(at_end))
+            def _():
+                for i in steps:
+                    self.step(self.order(i))
 
     def total(self, out):
         w = self.w
@@ -713,26 +740,8 @@
     return (r, jnp.clip(n + by, 0, 3), w)
 
 
-def load_pieces(pieces, target, sems, n):
-    own, by_x, by_y, far_a, far_b = pieces
-    rows = own.shape[0] // 2
-    copies = [
-        pltpu.make_async_copy(own, target.at[n], sems.at[0]),
-        pltpu.make_async_copy(by_x, target.at[n ^ 1], sems.at[1]),
-        pltpu.make_async_copy(by_y, target.at[n ^ 2], sems.at[2]),
-        pltpu.make_async_copy(far_a, target.at[n ^ 3, pl.ds(0, rows)], sems.at[3]),
-        pltpu.make_async_copy(far_b, target.at[n ^ 3, pl.ds(rows, rows)], sems.at[4]),
-    ]
-    for copy in copies:
-        copy.start()
-    return copies
-
-
-def project_kernel(
-    x, a0, a1, a2, a3, a4, tabs, q_out, kv_out, p1_out, kv, s_s, s_g, out_s, p1, in_s, p1_s
-):
+def project_kernel(x, p1, tabs, q_out, kv_out, kv, s_s, s_g, out_s):
     r, n, w = spot()
-    loads = load_pieces((a0, a1, a2, a3, a4), p1, in_s, n)
     greet(
         [
             (n >= 1, nar_device(r, n, w, -1)),
@@ -748,10 +757,6 @@
             device_id=nar_device(r, n, w, by), device_id_type=MESH,
         )
 
-    for load in loads:
-        load.wait()
-    p1_copy = pltpu.make_async_copy(p1, p1_out, p1_s)
-    p1_copy.start()
     lane = lax.broadcasted_iota(jnp.int32, (256, 128), 1)
     weight = p1[:, :, 0:384].reshape(2048, 384)
     for row in range(2):
@@ -798,28 +803,23 @@
             copy(row, 0, 2).wait_send()
 
     out.wait()
-    p1_copy.wait()
-
-
-def project(x, pieces, tabs):
+
+
+def project(x, p1, tabs):
     return comm_call(
         project_kernel, "project", 2,
         (
             jax.ShapeDtypeStruct((2, 512, 256), bf16),
             jax.ShapeDtypeStruct((2, 3, 512, 128), bf16),
-            jax.ShapeDtypeStruct((4, 512, 640), bf16),
         ),
-        [vmem()] + [hbm()] * 5 + [vmem()], [vmem(), hbm(), hbm()],
+        [vmem()] * 3, [vmem(), hbm()],
         [
             pltpu.VMEM((2, 3, 512, 128), bf16),
             pltpu.SemaphoreType.DMA((2, 3)),
             pltpu.SemaphoreType.DMA((2, 3)),
             pltpu.SemaphoreType.DMA(()),
-            pltpu.VMEM((4, 512, 640), bf16),
-            pltpu.SemaphoreType.DMA((5,)),
-            pltpu.SemaphoreType.DMA(()),
         ],
-        (x, *pieces, tabs), flops=10**10, sent=10**7,
+        (x, p1, tabs), flops=10**10, sent=10**7,
     )
 
 
@@ -1118,20 +1118,16 @@
 
 
 def ffn_kernel(
-    x, tops, *refs
+    x, tops, p2_all, gain, part_out, sum_out, gain_out, o0, o1, o2, o3, ra_out, rb_out,
+    theirs, mine, from_pt, from_up, from_dn, s0, s1, s2, s3, s4, s5,
+    act, dgu, stage, wide, out_s, give_s, give_g, keep_s, p2, in_s, n_s, n_g,
 ):
-    pieces, refs = refs[:15], refs[15:]
-    (
-        gain, part_out, sum_out, gain_out, o0, o1, o2, o3,
-        theirs, mine, from_pt, from_up, from_dn, s0, s1, s2, s3, s4, s5,
-        act, dgu, stage, wide, out_s, give_s, give_g, keep_s, p2, in_s,
-    ) = refs
     me = spot()
     r, n, w = me
-    loads = []
-    for j in range(3):
-        loads += load_pieces(pieces[5 * j : 5 * j + 5], p2.at[j], in_s.at[j], n)
-    greet(line_partners(r, n, w, 4))
+    loads = [pltpu.make_async_copy(p2_all.at[:, j], p2.at[j], in_s.at[j]) for j in range(3)]
+    for load in loads:
+        load.start()
+    greet(line_partners(r, n, w, 4) + square_partners(r, n, w))
     scatter = Scatter(
         mine, theirs, (from_pt, from_up, from_dn), (s0, s1, s2, s3, s4, s5), me, 4
     )
@@ -1144,6 +1140,60 @@
             stage.at[slot, row_slot], part_out.at[row, s], out_s.at[slot, row_slot]
         )
 
+    def hidden_tile(i, carry):
+        ft, row = i // 2, i % 2
+        rows = pl.ds(pl.multiple_of(row * 512, 512), 512)
+        columns = pl.ds(pl.multiple_of(ft * 256, 256), 256)
+        left = x[rows, :]
+        gate = jnp.dot(left, p2[0, :, :, columns].reshape(2048, 256), preferred_element_type=f32)
+        up = jnp.dot(left, p2[1, :, :, columns].reshape(2048, 256), preferred_element_type=f32)
+        f_rows = pl.ds(pl.multiple_of((ft % 2) * 256, 256), 256)
+        f_cols = pl.ds(pl.multiple_of((ft // 2) * 512, 512), 512)
+        right = jnp.concatenate([p2[2, nn, f_rows, f_cols] for nn in range(4)], axis=1)
+        dact = contract_last(tops[rows, :], right)
+        sig = 1.0 / (1.0 + jnp.exp(-gate))
+        silu = gate * sig
+        act[rows, columns] = (silu * up).astype(bf16)
+        dgu[rows, columns] = (dact * up * (sig * (1.0 + gate * (1.0 - sig)))).astype(bf16)
+        later = pl.ds(pl.multiple_of(1024 + ft * 256, 256), 256)
+        dgu[rows, later] = (dact * silu).astype(bf16)
+        return carry
+
+    lax.fori_loop(0, 8, hidden_tile, 0)
+
+    spread = Spread((o0, o1, o2, o3), (give_s, give_g, keep_s), me)
+    columns_here = pl.ds(pl.multiple_of(r * 1024, 1024), 1024)
+    slots = {2: 0, 0: 1, 1: 0}
+
+    def moved(which, half):
+        def place(target):
+            return target.at[which, :, columns_here]
+
+        return wide.at[slots[which], half], which, place, half == 0
+
+    def weights(which):
+        for half in range(2):
+            d_first = (jnp.where(half == 0, 1 - r, r)) * 1024
+
+            def weight_tile(i, carry):
+                d_rows = pl.ds(pl.multiple_of(d_first + i * 256, 256), 256)
+                source = x if which < 2 else tops
+                left = source[:, d_rows]
+                if which < 2:
+                    right = dgu[:, which * 1024 : which * 1024 + 1024]
+                else:
+                    right = act[...]
+                wide[slots[which], half, i] = contract_first(left, right).astype(bf16)
+                return carry
+
+            lax.fori_loop(0, 4, weight_tile, 0)
+            spread.start(*moved(which, half))
+
+    hops = [
+        push(o0.at[:, 2], ra_out, n_s.at[0], n_g.at[0], over_x(r, n, w)),
+        push(o2.at[:, 2], rb_out, n_s.at[1], n_g.at[1], over_y(r, n, w)),
+    ]
+    weights(2)
     for i in range(4):
         s = scatter.order(i)
         slot = i % 2
@@ -1152,32 +1202,6 @@
         if i >= 2:
             put(s, slot, 0, 1 - r).wait()
             put(s, slot, 1, r).wait()
-
-        def hidden_tile(ft, carry):
-            columns = pl.ds(pl.multiple_of(ft * 256, 256), 256)
-            left = jnp.concatenate([x[rows_t, :], x[rows_m, :]], axis=0)
-            gate = jnp.dot(left, p2[0, :, :, columns].reshape(2048, 256), preferred_element_type=f32)
-            up = jnp.dot(left, p2[1, :, :, columns].reshape(2048, 256), preferred_element_type=f32)
-            sig = 1.0 / (1.0 + jnp.exp(-gate))
-            silu = gate * sig
-            active = (silu * up).astype(bf16)
-            act[rows_t, columns] = active[0:128]
-            act[rows_m, columns] = active[128:256]
-            f_rows = pl.ds(pl.multiple_of((ft % 2) * 256, 256), 256)
-            f_cols = pl.ds(pl.multiple_of((ft // 2) * 512, 512), 512)
-            right = jnp.concatenate([p2[2, nn, f_rows, f_cols] for nn in range(4)], axis=1)
-            top = jnp.concatenate([tops[rows_t, :], tops[rows_m, :]], axis=0)
-            dact = contract_last(top, right)
-            dgate = (dact * up * (sig * (1.0 + gate * (1.0 - sig)))).astype(bf16)
-            dup = (dact * silu).astype(bf16)
-            dgu[rows_t, columns] = dgate[0:128]
-            dgu[rows_m, columns] = dgate[128:256]
-            later = pl.ds(pl.multiple_of(1024 + ft * 256, 256), 256)
-            dgu[rows_t, later] = dup[0:128]
-            dgu[rows_m, later] = dup[128:256]
-            return carry
-
-        lax.fori_loop(0, 4, hidden_tile, 0)
 
         def model_tile(dt, carry):
             nn, half = dt // 2, dt % 2
@@ -1204,60 +1228,42 @@
         scatter.pair(s).start()
         put(s, slot, 0, 1 - r).start()
         put(s, slot, 1, r).start()
+        if i == 0:
+            spread.wait_recv(*moved(2, 0))
+            spread.wait(*moved(2, 1))
+            for hop in hops:
+                hop.start()
+        else:
+            scatter.advance((i - 1,), (i - 2,) if i > 1 else ())
 
     def scale(rows):
         gain_out[rows, :] = gain_out[rows, :] / gain[...]
 
     each_rows(8, 8, scale)
-
-    spread = Spread((o0, o1, o2, o3), (give_s, give_g, keep_s), me)
-    columns_here = pl.ds(pl.multiple_of(r * 1024, 1024), 1024)
-
-    def moved(which, half):
-        def place(target):
-            return target.at[which, :, columns_here]
-
-        return wide.at[which % 2, half], which, place, half == 0
-
-    for which in range(3):
-        scatter.step(scatter.order(which))
-        if which == 2:
-            spread.wait_send(*moved(0, 0))
-            spread.wait(*moved(0, 1))
-        for half in range(2):
-            d_first = (jnp.where(half == 0, 1 - r, r)) * 1024
-
-            def weight_tile(i, carry):
-                d_rows = pl.ds(pl.multiple_of(d_first + i * 256, 256), 256)
-                source = x if which < 2 else tops
-                left = source[:, d_rows]
-                if which < 2:
-                    right = dgu[:, which * 1024 : which * 1024 + 1024]
-                else:
-                    right = act[...]
-                wide[which % 2, half, i] = contract_first(left, right).astype(bf16)
-                return carry
-
-            lax.fori_loop(0, 4, weight_tile, 0)
-            spread.start(*moved(which, half))
-    scatter.step(scatter.order(3))
+    scatter.advance((3,), ())
+    weights(0)
+    scatter.advance((), (2,))
+    spread.wait_send(*moved(2, 0))
+    weights(1)
+    scatter.advance((), (3,))
     scatter.total(sum_out)
     scatter.sent()
-    for which in range(3):
+    for which in (0, 1):
         spread.wait_recv(*moved(which, 0))
-        if which > 0:
-            spread.wait_send(*moved(which, 0))
-            spread.wait(*moved(which, 1))
+        spread.wait_send(*moved(which, 0))
+        spread.wait(*moved(which, 1))
     for slot in range(2):
         put(0, slot, 0, 1 - r).wait()
         put(0, slot, 1, r).wait()
+    for hop in hops:
+        hop.wait()
 
 
 def spread_shapes(*dims):
     return (jax.ShapeDtypeStruct((2,) + dims, bf16),) * 4
 
 
-def ffn_stage(x, tops, pieces, gain):
+def ffn_stage(x, tops, p2, gain):
     shard, width = 128, 2048
     return comm_call(
         ffn_kernel, "ffn", 4,
@@ -1266,8 +1272,9 @@
             jax.ShapeDtypeStruct((shard, width), f32),
             jax.ShapeDtypeStruct((8, width), f32),
         )
-        + spread_shapes(3, 128, width),
-        [vmem()] * 2 + [hbm()] * 15 + [vmem()], [hbm(), vmem(), vmem()] + [hbm()] * 4,
+        + spread_shapes(3, 128, width)
+        + (jax.ShapeDtypeStruct((2, 128, width), bf16),) * 2,
+        [vmem()] * 2 + [hbm()] + [vmem()], [hbm(), vmem(), vmem()] + [hbm()] * 6,
         [pltpu.VMEM((4, shard, width), bf16)] * 2
         + scatter_bufs(shard, width) + scatter_sems()
         + [
@@ -1278,8 +1285,9 @@
             pltpu.SemaphoreType.DMA((2, 2)),
         ]
         + spread_sems(3)
-        + [pltpu.VMEM((3, 4, 512, 1024), bf16), pltpu.SemaphoreType.DMA((3, 5))],
-        (x, tops, *pieces, gain), flops=4 * 10**10, sent=10**8,
+        + [pltpu.VMEM((3, 4, 512, 1024), bf16), pltpu.SemaphoreType.DMA((3,))]
+        + [pltpu.SemaphoreType.DMA((2,))] * 2,
+        (x, tops, p2, gain), flops=4 * 10**10, sent=10**8,
     )
 
 
@@ -1291,17 +1299,19 @@
 
 
 def branch_kernel(
-    total, mid, grad_top, gain, parts, p1, att, hid_out, gmid_out, datt_out, o0, o1, o2, o3,
-    mine, from_pt, from_up, from_dn, s0, s1, s2, s3, s4, s5,
-    buf, g0, g1, g2, g3, acc, wide, give_s, give_g, keep_s,
+    total, mid, grad_top, gain, p1, att, a_in, b_in, gmid_out, datt_out, o0, o1, o2, o3, ra_out, rb_out,
+    buf, g0, g1, g2, g3, wide, give_s, give_g, keep_s, n_s, n_g,
 ):
     me = spot()
     r, n, w = me
-    greet(line_partners(r, n, w, 4))
-    scatter = Scatter(
-        mine, parts.at[1 - r], (from_pt, from_up, from_dn), (s0, s1, s2, s3, s4, s5), me, 4
-    )
+    greet(line_partners(r, n, w, 4) + square_partners(r, n, w))
     gather = Gather(buf, (g0, g1, g2, g3), me, 4)
+    hops = [
+        push(a_in.at[:, 0:2], ra_out, n_s.at[0], n_g.at[0], over_x(r, n, w)),
+        push(b_in.at[:, 0:2], rb_out, n_s.at[1], n_g.at[1], over_y(r, n, w)),
+    ]
+    for hop in hops:
+        hop.start()
 
     def body(rows):
         grad = norm_back(mid[rows, :], gain[...], total[rows, :]) + grad_top[rows, :].astype(f32)
@@ -1310,18 +1320,8 @@
 
     each_rows(mid.shape[0], 16, body)
     gather.own()
-    for i in range(4):
-        scatter.pair(scatter.order(i)).start()
-
-    for s in range(4):
-        def fill(rows):
-            mine[s, rows, :] = parts[r, s, rows, :]
-
-        each_rows(128, 16, fill)
-    for i in range(4):
-        scatter.step(scatter.order(i))
-        if i < 3:
-            gather.step(i + 1)
+    for k in (1, 2, 3):
+        gather.step(k)
     gather.rest()
     for row in range(2):
         for pair in range(2):
@@ -1350,55 +1350,70 @@
 
         lax.fori_loop(0, 4, weight_tile, 0)
         spread.start(*moved(half))
-    scatter.total(acc)
-
-    def last(rows):
-        hid_out[rows, :] = (acc[rows, :] + mid[rows, :]).astype(bf16)
-
-    each_rows(mid.shape[0], 16, last)
-    scatter.sent()
     gather.sent()
     spread.wait(*moved(0))
     spread.wait(*moved(1))
-
-
-def branch_stage(total, mid, grad_top, gain, parts, p1, att):
+    for hop in hops:
+        hop.wait()
+
+
+def branch_stage(total, mid, grad_top, gain, p1, att, a_in, b_in):
     shard, width = mid.shape
     return comm_call(
         branch_kernel, "branch", 5,
         (
-            jax.ShapeDtypeStruct((shard, width), bf16),
             jax.ShapeDtypeStruct((shard, width), f32),
             jax.ShapeDtypeStruct((2, 512, 256), bf16),
         )
-        + spread_shapes(128, 512),
-        [vmem()] * 7, [vmem(), vmem(), vmem()] + [hbm()] * 4,
-        [pltpu.VMEM((4, shard, width), bf16)]
-        + scatter_bufs(shard, width) + scatter_sems()
-        + gather_scratch(shard, width)
+        + spread_shapes(128, 512)
+        + (jax.ShapeDtypeStruct((2, 2, 128, width), bf16),) * 2,
+        [vmem()] * 6 + [hbm()] * 2, [vmem(), vmem()] + [hbm()] * 6,
+        gather_scratch(shard, width)
+        + [pltpu.VMEM((2, 4, 256, 256), bf16)]
+        + spread_sems(1)
+        + [pltpu.SemaphoreType.DMA((2,))] * 2,
+        (total, mid, grad_top, gain, p1, att, a_in, b_in), flops=10**10, sent=10**8,
+    )
+
+
+def unproject_kernel(
+    dq, dkv, x, p1, tabs, gain, parts, mid, a_keep, b_keep, ra_gu, rb_gu, ra_d, rb_d, oa_in, ob_in,
+    part_out, gain_out, o0, o1, o2, o3, hid_out, ra_out, rb_out, roa_out, rob_out,
+    send, recv, both, wide_q, wide_kv, s_s, s_g, give_s, give_g, keep_s,
+    mine, from_pt, from_up, from_dn, s0, s1, s2, s3, s4, s5,
+    kept, came, acc, in_s, n_s, n_g, m_s,
+):
+    me = spot()
+    r, n, w = me
+    loads = []
+    for j, (keep, gate_up, down) in enumerate(((a_keep, ra_gu, ra_d), (b_keep, rb_gu, rb_d))):
+        loads += [
+            pltpu.make_async_copy(keep.at[1], kept.at[j], in_s.at[j, 0]),
+            pltpu.make_async_copy(gate_up.at[1], came.at[j, 0:2], in_s.at[j, 1]),
+            pltpu.make_async_copy(down.at[1], came.at[j, 2], in_s.at[j, 2]),
+        ]
+    loads.append(pltpu.make_async_copy(parts.at[r], mine, m_s))
+    for load in loads:
+        load.start()
+    greet(
+        line_partners(r, n, w, 4)
         + [
-            pltpu.VMEM((shard, width), f32),
-            pltpu.VMEM((2, 4, 256, 256), bf16),
-        ]
-        + spread_sems(1),
-        (total, mid, grad_top, gain, parts, p1, att), flops=10**10, sent=10**8,
-    )
-
-
-def unproject_kernel(
-    dq, dkv, x, p1, tabs, gain, part_out, gain_out, o0, o1, o2, o3,
-    send, recv, both, wide_q, wide_kv, s_s, s_g, give_s, give_g, keep_s,
-):
-    r, n, w = spot()
-    greet(
-        [
             (n >= 1, nar_device(r, n, w, -1)),
             (n >= 2, nar_device(r, n, w, -2)),
             (n <= 2, nar_device(r, n, w, 1)),
             (n <= 1, nar_device(r, n, w, 2)),
-            (n >= 0, (1 - r, n, w)),
         ]
-    )
+        + square_partners(r, n, w)
+    )
+    scatter = Scatter(
+        mine, parts.at[1 - r], (from_pt, from_up, from_dn), (s0, s1, s2, s3, s4, s5), me, 4
+    )
+    hops = [
+        push(kept.at[0], ra_out, n_s.at[0], n_g.at[0], over_y(r, n, w)),
+        push(kept.at[1], rb_out, n_s.at[1], n_g.at[1], over_x(r, n, w)),
+        push(oa_in, roa_out, n_s.at[2], n_g.at[2], over_x(r, n, w)),
+        push(ob_in, rob_out, n_s.at[3], n_g.at[3], over_y(r, n, w)),
+    ]
 
     def copy(row, slot, by):
         return pltpu.make_async_remote_copy(
@@ -1413,6 +1428,22 @@
                 send[row, slot] = dkv[row, slot].astype(bf16)
                 copy(row, slot, by).start()
 
+    for i in range(4):
+        scatter.pair(scatter.order(i)).start()
+    for load in loads:
+        load.wait()
+    for j in range(2):
+        for which in range(3):
+            def join(rows):
+                total = kept[j, which, rows, :].astype(f32) + came[j, which, rows, :].astype(f32)
+                kept[j, which, rows, :] = total.astype(bf16)
+
+            each_rows(128, 16, join)
+        hops[j].start()
+    hops[2].start()
+    hops[3].start()
+    scatter.advance((0, 1, 2, 3), ())
+
     spread = Spread((o0, o1, o2, o3), (give_s, give_g, keep_s), (r, n, w))
 
     def moved_q(half):
@@ -1443,6 +1474,7 @@
     for half in range(2):
         weight(half, slice(0, 256), wide_q)
         spread.start(*moved_q(half))
+    scatter.advance((), (0,))
     lane = lax.broadcasted_iota(jnp.int32, (128, 128), 1)
     for row in range(2):
         for slot, by in ((1, -1), (0, -2)):
@@ -1466,6 +1498,7 @@
     for half in range(2):
         weight(half, slice(256, 384), wide_kv)
         spread.start(*moved_kv(half))
+    scatter.advance((), (1,))
     gain_out[...] = jnp.zeros_like(gain_out)
 
     def model_tile(dt, carry):
@@ -1485,6 +1518,14 @@
 
     lax.fori_loop(0, 8, model_tile, 0)
     gain_out[...] = gain_out[...] / gain[...]
+    scatter.advance((), (2, 3))
+    scatter.total(acc)
+
+    def last(rows):
+        hid_out[rows, :] = (acc[rows, :] + mid[rows, :]).astype(bf16)
+
+    each_rows(128, 16, last)
+    scatter.sent()
     for row in range(2):
         for slot, by in ((1, -1), (0, -2)):
             @pl.when(n >= -by)
@@ -1494,17 +1535,23 @@
     for half in range(2):
         spread.wait(*moved_q(half))
         spread.wait(*moved_kv(half))
-
-
-def unproject(dq, dkv, x, p1, tabs, gain):
+    for hop in hops:
+        hop.wait()
+
+
+def unproject(*args):
     return comm_call(
         unproject_kernel, "unproject", 6,
         (
             jax.ShapeDtypeStruct((2, 4, 128, 2048), bf16),
             jax.ShapeDtypeStruct((8, 2048), f32),
         )
-        + spread_shapes(128, 768),
-        [vmem()] * 6, [vmem(), vmem()] + [hbm()] * 4,
+        + spread_shapes(128, 768)
+        + (jax.ShapeDtypeStruct((128, 2048), bf16),)
+        + (jax.ShapeDtypeStruct((3, 128, 2048), bf16),) * 2
+        + (jax.ShapeDtypeStruct((2, 128, 512), bf16),) * 2,
+        [vmem()] * 6 + [hbm(), vmem()] + [hbm()] * 8,
+        [vmem(), vmem()] + [hbm()] * 4 + [vmem()] + [hbm()] * 4,
         [
             pltpu.VMEM((2, 2, 512, 128), bf16),
             pltpu.VMEM((2, 2, 512, 128), bf16),
@@ -1514,15 +1561,28 @@
             pltpu.SemaphoreType.DMA((2, 2)),
             pltpu.SemaphoreType.DMA((2, 2)),
         ]
-        + spread_sems(2),
-        (dq, dkv, x, p1, tabs, gain), flops=10**10, sent=10**7,
+        + spread_sems(2)
+        + [pltpu.VMEM((4, 128, 2048), bf16)]
+        + scatter_bufs(128, 2048) + scatter_sems()
+        + [
+            pltpu.VMEM((2, 3, 128, 2048), bf16),
+            pltpu.VMEM((2, 3, 128, 2048), bf16),
+            pltpu.VMEM((128, 2048), f32),
+            pltpu.SemaphoreType.DMA((2, 3)),
+            pltpu.SemaphoreType.DMA((4,)),
+            pltpu.SemaphoreType.DMA((4,)),
+            pltpu.SemaphoreType.DMA(()),
+        ],
+        args, flops=10**10, sent=10**7,
     )
 
 
 def leave_kernel(
-    parts, hidden, gain, gmid, gains, grad_out, ga_out,
+    parts, hidden, gain, gmid, gains, qa_send, qa_keep, qb_send, qb_keep, oa_keep, ob_keep, oa_in, ob_in,
+    grad_out, ga_out, query_out, key_out, value_out, output_out,
     mine, from_pt, from_up, from_dn, s0, s1, s2, s3, s4, s5,
     acc, over_wid, summed, over_rest, w_s, w_g, t_s, t_g,
+    first_q, next_q, then_q, next_o, then_o, kv, n_s, n_g, k_s, k_g,
 ):
     me = spot()
     r, n, w = me
@@ -1531,6 +1591,21 @@
         ((r != a) | (n != b), (jnp.int32(a), jnp.int32(b), w)) for a in range(2) for b in range(4)
     ]
     greet(partners)
+    x_side, y_side = over_x(r, n, w), over_y(r, n, w)
+    q_hops = [
+        push(qa_send, first_q.at[0], n_s.at[0], n_g.at[0], x_side),
+        push(qb_send, first_q.at[1], n_s.at[1], n_g.at[1], y_side),
+    ]
+    q_later = [
+        push(next_q.at[0], then_q.at[0], n_s.at[2], n_g.at[2], y_side),
+        push(next_q.at[1], then_q.at[1], n_s.at[3], n_g.at[3], x_side),
+    ]
+    o_hops = [
+        push(next_o.at[0], then_o.at[0], n_s.at[4], n_g.at[4], y_side),
+        push(next_o.at[1], then_o.at[1], n_s.at[5], n_g.at[5], x_side),
+    ]
+    for hop in q_hops:
+        hop.start()
     scatter = Scatter(
         mine, parts.at[1 - r], (from_pt, from_up, from_dn), (s0, s1, s2, s3, s4, s5), me, 4
     )
@@ -1559,7 +1634,10 @@
             mine[s, rows, :] = parts[r, s, rows, :]
 
         each_rows(128, 16, fill)
-    scatter.step(scatter.order(0))
+    scatter.advance((0, 1, 2, 3), ())
+    for j, (keep, came) in enumerate(((oa_keep, oa_in), (ob_keep, ob_in))):
+        next_o[j] = (keep[1].astype(f32) + came[1].astype(f32)).astype(bf16)
+        o_hops[j].start()
     summed[...] = gains[...]
     for j in range(4):
         @pl.when(w != j)
@@ -1573,8 +1651,40 @@
             def _():
                 rest_copy(a, b, r * 4 + n).start()
 
-    for i in (1, 2, 3):
-        scatter.step(scatter.order(i))
+    for j, keep in enumerate((qa_keep, qb_keep)):
+        q_hops[j].wait_recv()
+        next_q[j] = (keep[1].astype(f32) + first_q[j, 1].astype(f32)).astype(bf16)
+        q_later[j].start()
+    scatter.advance((), (0, 1))
+    for j, keep in enumerate((qa_keep, qb_keep)):
+        q_later[j].wait_recv()
+        total = keep[0].astype(f32) + first_q[j, 0].astype(f32) + then_q[j].astype(f32)
+        query_out[j * 128 : j * 128 + 128, :] = total[:, 0:512]
+        kv[w, j * 128 : j * 128 + 128, :] = total[:, 512:768].astype(bf16)
+
+    def kv_copy(j, slot):
+        return pltpu.make_async_remote_copy(
+            kv.at[w], kv.at[w], k_s.at[j], k_g.at[slot],
+            device_id=(r, n, jnp.int32(j)), device_id_type=MESH,
+        )
+
+    def kv_wait(j):
+        return pltpu.make_async_remote_copy(
+            kv.at[j], kv.at[j], k_s.at[j], k_g.at[j],
+            device_id=(r, n, jnp.int32(j)), device_id_type=MESH,
+        )
+
+    for j in range(4):
+        @pl.when(w != j)
+        def _():
+            kv_copy(j, w).start()
+
+    scatter.advance((), (2, 3))
+    for j, (keep, came) in enumerate(((oa_keep, oa_in), (ob_keep, ob_in))):
+        o_hops[j].wait_recv()
+        output_out[j * 128 : j * 128 + 128, :] = (
+            keep[0].astype(f32) + came[0].astype(f32) + then_o[j].astype(f32)
+        )
     mine_block = r * 4 + n
     ga_out[0:1] = summed[pl.ds(mine_block, 1), :]
     ga_out[1:2] = summed[pl.ds(mine_block + 8, 1), :]
@@ -1594,7 +1704,24 @@
         grad_out[rows, :] = (grad + gmid[rows, :]).astype(bf16)
 
     each_rows(hidden.shape[0], 16, last)
+    lane = lax.broadcasted_iota(jnp.int32, (256, 128), 1)
+    for j in range(4):
+        @pl.when(w != j)
+        def _():
+            kv_wait(j).wait_recv()
+
+        even, odd = kv[j, :, 0:128].astype(f32), kv[j, :, 128:256].astype(f32)
+        here = slice(j * 128, j * 128 + 128)
+        key_out[:, here] = jnp.where(lane < 64, even, pltpu.roll(odd, 64, 1))
+        value_out[:, here] = jnp.where(lane < 64, pltpu.roll(even, 64, 1), odd)
     scatter.sent()
+    for hop in q_hops + q_later + o_hops:
+        hop.wait_send()
+    for j in range(4):
+        @pl.when(w != j)
+        def _():
+            kv_copy(j, w).wait_send()
+
     for j in range(4):
         @pl.when(w != j)
         def _():
@@ -1607,12 +1734,14 @@
                 rest_copy(a, b, r * 4 + n).wait_send()
 
 
-def leave(parts, hidden, gain, gmid, gains):
-    shard, width = hidden.shape
+def leave(*args):
+    shard, width = 128, 2048
+    grad = jax.ShapeDtypeStruct((256, 512), f32)
     return comm_call(
         leave_kernel, "leave", 7,
-        (jax.ShapeDtypeStruct((shard, width), bf16), jax.ShapeDtypeStruct((8, 256), f32)),
-        [vmem()] * 5, [vmem()] * 2,
+        (jax.ShapeDtypeStruct((shard, width), bf16), jax.ShapeDtypeStruct((8, 256), f32))
+        + (grad,) * 4,
+        [vmem()] * 13, [vmem()] * 6,
         [pltpu.VMEM((4, shard, width), bf16)]
         + scatter_bufs(shard, width) + scatter_sems()
         + [
@@ -1624,29 +1753,18 @@
             pltpu.SemaphoreType.DMA((4,)),
             pltpu.SemaphoreType.DMA((8,)),
             pltpu.SemaphoreType.DMA((8,)),
+            pltpu.VMEM((2, 2, 128, 768), bf16),
+            pltpu.VMEM((2, 128, 768), bf16),
+            pltpu.VMEM((2, 128, 768), bf16),
+            pltpu.VMEM((2, 128, 512), bf16),
+            pltpu.VMEM((2, 128, 512), bf16),
+            pltpu.VMEM((4, 256, 256), bf16),
+            pltpu.SemaphoreType.DMA((6,)),
+            pltpu.SemaphoreType.DMA((6,)),
+            pltpu.SemaphoreType.DMA((4,)),
+            pltpu.SemaphoreType.DMA((4,)),
         ],
-        (parts, hidden, gain, gmid, gains), flops=10**10, sent=10**8,
-    )
-
-
-def swap_nar(x, bit):
-    return lax.ppermute(x, "nar", [(i, i ^ bit) for i in range(4)])
-
-
-def nar_gather(shard):
-    rows = shard.shape[0] // 2
-    by_x, by_y = swap_nar(shard, 1), swap_nar(shard, 2)
-    return shard, by_x, by_y, swap_nar(by_x[:rows], 2), swap_nar(by_y[rows:], 1)
-
-
-def nar_scatter(a_send, a_keep, b_send, b_keep):
-    def halves(send, keep, first, then):
-        total = (keep.astype(f32) + swap_nar(send, first).astype(f32))
-        over = swap_nar(total[1].astype(bf16), then)
-        return total[0] + over.astype(f32)
-
-    return jnp.concatenate(
-        [halves(a_send, a_keep, 1, 2), halves(b_send, b_keep, 2, 1)], axis=-2
+        args, flops=10**10, sent=10**8,
     )
 
 
@@ -1672,10 +1790,15 @@
         axis=1,
     )
     down_half = half(w_down, 0)
-    p1_pieces = nar_gather(p1_shard)
-    gate_pieces = nar_gather(half(w_gate, 1))
-    up_pieces = nar_gather(half(w_up, 1))
-    down_pieces = nar_gather(jnp.concatenate([down_half[:512], down_half[512:]], axis=1))
+    p2_shard = jnp.stack(
+        [
+            half(w_gate, 1),
+            half(w_up, 1),
+            jnp.concatenate([down_half[:512], down_half[512:]], axis=1),
+        ]
+    )
+    p1 = lax.all_gather(p1_shard, "nar", axis=0)
+    p2 = lax.all_gather(p2_shard, "nar", axis=0)
 
     token_ids = n * 512 + jnp.arange(512, dtype=jnp.int32)
     doc_start, places = doc_layout(doc_lengths[0], token_ids)
@@ -1689,41 +1812,52 @@
 
     rows, tabs = enter(hidden, gain_a, tab)
     rows3, rows2 = rows.reshape(2, 512, 2048), rows.reshape(1024, 2048)
-    q, kv, p1 = project(rows3, p1_pieces, tabs)
+    q, kv = project(rows3, p1, tabs)
     low = tabs[:, ::QUERIES, 256].astype(jnp.int32).reshape(8)
     kv_flat = kv.reshape(2, 1536, 128)
     att, lse = attend(low, q, kv_flat, tabs)
     mid, ffn_rows, top_rows = middle_stage(att, p1, hidden, gain_f, grad_top)
-    parts, total, gain_f_part, *grads = ffn_stage(
-        ffn_rows.reshape(1024, 2048), top_rows.reshape(1024, 2048),
-        gate_pieces + up_pieces + down_pieces, gain_f,
-    )
-    summed = nar_scatter(*grads)
-    hidden_out, gmid, datt, *grad_o = branch_stage(
-        total, mid, grad_top, gain_f, parts, p1, att.reshape(1024, 256)
-    )
-    summed_o = nar_scatter(*grad_o)
+    parts, total, gain_f_part, a_send, a_keep, b_send, b_keep, ra_d, rb_d = ffn_stage(
+        ffn_rows.reshape(1024, 2048), top_rows.reshape(1024, 2048), p2, gain_f
+    )
+    gmid, datt, oa_send, oa_keep, ob_send, ob_keep, ra_gu, rb_gu = branch_stage(
+        total, mid, grad_top, gain_f, p1, att.reshape(1024, 256), a_send, b_send
+    )
     dq, dkv = attend_back(low, q, kv_flat, tabs, att, datt, lse)
-    dparts, gain_a_part, *grad_qkv = unproject(
-        dq, dkv.reshape(2, 3, 512, 128), rows2, p1, tabs, gain_a
-    )
-    summed_qkv = nar_scatter(*grad_qkv)
+    (
+        dparts, gain_a_part, qa_send, qa_keep, qb_send, qb_keep,
+        hidden_out, ra_last, rb_last, oa_came, ob_came,
+    ) = unproject(
+        dq, dkv.reshape(2, 3, 512, 128), rows2, p1, tabs, gain_a, parts, mid,
+        a_keep, b_keep, ra_gu, rb_gu, ra_d, rb_d, oa_send, ob_send,
+    )
     gains = jnp.concatenate(
         [gain_f_part.sum(axis=0).reshape(8, 256), gain_a_part.sum(axis=0).reshape(8, 256)], axis=0
     )
-    grad_in, gain_sums = leave(dparts, hidden, gain_a, gmid, gains)
-    kv_all = lax.all_gather(summed_qkv[:, 512:768].astype(bf16), "wid", axis=1, tiled=True)
-    kv_all = kv_all.astype(f32).reshape(256, KV, 2, HD)
+    grad_in, gain_sums, grad_query, grad_key, grad_value, output_sum = leave(
+        dparts, hidden, gain_a, gmid, gains,
+        qa_send, qa_keep, qb_send, qb_keep, oa_keep, ob_keep, oa_came, ob_came,
+    )
+
+    def joined(which):
+        def half_rows(keep, came, last):
+            return keep[0, which].astype(f32) + came.astype(f32) + last[which].astype(f32)
+
+        a_came, b_came = (ra_d[0], rb_d[0]) if which == 2 else (ra_gu[0, which], rb_gu[0, which])
+        return jnp.concatenate(
+            [half_rows(a_keep, a_came, ra_last), half_rows(b_keep, b_came, rb_last)], axis=0
+        )
+
     return (
         hidden_out[None],
         grad_in[None],
-        summed_qkv[:, 0:512],
-        kv_all[:, :, 0].reshape(256, KV * HD),
-        kv_all[:, :, 1].reshape(256, KV * HD),
-        summed_o.T,
-        summed[0],
-        summed[1],
-        summed[2].T,
+        grad_query,
+        grad_key,
+        grad_value,
+        output_sum.T,
+        joined(0),
+        joined(1),
+        joined(2).T,
         gain_sums[1],
         gain_sums[0],
     )

time: 717 us -> 542 us (0.76)
  waiting for transfers between devices: 104 us -> 0.06 us
  starting transfers between devices: 49.7 us -> 0.08 us
  blocking collectives: 16.1 us -> 0 us
  local copies, waits for them, and re-layouts: 34.2 us -> 19.3 us
  between operations: 1.24 us -> 14.3 us
    ppermute x28 -> x0, waiting for transfers between devices: 104 us -> none  [swap_nar(): return lax.ppermute(x, 'nar', [(i, i ^ bit) for i in range(4)])]
    ppermute x28 -> x0, starting transfers between devices: 49.7 us -> none  [swap_nar(): return lax.ppermute(x, 'nar', [(i, i ^ bit) for i in range(4)])]
    all_gather x1 -> x0, blocking collectives: 16.1 us -> none  [local_fast(): lax.all_gather(summed_qkv[:, 512:768].astype(bf16), 'wid', axis=1, tiled=...]
    slice x9 -> x0, local copies, waits for them, and re-layouts: 9.28 us -> none  [the longest x4 4.95 us: nar_gather(): by_x[:rows]]
  transfers between devices with their start and end apart: 28 -> 2, of which waited for: 9 -> 0; matrix products, arithmetic and copies ran while one was open for 5% -> 1% of each run, Pallas kernels for 38% -> 35%
where the time goes in v3:
time: 542 us; the launch traced here: 539 us
  Pallas kernels  487 us (90%)
  local copies, waits for them, and re-layouts  19.3 us (4%)
  other arithmetic  17.8 us (3%)
  between operations  14.3 us (3%)
    pallas_call x7, Pallas kernels, comm_call(): pl.pallas_call(kernel, out_shape=out_shape, in_specs=in_specs, out_specs=...  459 us
    pallas_call x1, Pallas kernels, attend_back(): pl.pallas_call(attend_back_kernel, out_shape=(jax.ShapeDtypeStruct((2, 51...  16.6 us
    unnamed x47, local copies, waits for them, and re-layouts  12.3 us
    pallas_call x1, Pallas kernels, attend(): pl.pallas_call(attend_kernel, out_shape=(jax.ShapeDtypeStruct((2, 512, 25...  11.8 us
  transfers between devices with their start and end apart: 2, of which 0 were waited for; matrix products, arithmetic and copies ran while one was open for 1% of the time, Pallas kernels for 35%

profile of v3, /device:TPU:0, one launch (start us, length us, event | category | flops | bytes accessed | tf_op | source)
XLA Modules:
  0.0 538.7 jit_solution(10830647935472795369)
XLA Ops:
  7.2 0.0 copy-start
  7.2 0.0 copy-start.14
  7.2 0.0 all-gather.5.cloned.1.call-start
  7.3 1.0 copy-done
  8.2 1.0 constant_dynamic-slice_fusion
  9.2 1.1 constant_dynamic-slice_fusion.2
  10.4 1.0 maximum_maximum_fusion
  11.4 0.0 all-gather.5.cloned.1.call-update
  11.4 0.0 all-gather.7.cloned.1.call-start
  11.4 0.0 copy-done.14
  11.5 0.0 copy-start.5
  11.5 0.0 copy-start.6
  11.5 0.1 constant_dynamic-slice_fusion.5
  11.6 0.1 maximum_bitcast_fusion.1
  11.7 1.4 copy-done.5
  13.1 0.6 copy-done.6
  13.7 0.2 dynamic-slice_bitcast_fusion
  13.9 2.0 pad_maximum_fusion
  15.8 0.0 all-gather.7.cloned.1.call-update
  15.9 0.6 copy-done.19
  16.5 0.2 reduce-window.4
  16.7 0.1 select_reduce_fusion
  16.8 0.0 copy-done.18
  16.8 1.0 multiply_sine_fusion
  17.8 0.1 broadcast_in_dim.22
  17.9 1.5 concatenate.24.tab
  19.4 47.1 %enter.1 = (bf16[2,4,128,2048]{3,2,1,0:T(8,128)(2,1)}, f32[2,512,384]{2,1,0:T(8,128)}) custom-call(bf16[128,2048]{1,0:T(8,128)(2,1)} %bitcast.85, f32[1,2048]{1,0:T(1,128)} %bitcast.91, f32[512,384]{1,0:T(8,128)} %concatenate.24.tab), custom_call_target="tpu_custom_call" | custom-call | flops 10000000000 | bytes 100000000 | tf_op jit(solution)/shard_map/enter/pallas_call | solution.py:660
  66.5 1.1 slice.75
  67.6 0.1 convert_reduce_fusion
  67.8 0.6 convert_element_type.116.low
  68.4 26.4 %project.1 = (bf16[2,512,256]{2,1,0:T(8,128)(2,1)}, bf16[2,3,512,128]{3,2,1,0:T(8,128)(2,1)}) custom-call(bf16[2,512,2048]{2,1,0:T(8,128)(2,1)} %bitcast.95, bf16[4,512,640]{2,1,0:T(8,128)(2,1)} %bitcast.79, f32[2,512,384]{2,1,0:T(8,128)} %get-tuple-element.56.tabs.starts.turns), custom_call_target="tpu_custom_call" | custom-call | flops 10000000000 | bytes 10000000 | tf_op jit(solution)/shard_map/project/pallas_call | solution.py:660
  94.8 11.8 %attend.1 = (bf16[2,512,256]{2,1,0:T(8,128)(2,1)}, f32[2,4,512,128]{3,2,1,0:T(8,128)}) custom-call(s32[8]{0:T(128)} %convert_element_type.116.low, bf16[2,512,256]{2,1,0:T(8,128)(2,1)} %get-tuple-element.58.q, bf16[2,1536,128]{2,1,0:T(8,128)(2,1)} %bitcast.100, f32[2,512,384]{2,1,0:T(8,128)} %get-tuple-element.56.tabs.starts.turns), custom_call_target="tpu_custom_call" | custom-call | flops 20000000000 | bytes 10000000 | tf_op jit(solution)/shard_map/attend/pallas_call | solution.py:917
  106.6 104.8 %middle.1 = (f32[128,2048]{1,0:T(8,128)}, bf16[2,4,128,2048]{3,2,1,0:T(8,128)(2,1)}, bf16[2,4,128,2048]{3,2,1,0:T(8,128)(2,1)}) custom-call(bf16[2,512,256]{2,1,0:T(8,128)(2,1)} %get-tuple-element.60.att, bf16[4,512,640]{2,1,0:T(8,128)(2,1)} %bitcast.80, bf16[128,2048]{1,0:T(8,128)(2,1)} %bitcast.86, f32[1,2048]{1,0:T(1,128)} %bitcast.88, ...), custom_call_target="tpu_custom_call" | custom-call | flops 10000000000 | bytes 200000000 | tf_op jit(solution)/shard_map/middle/pallas_call | solution.py:660
  211.4 0.0 all-gather.7.cloned.1.call-done
  211.4 88.6 %ffn.1 = (bf16[2,4,128,2048]{3,2,1,0:T(8,128)(2,1)}, f32[128,2048]{1,0:T(8,128)}, f32[8,2048]{1,0:T(8,128)}, bf16[2,3,128,2048]{3,2,1,0:T(8,128)(2,1)}, bf16[2,3...) custom-call(bf16[1024,2048]{1,0:T(8,128)(2,1)} %bitcast.97, ...), custom_call_target="tpu_custom_call" | custom-call | flops 40000000000 | bytes 100000000 | tf_op jit(solution)/shard_map/ffn/pallas_call | solution.py:660
  300.0 62.5 %branch.1 = (f32[128,2048]{1,0:T(8,128)}, bf16[2,512,256]{2,1,0:T(8,128)(2,1)}, bf16[2,128,512]{2,1,0:T(8,128)(2,1)}, bf16[2,128,512]{2,1,0:T(8,128)(2,1)}, bf16...) custom-call(f32[128,2048]{1,0:T(8,128)} %get-tuple-element.63.total,, ...), custom_call_target="tpu_custom_call" | custom-call | flops 10000000000 | bytes 100000000 | tf_op jit(solution)/shard_map/branch/pallas_call | solution.py:660
  362.5 16.6 %attend_back.1 = (bf16[2,512,256]{2,1,0:T(8,128)(2,1)}, f32[2,1536,128]{2,1,0:T(8,128)}) custom-call(s32[8]{0:T(128)} %convert_element_type.116.low, bf16[2,512,256]{2,1,0:T(8,128)(2,1)} %get-tuple-element.58.q, bf16[2,1536,128]{2,1,0:T(8,128)(2,1)} %bitcast.101, f32[2,512,384]{2,1,0:T(8,128)} %get-tuple-element.56.tabs.starts.turns, ...), custom_call_target="tpu_custom_call" | custom-call | flops 40000000000 | bytes 10000000 | tf_op jit(solution)/shard_map/attend_back/pallas_call | solution.py:977
  379.1 68.1 %unproject.1 = (bf16[2,4,128,2048]{3,2,1,0:T(8,128)(2,1)}, f32[8,2048]{1,0:T(8,128)}, bf16[2,128,768]{2,1,0:T(8,128)(2,1)}, bf16[2,128,768]{2,1,0:T(8,128)(2,1)}...) custom-call(bf16[2,512,256]{2,1,0:T(8,128)(2,1)} %get-tuple-element., ...), custom_call_target="tpu_custom_call" | custom-call | flops 10000000000 | bytes 10000000 | tf_op jit(solution)/shard_map/unproject/pallas_call | solution.py:660
  447.2 0.0 copy-done.8
  447.2 0.0 copy-start.3
  447.2 0.0 copy-start.4
  447.3 0.0 copy-start.7
  447.3 4.3 convert_add_fusion.4
  451.6 0.0 copy-done.3
  451.6 0.0 copy-done.7
  451.6 0.7 copy-done.15
  452.3 2.1 convert_add_fusion.5
  454.5 0.6 pad_maximum_fusion.3.gains
  455.1 61.2 %leave.1 = (bf16[128,2048]{1,0:T(8,128)(2,1)}, f32[8,256]{1,0:T(8,128)}, f32[256,512]{1,0:T(8,128)}, f32[256,512]{1,0:T(8,128)}, f32[256,512]{1,0:T(8,128)}, /*index=5*/f32[256,512]{1,0:T(8,128)}) custom-call(bf16[2,4,128,2048]{3,2,1,0:T(8,128)(2,1)} %get-tuple-element.81.parts, bf16[128,2048]{1,0:T(8,128)(2,1)} %bitcast.87, f32[1,2048]{1,0:T(1,128)} %bitcast.93, ...), custom_call_target="tpu_custom_call" | custom-call | flops 10000000000 | bytes 100000000 | tf_op jit(solution)/shard_map/leave/pallas_call | solution.py:660
  516.3 1.3 fusion.2
  517.7 2.0 copy.33
  519.7 1.7 maximum_bitcast_fusion
  521.4 1.8 copy.34
  523.2 3.2 pad_maximum_fusion.2
  526.4 1.5 pad_maximum_fusion.1
  527.9 0.0 copy-done.9
  527.9 0.0 copy-start.1
  527.9 0.8 copy.40
  528.7 0.8 copy.41
  529.5 0.8 copy.42
  530.3 0.0 copy-done.11
  530.3 0.8 copy.43
  531.1 0.0 copy-done.10
  531.1 0.8 copy.44
  (28 shorter events, 0.1 us)
Async XLA Ops:
  7.2 1.1 copy-start
  7.2 4.3 copy-start.14
  7.2 61.2 %all-gather.5.cloned.1.call-start = ((), (), s32[]{:S(2)}) async-start(), calls=%async_computation | async-start | bytes 3276800 | tf_op jit(solution)/shard_map/all_gather | solution.py:1800
  11.4 200.0 %all-gather.7.cloned.1.call-start = ((), (), s32[]{:S(2)}) async-start(), calls=%async_computation.1 | async-start | bytes 15728640 | tf_op jit(solution)/shard_map/all_gather | solution.py:1801
  11.5 1.6 copy-start.5
  11.5 2.2 copy-start.6
  15.8 0.7 copy-start.19
  15.8 0.9 copy-start.18
  379.1 68.1 %copy-start.8 = (bf16[2,2,128,2048]{3,2,1,0:T(8,128)(2,1)S(1)}, bf16[2,2,128,2048]{3,2,1,0:T(8,128)(2,1)}, u32[]{:S(2)}) copy-start(bf16[2,2,128,2048]{3,2,1,0:T(8,128)(2,1)} %get-tuple-element.75.rb_gu) | copy-start | bytes 6291460
  447.2 4.3 copy-start.3
  447.2 4.3 copy-start.4
  447.3 4.3 copy-start.7
  447.3 5.1 copy-start.15
  452.3 2.1 copy-start.17
  452.3 2.1 copy-start.16
  523.2 3.2 copy-start.2
  526.4 1.5 copy-start.9
  526.4 2.3 copy-start.13
  527.9 1.6 copy-start.12
  527.9 2.4 copy-start.11
  527.9 3.2 copy-start.10
  527.9 4.0 copy-start.1
Sparse Core Ops, SparseCore 0:
  11.5 42.2 all-gather.4
  55.6 132.6 all-gather.6

commit v4 on v3

--- a/solution.py
+++ b/solution.py
@@ -449,7 +449,8 @@
 
 
 class Gather:
-    def __init__(self, buf, sems, me, wid_count):
+    def __init__(self, buf, sems, me, wid_count, rows=slice(None)):
+        self.rows = rows
         self.buf, (self.up_s, self.dn_s, self.pt_s, self.got) = buf, sems
         self.r, self.n, self.w = me
         self.last = wid_count - 1
@@ -460,8 +461,8 @@
     def copy(self, j, sem, device, row=None):
         row = self.r if row is None else row
         return pltpu.make_async_remote_copy(
-            self.buf.at[row, j],
-            self.buf.at[row, j],
+            self.buf.at[row, j, self.rows],
+            self.buf.at[row, j, self.rows],
             sem.at[j],
             self.got.at[row, j],
             device_id=device,
@@ -740,16 +741,26 @@
     return (r, jnp.clip(n + by, 0, 3), w)
 
 
-def project_kernel(x, p1, tabs, q_out, kv_out, kv, s_s, s_g, out_s):
+def project_kernel(
+    x, p1, tabs, grad_top, q_out, kv_out, tops_out, kv, s_s, s_g, out_s, buf, g0, g1, g2, g3, tops_s
+):
     r, n, w = spot()
     greet(
-        [
+        line_partners(r, n, w, 4)
+        + [
             (n >= 1, nar_device(r, n, w, -1)),
             (n >= 2, nar_device(r, n, w, -2)),
             (n <= 2, nar_device(r, n, w, 1)),
             (n <= 1, nar_device(r, n, w, 2)),
         ]
     )
+    gather = Gather(buf, (g0, g1, g2, g3), (r, n, w), 4)
+
+    def keep(rows):
+        buf[r, w, rows, :] = grad_top[rows, :]
+
+    each_rows(64, 16, keep)
+    gather.own()
 
     def copy(row, slot, by):
         return pltpu.make_async_remote_copy(
@@ -785,6 +796,11 @@
             def _():
                 kv[row, slot] = jnp.zeros((512, 128), bf16)
 
+    for k in (1, 2, 3):
+        gather.step(k)
+    gather.rest()
+    tops_copy = pltpu.make_async_copy(buf, tops_out, tops_s)
+    tops_copy.start()
     for row in range(2):
         for slot, least, by in ((1, 1, 1), (0, 2, 2)):
             @pl.when(n >= least)
@@ -802,24 +818,29 @@
         def _():
             copy(row, 0, 2).wait_send()
 
+    gather.sent()
     out.wait()
-
-
-def project(x, p1, tabs):
+    tops_copy.wait()
+
+
+def project(x, p1, tabs, grad_top):
     return comm_call(
         project_kernel, "project", 2,
         (
             jax.ShapeDtypeStruct((2, 512, 256), bf16),
             jax.ShapeDtypeStruct((2, 3, 512, 128), bf16),
+            jax.ShapeDtypeStruct((2, 4, 64, 2048), bf16),
         ),
-        [vmem()] * 3, [vmem(), hbm()],
+        [vmem()] * 4, [vmem(), hbm(), hbm()],
         [
             pltpu.VMEM((2, 3, 512, 128), bf16),
             pltpu.SemaphoreType.DMA((2, 3)),
             pltpu.SemaphoreType.DMA((2, 3)),
             pltpu.SemaphoreType.DMA(()),
-        ],
-        (x, p1, tabs), flops=10**10, sent=10**7,
+        ]
+        + gather_scratch(64, 2048)
+        + [pltpu.SemaphoreType.DMA(())],
+        (x, p1, tabs, grad_top), flops=10**10, sent=10**7,
     )
 
 
@@ -998,9 +1019,8 @@
 
 
 def middle_kernel(
-    att, p1, hidden, gain, grad_top, mid_out, ffn_out, grad_out,
-    theirs, mine, from_pt, from_up, from_dn, s0, s1, s2, s3, s4, s5,
-    gbuf, g0, g1, g2, g3, fbuf, h0, h1, h2, h3, out_s,
+    att, p1, hidden, gain, mid_out, ffn_out,
+    theirs, mine, from_pt, from_up, from_dn, s0, s1, s2, s3, s4, s5, fbuf, h0, h1, h2, h3, out_s,
 ):
     me = spot()
     r, n, w = me
@@ -1008,13 +1028,7 @@
     scatter = Scatter(
         mine, theirs, (from_pt, from_up, from_dn), (s0, s1, s2, s3, s4, s5), me, 4
     )
-    tops = Gather(gbuf, (g0, g1, g2, g3), me, 4)
     ffn = Gather(fbuf, (h0, h1, h2, h3), me, 4)
-
-    def keep(rows):
-        gbuf[r, w, rows, :] = grad_top[rows, :]
-
-    each_rows(grad_top.shape[0], 16, keep)
     for i in range(4):
         s = scatter.order(i)
         rows = pl.ds(pl.multiple_of(s * 128, 128), 128)
@@ -1028,10 +1042,6 @@
         scatter.pair(s).start()
     for i in range(4):
         scatter.step(scatter.order(i))
-        if i == 0:
-            tops.own()
-        else:
-            tops.step(i)
     scatter.total(mid_out)
 
     def body(rows):
@@ -1041,33 +1051,28 @@
 
     each_rows(hidden.shape[0], 16, body)
     ffn.own()
-    tops.rest()
-    out_g = pltpu.make_async_copy(gbuf, grad_out, out_s.at[0])
-    out_g.start()
     for k in (1, 2, 3):
         ffn.step(k)
     ffn.rest()
-    out_f = pltpu.make_async_copy(fbuf, ffn_out, out_s.at[1])
+    out_f = pltpu.make_async_copy(fbuf, ffn_out, out_s)
     out_f.start()
     scatter.sent()
-    tops.sent()
     ffn.sent()
-    out_g.wait()
     out_f.wait()
 
 
-def middle_stage(att, p1, hidden, gain, grad_top):
+def middle_stage(att, p1, hidden, gain):
     shard, width = hidden.shape
     rows = jax.ShapeDtypeStruct((2, 4, shard, width), bf16)
     return comm_call(
         middle_kernel, "middle", 3,
-        (jax.ShapeDtypeStruct((shard, width), f32), rows, rows),
-        [vmem()] * 5, [vmem(), hbm(), hbm()],
+        (jax.ShapeDtypeStruct((shard, width), f32), rows),
+        [vmem()] * 4, [vmem(), hbm()],
         [pltpu.VMEM((4, shard, width), bf16)] * 2
         + scatter_bufs(shard, width) + scatter_sems()
-        + gather_scratch(shard, width) + gather_scratch(shard, width)
-        + [pltpu.SemaphoreType.DMA((2,))],
-        (att, p1, hidden, gain, grad_top), flops=10**10, sent=2 * 10**8,
+        + gather_scratch(shard, width)
+        + [pltpu.SemaphoreType.DMA(())],
+        (att, p1, hidden, gain), flops=10**10, sent=2 * 10**8,
     )
 
 
@@ -1118,27 +1123,33 @@
 
 
 def ffn_kernel(
-    x, tops, p2_all, gain, part_out, sum_out, gain_out, o0, o1, o2, o3, ra_out, rb_out,
+    x, tops_in, grad_top, p2_all, gain,
+    part_out, sum_out, gain_out, o0, o1, o2, o3, ra_out, rb_out,
     theirs, mine, from_pt, from_up, from_dn, s0, s1, s2, s3, s4, s5,
-    act, dgu, stage, wide, out_s, give_s, give_g, keep_s, p2, in_s, n_s, n_g,
+    act, dgu, wide, out_s, give_s, give_g, keep_s, p2, in_s, n_s, n_g,
+    tops4, h0, h1, h2, h3, tops_s,
 ):
     me = spot()
     r, n, w = me
     loads = [pltpu.make_async_copy(p2_all.at[:, j], p2.at[j], in_s.at[j]) for j in range(3)]
+    loads.append(pltpu.make_async_copy(tops_in, tops4.at[:, :, 0:64], tops_s))
     for load in loads:
         load.start()
     greet(line_partners(r, n, w, 4) + square_partners(r, n, w))
     scatter = Scatter(
         mine, theirs, (from_pt, from_up, from_dn), (s0, s1, s2, s3, s4, s5), me, 4
     )
+    late = pl.ds(64, 64)
+    gather = Gather(tops4, (h0, h1, h2, h3), me, 4, late)
+
+    def keep(rows):
+        tops4[r, w, pl.ds(64 + rows.start, 16), :] = grad_top[pl.ds(64 + rows.start, 16), :]
+
+    each_rows(64, 16, keep)
+    gather.own()
     gain_out[...] = jnp.zeros_like(gain_out)
-    for load in loads:
-        load.wait()
-
-    def put(s, slot, row_slot, row):
-        return pltpu.make_async_copy(
-            stage.at[slot, row_slot], part_out.at[row, s], out_s.at[slot, row_slot]
-        )
+    loads[0].wait()
+    loads[1].wait()
 
     def hidden_tile(i, carry):
         ft, row = i // 2, i % 2
@@ -1147,19 +1158,61 @@
         left = x[rows, :]
         gate = jnp.dot(left, p2[0, :, :, columns].reshape(2048, 256), preferred_element_type=f32)
         up = jnp.dot(left, p2[1, :, :, columns].reshape(2048, 256), preferred_element_type=f32)
-        f_rows = pl.ds(pl.multiple_of((ft % 2) * 256, 256), 256)
-        f_cols = pl.ds(pl.multiple_of((ft // 2) * 512, 512), 512)
-        right = jnp.concatenate([p2[2, nn, f_rows, f_cols] for nn in range(4)], axis=1)
-        dact = contract_last(tops[rows, :], right)
         sig = 1.0 / (1.0 + jnp.exp(-gate))
         silu = gate * sig
         act[rows, columns] = (silu * up).astype(bf16)
-        dgu[rows, columns] = (dact * up * (sig * (1.0 + gate * (1.0 - sig)))).astype(bf16)
+        dgu[rows, columns] = (up * (sig * (1.0 + gate * (1.0 - sig)))).astype(bf16)
         later = pl.ds(pl.multiple_of(1024 + ft * 256, 256), 256)
-        dgu[rows, later] = (dact * silu).astype(bf16)
+        dgu[rows, later] = silu.astype(bf16)
         return carry
 
-    lax.fori_loop(0, 8, hidden_tile, 0)
+    lax.fori_loop(0, 4, hidden_tile, 0)
+    gather.step(1)
+    lax.fori_loop(4, 8, hidden_tile, 0)
+    gather.step(2)
+    loads[2].wait()
+
+    def down_tile(dt, carry):
+        nn, half = dt // 2, dt % 2
+        columns = pl.ds(pl.multiple_of(dt * 256, 256), 256)
+        inner = pl.ds(pl.multiple_of(half * 256, 256), 256)
+        other = pl.ds(pl.multiple_of(512 + half * 256, 256), 256)
+        right = jnp.concatenate([p2[2, nn, :, inner], p2[2, nn, :, other]], axis=0)
+        for row, stage in ((0, theirs), (1, mine)):
+            part = jnp.dot(act[row * 512 : row * 512 + 512, :], right, preferred_element_type=f32)
+            stage[:, :, columns] = part.astype(bf16).reshape(4, 128, 256)
+        return carry
+
+    lax.fori_loop(0, 8, down_tile, 0)
+    puts = [
+        pltpu.make_async_copy(theirs, part_out.at[0], out_s.at[0]),
+        pltpu.make_async_copy(mine, part_out.at[1], out_s.at[1]),
+    ]
+    for put in puts:
+        put.start()
+    gather.step(3)
+    gather.rest()
+    loads[3].wait()
+
+    def top_rows(row):
+        return tops4[row].reshape(512, 2048)
+
+    def back_tile(ft, carry):
+        columns = pl.ds(pl.multiple_of(ft * 256, 256), 256)
+        f_rows = pl.ds(pl.multiple_of((ft % 2) * 256, 256), 256)
+        f_cols = pl.ds(pl.multiple_of((ft // 2) * 512, 512), 512)
+        later = pl.ds(pl.multiple_of(1024 + ft * 256, 256), 256)
+        right = jnp.concatenate([p2[2, nn, f_rows, f_cols] for nn in range(4)], axis=1)
+        for row in range(2):
+            rows = slice(row * 512, row * 512 + 512)
+            dact = contract_last(top_rows(row), right)
+            dgu[rows, columns] = (dact * dgu[rows, columns].astype(f32)).astype(bf16)
+            dgu[rows, later] = (dact * dgu[rows, later].astype(f32)).astype(bf16)
+        return carry
+
+    lax.fori_loop(0, 4, back_tile, 0)
+    for put in puts:
+        put.wait()
 
     spread = Spread((o0, o1, o2, o3), (give_s, give_g, keep_s), me)
     columns_here = pl.ds(pl.multiple_of(r * 1024, 1024), 1024)
@@ -1171,43 +1224,43 @@
 
         return wide.at[slots[which], half], which, place, half == 0
 
-    def weights(which):
+    def weights(which, between=None):
         for half in range(2):
             d_first = (jnp.where(half == 0, 1 - r, r)) * 1024
 
             def weight_tile(i, carry):
-                d_rows = pl.ds(pl.multiple_of(d_first + i * 256, 256), 256)
-                source = x if which < 2 else tops
-                left = source[:, d_rows]
+                d_cols = pl.ds(pl.multiple_of(d_first + i * 256, 256), 256)
                 if which < 2:
+                    left = x[:, d_cols]
                     right = dgu[:, which * 1024 : which * 1024 + 1024]
                 else:
+                    left = tops4[:, :, :, d_cols].reshape(1024, 256)
                     right = act[...]
                 wide[slots[which], half, i] = contract_first(left, right).astype(bf16)
                 return carry
 
             lax.fori_loop(0, 4, weight_tile, 0)
             spread.start(*moved(which, half))
-
-    hops = [
-        push(o0.at[:, 2], ra_out, n_s.at[0], n_g.at[0], over_x(r, n, w)),
-        push(o2.at[:, 2], rb_out, n_s.at[1], n_g.at[1], over_y(r, n, w)),
-    ]
+            if half == 0 and between is not None:
+                between()
+
+    def hop(which, at):
+        return (
+            push(o0.at[:, which], ra_out.at[at], n_s.at[0, at], n_g.at[0, at], over_x(r, n, w)),
+            push(o2.at[:, which], rb_out.at[at], n_s.at[1, at], n_g.at[1, at], over_y(r, n, w)),
+        )
+
+    hops = hop(2, 0) + hop(0, 1)
     weights(2)
     for i in range(4):
         s = scatter.order(i)
-        slot = i % 2
         rows_t = pl.ds(pl.multiple_of((1 - r) * 512 + s * 128, 128), 128)
         rows_m = pl.ds(pl.multiple_of(r * 512 + s * 128, 128), 128)
-        if i >= 2:
-            put(s, slot, 0, 1 - r).wait()
-            put(s, slot, 1, r).wait()
 
         def model_tile(dt, carry):
             nn, half = dt // 2, dt % 2
             columns = pl.ds(pl.multiple_of(dt * 256, 256), 256)
             inner = pl.ds(pl.multiple_of(half * 256, 256), 256)
-            other = pl.ds(pl.multiple_of(512 + half * 256, 256), 256)
             left = jnp.concatenate([dgu[rows_t, :], dgu[rows_m, :]], axis=0)
             right = jnp.concatenate([p2[0, nn, inner, :], p2[1, nn, inner, :]], axis=1)
             part = contract_last(left, right)
@@ -1217,44 +1270,36 @@
             part = part.astype(bf16)
             theirs[s, :, columns] = part[0:128]
             mine[s, :, columns] = part[128:256]
-            left = jnp.concatenate([act[rows_t, :], act[rows_m, :]], axis=0)
-            right = jnp.concatenate([p2[2, nn, :, inner], p2[2, nn, :, other]], axis=0)
-            part = jnp.dot(left, right, preferred_element_type=f32).astype(bf16)
-            stage[slot, 0, :, columns] = part[0:128]
-            stage[slot, 1, :, columns] = part[128:256]
             return carry
 
         lax.fori_loop(0, 8, model_tile, 0)
         scatter.pair(s).start()
-        put(s, slot, 0, 1 - r).start()
-        put(s, slot, 1, r).start()
+        if i < 2:
+            which = (2, 0)[i]
+            spread.wait_recv(*moved(which, 0))
+            spread.wait(*moved(which, 1))
+            hops[2 * i].start()
+            hops[2 * i + 1].start()
         if i == 0:
-            spread.wait_recv(*moved(2, 0))
-            spread.wait(*moved(2, 1))
-            for hop in hops:
-                hop.start()
-        else:
-            scatter.advance((i - 1,), (i - 2,) if i > 1 else ())
+            weights(0)
+            scatter.advance((0,), ())
+        elif i > 1:
+            scatter.advance((i - 1,), (i - 2,))
 
     def scale(rows):
         gain_out[rows, :] = gain_out[rows, :] / gain[...]
 
     each_rows(8, 8, scale)
-    scatter.advance((3,), ())
-    weights(0)
-    scatter.advance((), (2,))
     spread.wait_send(*moved(2, 0))
-    weights(1)
+    weights(1, lambda: scatter.advance((3,), (2,)))
     scatter.advance((), (3,))
     scatter.total(sum_out)
     scatter.sent()
-    for which in (0, 1):
-        spread.wait_recv(*moved(which, 0))
-        spread.wait_send(*moved(which, 0))
-        spread.wait(*moved(which, 1))
-    for slot in range(2):
-        put(0, slot, 0, 1 - r).wait()
-        put(0, slot, 1, r).wait()
+    gather.sent()
+    spread.wait_send(*moved(0, 0))
+    spread.wait_recv(*moved(1, 0))
+    spread.wait_send(*moved(1, 0))
+    spread.wait(*moved(1, 1))
     for hop in hops:
         hop.wait()
 
@@ -1263,7 +1308,7 @@
     return (jax.ShapeDtypeStruct((2,) + dims, bf16),) * 4
 
 
-def ffn_stage(x, tops, p2, gain):
+def ffn_stage(*args):
     shard, width = 128, 2048
     return comm_call(
         ffn_kernel, "ffn", 4,
@@ -1273,21 +1318,22 @@
             jax.ShapeDtypeStruct((8, width), f32),
         )
         + spread_shapes(3, 128, width)
-        + (jax.ShapeDtypeStruct((2, 128, width), bf16),) * 2,
-        [vmem()] * 2 + [hbm()] + [vmem()], [hbm(), vmem(), vmem()] + [hbm()] * 6,
+        + (jax.ShapeDtypeStruct((2, 2, 128, width), bf16),) * 2,
+        [vmem(), hbm(), vmem(), hbm(), vmem()], [hbm(), vmem(), vmem()] + [hbm()] * 6,
         [pltpu.VMEM((4, shard, width), bf16)] * 2
         + scatter_bufs(shard, width) + scatter_sems()
         + [
             pltpu.VMEM((1024, 1024), bf16),
             pltpu.VMEM((1024, 2048), bf16),
-            pltpu.VMEM((2, 2, shard, width), bf16),
             pltpu.VMEM((2, 2, 4, 256, 1024), bf16),
-            pltpu.SemaphoreType.DMA((2, 2)),
+            pltpu.SemaphoreType.DMA((2,)),
         ]
         + spread_sems(3)
         + [pltpu.VMEM((3, 4, 512, 1024), bf16), pltpu.SemaphoreType.DMA((3,))]
-        + [pltpu.SemaphoreType.DMA((2,))] * 2,
-        (x, tops, p2, gain), flops=4 * 10**10, sent=10**8,
+        + [pltpu.SemaphoreType.DMA((2, 2))] * 2
+        + gather_scratch(shard, width)
+        + [pltpu.SemaphoreType.DMA(())],
+        args, flops=4 * 10**10, sent=10**8,
     )
 
 
@@ -1299,19 +1345,30 @@
 
 
 def branch_kernel(
-    total, mid, grad_top, gain, p1, att, a_in, b_in, gmid_out, datt_out, o0, o1, o2, o3, ra_out, rb_out,
-    buf, g0, g1, g2, g3, wide, give_s, give_g, keep_s, n_s, n_g,
+    total, mid, grad_top, gain, p1, att, a_in, b_in, a_keep, b_keep, a_came, b_came,
+    gmid_out, datt_out, o0, o1, o2, o3, ra_out, rb_out, la_out, lb_out,
+    buf, g0, g1, g2, g3, wide, give_s, give_g, keep_s, n_s, n_g, kept, came, in_s,
 ):
     me = spot()
     r, n, w = me
     greet(line_partners(r, n, w, 4) + square_partners(r, n, w))
     gather = Gather(buf, (g0, g1, g2, g3), me, 4)
     hops = [
-        push(a_in.at[:, 0:2], ra_out, n_s.at[0], n_g.at[0], over_x(r, n, w)),
-        push(b_in.at[:, 0:2], rb_out, n_s.at[1], n_g.at[1], over_y(r, n, w)),
+        push(a_in.at[:, 1], ra_out, n_s.at[0], n_g.at[0], over_x(r, n, w)),
+        push(b_in.at[:, 1], rb_out, n_s.at[1], n_g.at[1], over_y(r, n, w)),
+        push(kept.at[0], la_out, n_s.at[2], n_g.at[2], over_y(r, n, w)),
+        push(kept.at[1], lb_out, n_s.at[3], n_g.at[3], over_x(r, n, w)),
     ]
-    for hop in hops:
-        hop.start()
+    loads = []
+    for j, (keep, first) in enumerate(((a_keep, a_came), (b_keep, b_came))):
+        loads += [
+            pltpu.make_async_copy(keep.at[1, 2], kept.at[j], in_s.at[j, 0]),
+            pltpu.make_async_copy(first.at[0, 1], came.at[j], in_s.at[j, 1]),
+        ]
+    for load in loads:
+        load.start()
+    hops[0].start()
+    hops[1].start()
 
     def body(rows):
         grad = norm_back(mid[rows, :], gain[...], total[rows, :]) + grad_top[rows, :].astype(f32)
@@ -1320,6 +1377,14 @@
 
     each_rows(mid.shape[0], 16, body)
     gather.own()
+    for load in loads:
+        load.wait()
+    for j in range(2):
+        def join(rows):
+            kept[j, rows, :] = (kept[j, rows, :].astype(f32) + came[j, rows, :].astype(f32)).astype(bf16)
+
+        each_rows(128, 16, join)
+        hops[2 + j].start()
     for k in (1, 2, 3):
         gather.step(k)
     gather.rest()
@@ -1357,8 +1422,8 @@
         hop.wait()
 
 
-def branch_stage(total, mid, grad_top, gain, p1, att, a_in, b_in):
-    shard, width = mid.shape
+def branch_stage(*args):
+    shard, width = 128, 2048
     return comm_call(
         branch_kernel, "branch", 5,
         (
@@ -1366,18 +1431,21 @@
             jax.ShapeDtypeStruct((2, 512, 256), bf16),
         )
         + spread_shapes(128, 512)
-        + (jax.ShapeDtypeStruct((2, 2, 128, width), bf16),) * 2,
-        [vmem()] * 6 + [hbm()] * 2, [vmem(), vmem()] + [hbm()] * 6,
+        + (jax.ShapeDtypeStruct((2, 128, width), bf16),) * 2
+        + (jax.ShapeDtypeStruct((128, width), bf16),) * 2,
+        [vmem()] * 6 + [hbm()] * 6, [vmem(), vmem()] + [hbm()] * 8,
         gather_scratch(shard, width)
         + [pltpu.VMEM((2, 4, 256, 256), bf16)]
         + spread_sems(1)
-        + [pltpu.SemaphoreType.DMA((2,))] * 2,
-        (total, mid, grad_top, gain, p1, att, a_in, b_in), flops=10**10, sent=10**8,
+        + [pltpu.SemaphoreType.DMA((4,))] * 2
+        + [pltpu.VMEM((2, 128, width), bf16)] * 2
+        + [pltpu.SemaphoreType.DMA((2, 2))],
+        args, flops=10**10, sent=10**8,
     )
 
 
 def unproject_kernel(
-    dq, dkv, x, p1, tabs, gain, parts, mid, a_keep, b_keep, ra_gu, rb_gu, ra_d, rb_d, oa_in, ob_in,
+    dq, dkv, x, p1, tabs, gain, parts, mid, a_keep, b_keep, a_gate, b_gate, a_up, b_up, oa_in, ob_in,
     part_out, gain_out, o0, o1, o2, o3, hid_out, ra_out, rb_out, roa_out, rob_out,
     send, recv, both, wide_q, wide_kv, s_s, s_g, give_s, give_g, keep_s,
     mine, from_pt, from_up, from_dn, s0, s1, s2, s3, s4, s5,
@@ -1386,11 +1454,11 @@
     me = spot()
     r, n, w = me
     loads = []
-    for j, (keep, gate_up, down) in enumerate(((a_keep, ra_gu, ra_d), (b_keep, rb_gu, rb_d))):
+    for j, (keep, gate, up) in enumerate(((a_keep, a_gate, a_up), (b_keep, b_gate, b_up))):
         loads += [
-            pltpu.make_async_copy(keep.at[1], kept.at[j], in_s.at[j, 0]),
-            pltpu.make_async_copy(gate_up.at[1], came.at[j, 0:2], in_s.at[j, 1]),
-            pltpu.make_async_copy(down.at[1], came.at[j, 2], in_s.at[j, 2]),
+            pltpu.make_async_copy(keep.at[1, 0:2], kept.at[j], in_s.at[j, 0]),
+            pltpu.make_async_copy(gate.at[1, 1], came.at[j, 0], in_s.at[j, 1]),
+            pltpu.make_async_copy(up.at[1], came.at[j, 1], in_s.at[j, 2]),
         ]
     loads.append(pltpu.make_async_copy(parts.at[r], mine, m_s))
     for load in loads:
@@ -1433,7 +1501,7 @@
     for load in loads:
         load.wait()
     for j in range(2):
-        for which in range(3):
+        for which in range(2):
             def join(rows):
                 total = kept[j, which, rows, :].astype(f32) + came[j, which, rows, :].astype(f32)
                 kept[j, which, rows, :] = total.astype(bf16)
@@ -1548,7 +1616,7 @@
         )
         + spread_shapes(128, 768)
         + (jax.ShapeDtypeStruct((128, 2048), bf16),)
-        + (jax.ShapeDtypeStruct((3, 128, 2048), bf16),) * 2
+        + (jax.ShapeDtypeStruct((2, 128, 2048), bf16),) * 2
         + (jax.ShapeDtypeStruct((2, 128, 512), bf16),) * 2,
         [vmem()] * 6 + [hbm(), vmem()] + [hbm()] * 8,
         [vmem(), vmem()] + [hbm()] * 4 + [vmem()] + [hbm()] * 4,
@@ -1565,8 +1633,8 @@
         + [pltpu.VMEM((4, 128, 2048), bf16)]
         + scatter_bufs(128, 2048) + scatter_sems()
         + [
-            pltpu.VMEM((2, 3, 128, 2048), bf16),
-            pltpu.VMEM((2, 3, 128, 2048), bf16),
+            pltpu.VMEM((2, 2, 128, 2048), bf16),
+            pltpu.VMEM((2, 2, 128, 2048), bf16),
             pltpu.VMEM((128, 2048), f32),
             pltpu.SemaphoreType.DMA((2, 3)),
             pltpu.SemaphoreType.DMA((4,)),
@@ -1812,16 +1880,17 @@
 
     rows, tabs = enter(hidden, gain_a, tab)
     rows3, rows2 = rows.reshape(2, 512, 2048), rows.reshape(1024, 2048)
-    q, kv = project(rows3, p1, tabs)
+    q, kv, tops = project(rows3, p1, tabs, grad_top)
     low = tabs[:, ::QUERIES, 256].astype(jnp.int32).reshape(8)
     kv_flat = kv.reshape(2, 1536, 128)
     att, lse = attend(low, q, kv_flat, tabs)
-    mid, ffn_rows, top_rows = middle_stage(att, p1, hidden, gain_f, grad_top)
-    parts, total, gain_f_part, a_send, a_keep, b_send, b_keep, ra_d, rb_d = ffn_stage(
-        ffn_rows.reshape(1024, 2048), top_rows.reshape(1024, 2048), p2, gain_f
-    )
-    gmid, datt, oa_send, oa_keep, ob_send, ob_keep, ra_gu, rb_gu = branch_stage(
-        total, mid, grad_top, gain_f, p1, att.reshape(1024, 256), a_send, b_send
+    mid, ffn_rows = middle_stage(att, p1, hidden, gain_f)
+    parts, total, gain_f_part, a_send, a_keep, b_send, b_keep, ra_dg, rb_dg = ffn_stage(
+        ffn_rows.reshape(1024, 2048), tops, grad_top, p2, gain_f
+    )
+    gmid, datt, oa_send, oa_keep, ob_send, ob_keep, ra_u, rb_u, la_d, lb_d = branch_stage(
+        total, mid, grad_top, gain_f, p1, att.reshape(1024, 256),
+        a_send, b_send, a_keep, b_keep, ra_dg, rb_dg,
     )
     dq, dkv = attend_back(low, q, kv_flat, tabs, att, datt, lse)
     (
@@ -1829,7 +1898,7 @@
         hidden_out, ra_last, rb_last, oa_came, ob_came,
     ) = unproject(
         dq, dkv.reshape(2, 3, 512, 128), rows2, p1, tabs, gain_a, parts, mid,
-        a_keep, b_keep, ra_gu, rb_gu, ra_d, rb_d, oa_send, ob_send,
+        a_keep, b_keep, ra_dg, rb_dg, ra_u, rb_u, oa_send, ob_send,
     )
     gains = jnp.concatenate(
         [gain_f_part.sum(axis=0).reshape(8, 256), gain_a_part.sum(axis=0).reshape(8, 256)], axis=0
@@ -1841,11 +1910,15 @@
 
     def joined(which):
         def half_rows(keep, came, last):
-            return keep[0, which].astype(f32) + came.astype(f32) + last[which].astype(f32)
-
-        a_came, b_came = (ra_d[0], rb_d[0]) if which == 2 else (ra_gu[0, which], rb_gu[0, which])
+            return keep[0, which].astype(f32) + came.astype(f32) + last.astype(f32)
+
+        a_came, b_came, a_last, b_last = (
+            (ra_dg[1, 0], rb_dg[1, 0], ra_last[0], rb_last[0]),
+            (ra_u[0], rb_u[0], ra_last[1], rb_last[1]),
+            (ra_dg[0, 0], rb_dg[0, 0], la_d, lb_d),
+        )[which]
         return jnp.concatenate(
-            [half_rows(a_keep, a_came, ra_last), half_rows(b_keep, b_came, rb_last)], axis=0
+            [half_rows(a_keep, a_came, a_last), half_rows(b_keep, b_came, b_last)], axis=0
         )
 
     return (

time: 542 us -> 520 us (0.959)
  Pallas kernels: 487 us -> 466 us
    pallas_call x7, Pallas kernels: 459 us -> 437 us  [comm_call(): pl.pallas_call(kernel, out_shape=out_shape, in_specs=in_specs, out_specs=...]
    unnamed x47 -> x51, local copies, waits for them, and re-layouts: 12.3 us -> 12.2 us
  transfers between devices with their start and end apart: 2 -> 2, of which waited for: 0 -> 0; matrix products, arithmetic and copies ran while one was open for 1% -> 1% of each run, Pallas kernels for 35% -> 34%
where the time goes in v4:
time: 520 us; the launch traced here: 515 us
  Pallas kernels  466 us (90%)
  local copies, waits for them, and re-layouts  19.3 us (4%)
  other arithmetic  15.6 us (3%)
  between operations  14.4 us (3%)
    pallas_call x7, Pallas kernels, comm_call(): pl.pallas_call(kernel, out_shape=out_shape, in_specs=in_specs, out_specs=...  437 us
    pallas_call x1, Pallas kernels, attend_back(): pl.pallas_call(attend_back_kernel, out_shape=(jax.ShapeDtypeStruct((2, 51...  16.6 us
    unnamed x51, local copies, waits for them, and re-layouts  12.2 us
    pallas_call x1, Pallas kernels, attend(): pl.pallas_call(attend_kernel, out_shape=(jax.ShapeDtypeStruct((2, 512, 25...  11.8 us
  transfers between devices with their start and end apart: 2, of which 0 were waited for; matrix products, arithmetic and copies ran while one was open for 1% of the time, Pallas kernels for 34%

profile of v4, /device:TPU:0, one launch (start us, length us, event | category | flops | bytes accessed | tf_op | source)
XLA Modules:
  0.0 515.2 jit_solution(2518560743224029329)
XLA Ops:
  7.2 0.0 copy-start
  7.2 0.0 copy-start.15
  7.2 0.0 all-gather.5.cloned.1.call-start
  7.3 1.0 copy-done
  8.2 1.0 constant_dynamic-slice_fusion
  9.2 1.1 constant_dynamic-slice_fusion.2
  10.4 1.0 maximum_maximum_fusion
  11.4 0.0 all-gather.5.cloned.1.call-update
  11.4 0.0 all-gather.7.cloned.1.call-start
  11.4 0.0 copy-done.15
  11.5 0.0 copy-start.6
  11.5 0.0 copy-start.7
  11.5 0.1 constant_dynamic-slice_fusion.5
  11.6 0.1 maximum_bitcast_fusion.1
  11.7 1.4 copy-done.6
  13.1 0.6 copy-done.7
  13.7 0.2 dynamic-slice_bitcast_fusion
  13.9 2.0 pad_maximum_fusion
  15.8 0.0 all-gather.7.cloned.1.call-update
  15.9 0.6 copy-done.21
  16.5 0.2 reduce-window.4
  16.7 0.1 select_reduce_fusion
  16.8 0.0 copy-done.20
  16.8 1.0 multiply_sine_fusion
  17.8 0.1 broadcast_in_dim.22
  17.9 1.5 concatenate.24.tab
  19.4 47.1 %enter.1 = (bf16[2,4,128,2048]{3,2,1,0:T(8,128)(2,1)}, f32[2,512,384]{2,1,0:T(8,128)}) custom-call(bf16[128,2048]{1,0:T(8,128)(2,1)} %bitcast.79, f32[1,2048]{1,0:T(1,128)} %bitcast.85, f32[512,384]{1,0:T(8,128)} %concatenate.24.tab), custom_call_target="tpu_custom_call" | custom-call | flops 10000000000 | bytes 100000000 | tf_op jit(solution)/shard_map/enter/pallas_call | solution.py:661
  66.5 1.1 slice.69
  67.6 0.1 convert_reduce_fusion
  67.8 0.6 convert_element_type.110.low
  68.4 31.6 %project.1 = (bf16[2,512,256]{2,1,0:T(8,128)(2,1)}, bf16[2,3,512,128]{3,2,1,0:T(8,128)(2,1)}, bf16[2,4,64,2048]{3,2,1,0:T(8,128)(2,1)}) custom-call(bf16[2,512,2048]{2,1,0:T(8,128)(2,1)} %bitcast.89, bf16[4,512,640]{2,1,0:T(8,128)(2,1)} %bitcast.72, f32[2,512,384]{2,1,0:T(8,128)} %get-tuple-element.58.tabs.starts.turns, bf16[128,2048]{1,0:T(8,128)(2,1)} %bitcast.76), custom_call_target="tpu_custom_call" | custom-call | flops 10000000000 | bytes 10000000 | tf_op jit(solution)/shard_map/project/pallas_call | solution.py:661
  100.0 11.8 %attend.1 = (bf16[2,512,256]{2,1,0:T(8,128)(2,1)}, f32[2,4,512,128]{3,2,1,0:T(8,128)}) custom-call(s32[8]{0:T(128)} %convert_element_type.110.low, bf16[2,512,256]{2,1,0:T(8,128)(2,1)} %get-tuple-element.60.q, bf16[2,1536,128]{2,1,0:T(8,128)(2,1)} %bitcast.93, f32[2,512,384]{2,1,0:T(8,128)} %get-tuple-element.58.tabs.starts.turns), custom_call_target="tpu_custom_call" | custom-call | flops 20000000000 | bytes 10000000 | tf_op jit(solution)/shard_map/attend/pallas_call | solution.py:938
  111.8 84.9 %middle.1 = (f32[128,2048]{1,0:T(8,128)}, bf16[2,4,128,2048]{3,2,1,0:T(8,128)(2,1)}) custom-call(bf16[2,512,256]{2,1,0:T(8,128)(2,1)} %get-tuple-element.62.att, bf16[4,512,640]{2,1,0:T(8,128)(2,1)} %bitcast.73, bf16[128,2048]{1,0:T(8,128)(2,1)} %bitcast.80, f32[1,2048]{1,0:T(1,128)} %bitcast.82), custom_call_target="tpu_custom_call" | custom-call | flops 10000000000 | bytes 200000000 | tf_op jit(solution)/shard_map/middle/pallas_call | solution.py:661
  196.6 0.0 all-gather.7.cloned.1.call-done
  196.7 102.2 %ffn.1 = (bf16[2,4,128,2048]{3,2,1,0:T(8,128)(2,1)}, f32[128,2048]{1,0:T(8,128)}, f32[8,2048]{1,0:T(8,128)}, bf16[2,3,128,2048]{3,2,1,0:T(8,128)(2,1)}, bf16[2,3...) custom-call(bf16[1024,2048]{1,0:T(8,128)(2,1)} %bitcast.91, ...), custom_call_target="tpu_custom_call" | custom-call | flops 40000000000 | bytes 100000000 | tf_op jit(solution)/shard_map/ffn/pallas_call | solution.py:661
  298.9 51.6 %branch.1 = (f32[128,2048]{1,0:T(8,128)}, bf16[2,512,256]{2,1,0:T(8,128)(2,1)}, bf16[2,128,512]{2,1,0:T(8,128)(2,1)}, bf16[2,128,512]{2,1,0:T(8,128)(2,1)}, bf16...) custom-call(f32[128,2048]{1,0:T(8,128)} %get-tuple-element.65.total,, ...), custom_call_target="tpu_custom_call" | custom-call | flops 10000000000 | bytes 100000000 | tf_op jit(solution)/shard_map/branch/pallas_call | solution.py:661
  350.5 16.6 %attend_back.1 = (bf16[2,512,256]{2,1,0:T(8,128)(2,1)}, f32[2,1536,128]{2,1,0:T(8,128)}) custom-call(s32[8]{0:T(128)} %convert_element_type.110.low, bf16[2,512,256]{2,1,0:T(8,128)(2,1)} %get-tuple-element.60.q, bf16[2,1536,128]{2,1,0:T(8,128)(2,1)} %bitcast.94, f32[2,512,384]{2,1,0:T(8,128)} %get-tuple-element.58.tabs.starts.turns, ...), custom_call_target="tpu_custom_call" | custom-call | flops 40000000000 | bytes 10000000 | tf_op jit(solution)/shard_map/attend_back/pallas_call | solution.py:998
  367.1 58.2 %unproject.1 = (bf16[2,4,128,2048]{3,2,1,0:T(8,128)(2,1)}, f32[8,2048]{1,0:T(8,128)}, bf16[2,128,768]{2,1,0:T(8,128)(2,1)}, bf16[2,128,768]{2,1,0:T(8,128)(2,1)}...) custom-call(bf16[2,512,256]{2,1,0:T(8,128)(2,1)} %get-tuple-element., ...), custom_call_target="tpu_custom_call" | custom-call | flops 10000000000 | bytes 10000000 | tf_op jit(solution)/shard_map/unproject/pallas_call | solution.py:661
  425.4 0.0 copy-done.9
  425.5 3.9 bitcast_add_fusion
  429.4 0.0 copy-done.4
  429.4 0.0 copy-done.8
  429.4 0.3 copy-done.16
  429.7 0.5 copy-done.17
  430.1 2.1 bitcast_add_fusion.1
  432.3 0.1 maximum_bitcast_fusion
  432.4 0.0 copy-start.19
  432.4 0.0 copy-start.18
  432.4 1.8 copy.34
  434.3 0.0 copy-done.19
  434.3 0.6 pad_maximum_fusion.3.gains
  435.0 61.7 %leave.1 = (bf16[128,2048]{1,0:T(8,128)(2,1)}, f32[8,256]{1,0:T(8,128)}, f32[256,512]{1,0:T(8,128)}, f32[256,512]{1,0:T(8,128)}, f32[256,512]{1,0:T(8,128)}, /*index=5*/f32[256,512]{1,0:T(8,128)}) custom-call(bf16[2,4,128,2048]{3,2,1,0:T(8,128)(2,1)} %get-tuple-element.83.parts, bf16[128,2048]{1,0:T(8,128)(2,1)} %bitcast.81, f32[1,2048]{1,0:T(1,128)} %bitcast.87, ...), custom_call_target="tpu_custom_call" | custom-call | flops 10000000000 | bytes 100000000 | tf_op jit(solution)/shard_map/leave/pallas_call | solution.py:661
  496.7 1.3 fusion.2
  498.0 2.0 copy.33
  500.0 2.8 pad_maximum_fusion.1
  502.8 1.5 pad_maximum_fusion.2
  504.3 0.0 copy-start.1
  504.3 0.8 copy.40
  505.1 0.0 copy-done.14
  505.1 0.8 copy.41
  505.9 0.8 copy.42
  506.7 0.8 copy.43
  507.5 0.8 copy.44
  508.3 0.0 copy-done.1
  (32 shorter events, 0.1 us)
Async XLA Ops:
  7.2 1.1 copy-start
  7.2 4.3 copy-start.15
  7.2 61.2 %all-gather.5.cloned.1.call-start = ((), (), s32[]{:S(2)}) async-start(), calls=%async_computation | async-start | bytes 3276800 | tf_op jit(solution)/shard_map/all_gather | solution.py:1868
  11.4 185.3 %all-gather.7.cloned.1.call-start = ((), (), s32[]{:S(2)}) async-start(), calls=%async_computation.1 | async-start | bytes 15728640 | tf_op jit(solution)/shard_map/all_gather | solution.py:1869
  11.5 1.6 copy-start.6
  11.5 2.2 copy-start.7
  15.8 0.7 copy-start.21
  15.8 0.9 copy-start.20
  367.1 58.3 %copy-start.9 = (bf16[2,2,128,2048]{3,2,1,0:T(8,128)(2,1)S(1)}, bf16[2,2,128,2048]{3,2,1,0:T(8,128)(2,1)}, u32[]{:S(2)}) copy-start(bf16[2,2,128,2048]{3,2,1,0:T(8,128)(2,1)} %get-tuple-element.72.b_came.b_gate) | copy-start | bytes 6291460
  425.4 4.0 copy-start.4
  425.4 4.0 copy-start.5
  425.4 4.0 copy-start.8
  425.4 4.2 copy-start.16
  425.4 4.7 copy-start.17
  432.4 1.8 copy-start.19
  432.4 1.9 copy-start.18
  435.0 65.1 %copy-start.2 = (f32[128,2048]{1,0:T(8,128)S(1)}, f32[128,2048]{1,0:T(8,128)}, u32[]{:S(2)}) copy-start(f32[128,2048]{1,0:T(8,128)} %get-tuple-element.163) | copy-start | bytes 3145732
  500.0 2.8 copy-start.3
  502.8 1.5 copy-start.10
  502.8 2.3 copy-start.14
  504.3 1.6 copy-start.13
  504.3 2.4 copy-start.12
  504.3 3.2 copy-start.11
  504.3 4.0 copy-start.1
Sparse Core Ops, SparseCore 0:
  11.5 42.2 all-gather.4
  55.6 132.6 all-gather.6

commit v5 on v4

--- a/solution.py
+++ b/solution.py
@@ -955,65 +955,6 @@
     )(low, q, kv, tabs)
 
 
-def attend_back_kernel(low, q, kv, starts, turns, att, grad, lse, dq_out, dkv_out, dkv):
-    row, block = pl.program_id(0), pl.program_id(1)
-    first, end, first_query = key_tiles(low, row, block)
-
-    @pl.when(block == 0)
-    def _():
-        dkv[...] = jnp.zeros_like(dkv)
-
-    query = stack_low(q[0].astype(f32)).astype(bf16)
-    grads = stack_high(grad[0].astype(f32))
-    inner = jnp.sum(grads * stack_high(att[0].astype(f32)), axis=1, keepdims=True)
-    grads = grads.astype(bf16)
-    logsum = jnp.concatenate([lse[0, 0]] * (KEYS // 128), axis=1)
-
-    def body(tile, dq):
-        rows = pl.ds(pl.multiple_of(tile * KEYS, KEYS), KEYS)
-        both = kv[0, rows, :]
-        ok = allowed_tile(starts[0], tile, first_query)
-        scores = contract_last(query, both) * 0.125
-        prob = jnp.where(ok, jnp.exp(scores - logsum), 0.0)
-        grad_prob = contract_last(grads, both)
-        grad_scores = (prob * (grad_prob - inner)).astype(bf16)
-        dkv[rows, :] += contract_first(grad_scores, query) * 0.125 + contract_first(
-            prob.astype(bf16), grads
-        )
-        return dq + jnp.dot(grad_scores, both, preferred_element_type=f32)
-
-    dq = lax.fori_loop(first, end, body, jnp.zeros((4 * QUERIES, 128), f32))
-    flat = unstack(dq, True) * 0.125
-    cosine, sine = turns[0, :, 0:128], -turns[0, :, 128:256]
-    dq_out[0, :, 0:128] = turn(flat[:, 0:128], cosine, sine).astype(bf16)
-    dq_out[0, :, 128:256] = turn(flat[:, 128:256], cosine, sine).astype(bf16)
-
-    @pl.when(block == 3)
-    def _():
-        dkv_out[0] = dkv[...]
-
-
-def attend_back(low, q, kv, tabs, att, grad, lse):
-    tile = pl.BlockSpec((1, QUERIES, 256), lambda i, j, low: (i, j, 0))
-    return pl.pallas_call(
-        attend_back_kernel,
-        out_shape=(
-            jax.ShapeDtypeStruct((2, 512, 256), bf16),
-            jax.ShapeDtypeStruct((2, 1536, 128), f32),
-        ),
-        grid_spec=pltpu.PrefetchScalarGridSpec(
-            num_scalar_prefetch=1, grid=(2, 4),
-            in_specs=attend_specs()
-            + [tile, tile, tile, pl.BlockSpec((1, 1, 4 * QUERIES, 128), lambda i, j, low: (i, j, 0, 0))],
-            out_specs=[tile, pl.BlockSpec((1, 1536, 128), lambda i, j, low: (i, 0, 0))],
-            scratch_shapes=[pltpu.VMEM((1536, 128), f32)],
-        ),
-        compiler_params=pltpu.CompilerParams(vmem_limit_bytes=VMEM_LIMIT),
-        cost_estimate=pl.CostEstimate(flops=4 * 10**10, bytes_accessed=10**7, transcendentals=10**7),
-        name="attend_back",
-    )(low, q, kv, tabs, tabs, att, grad, lse)
-
-
 def out_block(p1, nn, half):
     return p1[nn, half * 256 : half * 256 + 256, 384:640]
 
@@ -1445,11 +1386,11 @@
 
 
 def unproject_kernel(
-    dq, dkv, x, p1, tabs, gain, parts, mid, a_keep, b_keep, a_gate, b_gate, a_up, b_up, oa_in, ob_in,
+    q, kv, att, grad, lse, x, p1, tabs, gain, parts, mid, a_keep, b_keep, a_gate, b_gate, a_up, b_up, oa_in, ob_in,
     part_out, gain_out, o0, o1, o2, o3, hid_out, ra_out, rb_out, roa_out, rob_out,
     send, recv, both, wide_q, wide_kv, s_s, s_g, give_s, give_g, keep_s,
     mine, from_pt, from_up, from_dn, s0, s1, s2, s3, s4, s5,
-    kept, came, acc, in_s, n_s, n_g, m_s,
+    kept, came, acc, in_s, n_s, n_g, m_s, dkv,
 ):
     me = spot()
     r, n, w = me
@@ -1489,13 +1430,6 @@
             device_id=nar_device(r, n, w, by), device_id_type=MESH,
         )
 
-    for row in range(2):
-        for slot, by in ((1, -1), (0, -2)):
-            @pl.when(n >= -by)
-            def _():
-                send[row, slot] = dkv[row, slot].astype(bf16)
-                copy(row, slot, by).start()
-
     for i in range(4):
         scatter.pair(scatter.order(i)).start()
     for load in loads:
@@ -1512,6 +1446,60 @@
     hops[3].start()
     scatter.advance((0, 1, 2, 3), ())
 
+    def attention(i, carry):
+        row, block = i // 4, i % 4
+        first_query = 1024 + block * QUERIES
+        here = pl.ds(pl.multiple_of(block * QUERIES, QUERIES), QUERIES)
+
+        @pl.when(block == 0)
+        def _():
+            dkv[row] = jnp.zeros((1536, 128), f32)
+
+        query = stack_low(q[row, here, :].astype(f32)).astype(bf16)
+        grads = stack_high(grad[row, here, :].astype(f32))
+        inner = jnp.sum(grads * stack_high(att[row, here, :].astype(f32)), axis=1, keepdims=True)
+        grads = grads.astype(bf16)
+        logsum = jnp.concatenate([lse[row, block]] * (KEYS // 128), axis=1)
+        starts = tabs[row, here, 256:384]
+
+        def key_tile(step, dq):
+            tile = block // 2 + step
+            rows = pl.ds(pl.multiple_of(tile * KEYS, KEYS), KEYS)
+            pair = kv[row, rows, :]
+            ok = allowed_tile(starts, tile, first_query)
+            scores = contract_last(query, pair) * 0.125
+            prob = jnp.where(ok, jnp.exp(scores - logsum), 0.0)
+            grad_prob = contract_last(grads, pair)
+            grad_scores = (prob * (grad_prob - inner)).astype(bf16)
+            dkv[row, rows, :] += contract_first(grad_scores, query) * 0.125 + contract_first(
+                prob.astype(bf16), grads
+            )
+            return dq + jnp.dot(grad_scores, pair, preferred_element_type=f32)
+
+        dq = lax.fori_loop(0, 5, key_tile, jnp.zeros((4 * QUERIES, 128), f32))
+        flat = unstack(dq, True) * 0.125
+        cosine, sine = tabs[row, here, 0:128], -tabs[row, here, 128:256]
+        there = pl.ds(pl.multiple_of(i * QUERIES, QUERIES), QUERIES)
+        both[there, 0:128] = turn(flat[:, 0:128], cosine, sine).astype(bf16)
+        both[there, 128:256] = turn(flat[:, 128:256], cosine, sine).astype(bf16)
+
+        @pl.when(block == 3)
+        def _():
+            for slot, by in ((1, -1), (0, -2)):
+                @pl.when(n >= -by)
+                def _():
+                    send[row, slot] = dkv[row, slot * 512 : slot * 512 + 512, :].astype(bf16)
+                    copy(row, slot, by).start()
+
+        @pl.when(i == 3)
+        def _():
+            scatter.advance((), (0,))
+
+        return carry
+
+    lax.fori_loop(0, 8, attention, 0)
+    scatter.advance((), (1,))
+
     spread = Spread((o0, o1, o2, o3), (give_s, give_g, keep_s), (r, n, w))
 
     def moved_q(half):
@@ -1525,9 +1513,6 @@
             return target.at[:, pl.ds(pl.multiple_of(512 + r * 128, 128), 128)]
 
         return wide_kv.at[half], 1, place, half == 0
-
-    for row in range(2):
-        both[row * 512 : row * 512 + 512, 0:256] = dq[row]
 
     def weight(half, columns, wide):
         d_first = (jnp.where(half == 0, 1 - r, r)) * 1024
@@ -1542,7 +1527,6 @@
     for half in range(2):
         weight(half, slice(0, 256), wide_q)
         spread.start(*moved_q(half))
-    scatter.advance((), (0,))
     lane = lax.broadcasted_iota(jnp.int32, (128, 128), 1)
     for row in range(2):
         for slot, by in ((1, -1), (0, -2)):
@@ -1552,7 +1536,7 @@
 
         def tile(i, carry):
             rows = pl.ds(pl.multiple_of(i * 128, 128), 128)
-            total = dkv[row, 2, rows, :]
+            total = dkv[row, pl.ds(pl.multiple_of(1024 + i * 128, 128), 128), :]
             zero = jnp.zeros_like(total)
             total = total + jnp.where(n <= 2, recv[row, 1, rows, :].astype(f32), zero)
             total = total + jnp.where(n <= 1, recv[row, 0, rows, :].astype(f32), zero)
@@ -1566,7 +1550,7 @@
     for half in range(2):
         weight(half, slice(256, 384), wide_kv)
         spread.start(*moved_kv(half))
-    scatter.advance((), (1,))
+    scatter.advance((), (2,))
     gain_out[...] = jnp.zeros_like(gain_out)
 
     def model_tile(dt, carry):
@@ -1586,7 +1570,7 @@
 
     lax.fori_loop(0, 8, model_tile, 0)
     gain_out[...] = gain_out[...] / gain[...]
-    scatter.advance((), (2, 3))
+    scatter.advance((), (3,))
     scatter.total(acc)
 
     def last(rows):
@@ -1618,7 +1602,7 @@
         + (jax.ShapeDtypeStruct((128, 2048), bf16),)
         + (jax.ShapeDtypeStruct((2, 128, 2048), bf16),) * 2
         + (jax.ShapeDtypeStruct((2, 128, 512), bf16),) * 2,
-        [vmem()] * 6 + [hbm(), vmem()] + [hbm()] * 8,
+        [vmem()] * 9 + [hbm(), vmem()] + [hbm()] * 8,
         [vmem(), vmem()] + [hbm()] * 4 + [vmem()] + [hbm()] * 4,
         [
             pltpu.VMEM((2, 2, 512, 128), bf16),
@@ -1640,6 +1624,7 @@
             pltpu.SemaphoreType.DMA((4,)),
             pltpu.SemaphoreType.DMA((4,)),
             pltpu.SemaphoreType.DMA(()),
+            pltpu.VMEM((2, 1536, 128), f32),
         ],
         args, flops=10**10, sent=10**7,
     )
@@ -1892,12 +1877,11 @@
         total, mid, grad_top, gain_f, p1, att.reshape(1024, 256),
         a_send, b_send, a_keep, b_keep, ra_dg, rb_dg,
     )
-    dq, dkv = attend_back(low, q, kv_flat, tabs, att, datt, lse)
     (
         dparts, gain_a_part, qa_send, qa_keep, qb_send, qb_keep,
         hidden_out, ra_last, rb_last, oa_came, ob_came,
     ) = unproject(
-        dq, dkv.reshape(2, 3, 512, 128), rows2, p1, tabs, gain_a, parts, mid,
+        q, kv_flat, att, datt, lse, rows2, p1, tabs, gain_a, parts, mid,
         a_keep, b_keep, ra_dg, rb_dg, ra_u, rb_u, oa_send, ob_send,
     )
     gains = jnp.concatenate(

time: 520 us -> 509 us (0.979)
  Pallas kernels: 466 us -> 455 us
    pallas_call x1 -> x0, Pallas kernels: 16.6 us -> none  [attend_back(): pl.pallas_call(attend_back_kernel, out_shape=(jax.ShapeDtypeStruct((2, 51...]
    pallas_call x7, Pallas kernels: 437 us -> 444 us  [comm_call(): pl.pallas_call(kernel, out_shape=out_shape, in_specs=in_specs, out_specs=...]
  transfers between devices with their start and end apart: 2 -> 2, of which waited for: 0 -> 0; matrix products, arithmetic and copies ran while one was open for 1% -> 1% of each run, Pallas kernels for 34% -> 35%
where the time goes in v5:
time: 509 us; the launch traced here: 505 us
  Pallas kernels  455 us (89%)
  local copies, waits for them, and re-layouts  19.3 us (4%)
  other arithmetic  15.6 us (3%)
  between operations  14.4 us (3%)
    pallas_call x7, Pallas kernels, comm_call(): pl.pallas_call(kernel, out_shape=out_shape, in_specs=in_specs, out_specs=...  444 us
    unnamed x51, local copies, waits for them, and re-layouts  12.2 us
    pallas_call x1, Pallas kernels, attend(): pl.pallas_call(attend_kernel, out_shape=(jax.ShapeDtypeStruct((2, 512, 25...  11.2 us
  transfers between devices with their start and end apart: 2, of which 0 were waited for; matrix products, arithmetic and copies ran while one was open for 1% of the time, Pallas kernels for 35%

profile of v5, /device:TPU:0, one launch (start us, length us, event | category | flops | bytes accessed | tf_op | source)
XLA Modules:
  0.0 504.8 jit_solution(9423079205163871517)
XLA Ops:
  7.2 0.0 copy-start
  7.2 0.0 all-gather.5.cloned.1.call-start
  7.3 1.0 copy-done
  8.2 1.0 constant_dynamic-slice_fusion
  9.2 1.1 constant_dynamic-slice_fusion.2
  10.4 1.0 maximum_maximum_fusion
  11.4 0.0 all-gather.5.cloned.1.call-update
  11.4 0.0 all-gather.7.cloned.1.call-start
  11.5 0.0 copy-start.6
  11.5 0.0 copy-start.7
  11.5 0.1 constant_dynamic-slice_fusion.5
  11.6 0.1 maximum_bitcast_fusion.1
  11.7 1.4 copy-done.6
  13.1 0.6 copy-done.7
  13.7 0.2 dynamic-slice_bitcast_fusion
  13.9 2.0 pad_maximum_fusion
  15.8 0.0 all-gather.7.cloned.1.call-update
  15.9 0.6 copy-done.21
  16.5 0.2 reduce-window.4
  16.7 0.1 select_reduce_fusion
  16.8 0.0 copy-done.20
  16.8 1.0 multiply_sine_fusion
  17.8 0.1 broadcast_in_dim.22
  17.9 1.5 concatenate.24.tab
  19.4 47.1 %enter.1 = (bf16[2,4,128,2048]{3,2,1,0:T(8,128)(2,1)}, f32[2,512,384]{2,1,0:T(8,128)}) custom-call(bf16[128,2048]{1,0:T(8,128)(2,1)} %bitcast.78, f32[1,2048]{1,0:T(1,128)} %bitcast.84, f32[512,384]{1,0:T(8,128)} %concatenate.24.tab), custom_call_target="tpu_custom_call" | custom-call | flops 10000000000 | bytes 100000000 | tf_op jit(solution)/shard_map/enter/pallas_call | solution.py:661
  66.5 1.1 slice.71
  67.6 0.1 convert_reduce_fusion
  67.8 0.6 convert_element_type.110.low
  68.4 31.6 %project.1 = (bf16[2,512,256]{2,1,0:T(8,128)(2,1)}, bf16[2,3,512,128]{3,2,1,0:T(8,128)(2,1)}, bf16[2,4,64,2048]{3,2,1,0:T(8,128)(2,1)}) custom-call(bf16[2,512,2048]{2,1,0:T(8,128)(2,1)} %bitcast.88, bf16[4,512,640]{2,1,0:T(8,128)(2,1)} %bitcast.71, f32[2,512,384]{2,1,0:T(8,128)} %get-tuple-element.57.tabs.starts, bf16[128,2048]{1,0:T(8,128)(2,1)} %bitcast.75), custom_call_target="tpu_custom_call" | custom-call | flops 10000000000 | bytes 10000000 | tf_op jit(solution)/shard_map/project/pallas_call | solution.py:661
  100.0 11.2 %attend.1 = (bf16[2,512,256]{2,1,0:T(8,128)(2,1)}, f32[2,4,512,128]{3,2,1,0:T(8,128)}) custom-call(s32[8]{0:T(128)} %convert_element_type.110.low, bf16[2,512,256]{2,1,0:T(8,128)(2,1)} %get-tuple-element.58.q, bf16[2,1536,128]{2,1,0:T(8,128)(2,1)} %bitcast.91, f32[2,512,384]{2,1,0:T(8,128)} %get-tuple-element.57.tabs.starts), custom_call_target="tpu_custom_call" | custom-call | flops 20000000000 | bytes 10000000 | tf_op jit(solution)/shard_map/attend/pallas_call | solution.py:938
  111.2 84.9 %middle.1 = (f32[128,2048]{1,0:T(8,128)}, bf16[2,4,128,2048]{3,2,1,0:T(8,128)(2,1)}) custom-call(bf16[2,512,256]{2,1,0:T(8,128)(2,1)} %get-tuple-element.60.att, bf16[4,512,640]{2,1,0:T(8,128)(2,1)} %bitcast.72, bf16[128,2048]{1,0:T(8,128)(2,1)} %bitcast.79, f32[1,2048]{1,0:T(1,128)} %bitcast.81), custom_call_target="tpu_custom_call" | custom-call | flops 10000000000 | bytes 200000000 | tf_op jit(solution)/shard_map/middle/pallas_call | solution.py:661
  196.1 0.0 all-gather.7.cloned.1.call-done
  196.1 102.5 %ffn.1 = (bf16[2,4,128,2048]{3,2,1,0:T(8,128)(2,1)}, f32[128,2048]{1,0:T(8,128)}, f32[8,2048]{1,0:T(8,128)}, bf16[2,3,128,2048]{3,2,1,0:T(8,128)(2,1)}, bf16[2,3...) custom-call(bf16[1024,2048]{1,0:T(8,128)(2,1)} %bitcast.90, ...), custom_call_target="tpu_custom_call" | custom-call | flops 40000000000 | bytes 100000000 | tf_op jit(solution)/shard_map/ffn/pallas_call | solution.py:661
  298.6 51.3 %branch.1 = (f32[128,2048]{1,0:T(8,128)}, bf16[2,512,256]{2,1,0:T(8,128)(2,1)}, bf16[2,128,512]{2,1,0:T(8,128)(2,1)}, bf16[2,128,512]{2,1,0:T(8,128)(2,1)}, bf16...) custom-call(f32[128,2048]{1,0:T(8,128)} %get-tuple-element.63.total,, ...), custom_call_target="tpu_custom_call" | custom-call | flops 10000000000 | bytes 100000000 | tf_op jit(solution)/shard_map/branch/pallas_call | solution.py:661
  349.9 0.0 copy-start.9
  349.9 64.3 %unproject.1 = (bf16[2,4,128,2048]{3,2,1,0:T(8,128)(2,1)}, f32[8,2048]{1,0:T(8,128)}, bf16[2,128,768]{2,1,0:T(8,128)(2,1)}, bf16[2,128,768]{2,1,0:T(8,128)(2,1)}...) custom-call(bf16[2,512,256]{2,1,0:T(8,128)(2,1)} %get-tuple-element., ...), custom_call_target="tpu_custom_call" | custom-call | flops 10000000000 | bytes 10000000 | tf_op jit(solution)/shard_map/unproject/pallas_call | solution.py:661
  414.2 0.0 copy-done.9
  414.2 0.0 copy-start.4
  414.2 0.0 copy-start.5
  414.3 0.0 copy-start.8
  414.3 0.0 copy-start.16
  414.3 0.0 copy-start.17
  414.3 3.9 bitcast_add_fusion
  418.2 0.0 copy-done.5
  418.2 0.0 copy-done.8
  418.2 0.3 copy-done.16
  418.5 0.5 copy-done.17
  419.0 2.1 bitcast_add_fusion.1
  421.1 0.1 maximum_bitcast_fusion
  421.3 1.8 copy.34
  423.2 0.6 pad_maximum_fusion.3.gains
  423.8 62.6 %leave.1 = (bf16[128,2048]{1,0:T(8,128)(2,1)}, f32[8,256]{1,0:T(8,128)}, f32[256,512]{1,0:T(8,128)}, f32[256,512]{1,0:T(8,128)}, f32[256,512]{1,0:T(8,128)}, /*index=5*/f32[256,512]{1,0:T(8,128)}) custom-call(bf16[2,4,128,2048]{3,2,1,0:T(8,128)(2,1)} %get-tuple-element.79.parts, bf16[128,2048]{1,0:T(8,128)(2,1)} %bitcast.80, f32[1,2048]{1,0:T(1,128)} %bitcast.86, ...), custom_call_target="tpu_custom_call" | custom-call | flops 10000000000 | bytes 100000000 | tf_op jit(solution)/shard_map/leave/pallas_call | solution.py:661
  486.3 1.3 fusion.2
  487.7 2.0 copy.33
  489.7 2.8 pad_maximum_fusion.1
  492.5 0.0 copy-done.3
  492.5 1.5 pad_maximum_fusion.2
  494.0 0.0 copy-start.1
  494.0 0.8 copy.40
  494.8 0.8 copy.41
  495.6 0.8 copy.42
  496.4 0.8 copy.43
  497.2 0.0 copy-done.11
  497.2 0.8 copy.44
  (31 shorter events, 0.1 us)
Async XLA Ops:
  7.2 1.1 copy-start
  7.2 4.3 copy-start.15
  7.2 61.2 %all-gather.5.cloned.1.call-start = ((), (), s32[]{:S(2)}) async-start(), calls=%async_computation | async-start | bytes 3276800 | tf_op jit(solution)/shard_map/all_gather | solution.py:1853
  11.4 184.7 %all-gather.7.cloned.1.call-start = ((), (), s32[]{:S(2)}) async-start(), calls=%async_computation.1 | async-start | bytes 15728640 | tf_op jit(solution)/shard_map/all_gather | solution.py:1854
  11.5 1.6 copy-start.6
  11.5 2.2 copy-start.7
  15.8 0.7 copy-start.21
  15.8 0.9 copy-start.20
  349.9 64.3 %copy-start.9 = (bf16[2,2,128,2048]{3,2,1,0:T(8,128)(2,1)S(1)}, bf16[2,2,128,2048]{3,2,1,0:T(8,128)(2,1)}, u32[]{:S(2)}) copy-start(bf16[2,2,128,2048]{3,2,1,0:T(8,128)(2,1)} %get-tuple-element.70.b_came.b_gate) | copy-start | bytes 6291460
  414.2 4.0 copy-start.4
  414.2 4.0 copy-start.5
  414.3 4.0 copy-start.8
  414.3 4.2 copy-start.16
  414.3 4.7 copy-start.17
  421.2 1.8 copy-start.19
  421.2 1.9 copy-start.18
  423.8 66.0 %copy-start.2 = (f32[128,2048]{1,0:T(8,128)S(1)}, f32[128,2048]{1,0:T(8,128)}, u32[]{:S(2)}) copy-start(f32[128,2048]{1,0:T(8,128)} %get-tuple-element.159) | copy-start | bytes 3145732
  489.7 2.8 copy-start.3
  492.5 1.5 copy-start.10
  492.5 2.3 copy-start.14
  494.0 1.6 copy-start.13
  494.0 2.4 copy-start.12
  494.0 3.2 copy-start.11
  494.0 4.0 copy-start.1
Sparse Core Ops, SparseCore 0:
  11.5 42.2 all-gather.4
  55.6 132.6 all-gather.6

commit v6 on v5

--- a/solution.py
+++ b/solution.py
@@ -501,6 +501,15 @@
             self.arrive(self.r, above)
             self.pass_on(above, False, True)
 
+    def advance(self, edge_steps, inner_steps):
+        at_end = (self.w == 0) | (self.w == self.last)
+        for ends, steps in ((True, edge_steps), (False, inner_steps)):
+            if steps:
+                @pl.when(at_end if ends else jnp.logical_not(at_end))
+                def _():
+                    for k in steps:
+                        self.step(k)
+
     def rest(self):
         for j in range(self.last + 1):
             self.arrive(1 - self.r, j)
@@ -527,37 +536,43 @@
 
 
 class Scatter:
-    def __init__(self, mine, theirs, bufs, sems, me, wid_count):
+    def __init__(self, mine, theirs, bufs, sems, me, wid_count, first=0, count=None):
         self.mine, self.theirs = mine, theirs
         self.from_pt, self.from_up, self.from_dn = bufs
         self.pt_s, self.pt_g, self.up_s, self.up_g, self.dn_s, self.dn_g = sems
         self.r, self.n, self.w = me
+        self.first, self.count = first, mine.shape[1] if count is None else count
+        self.rows = pl.ds(first, self.count)
         self.last = wid_count - 1
         self.up = (self.r, self.n, jnp.minimum(self.w + 1, self.last))
         self.dn = (self.r, self.n, jnp.maximum(self.w - 1, 0))
         self.pt = (1 - self.r, self.n, self.w)
 
     def order(self, i):
-        low, high = (3, 0, 2, 1)[i], (0, 3, 1, 2)[i]
-        return jnp.where(self.w < 2, low, high)
+        low = jnp.where(i == 0, 3, jnp.where(i == 1, 0, jnp.where(i == 2, 2, 1)))
+        return jnp.where(self.w < 2, low, 3 - low)
+
+    def send(self, source, target, sent, got, s, device):
+        return pltpu.make_async_remote_copy(
+            source.at[s, self.rows], target.at[s, self.rows], sent.at[s], got.at[s],
+            device_id=device, device_id_type=MESH,
+        )
 
     def pair(self, s):
-        return pltpu.make_async_remote_copy(
-            self.theirs.at[s], self.from_pt.at[s], self.pt_s.at[s], self.pt_g.at[s],
-            device_id=self.pt, device_id_type=MESH,
-        )
+        return self.send(self.theirs, self.from_pt, self.pt_s, self.pt_g, s, self.pt)
 
     def climb(self, s):
-        return pltpu.make_async_remote_copy(
-            self.mine.at[s], self.from_dn.at[s], self.up_s.at[s], self.up_g.at[s],
-            device_id=self.up, device_id_type=MESH,
-        )
+        return self.send(self.mine, self.from_dn, self.up_s, self.up_g, s, self.up)
 
     def fall(self, s):
-        return pltpu.make_async_remote_copy(
-            self.mine.at[s], self.from_up.at[s], self.dn_s.at[s], self.dn_g.at[s],
-            device_id=self.dn, device_id_type=MESH,
-        )
+        return self.send(self.mine, self.from_up, self.dn_s, self.dn_g, s, self.dn)
+
+    def each(self, body):
+        def run(i, carry):
+            body(pl.ds(pl.multiple_of(self.first + i * 16, 16), 16))
+            return carry
+
+        lax.fori_loop(0, self.count // 16, run, 0)
 
     def add(self, s, others):
         def body(rows):
@@ -566,7 +581,7 @@
                 total = total + other[s, rows, :].astype(f32)
             self.mine[s, rows, :] = total.astype(bf16)
 
-        each_rows(self.mine.shape[1], 16, body)
+        self.each(body)
 
     def step(self, s):
         self.pair(s).wait_recv()
@@ -597,10 +612,14 @@
         for ends, steps in ((True, edge_steps), (False, inner_steps)):
             at_end = (self.w == 0) | (self.w == self.last)
 
-            @pl.when(at_end if ends else jnp.logical_not(at_end))
-            def _():
-                for i in steps:
-                    self.step(self.order(i))
+            def body(i, carry):
+                self.step(self.order(i))
+                return carry
+
+            if steps:
+                @pl.when(at_end if ends else jnp.logical_not(at_end))
+                def _():
+                    lax.fori_loop(steps[0], steps[-1] + 1, body, 0)
 
     def total(self, out):
         w = self.w
@@ -608,7 +627,7 @@
         def first(rows):
             out[rows, :] = self.mine[w, rows, :].astype(f32) + self.from_pt[w, rows, :].astype(f32)
 
-        each_rows(out.shape[0], 16, first)
+        self.each(first)
 
         @pl.when(w > 0)
         def _():
@@ -617,7 +636,7 @@
             def more(rows):
                 out[rows, :] += self.from_dn[w, rows, :].astype(f32)
 
-            each_rows(out.shape[0], 16, more)
+            self.each(more)
 
         @pl.when(w < self.last)
         def _():
@@ -626,7 +645,7 @@
             def more(rows):
                 out[rows, :] += self.from_up[w, rows, :].astype(f32)
 
-            each_rows(out.shape[0], 16, more)
+            self.each(more)
 
     def sent(self):
         for s in range(self.last + 1):
@@ -960,18 +979,23 @@
 
 
 def middle_kernel(
-    att, p1, hidden, gain, mid_out, ffn_out,
-    theirs, mine, from_pt, from_up, from_dn, s0, s1, s2, s3, s4, s5, fbuf, h0, h1, h2, h3, out_s,
+    att, p1, hidden, gain, mid_out, ffn_out, theirs, mine, from_pt, from_up, from_dn, *refs
 ):
+    s_sems, g_sems, refs = refs[:12], refs[13:21], (refs[12], refs[21])
+    fbuf, out_s = refs
     me = spot()
     r, n, w = me
     greet(line_partners(r, n, w, 4))
-    scatter = Scatter(
-        mine, theirs, (from_pt, from_up, from_dn), (s0, s1, s2, s3, s4, s5), me, 4
-    )
-    ffn = Gather(fbuf, (h0, h1, h2, h3), me, 4)
-    for i in range(4):
-        s = scatter.order(i)
+    sums = [
+        Scatter(
+            mine, theirs, (from_pt, from_up, from_dn), s_sems[6 * c : 6 * c + 6], me, 4, 64 * c, 64
+        )
+        for c in range(2)
+    ]
+    gathers = [Gather(fbuf, g_sems[4 * c : 4 * c + 4], me, 4, pl.ds(64 * c, 64)) for c in range(2)]
+
+    def shard(i, carry):
+        s = sums[0].order(i)
         rows = pl.ds(pl.multiple_of(s * 128, 128), 128)
         left = jnp.concatenate([att[1 - r, rows, :], att[r, rows, :]], axis=0)
         for nn in range(4):
@@ -980,25 +1004,41 @@
                 columns = slice(nn * 512 + half * 256, nn * 512 + half * 256 + 256)
                 theirs[s, :, columns] = part[0:128]
                 mine[s, :, columns] = part[128:256]
-        scatter.pair(s).start()
-    for i in range(4):
-        scatter.step(scatter.order(i))
-    scatter.total(mid_out)
-
-    def body(rows):
-        middle = mid_out[rows, :] + hidden[rows, :].astype(f32)
-        mid_out[rows, :] = middle
-        fbuf[r, w, rows, :] = norm_rows(middle, gain[...]).astype(bf16)
-
-    each_rows(hidden.shape[0], 16, body)
-    ffn.own()
+        sums[0].pair(s).start()
+        sums[1].pair(s).start()
+        return carry
+
+    lax.fori_loop(0, 4, shard, 0)
+
+    def finish(c):
+        sums[c].total(mid_out)
+
+        def body(rows):
+            middle = mid_out[rows, :] + hidden[rows, :].astype(f32)
+            mid_out[rows, :] = middle
+            fbuf[r, w, rows, :] = norm_rows(middle, gain[...]).astype(bf16)
+
+        sums[c].each(body)
+        gathers[c].own()
+
+    sums[0].advance((0, 1, 2, 3), (0, 1, 2, 3))
+    sums[1].advance((0, 1, 2, 3), ())
+    finish(0)
+    sums[1].advance((), (0, 1))
+    gathers[0].advance((), (1,))
+    sums[1].advance((), (2, 3))
+    finish(1)
+    gathers[0].advance((1, 2), (2,))
+    gathers[0].step(3)
     for k in (1, 2, 3):
-        ffn.step(k)
-    ffn.rest()
+        gathers[1].step(k)
+    gathers[0].rest()
+    gathers[1].rest()
     out_f = pltpu.make_async_copy(fbuf, ffn_out, out_s)
     out_f.start()
-    scatter.sent()
-    ffn.sent()
+    for c in range(2):
+        sums[c].sent()
+        gathers[c].sent()
     out_f.wait()
 
 
@@ -1010,8 +1050,8 @@
         (jax.ShapeDtypeStruct((shard, width), f32), rows),
         [vmem()] * 4, [vmem(), hbm()],
         [pltpu.VMEM((4, shard, width), bf16)] * 2
-        + scatter_bufs(shard, width) + scatter_sems()
-        + gather_scratch(shard, width)
+        + scatter_bufs(shard, width) + scatter_sems() * 2
+        + gather_scratch(shard, width) + gather_sems()
         + [pltpu.SemaphoreType.DMA(())],
         (att, p1, hidden, gain), flops=10**10, sent=2 * 10**8,
     )

time: 509 us -> 513 us (level)
  no operation moved by 1% of the time
where the time goes in v6:
time: 513 us; the launch traced here: 508 us
  Pallas kernels  459 us (89%)
  local copies, waits for them, and re-layouts  19.3 us (4%)
  other arithmetic  15.6 us (3%)
  between operations  14.4 us (3%)
    pallas_call x7, Pallas kernels, comm_call(): pl.pallas_call(kernel, out_shape=out_shape, in_specs=in_specs, out_specs=...  448 us
    unnamed x51, local copies, waits for them, and re-layouts  12.2 us
    pallas_call x1, Pallas kernels, attend(): pl.pallas_call(attend_kernel, out_shape=(jax.ShapeDtypeStruct((2, 512, 25...  10.8 us
  transfers between devices with their start and end apart: 2, of which 0 were waited for; matrix products, arithmetic and copies ran while one was open for 1% of the time, Pallas kernels for 35%

profile of v6, /device:TPU:0, one launch (start us, length us, event | category | flops | bytes accessed | tf_op | source)
XLA Modules:
  0.0 508.3 jit_solution(6396582270913418157)
XLA Ops:
  7.2 0.0 copy-start
  7.2 0.0 copy-start.15
  7.2 0.0 all-gather.5.cloned.1.call-start
  7.3 1.0 copy-done
  8.2 1.0 constant_dynamic-slice_fusion
  9.2 1.1 constant_dynamic-slice_fusion.2
  10.4 1.0 maximum_maximum_fusion
  11.4 0.0 all-gather.5.cloned.1.call-update
  11.4 0.0 all-gather.7.cloned.1.call-start
  11.4 0.0 copy-done.15
  11.5 0.0 copy-start.6
  11.5 0.0 copy-start.7
  11.5 0.1 constant_dynamic-slice_fusion.5
  11.6 0.1 maximum_bitcast_fusion.1
  11.7 1.4 copy-done.6
  13.1 0.6 copy-done.7
  13.7 0.2 dynamic-slice_bitcast_fusion
  13.9 2.0 pad_maximum_fusion
  15.8 0.0 all-gather.7.cloned.1.call-update
  15.9 0.6 copy-done.21
  16.5 0.2 reduce-window.4
  16.7 0.1 select_reduce_fusion
  16.8 1.0 multiply_sine_fusion
  17.8 0.1 broadcast_in_dim.22
  17.9 1.5 concatenate.24.tab
  19.4 47.1 %enter.1 = (bf16[2,4,128,2048]{3,2,1,0:T(8,128)(2,1)}, f32[2,512,384]{2,1,0:T(8,128)}) custom-call(bf16[128,2048]{1,0:T(8,128)(2,1)} %bitcast.78, f32[1,2048]{1,0:T(1,128)} %bitcast.84, f32[512,384]{1,0:T(8,128)} %concatenate.24.tab), custom_call_target="tpu_custom_call" | custom-call | flops 10000000000 | bytes 100000000 | tf_op jit(solution)/shard_map/enter/pallas_call | solution.py:680
  66.5 1.1 slice.71
  67.6 0.1 convert_reduce_fusion
  67.8 0.6 convert_element_type.110.low
  68.4 31.6 %project.1 = (bf16[2,512,256]{2,1,0:T(8,128)(2,1)}, bf16[2,3,512,128]{3,2,1,0:T(8,128)(2,1)}, bf16[2,4,64,2048]{3,2,1,0:T(8,128)(2,1)}) custom-call(bf16[2,512,2048]{2,1,0:T(8,128)(2,1)} %bitcast.88, bf16[4,512,640]{2,1,0:T(8,128)(2,1)} %bitcast.71, f32[2,512,384]{2,1,0:T(8,128)} %get-tuple-element.57.tabs.starts, bf16[128,2048]{1,0:T(8,128)(2,1)} %bitcast.75), custom_call_target="tpu_custom_call" | custom-call | flops 10000000000 | bytes 10000000 | tf_op jit(solution)/shard_map/project/pallas_call | solution.py:680
  100.0 10.8 %attend.1 = (bf16[2,512,256]{2,1,0:T(8,128)(2,1)}, f32[2,4,512,128]{3,2,1,0:T(8,128)}) custom-call(s32[8]{0:T(128)} %convert_element_type.110.low, bf16[2,512,256]{2,1,0:T(8,128)(2,1)} %get-tuple-element.58.q, bf16[2,1536,128]{2,1,0:T(8,128)(2,1)} %bitcast.91, f32[2,512,384]{2,1,0:T(8,128)} %get-tuple-element.57.tabs.starts), custom_call_target="tpu_custom_call" | custom-call | flops 20000000000 | bytes 10000000 | tf_op jit(solution)/shard_map/attend/pallas_call | solution.py:957
  110.8 86.9 %middle.1 = (f32[128,2048]{1,0:T(8,128)}, bf16[2,4,128,2048]{3,2,1,0:T(8,128)(2,1)}) custom-call(bf16[2,512,256]{2,1,0:T(8,128)(2,1)} %get-tuple-element.60.att, bf16[4,512,640]{2,1,0:T(8,128)(2,1)} %bitcast.72, bf16[128,2048]{1,0:T(8,128)(2,1)} %bitcast.79, f32[1,2048]{1,0:T(1,128)} %bitcast.81), custom_call_target="tpu_custom_call" | custom-call | flops 10000000000 | bytes 200000000 | tf_op jit(solution)/shard_map/middle/pallas_call | solution.py:680
  197.7 0.0 all-gather.7.cloned.1.call-done
  197.8 105.1 %ffn.1 = (bf16[2,4,128,2048]{3,2,1,0:T(8,128)(2,1)}, f32[128,2048]{1,0:T(8,128)}, f32[8,2048]{1,0:T(8,128)}, bf16[2,3,128,2048]{3,2,1,0:T(8,128)(2,1)}, bf16[2,3...) custom-call(bf16[1024,2048]{1,0:T(8,128)(2,1)} %bitcast.90, ...), custom_call_target="tpu_custom_call" | custom-call | flops 40000000000 | bytes 100000000 | tf_op jit(solution)/shard_map/ffn/pallas_call | solution.py:680
  302.8 52.8 %branch.1 = (f32[128,2048]{1,0:T(8,128)}, bf16[2,512,256]{2,1,0:T(8,128)(2,1)}, bf16[2,128,512]{2,1,0:T(8,128)(2,1)}, bf16[2,128,512]{2,1,0:T(8,128)(2,1)}, bf16...) custom-call(f32[128,2048]{1,0:T(8,128)} %get-tuple-element.63.total,, ...), custom_call_target="tpu_custom_call" | custom-call | flops 10000000000 | bytes 100000000 | tf_op jit(solution)/shard_map/branch/pallas_call | solution.py:680
  355.7 62.0 %unproject.1 = (bf16[2,4,128,2048]{3,2,1,0:T(8,128)(2,1)}, f32[8,2048]{1,0:T(8,128)}, bf16[2,128,768]{2,1,0:T(8,128)(2,1)}, bf16[2,128,768]{2,1,0:T(8,128)(2,1)}...) custom-call(bf16[2,512,256]{2,1,0:T(8,128)(2,1)} %get-tuple-element., ...), custom_call_target="tpu_custom_call" | custom-call | flops 10000000000 | bytes 10000000 | tf_op jit(solution)/shard_map/unproject/pallas_call | solution.py:680
  417.7 0.0 copy-done.9
  417.7 0.0 copy-start.4
  417.7 0.0 copy-start.5
  417.7 0.0 copy-start.8
  417.7 0.0 copy-start.16
  417.7 0.0 copy-start.17
  417.7 3.9 bitcast_add_fusion
  421.6 0.0 copy-done.5
  421.6 0.0 copy-done.8
  421.7 0.3 copy-done.16
  422.0 0.5 copy-done.17
  422.4 2.1 bitcast_add_fusion.1
  424.5 0.1 maximum_bitcast_fusion
  424.7 1.8 copy.34
  426.6 0.6 pad_maximum_fusion.3.gains
  427.2 62.6 %leave.1 = (bf16[128,2048]{1,0:T(8,128)(2,1)}, f32[8,256]{1,0:T(8,128)}, f32[256,512]{1,0:T(8,128)}, f32[256,512]{1,0:T(8,128)}, f32[256,512]{1,0:T(8,128)}, /*index=5*/f32[256,512]{1,0:T(8,128)}) custom-call(bf16[2,4,128,2048]{3,2,1,0:T(8,128)(2,1)} %get-tuple-element.79.parts, bf16[128,2048]{1,0:T(8,128)(2,1)} %bitcast.80, f32[1,2048]{1,0:T(1,128)} %bitcast.86, ...), custom_call_target="tpu_custom_call" | custom-call | flops 10000000000 | bytes 100000000 | tf_op jit(solution)/shard_map/leave/pallas_call | solution.py:680
  489.8 1.3 fusion.2
  491.1 2.0 copy.33
  493.2 2.8 pad_maximum_fusion.1
  496.0 0.0 copy-done.3
  496.0 1.5 pad_maximum_fusion.2
  497.4 0.0 copy-start.1
  497.5 0.8 copy.40
  498.3 0.8 copy.41
  499.0 0.8 copy.42
  499.8 0.8 copy.43
  500.6 0.0 copy-done.11
  500.6 0.8 copy.44
  (31 shorter events, 0.1 us)
Async XLA Ops:
  7.2 1.1 copy-start
  7.2 4.3 copy-start.15
  7.2 61.2 %all-gather.5.cloned.1.call-start = ((), (), s32[]{:S(2)}) async-start(), calls=%async_computation | async-start | bytes 3276800 | tf_op jit(solution)/shard_map/all_gather | solution.py:1893
  11.4 186.4 %all-gather.7.cloned.1.call-start = ((), (), s32[]{:S(2)}) async-start(), calls=%async_computation.1 | async-start | bytes 15728640 | tf_op jit(solution)/shard_map/all_gather | solution.py:1894
  11.5 1.6 copy-start.6
  11.5 2.2 copy-start.7
  15.8 0.7 copy-start.21
  15.8 0.9 copy-start.20
  355.7 62.0 %copy-start.9 = (bf16[2,2,128,2048]{3,2,1,0:T(8,128)(2,1)S(1)}, bf16[2,2,128,2048]{3,2,1,0:T(8,128)(2,1)}, u32[]{:S(2)}) copy-start(bf16[2,2,128,2048]{3,2,1,0:T(8,128)(2,1)} %get-tuple-element.70.b_came.b_gate) | copy-start | bytes 6291460
  417.7 4.0 copy-start.4
  417.7 4.0 copy-start.5
  417.7 4.0 copy-start.8
  417.7 4.2 copy-start.16
  417.7 4.7 copy-start.17
  424.7 1.8 copy-start.19
  424.7 1.9 copy-start.18
  427.2 65.9 %copy-start.2 = (f32[128,2048]{1,0:T(8,128)S(1)}, f32[128,2048]{1,0:T(8,128)}, u32[]{:S(2)}) copy-start(f32[128,2048]{1,0:T(8,128)} %get-tuple-element.159) | copy-start | bytes 3145732
  493.2 2.8 copy-start.3
  496.0 1.5 copy-start.10
  496.0 2.3 copy-start.14
  497.4 1.6 copy-start.13
  497.4 2.4 copy-start.12
  497.4 3.2 copy-start.11
  497.4 4.0 copy-start.1
Sparse Core Ops, SparseCore 0:
  11.5 42.2 all-gather.4
  55.6 132.6 all-gather.6

commit v7 on v6

--- a/solution.py
+++ b/solution.py
@@ -449,8 +449,8 @@
 
 
 class Gather:
-    def __init__(self, buf, sems, me, wid_count, rows=slice(None)):
-        self.rows = rows
+    def __init__(self, buf, sems, me, wid_count, rows=slice(None), pair=True):
+        self.rows, self.both = rows, pair
         self.buf, (self.up_s, self.dn_s, self.pt_s, self.got) = buf, sems
         self.r, self.n, self.w = me
         self.last = wid_count - 1
@@ -459,7 +459,7 @@
         self.pt = (1 - self.r, self.n, self.w)
 
     def copy(self, j, sem, device, row=None):
-        row = self.r if row is None else row
+        row = (self.r if self.both else 0) if row is None else row
         return pltpu.make_async_remote_copy(
             self.buf.at[row, j, self.rows],
             self.buf.at[row, j, self.rows],
@@ -480,7 +480,8 @@
             def _():
                 self.copy(j, self.dn_s, self.dn).start()
 
-        self.copy(j, self.pt_s, self.pt).start()
+        if self.both:
+            self.copy(j, self.pt_s, self.pt).start()
 
     def own(self):
         self.pass_on(self.w, True, True)
@@ -493,12 +494,12 @@
 
         @pl.when(below >= 0)
         def _():
-            self.arrive(self.r, below)
+            self.arrive(None, below)
             self.pass_on(below, True, False)
 
         @pl.when(above <= self.last)
         def _():
-            self.arrive(self.r, above)
+            self.arrive(None, above)
             self.pass_on(above, False, True)
 
     def advance(self, edge_steps, inner_steps):
@@ -524,7 +525,8 @@
             def _():
                 self.copy(j, self.dn_s, self.dn).wait_send()
 
-            self.copy(j, self.pt_s, self.pt).wait_send()
+            if self.both:
+                self.copy(j, self.pt_s, self.pt).wait_send()
 
 
 def gather_scratch(shard, width):
@@ -910,17 +912,13 @@
     return jnp.concatenate([ok] * 4, axis=0)
 
 
-def key_tiles(low, row, block):
+def attend_kernel(q, kv, starts, out, lse):
+    block = pl.program_id(1)
     first_query = 1024 + block * QUERIES
-    return low[row * 4 + block] // KEYS, first_query // KEYS + 1, first_query
-
-
-def attend_kernel(low, q, kv, starts, out, lse):
-    row, block = pl.program_id(0), pl.program_id(1)
-    first, end, first_query = key_tiles(low, row, block)
     query = stack_low(q[0].astype(f32)).astype(bf16)
 
-    def body(tile, carry):
+    def body(step, carry):
+        tile = block // 2 + step
         top, total, acc = carry
         both = kv[0, pl.ds(pl.multiple_of(tile * KEYS, KEYS), KEYS), :]
         scores = contract_last(query, both) * 0.125
@@ -934,12 +932,13 @@
         return new_top, total, acc
 
     top, total, acc = lax.fori_loop(
-        first, end, body,
+        0, 5, body,
         (
             jnp.full((4 * QUERIES, 1), masked_score, f32),
             jnp.zeros((4 * QUERIES, 1), f32),
             jnp.zeros((4 * QUERIES, 128), f32),
         ),
+        unroll=True,
     )
     out[0] = unstack(acc / total, False).astype(bf16)
     lse[0, 0] = jnp.broadcast_to(top + jnp.log(total), (4 * QUERIES, 128))
@@ -947,31 +946,31 @@
 
 def attend_specs():
     return [
-        pl.BlockSpec((1, QUERIES, 256), lambda i, j, low: (i, j, 0)),
-        pl.BlockSpec((1, 1536, 128), lambda i, j, low: (i, 0, 0)),
-        pl.BlockSpec((1, QUERIES, 128), lambda i, j, low: (i, j, 2)),
+        pl.BlockSpec((1, QUERIES, 256), lambda i, j: (i, j, 0)),
+        pl.BlockSpec((1, 1536, 128), lambda i, j: (i, 0, 0)),
+        pl.BlockSpec((1, QUERIES, 128), lambda i, j: (i, j, 2)),
     ]
 
 
-def attend(low, q, kv, tabs):
+def attend(q, kv, tabs):
     return pl.pallas_call(
         attend_kernel,
         out_shape=(
             jax.ShapeDtypeStruct((2, 512, 256), bf16),
             jax.ShapeDtypeStruct((2, 4, 4 * QUERIES, 128), f32),
         ),
-        grid_spec=pltpu.PrefetchScalarGridSpec(
-            num_scalar_prefetch=1, grid=(2, 4),
+        grid_spec=pl.GridSpec(
+            grid=(2, 4),
             in_specs=attend_specs(),
             out_specs=[
-                pl.BlockSpec((1, QUERIES, 256), lambda i, j, low: (i, j, 0)),
-                pl.BlockSpec((1, 1, 4 * QUERIES, 128), lambda i, j, low: (i, j, 0, 0)),
+                pl.BlockSpec((1, QUERIES, 256), lambda i, j: (i, j, 0)),
+                pl.BlockSpec((1, 1, 4 * QUERIES, 128), lambda i, j: (i, j, 0, 0)),
             ],
         ),
         compiler_params=pltpu.CompilerParams(vmem_limit_bytes=VMEM_LIMIT),
         cost_estimate=pl.CostEstimate(flops=2 * 10**10, bytes_accessed=10**7, transcendentals=10**7),
         name="attend",
-    )(low, q, kv, tabs)
+    )(q, kv, tabs)
 
 
 def out_block(p1, nn, half):
@@ -979,23 +978,18 @@
 
 
 def middle_kernel(
-    att, p1, hidden, gain, mid_out, ffn_out, theirs, mine, from_pt, from_up, from_dn, *refs
+    att, p1, hidden, gain, mid_out, ffn_out,
+    theirs, mine, from_pt, from_up, from_dn, s0, s1, s2, s3, s4, s5, fbuf, h0, h1, h2, h3, out_s,
 ):
-    s_sems, g_sems, refs = refs[:12], refs[13:21], (refs[12], refs[21])
-    fbuf, out_s = refs
     me = spot()
     r, n, w = me
     greet(line_partners(r, n, w, 4))
-    sums = [
-        Scatter(
-            mine, theirs, (from_pt, from_up, from_dn), s_sems[6 * c : 6 * c + 6], me, 4, 64 * c, 64
-        )
-        for c in range(2)
-    ]
-    gathers = [Gather(fbuf, g_sems[4 * c : 4 * c + 4], me, 4, pl.ds(64 * c, 64)) for c in range(2)]
-
+    scatter = Scatter(
+        mine, theirs, (from_pt, from_up, from_dn), (s0, s1, s2, s3, s4, s5), me, 4
+    )
+    ffn = Gather(fbuf, (h0, h1, h2, h3), me, 4)
     def shard(i, carry):
-        s = sums[0].order(i)
+        s = scatter.order(i)
         rows = pl.ds(pl.multiple_of(s * 128, 128), 128)
         left = jnp.concatenate([att[1 - r, rows, :], att[r, rows, :]], axis=0)
         for nn in range(4):
@@ -1004,41 +998,27 @@
                 columns = slice(nn * 512 + half * 256, nn * 512 + half * 256 + 256)
                 theirs[s, :, columns] = part[0:128]
                 mine[s, :, columns] = part[128:256]
-        sums[0].pair(s).start()
-        sums[1].pair(s).start()
+        scatter.pair(s).start()
         return carry
 
     lax.fori_loop(0, 4, shard, 0)
-
-    def finish(c):
-        sums[c].total(mid_out)
-
-        def body(rows):
-            middle = mid_out[rows, :] + hidden[rows, :].astype(f32)
-            mid_out[rows, :] = middle
-            fbuf[r, w, rows, :] = norm_rows(middle, gain[...]).astype(bf16)
-
-        sums[c].each(body)
-        gathers[c].own()
-
-    sums[0].advance((0, 1, 2, 3), (0, 1, 2, 3))
-    sums[1].advance((0, 1, 2, 3), ())
-    finish(0)
-    sums[1].advance((), (0, 1))
-    gathers[0].advance((), (1,))
-    sums[1].advance((), (2, 3))
-    finish(1)
-    gathers[0].advance((1, 2), (2,))
-    gathers[0].step(3)
+    scatter.advance((0, 1, 2, 3), (0, 1, 2, 3))
+    scatter.total(mid_out)
+
+    def body(rows):
+        middle = mid_out[rows, :] + hidden[rows, :].astype(f32)
+        mid_out[rows, :] = middle
+        fbuf[r, w, rows, :] = norm_rows(middle, gain[...]).astype(bf16)
+
+    each_rows(hidden.shape[0], 16, body)
+    ffn.own()
     for k in (1, 2, 3):
-        gathers[1].step(k)
-    gathers[0].rest()
-    gathers[1].rest()
+        ffn.step(k)
+    ffn.rest()
     out_f = pltpu.make_async_copy(fbuf, ffn_out, out_s)
     out_f.start()
-    for c in range(2):
-        sums[c].sent()
-        gathers[c].sent()
+    scatter.sent()
+    ffn.sent()
     out_f.wait()
 
 
@@ -1050,8 +1030,8 @@
         (jax.ShapeDtypeStruct((shard, width), f32), rows),
         [vmem()] * 4, [vmem(), hbm()],
         [pltpu.VMEM((4, shard, width), bf16)] * 2
-        + scatter_bufs(shard, width) + scatter_sems() * 2
-        + gather_scratch(shard, width) + gather_sems()
+        + scatter_bufs(shard, width) + scatter_sems()
+        + gather_scratch(shard, width)
         + [pltpu.SemaphoreType.DMA(())],
         (att, p1, hidden, gain), flops=10**10, sent=2 * 10**8,
     )
@@ -1516,7 +1496,7 @@
             )
             return dq + jnp.dot(grad_scores, pair, preferred_element_type=f32)
 
-        dq = lax.fori_loop(0, 5, key_tile, jnp.zeros((4 * QUERIES, 128), f32))
+        dq = lax.fori_loop(0, 5, key_tile, jnp.zeros((4 * QUERIES, 128), f32), unroll=True)
         flat = unstack(dq, True) * 0.125
         cosine, sine = tabs[row, here, 0:128], -tabs[row, here, 128:256]
         there = pl.ds(pl.multiple_of(i * QUERIES, QUERIES), QUERIES)
@@ -1675,15 +1655,18 @@
     grad_out, ga_out, query_out, key_out, value_out, output_out,
     mine, from_pt, from_up, from_dn, s0, s1, s2, s3, s4, s5,
     acc, over_wid, summed, over_rest, w_s, w_g, t_s, t_g,
-    first_q, next_q, then_q, next_o, then_o, kv, n_s, n_g, k_s, k_g,
+    first_q, next_q, then_q, next_o, then_o, kv, n_s, n_g, k0, k1, k2, k3, m_s,
 ):
     me = spot()
     r, n, w = me
+    own_parts = pltpu.make_async_copy(parts.at[r], mine, m_s)
+    own_parts.start()
     partners = [(w != j, (r, n, jnp.int32(j))) for j in range(4)]
     partners += [
         ((r != a) | (n != b), (jnp.int32(a), jnp.int32(b), w)) for a in range(2) for b in range(4)
     ]
     greet(partners)
+    kv_gather = Gather(kv, (k0, k1, k2, k3), me, 4, pair=False)
     x_side, y_side = over_x(r, n, w), over_y(r, n, w)
     q_hops = [
         push(qa_send, first_q.at[0], n_s.at[0], n_g.at[0], x_side),
@@ -1722,12 +1705,8 @@
         def _():
             wid_copy(j, w).start()
 
-    for s in range(4):
-        def fill(rows):
-            mine[s, rows, :] = parts[r, s, rows, :]
-
-        each_rows(128, 16, fill)
-    scatter.advance((0, 1, 2, 3), ())
+    own_parts.wait()
+    scatter.advance((0, 1, 2), ())
     for j, (keep, came) in enumerate(((oa_keep, oa_in), (ob_keep, ob_in))):
         next_o[j] = (keep[1].astype(f32) + came[1].astype(f32)).astype(bf16)
         o_hops[j].start()
@@ -1748,31 +1727,17 @@
         q_hops[j].wait_recv()
         next_q[j] = (keep[1].astype(f32) + first_q[j, 1].astype(f32)).astype(bf16)
         q_later[j].start()
-    scatter.advance((), (0, 1))
+    scatter.advance((), (0,))
     for j, keep in enumerate((qa_keep, qb_keep)):
         q_later[j].wait_recv()
         total = keep[0].astype(f32) + first_q[j, 0].astype(f32) + then_q[j].astype(f32)
         query_out[j * 128 : j * 128 + 128, :] = total[:, 0:512]
-        kv[w, j * 128 : j * 128 + 128, :] = total[:, 512:768].astype(bf16)
-
-    def kv_copy(j, slot):
-        return pltpu.make_async_remote_copy(
-            kv.at[w], kv.at[w], k_s.at[j], k_g.at[slot],
-            device_id=(r, n, jnp.int32(j)), device_id_type=MESH,
-        )
-
-    def kv_wait(j):
-        return pltpu.make_async_remote_copy(
-            kv.at[j], kv.at[j], k_s.at[j], k_g.at[j],
-            device_id=(r, n, jnp.int32(j)), device_id_type=MESH,
-        )
-
-    for j in range(4):
-        @pl.when(w != j)
-        def _():
-            kv_copy(j, w).start()
-
-    scatter.advance((), (2, 3))
+        kv[0, w, j * 128 : j * 128 + 128, :] = total[:, 512:768].astype(bf16)
+    kv_gather.own()
+    scatter.advance((3,), (1, 2))
+    kv_gather.advance((), (1,))
+    scatter.advance((), (3,))
+    kv_gather.advance((), (2,))
     for j, (keep, came) in enumerate(((oa_keep, oa_in), (ob_keep, ob_in))):
         o_hops[j].wait_recv()
         output_out[j * 128 : j * 128 + 128, :] = (
@@ -1797,24 +1762,17 @@
         grad_out[rows, :] = (grad + gmid[rows, :]).astype(bf16)
 
     each_rows(hidden.shape[0], 16, last)
+    kv_gather.advance((1, 2, 3), (3,))
     lane = lax.broadcasted_iota(jnp.int32, (256, 128), 1)
     for j in range(4):
-        @pl.when(w != j)
-        def _():
-            kv_wait(j).wait_recv()
-
-        even, odd = kv[j, :, 0:128].astype(f32), kv[j, :, 128:256].astype(f32)
+        even, odd = kv[0, j, :, 0:128].astype(f32), kv[0, j, :, 128:256].astype(f32)
         here = slice(j * 128, j * 128 + 128)
         key_out[:, here] = jnp.where(lane < 64, even, pltpu.roll(odd, 64, 1))
         value_out[:, here] = jnp.where(lane < 64, pltpu.roll(even, 64, 1), odd)
     scatter.sent()
+    kv_gather.sent()
     for hop in q_hops + q_later + o_hops:
         hop.wait_send()
-    for j in range(4):
-        @pl.when(w != j)
-        def _():
-            kv_copy(j, w).wait_send()
-
     for j in range(4):
         @pl.when(w != j)
         def _():
@@ -1834,7 +1792,7 @@
         leave_kernel, "leave", 7,
         (jax.ShapeDtypeStruct((shard, width), bf16), jax.ShapeDtypeStruct((8, 256), f32))
         + (grad,) * 4,
-        [vmem()] * 13, [vmem()] * 6,
+        [hbm()] + [vmem()] * 12, [vmem()] * 6,
         [pltpu.VMEM((4, shard, width), bf16)]
         + scatter_bufs(shard, width) + scatter_sems()
         + [
@@ -1851,12 +1809,12 @@
             pltpu.VMEM((2, 128, 768), bf16),
             pltpu.VMEM((2, 128, 512), bf16),
             pltpu.VMEM((2, 128, 512), bf16),
-            pltpu.VMEM((4, 256, 256), bf16),
+            pltpu.VMEM((1, 4, 256, 256), bf16),
             pltpu.SemaphoreType.DMA((6,)),
             pltpu.SemaphoreType.DMA((6,)),
-            pltpu.SemaphoreType.DMA((4,)),
-            pltpu.SemaphoreType.DMA((4,)),
-        ],
+        ]
+        + gather_sems()
+        + [pltpu.SemaphoreType.DMA(())],
         args, flops=10**10, sent=10**8,
     )
 
@@ -1906,9 +1864,8 @@
     rows, tabs = enter(hidden, gain_a, tab)
     rows3, rows2 = rows.reshape(2, 512, 2048), rows.reshape(1024, 2048)
     q, kv, tops = project(rows3, p1, tabs, grad_top)
-    low = tabs[:, ::QUERIES, 256].astype(jnp.int32).reshape(8)
     kv_flat = kv.reshape(2, 1536, 128)
-    att, lse = attend(low, q, kv_flat, tabs)
+    att, lse = attend(q, kv_flat, tabs)
     mid, ffn_rows = middle_stage(att, p1, hidden, gain_f)
     parts, total, gain_f_part, a_send, a_keep, b_send, b_keep, ra_dg, rb_dg = ffn_stage(
         ffn_rows.reshape(1024, 2048), tops, grad_top, p2, gain_f

time: 513 us -> 495 us (0.965)
  Pallas kernels: 459 us -> 446 us
    pallas_call x7, Pallas kernels: 448 us -> 432 us  [comm_call(): pl.pallas_call(kernel, out_shape=out_shape, in_specs=in_specs, out_specs=...]
  transfers between devices with their start and end apart: 2 -> 2, of which waited for: 0 -> 0; matrix products, arithmetic and copies ran while one was open for 1% -> 1% of each run, Pallas kernels for 35% -> 36%
where the time goes in v7:
time: 495 us; the launch traced here: 494 us
  Pallas kernels  446 us (90%)
  local copies, waits for them, and re-layouts  17.6 us (4%)
  other arithmetic  15.5 us (3%)
  between operations  14.4 us (3%)
    pallas_call x7, Pallas kernels, comm_call(): pl.pallas_call(kernel, out_shape=out_shape, in_specs=in_specs, out_specs=...  432 us
    pallas_call x1, Pallas kernels, attend(): pl.pallas_call(attend_kernel, out_shape=(jax.ShapeDtypeStruct((2, 512, 25...  14.2 us
    unnamed x51, local copies, waits for them, and re-layouts  12.2 us
  transfers between devices with their start and end apart: 2, of which 0 were waited for; matrix products, arithmetic and copies ran while one was open for 1% of the time, Pallas kernels for 36%

profile of v7, /device:TPU:0, one launch (start us, length us, event | category | flops | bytes accessed | tf_op | source)
XLA Modules:
  0.0 493.7 jit_solution(13322103230556915782)
XLA Ops:
  7.2 0.0 copy-start
  7.2 0.0 copy-start.15
  7.2 0.0 all-gather.5.cloned.1.call-start
  7.3 1.0 copy-done
  8.2 1.0 constant_dynamic-slice_fusion
  9.2 1.1 constant_dynamic-slice_fusion.2
  10.4 1.0 maximum_maximum_fusion
  11.4 0.0 all-gather.5.cloned.1.call-update
  11.4 0.0 all-gather.7.cloned.1.call-start
  11.4 0.0 copy-done.15
  11.5 0.0 copy-start.6
  11.5 0.0 copy-start.7
  11.5 0.1 constant_dynamic-slice_fusion.5
  11.6 0.1 maximum_bitcast_fusion.1
  11.7 1.4 copy-done.6
  13.1 0.6 copy-done.7
  13.7 0.2 dynamic-slice_bitcast_fusion
  13.9 2.0 pad_maximum_fusion
  15.8 0.0 all-gather.7.cloned.1.call-update
  15.9 0.6 copy-done.21
  16.5 0.2 reduce-window.4
  16.7 0.1 select_reduce_fusion
  16.8 0.0 copy-done.20
  16.8 1.0 multiply_sine_fusion
  17.8 0.1 broadcast_in_dim.22
  17.9 1.5 concatenate.24.tab
  19.4 47.1 %enter.1 = (bf16[2,4,128,2048]{3,2,1,0:T(8,128)(2,1)}, f32[2,512,384]{2,1,0:T(8,128)}) custom-call(bf16[128,2048]{1,0:T(8,128)(2,1)} %bitcast.78, f32[1,2048]{1,0:T(1,128)} %bitcast.84, f32[512,384]{1,0:T(8,128)} %concatenate.24.tab), custom_call_target="tpu_custom_call" | custom-call | flops 10000000000 | bytes 100000000 | tf_op jit(solution)/shard_map/enter/pallas_call | solution.py:682
  66.5 0.0 all-gather.5.cloned.1.call-done
  66.5 32.2 %project.1 = (bf16[2,512,256]{2,1,0:T(8,128)(2,1)}, bf16[2,3,512,128]{3,2,1,0:T(8,128)(2,1)}, bf16[2,4,64,2048]{3,2,1,0:T(8,128)(2,1)}) custom-call(bf16[2,512,2048]{2,1,0:T(8,128)(2,1)} %bitcast.88, bf16[4,512,640]{2,1,0:T(8,128)(2,1)} %bitcast.71, f32[2,512,384]{2,1,0:T(8,128)} %get-tuple-element.57.tabs.starts, bf16[128,2048]{1,0:T(8,128)(2,1)} %bitcast.75), custom_call_target="tpu_custom_call" | custom-call | flops 10000000000 | bytes 10000000 | tf_op jit(solution)/shard_map/project/pallas_call | solution.py:682
  98.7 14.2 %attend.1 = (bf16[2,512,256]{2,1,0:T(8,128)(2,1)}, f32[2,4,512,128]{3,2,1,0:T(8,128)}) custom-call(bf16[2,512,256]{2,1,0:T(8,128)(2,1)} %get-tuple-element.58.q, bf16[2,1536,128]{2,1,0:T(8,128)(2,1)} %bitcast.91, f32[2,512,384]{2,1,0:T(8,128)} %get-tuple-element.57.tabs.starts), custom_call_target="tpu_custom_call" | custom-call | flops 20000000000 | bytes 10000000 | tf_op jit(solution)/shard_map/attend/pallas_call | solution.py:956
  112.9 85.0 %middle.1 = (f32[128,2048]{1,0:T(8,128)}, bf16[2,4,128,2048]{3,2,1,0:T(8,128)(2,1)}) custom-call(bf16[2,512,256]{2,1,0:T(8,128)(2,1)} %get-tuple-element.60.att, bf16[4,512,640]{2,1,0:T(8,128)(2,1)} %bitcast.72, bf16[128,2048]{1,0:T(8,128)(2,1)} %bitcast.79, f32[1,2048]{1,0:T(1,128)} %bitcast.81), custom_call_target="tpu_custom_call" | custom-call | flops 10000000000 | bytes 200000000 | tf_op jit(solution)/shard_map/middle/pallas_call | solution.py:682
  197.9 0.0 all-gather.7.cloned.1.call-done
  198.0 94.0 %ffn.1 = (bf16[2,4,128,2048]{3,2,1,0:T(8,128)(2,1)}, f32[128,2048]{1,0:T(8,128)}, f32[8,2048]{1,0:T(8,128)}, bf16[2,3,128,2048]{3,2,1,0:T(8,128)(2,1)}, bf16[2,3...) custom-call(bf16[1024,2048]{1,0:T(8,128)(2,1)} %bitcast.90, ...), custom_call_target="tpu_custom_call" | custom-call | flops 40000000000 | bytes 100000000 | tf_op jit(solution)/shard_map/ffn/pallas_call | solution.py:682
  292.0 51.9 %branch.1 = (f32[128,2048]{1,0:T(8,128)}, bf16[2,512,256]{2,1,0:T(8,128)(2,1)}, bf16[2,128,512]{2,1,0:T(8,128)(2,1)}, bf16[2,128,512]{2,1,0:T(8,128)(2,1)}, bf16...) custom-call(f32[128,2048]{1,0:T(8,128)} %get-tuple-element.63.total,, ...), custom_call_target="tpu_custom_call" | custom-call | flops 10000000000 | bytes 100000000 | tf_op jit(solution)/shard_map/branch/pallas_call | solution.py:682
  343.9 0.0 copy-start.9
  343.9 58.2 %unproject.1 = (bf16[2,4,128,2048]{3,2,1,0:T(8,128)(2,1)}, f32[8,2048]{1,0:T(8,128)}, bf16[2,128,768]{2,1,0:T(8,128)(2,1)}, bf16[2,128,768]{2,1,0:T(8,128)(2,1)}...) custom-call(bf16[2,512,256]{2,1,0:T(8,128)(2,1)} %get-tuple-element., ...), custom_call_target="tpu_custom_call" | custom-call | flops 10000000000 | bytes 10000000 | tf_op jit(solution)/shard_map/unproject/pallas_call | solution.py:682
  402.1 0.0 copy-done.9
  402.1 0.0 copy-start.4
  402.2 0.0 copy-start.5
  402.2 0.0 copy-start.8
  402.2 0.0 copy-start.16
  402.2 3.9 bitcast_add_fusion
  406.1 0.0 copy-done.4
  406.1 0.0 copy-done.8
  406.1 0.3 copy-done.16
  406.4 0.5 copy-done.17
  406.9 2.1 bitcast_add_fusion.1
  409.0 0.1 maximum_bitcast_fusion
  409.2 1.8 copy.32
  411.0 0.0 copy-done.19
  411.1 0.6 pad_maximum_fusion.3.gains
  411.7 63.4 %leave.1 = (bf16[128,2048]{1,0:T(8,128)(2,1)}, f32[8,256]{1,0:T(8,128)}, f32[256,512]{1,0:T(8,128)}, f32[256,512]{1,0:T(8,128)}, f32[256,512]{1,0:T(8,128)}, /*index=5*/f32[256,512]{1,0:T(8,128)}) custom-call(bf16[2,4,128,2048]{3,2,1,0:T(8,128)(2,1)} %get-tuple-element.79.parts, bf16[128,2048]{1,0:T(8,128)(2,1)} %bitcast.80, f32[1,2048]{1,0:T(1,128)} %bitcast.86, ...), custom_call_target="tpu_custom_call" | custom-call | flops 10000000000 | bytes 100000000 | tf_op jit(solution)/shard_map/leave/pallas_call | solution.py:682
  475.2 1.3 fusion.2
  476.5 2.0 copy.31
  478.5 2.8 pad_maximum_fusion.1
  481.3 1.5 pad_maximum_fusion.2
  482.8 0.0 copy-start.1
  482.8 0.8 copy.38
  483.6 0.0 copy-done.14
  483.6 0.8 copy.39
  484.4 0.8 copy.40
  485.2 0.8 copy.41
  486.0 0.8 copy.42
  486.8 0.0 copy-done.1
  (28 shorter events, 0.1 us)
Async XLA Ops:
  7.2 1.1 copy-start
  7.2 4.3 copy-start.15
  7.2 59.3 %all-gather.5.cloned.1.call-start = ((), (), s32[]{:S(2)}) async-start(), calls=%async_computation | async-start | bytes 3276800 | tf_op jit(solution)/shard_map/all_gather | solution.py:1851
  11.4 186.6 %all-gather.7.cloned.1.call-start = ((), (), s32[]{:S(2)}) async-start(), calls=%async_computation.1 | async-start | bytes 15728640 | tf_op jit(solution)/shard_map/all_gather | solution.py:1852
  11.5 1.6 copy-start.6
  11.5 2.2 copy-start.7
  15.8 0.7 copy-start.21
  15.8 0.9 copy-start.20
  343.9 58.2 %copy-start.9 = (bf16[2,2,128,2048]{3,2,1,0:T(8,128)(2,1)S(1)}, bf16[2,2,128,2048]{3,2,1,0:T(8,128)(2,1)}, u32[]{:S(2)}) copy-start(bf16[2,2,128,2048]{3,2,1,0:T(8,128)(2,1)} %get-tuple-element.70.b_came.b_gate) | copy-start | bytes 6291460
  402.1 4.0 copy-start.4
  402.2 4.0 copy-start.5
  402.2 4.0 copy-start.8
  402.2 4.2 copy-start.16
  402.2 4.7 copy-start.17
  409.2 1.8 copy-start.19
  409.2 1.9 copy-start.18
  411.7 66.8 %copy-start.2 = (f32[128,2048]{1,0:T(8,128)S(1)}, f32[128,2048]{1,0:T(8,128)}, u32[]{:S(2)}) copy-start(f32[128,2048]{1,0:T(8,128)} %get-tuple-element.148) | copy-start | bytes 3145732
  478.5 2.8 copy-start.3
  481.3 1.5 copy-start.10
  481.3 2.3 copy-start.14
  482.8 1.6 copy-start.13
  482.8 2.4 copy-start.12
  482.8 3.2 copy-start.11
  482.8 4.0 copy-start.1
Sparse Core Ops, SparseCore 0:
  11.5 42.2 all-gather.4
  55.6 132.6 all-gather.6

commit v8 on v7

--- a/solution.py
+++ b/solution.py
@@ -448,6 +448,56 @@
     )
 
 
+class Square:
+    def __init__(self, shard, full, sems, me):
+        self.shard, self.full = shard, full
+        self.sent, self.got = sems
+        r, n, w = me
+        self.n, self.x, self.y = n, n + 1 - 2 * (n % 2), (n + 2) % 4
+        self.by_x, self.by_y = over_x(*me), over_y(*me)
+        size = shard.shape[0] // 2
+        self.upper, self.lower = pl.ds(0, size), pl.ds(size, size)
+
+    def first(self, k, place):
+        return push(
+            self.shard, self.full.at[place], self.sent.at[k], self.got.at[k],
+            (self.by_x, self.by_y)[k],
+        )
+
+    def second(self, k, place):
+        part = self.full.at[place, (self.upper, self.lower)[k]]
+        return push(
+            part, part, self.sent.at[2 + k], self.got.at[2 + k], (self.by_y, self.by_x)[k]
+        )
+
+    def start(self):
+        self.first(0, self.n).start()
+        self.first(1, self.n).start()
+
+    def turn(self):
+        self.first(0, self.x).wait_recv()
+        self.second(0, self.x).start()
+        self.first(1, self.y).wait_recv()
+        self.second(1, self.y).start()
+
+    def finish(self):
+        for k in range(2):
+            self.second(k, 3 - self.n).wait_recv()
+            self.first(k, self.n).wait_send()
+            self.second(k, (self.x, self.y)[k]).wait_send()
+
+
+def square_sems():
+    return [pltpu.SemaphoreType.DMA((4,))] * 2
+
+
+def fetch(own, full, target, sems, n):
+    copies = [pltpu.make_async_copy(own, target.at[n], sems.at[0])]
+    for k, place in enumerate((n + 1 - 2 * (n % 2), (n + 2) % 4, 3 - n)):
+        copies.append(pltpu.make_async_copy(full.at[place], target.at[place], sems.at[1 + k]))
+    return copies
+
+
 class Gather:
     def __init__(self, buf, sems, me, wid_count, rows=slice(None), pair=True):
         self.rows, self.both = rows, pair
@@ -704,10 +754,19 @@
     return x * cosine + swapped * sine
 
 
-def enter_kernel(hidden, gain, tab, rows_out, tabs_out, buf, up_s, dn_s, pt_s, got, tabs, tab_s, tab_g, out_s):
+def enter_kernel(
+    hidden, gain, tab, p1_own, down_own, rows_out, tabs_out, p1_out, down_out,
+    buf, up_s, dn_s, pt_s, got, tabs, tab_s, tab_g, out_s, p1_s, p1_g, down_s, down_g, p1_here, here_s,
+):
     me = spot()
     r, n, w = me
-    greet(line_partners(r, n, w, 4))
+    bring = pltpu.make_async_copy(p1_own, p1_here, here_s.at[0])
+    bring.start()
+    greet(line_partners(r, n, w, 4) + square_partners(r, n, w))
+    p1 = Square(p1_own, p1_out, (p1_s, p1_g), me)
+    down = Square(down_own.at[0:256], down_out, (down_s, down_g), me)
+    p1.start()
+    down.start()
     gather = Gather(buf, (up_s, dn_s, pt_s, got), me, 4)
     tab_copy = pltpu.make_async_remote_copy(
         tab, tabs.at[r], tab_s, tab_g, device_id=(1 - r, n, w), device_id_type=MESH
@@ -724,8 +783,14 @@
         tabs[r, rows, :] = tab[rows, :]
 
     each_rows(tab.shape[0], 16, keep)
-    for k in (1, 2, 3):
-        gather.step(k)
+    bring.wait()
+    settle = pltpu.make_async_copy(p1_here, p1_out.at[n], here_s.at[1])
+    settle.start()
+    gather.step(1)
+    p1.turn()
+    gather.step(2)
+    down.turn()
+    gather.step(3)
     gather.rest()
     out = pltpu.make_async_copy(buf, rows_out, out_s.at[0])
     out.start()
@@ -733,28 +798,35 @@
     out_tab = pltpu.make_async_copy(tabs, tabs_out, out_s.at[1])
     out_tab.start()
     gather.sent()
+    p1.finish()
+    down.finish()
+    settle.wait()
     tab_copy.wait_send()
     out.wait()
     out_tab.wait()
 
 
-def enter(hidden, gain, tab):
+def enter(hidden, gain, tab, p1_own, down_own):
     shard, width = hidden.shape
     return comm_call(
         enter_kernel, "enter", 1,
         (
             jax.ShapeDtypeStruct((2, 4, shard, width), bf16),
             jax.ShapeDtypeStruct((2,) + tab.shape, f32),
+            jax.ShapeDtypeStruct((4,) + p1_own.shape, bf16),
+            jax.ShapeDtypeStruct((4, 256, 1024), bf16),
         ),
-        [vmem()] * 3, [hbm()] * 2,
+        [vmem()] * 3 + [hbm()] * 2, [hbm()] * 4,
         gather_scratch(shard, width)
         + [
             pltpu.VMEM((2,) + tab.shape, f32),
             pltpu.SemaphoreType.DMA(()),
             pltpu.SemaphoreType.DMA(()),
             pltpu.SemaphoreType.DMA((2,)),
-        ],
-        (hidden, gain, tab), flops=10**10, sent=10**8,
+        ]
+        + square_sems() * 2
+        + [pltpu.VMEM(p1_own.shape, bf16), pltpu.SemaphoreType.DMA((2,))],
+        (hidden, gain, tab, p1_own, down_own), flops=10**10, sent=10**8,
     )
 
 
@@ -763,7 +835,8 @@
 
 
 def project_kernel(
-    x, p1, tabs, grad_top, q_out, kv_out, tops_out, kv, s_s, s_g, out_s, buf, g0, g1, g2, g3, tops_s
+    x, p1, tabs, grad_top, down_own, q_out, kv_out, tops_out, down_out,
+    kv, s_s, s_g, out_s, buf, g0, g1, g2, g3, tops_s, down_s, down_g,
 ):
     r, n, w = spot()
     greet(
@@ -789,6 +862,7 @@
             device_id=nar_device(r, n, w, by), device_id_type=MESH,
         )
 
+    down = Square(down_own.at[256:512], down_out, (down_s, down_g), (r, n, w))
     lane = lax.broadcasted_iota(jnp.int32, (256, 128), 1)
     weight = p1[:, :, 0:384].reshape(2048, 384)
     for row in range(2):
@@ -817,8 +891,11 @@
             def _():
                 kv[row, slot] = jnp.zeros((512, 128), bf16)
 
-    for k in (1, 2, 3):
-        gather.step(k)
+    down.start()
+    gather.step(1)
+    gather.step(2)
+    down.turn()
+    gather.step(3)
     gather.rest()
     tops_copy = pltpu.make_async_copy(buf, tops_out, tops_s)
     tops_copy.start()
@@ -840,19 +917,21 @@
             copy(row, 0, 2).wait_send()
 
     gather.sent()
+    down.finish()
     out.wait()
     tops_copy.wait()
 
 
-def project(x, p1, tabs, grad_top):
+def project(*args):
     return comm_call(
         project_kernel, "project", 2,
         (
             jax.ShapeDtypeStruct((2, 512, 256), bf16),
             jax.ShapeDtypeStruct((2, 3, 512, 128), bf16),
             jax.ShapeDtypeStruct((2, 4, 64, 2048), bf16),
+            jax.ShapeDtypeStruct((4, 256, 1024), bf16),
         ),
-        [vmem()] * 4, [vmem(), hbm(), hbm()],
+        [vmem()] * 4 + [hbm()], [vmem(), hbm(), hbm(), hbm()],
         [
             pltpu.VMEM((2, 3, 512, 128), bf16),
             pltpu.SemaphoreType.DMA((2, 3)),
@@ -860,8 +939,9 @@
             pltpu.SemaphoreType.DMA(()),
         ]
         + gather_scratch(64, 2048)
-        + [pltpu.SemaphoreType.DMA(())],
-        (x, p1, tabs, grad_top), flops=10**10, sent=10**7,
+        + [pltpu.SemaphoreType.DMA(())]
+        + square_sems(),
+        args, flops=10**10, sent=10**7,
     )
 
 
@@ -978,12 +1058,17 @@
 
 
 def middle_kernel(
-    att, p1, hidden, gain, mid_out, ffn_out,
+    att, p1, hidden, gain, gate_own, up_own, mid_out, ffn_out, gate_out, up_out,
     theirs, mine, from_pt, from_up, from_dn, s0, s1, s2, s3, s4, s5, fbuf, h0, h1, h2, h3, out_s,
+    gate_s, gate_g, up_s, up_g,
 ):
     me = spot()
     r, n, w = me
-    greet(line_partners(r, n, w, 4))
+    greet(line_partners(r, n, w, 4) + square_partners(r, n, w))
+    gate = Square(gate_own, gate_out, (gate_s, gate_g), me)
+    up = Square(up_own, up_out, (up_s, up_g), me)
+    gate.start()
+    up.start()
     scatter = Scatter(
         mine, theirs, (from_pt, from_up, from_dn), (s0, s1, s2, s3, s4, s5), me, 4
     )
@@ -1012,6 +1097,8 @@
 
     each_rows(hidden.shape[0], 16, body)
     ffn.own()
+    gate.turn()
+    up.turn()
     for k in (1, 2, 3):
         ffn.step(k)
     ffn.rest()
@@ -1019,21 +1106,25 @@
     out_f.start()
     scatter.sent()
     ffn.sent()
+    gate.finish()
+    up.finish()
     out_f.wait()
 
 
-def middle_stage(att, p1, hidden, gain):
+def middle_stage(att, p1, hidden, gain, gate_own, up_own):
     shard, width = hidden.shape
     rows = jax.ShapeDtypeStruct((2, 4, shard, width), bf16)
     return comm_call(
         middle_kernel, "middle", 3,
-        (jax.ShapeDtypeStruct((shard, width), f32), rows),
-        [vmem()] * 4, [vmem(), hbm()],
+        (jax.ShapeDtypeStruct((shard, width), f32), rows)
+        + (jax.ShapeDtypeStruct((4, 512, 1024), bf16),) * 2,
+        [vmem()] * 4 + [hbm()] * 2, [vmem()] + [hbm()] * 3,
         [pltpu.VMEM((4, shard, width), bf16)] * 2
         + scatter_bufs(shard, width) + scatter_sems()
         + gather_scratch(shard, width)
-        + [pltpu.SemaphoreType.DMA(())],
-        (att, p1, hidden, gain), flops=10**10, sent=2 * 10**8,
+        + [pltpu.SemaphoreType.DMA(())]
+        + square_sems() * 2,
+        (att, p1, hidden, gain, gate_own, up_own), flops=10**10, sent=2 * 10**8,
     )
 
 
@@ -1084,7 +1175,7 @@
 
 
 def ffn_kernel(
-    x, tops_in, grad_top, p2_all, gain,
+    x, tops_in, grad_top, gate_own, gate_in, up_own, up_in, down_own, down_a, down_b, gain,
     part_out, sum_out, gain_out, o0, o1, o2, o3, ra_out, rb_out,
     theirs, mine, from_pt, from_up, from_dn, s0, s1, s2, s3, s4, s5,
     act, dgu, wide, out_s, give_s, give_g, keep_s, p2, in_s, n_s, n_g,
@@ -1092,10 +1183,21 @@
 ):
     me = spot()
     r, n, w = me
-    loads = [pltpu.make_async_copy(p2_all.at[:, j], p2.at[j], in_s.at[j]) for j in range(3)]
-    loads.append(pltpu.make_async_copy(tops_in, tops4.at[:, :, 0:64], tops_s))
-    for load in loads:
-        load.start()
+    loads = [
+        fetch(gate_own, gate_in, p2.at[0], in_s.at[0], n),
+        fetch(up_own, up_in, p2.at[1], in_s.at[1], n),
+        fetch(down_own.at[0:256], down_a, p2.at[2, :, 0:256], in_s.at[2], n)
+        + fetch(down_own.at[256:512], down_b, p2.at[2, :, 256:512], in_s.at[3], n),
+        [pltpu.make_async_copy(tops_in, tops4.at[:, :, 0:64], tops_s)],
+    ]
+    for group in loads:
+        for load in group:
+            load.start()
+
+    def loaded(k):
+        for load in loads[k]:
+            load.wait()
+
     greet(line_partners(r, n, w, 4) + square_partners(r, n, w))
     scatter = Scatter(
         mine, theirs, (from_pt, from_up, from_dn), (s0, s1, s2, s3, s4, s5), me, 4
@@ -1109,8 +1211,8 @@
     each_rows(64, 16, keep)
     gather.own()
     gain_out[...] = jnp.zeros_like(gain_out)
-    loads[0].wait()
-    loads[1].wait()
+    loaded(0)
+    loaded(1)
 
     def hidden_tile(i, carry):
         ft, row = i // 2, i % 2
@@ -1131,7 +1233,7 @@
     gather.step(1)
     lax.fori_loop(4, 8, hidden_tile, 0)
     gather.step(2)
-    loads[2].wait()
+    loaded(2)
 
     def down_tile(dt, carry):
         nn, half = dt // 2, dt % 2
@@ -1153,7 +1255,7 @@
         put.start()
     gather.step(3)
     gather.rest()
-    loads[3].wait()
+    loaded(3)
 
     def top_rows(row):
         return tops4[row].reshape(512, 2048)
@@ -1280,7 +1382,7 @@
         )
         + spread_shapes(3, 128, width)
         + (jax.ShapeDtypeStruct((2, 2, 128, width), bf16),) * 2,
-        [vmem(), hbm(), vmem(), hbm(), vmem()], [hbm(), vmem(), vmem()] + [hbm()] * 6,
+        [vmem(), hbm(), vmem()] + [hbm()] * 7 + [vmem()], [hbm(), vmem(), vmem()] + [hbm()] * 6,
         [pltpu.VMEM((4, shard, width), bf16)] * 2
         + scatter_bufs(shard, width) + scatter_sems()
         + [
@@ -1290,7 +1392,7 @@
             pltpu.SemaphoreType.DMA((2,)),
         ]
         + spread_sems(3)
-        + [pltpu.VMEM((3, 4, 512, 1024), bf16), pltpu.SemaphoreType.DMA((3,))]
+        + [pltpu.VMEM((3, 4, 512, 1024), bf16), pltpu.SemaphoreType.DMA((4, 4))]
         + [pltpu.SemaphoreType.DMA((2, 2))] * 2
         + gather_scratch(shard, width)
         + [pltpu.SemaphoreType.DMA(())],
@@ -1841,15 +1943,8 @@
         axis=1,
     )
     down_half = half(w_down, 0)
-    p2_shard = jnp.stack(
-        [
-            half(w_gate, 1),
-            half(w_up, 1),
-            jnp.concatenate([down_half[:512], down_half[512:]], axis=1),
-        ]
-    )
-    p1 = lax.all_gather(p1_shard, "nar", axis=0)
-    p2 = lax.all_gather(p2_shard, "nar", axis=0)
+    gate_own, up_own = half(w_gate, 1), half(w_up, 1)
+    down_own = jnp.concatenate([down_half[:512], down_half[512:]], axis=1)
 
     token_ids = n * 512 + jnp.arange(512, dtype=jnp.int32)
     doc_start, places = doc_layout(doc_lengths[0], token_ids)
@@ -1861,14 +1956,15 @@
         axis=1,
     )
 
-    rows, tabs = enter(hidden, gain_a, tab)
+    rows, tabs, p1, down_a = enter(hidden, gain_a, tab, p1_shard, down_own)
     rows3, rows2 = rows.reshape(2, 512, 2048), rows.reshape(1024, 2048)
-    q, kv, tops = project(rows3, p1, tabs, grad_top)
+    q, kv, tops, down_b = project(rows3, p1, tabs, grad_top, down_own)
     kv_flat = kv.reshape(2, 1536, 128)
     att, lse = attend(q, kv_flat, tabs)
-    mid, ffn_rows = middle_stage(att, p1, hidden, gain_f)
+    mid, ffn_rows, gate_all, up_all = middle_stage(att, p1, hidden, gain_f, gate_own, up_own)
     parts, total, gain_f_part, a_send, a_keep, b_send, b_keep, ra_dg, rb_dg = ffn_stage(
-        ffn_rows.reshape(1024, 2048), tops, grad_top, p2, gain_f
+        ffn_rows.reshape(1024, 2048), tops, grad_top,
+        gate_own, gate_all, up_own, up_all, down_own, down_a, down_b, gain_f,
     )
     gmid, datt, oa_send, oa_keep, ob_send, ob_keep, ra_u, rb_u, la_d, lb_d = branch_stage(
         total, mid, grad_top, gain_f, p1, att.reshape(1024, 256),

time: 495 us -> 489 us (0.988)
  between operations: 14.4 us -> 0.92 us
  Pallas kernels: 446 us -> 452 us
    pallas_call x7, Pallas kernels: 432 us -> 437 us  [comm_call(): pl.pallas_call(kernel, out_shape=out_shape, in_specs=in_specs, out_specs=...]
    unnamed x51 -> x49, local copies, waits for them, and re-layouts: 12.2 us -> 10.1 us
  transfers between devices with their start and end apart: 2 -> 0, of which waited for: 0 -> 0; matrix products, arithmetic and copies ran while one was open for 1% -> 0% of each run, Pallas kernels for 36% -> 0%
where the time goes in v8:
time: 489 us; the launch traced here: 485 us
  Pallas kernels  452 us (92%)
  local copies, waits for them, and re-layouts  16.8 us (3%)
  other arithmetic  15.8 us (3%)
    pallas_call x7, Pallas kernels, comm_call(): pl.pallas_call(kernel, out_shape=out_shape, in_specs=in_specs, out_specs=...  437 us
    pallas_call x1, Pallas kernels, attend(): pl.pallas_call(attend_kernel, out_shape=(jax.ShapeDtypeStruct((2, 512, 25...  14.2 us
    unnamed x49, local copies, waits for them, and re-layouts  10.1 us

profile of v8, /device:TPU:0, one launch (start us, length us, event | category | flops | bytes accessed | tf_op | source)
XLA Modules:
  0.0 485.1 jit_solution(17817232235511222364)
XLA Ops:
  0.6 0.0 copy-start
  0.7 0.0 copy-start.20
  0.7 0.9 reduce-window.4
  1.6 0.7 fusion.1
  2.2 0.1 select_reduce_fusion
  2.3 0.1 broadcast_in_dim.22
  2.5 1.1 constant_dynamic-slice_fusion.4
  3.6 1.0 constant_dynamic-slice_fusion
  4.6 0.0 copy-done
  4.6 1.0 maximum_maximum_fusion.p1_own
  5.7 0.0 copy-done.20
  5.7 1.0 multiply_sine_fusion
  6.7 1.5 concatenate.24.tab
  8.1 0.0 copy-done.15
  8.1 0.1 constant_dynamic-slice_fusion.7
  8.2 1.1 pad_maximum_fusion.2.down_own
  9.3 0.8 copy-done.6
  10.1 0.6 copy-done.7
  10.7 1.5 constant_dynamic-slice_fusion.1
  12.3 46.3 %enter.1 = (bf16[2,4,128,2048]{3,2,1,0:T(8,128)(2,1)}, f32[2,512,384]{2,1,0:T(8,128)}, bf16[4,512,640]{2,1,0:T(8,128)(2,1)}, bf16[4,256,1024]{2,1,0:T(8,128)(2,1)}) custom-call(bf16[128,2048]{1,0:T(8,128)(2,1)} %bitcast.65, f32[1,2048]{1,0:T(1,128)} %bitcast.71, f32[512,384]{1,0:T(8,128)} %concatenate.24.tab, bf16[512,640]{1,0:T(8,128)(2,1)} %maximum_maximum_fusion.p1_own, ...), custom_call_target="tpu_custom_call" | custom-call | flops 10000000000 | bytes 100000000 | tf_op jit(solution)/shard_map/enter/pallas_call | solution.py:732
  58.5 37.3 %project.1 = (bf16[2,512,256]{2,1,0:T(8,128)(2,1)}, bf16[2,3,512,128]{3,2,1,0:T(8,128)(2,1)}, bf16[2,4,64,2048]{3,2,1,0:T(8,128)(2,1)}, bf16[4,256,1024]{2,1,0:T(8,128)(2,1)}) custom-call(bf16[2,512,2048]{2,1,0:T(8,128)(2,1)} %bitcast.75, bf16[4,512,640]{2,1,0:T(8,128)(2,1)} %get-tuple-element.62.p1, f32[2,512,384]{2,1,0:T(8,128)} %get-tuple-element.63.tabs.starts, ...), custom_call_target="tpu_custom_call" | custom-call | flops 10000000000 | bytes 10000000 | tf_op jit(solution)/shard_map/project/pallas_call | solution.py:732
  95.9 14.2 %attend.1 = (bf16[2,512,256]{2,1,0:T(8,128)(2,1)}, f32[2,4,512,128]{3,2,1,0:T(8,128)}) custom-call(bf16[2,512,256]{2,1,0:T(8,128)(2,1)} %get-tuple-element.64.q, bf16[2,1536,128]{2,1,0:T(8,128)(2,1)} %bitcast.78, f32[2,512,384]{2,1,0:T(8,128)} %get-tuple-element.63.tabs.starts), custom_call_target="tpu_custom_call" | custom-call | flops 20000000000 | bytes 10000000 | tf_op jit(solution)/shard_map/attend/pallas_call | solution.py:1036
  110.1 86.4 %middle.1 = (f32[128,2048]{1,0:T(8,128)}, bf16[2,4,128,2048]{3,2,1,0:T(8,128)(2,1)}, bf16[4,512,1024]{2,1,0:T(8,128)(2,1)}, bf16[4,512,1024]{2,1,0:T(8,128)(2,1)}) custom-call(bf16[2,512,256]{2,1,0:T(8,128)(2,1)} %get-tuple-element.66.att, bf16[4,512,640]{2,1,0:T(8,128)(2,1)} %get-tuple-element.62.p1, bf16[128,2048]{1,0:T(8,128)(2,1)} %bitcast.66, ...), custom_call_target="tpu_custom_call" | custom-call | flops 10000000000 | bytes 200000000 | tf_op jit(solution)/shard_map/middle/pallas_call | solution.py:732
  196.6 94.7 %ffn.1 = (bf16[2,4,128,2048]{3,2,1,0:T(8,128)(2,1)}, f32[128,2048]{1,0:T(8,128)}, f32[8,2048]{1,0:T(8,128)}, bf16[2,3,128,2048]{3,2,1,0:T(8,128)(2,1)}, bf16[2,3...) custom-call(bf16[1024,2048]{1,0:T(8,128)(2,1)} %bitcast.77, ...), custom_call_target="tpu_custom_call" | custom-call | flops 40000000000 | bytes 100000000 | tf_op jit(solution)/shard_map/ffn/pallas_call | solution.py:732
  291.3 53.5 %branch.1 = (f32[128,2048]{1,0:T(8,128)}, bf16[2,512,256]{2,1,0:T(8,128)(2,1)}, bf16[2,128,512]{2,1,0:T(8,128)(2,1)}, bf16[2,128,512]{2,1,0:T(8,128)(2,1)}, bf16...) custom-call(f32[128,2048]{1,0:T(8,128)} %get-tuple-element.73.total,, ...), custom_call_target="tpu_custom_call" | custom-call | flops 10000000000 | bytes 100000000 | tf_op jit(solution)/shard_map/branch/pallas_call | solution.py:732
  344.8 0.0 copy-start.9
  344.8 54.0 %unproject.1 = (bf16[2,4,128,2048]{3,2,1,0:T(8,128)(2,1)}, f32[8,2048]{1,0:T(8,128)}, bf16[2,128,768]{2,1,0:T(8,128)(2,1)}, bf16[2,128,768]{2,1,0:T(8,128)(2,1)}...) custom-call(bf16[2,512,256]{2,1,0:T(8,128)(2,1)} %get-tuple-element., ...), custom_call_target="tpu_custom_call" | custom-call | flops 10000000000 | bytes 10000000 | tf_op jit(solution)/shard_map/unproject/pallas_call | solution.py:732
  398.8 0.0 copy-done.9
  398.8 0.0 copy-start.4
  398.8 0.0 copy-start.5
  398.8 0.0 copy-start.8
  398.8 0.0 copy-start.16
  398.9 0.0 copy-start.17
  398.9 3.9 bitcast_add_fusion
  402.8 0.0 copy-done.4
  402.8 0.0 copy-done.5
  402.8 0.0 copy-done.8
  402.8 0.3 copy-done.16
  403.1 0.5 copy-done.17
  403.6 2.1 bitcast_add_fusion.1
  405.6 0.1 maximum_bitcast_fusion
  405.8 0.0 copy-start.19
  405.8 0.0 copy-start.18
  405.8 1.8 copy.30
  407.6 0.0 copy-done.19
  407.6 0.0 copy-done.18
  407.7 0.6 pad_maximum_fusion.3.gains
  408.3 65.1 %leave.1 = (bf16[128,2048]{1,0:T(8,128)(2,1)}, f32[8,256]{1,0:T(8,128)}, f32[256,512]{1,0:T(8,128)}, f32[256,512]{1,0:T(8,128)}, f32[256,512]{1,0:T(8,128)}, /*index=5*/f32[256,512]{1,0:T(8,128)}) custom-call(bf16[2,4,128,2048]{3,2,1,0:T(8,128)(2,1)} %get-tuple-element.89.parts, bf16[128,2048]{1,0:T(8,128)(2,1)} %bitcast.67, f32[1,2048]{1,0:T(1,128)} %bitcast.73, ...), custom_call_target="tpu_custom_call" | custom-call | flops 10000000000 | bytes 100000000 | tf_op jit(solution)/shard_map/leave/pallas_call | solution.py:732
  473.4 1.3 fusion.2
  474.8 2.0 copy.29
  476.8 0.0 copy-done.2
  476.8 2.8 pad_maximum_fusion
  479.6 0.0 copy-done.3
  479.6 1.5 pad_maximum_fusion.1
  481.1 0.0 copy-done.10
  481.1 0.0 copy-start.1
  481.1 0.8 copy.36
  481.9 0.0 copy-done.14
  481.9 0.8 copy.37
  482.7 0.0 copy-done.13
  482.7 0.8 copy.38
  483.5 0.0 copy-done.12
  483.5 0.8 copy.39
  484.3 0.8 copy.40
  (19 shorter events, 0.1 us)
Async XLA Ops:
  0.6 3.9 copy-start
  0.7 5.0 %copy-start.20 = (f32[32]{0:T(128)S(1)}, f32[32]{0:T(128)}, u32[]{:S(2)}) copy-start(f32[32]{0:T(128)} %constant.36.clone) | copy-start | bytes 388
  5.7 2.5 copy-start.15
  8.1 2.0 copy-start.6
  8.1 2.6 copy-start.7
  344.8 54.0 %copy-start.9 = (bf16[2,2,128,2048]{3,2,1,0:T(8,128)(2,1)S(1)}, bf16[2,2,128,2048]{3,2,1,0:T(8,128)(2,1)}, u32[]{:S(2)}) copy-start(bf16[2,2,128,2048]{3,2,1,0:T(8,128)(2,1)} %get-tuple-element.80.b_came.b_gate) | copy-start | bytes 6291460
  398.8 4.0 copy-start.4
  398.8 4.0 copy-start.5
  398.8 4.0 copy-start.8
  398.8 4.2 copy-start.16
  398.9 4.7 copy-start.17
  405.8 1.8 copy-start.19
  405.8 1.9 copy-start.18
  408.3 68.5 %copy-start.2 = (f32[128,2048]{1,0:T(8,128)S(1)}, f32[128,2048]{1,0:T(8,128)}, u32[]{:S(2)}) copy-start(f32[128,2048]{1,0:T(8,128)} %get-tuple-element.147) | copy-start | bytes 3145732
  476.8 2.8 copy-start.3
  479.6 1.5 copy-start.10
  479.6 2.3 copy-start.14
  481.1 1.6 copy-start.13
  481.1 2.4 copy-start.12
  481.1 3.2 copy-start.11
  481.1 4.0 copy-start.1

commit v9 on v8

--- a/solution.py
+++ b/solution.py
@@ -835,8 +835,7 @@
 
 
 def project_kernel(
-    x, p1, tabs, grad_top, down_own, q_out, kv_out, tops_out, down_out,
-    kv, s_s, s_g, out_s, buf, g0, g1, g2, g3, tops_s, down_s, down_g,
+    x, p1, tabs, grad_top, q_out, kv_out, tops_out, kv, s_s, s_g, out_s, buf, g0, g1, g2, g3, tops_s
 ):
     r, n, w = spot()
     greet(
@@ -862,7 +861,6 @@
             device_id=nar_device(r, n, w, by), device_id_type=MESH,
         )
 
-    down = Square(down_own.at[256:512], down_out, (down_s, down_g), (r, n, w))
     lane = lax.broadcasted_iota(jnp.int32, (256, 128), 1)
     weight = p1[:, :, 0:384].reshape(2048, 384)
     for row in range(2):
@@ -891,11 +889,8 @@
             def _():
                 kv[row, slot] = jnp.zeros((512, 128), bf16)
 
-    down.start()
-    gather.step(1)
-    gather.step(2)
-    down.turn()
-    gather.step(3)
+    for k in (1, 2, 3):
+        gather.step(k)
     gather.rest()
     tops_copy = pltpu.make_async_copy(buf, tops_out, tops_s)
     tops_copy.start()
@@ -917,21 +912,19 @@
             copy(row, 0, 2).wait_send()
 
     gather.sent()
-    down.finish()
     out.wait()
     tops_copy.wait()
 
 
-def project(*args):
+def project(x, p1, tabs, grad_top):
     return comm_call(
         project_kernel, "project", 2,
         (
             jax.ShapeDtypeStruct((2, 512, 256), bf16),
             jax.ShapeDtypeStruct((2, 3, 512, 128), bf16),
             jax.ShapeDtypeStruct((2, 4, 64, 2048), bf16),
-            jax.ShapeDtypeStruct((4, 256, 1024), bf16),
         ),
-        [vmem()] * 4 + [hbm()], [vmem(), hbm(), hbm(), hbm()],
+        [vmem()] * 4, [vmem(), hbm(), hbm()],
         [
             pltpu.VMEM((2, 3, 512, 128), bf16),
             pltpu.SemaphoreType.DMA((2, 3)),
@@ -939,9 +932,8 @@
             pltpu.SemaphoreType.DMA(()),
         ]
         + gather_scratch(64, 2048)
-        + [pltpu.SemaphoreType.DMA(())]
-        + square_sems(),
-        args, flops=10**10, sent=10**7,
+        + [pltpu.SemaphoreType.DMA(())],
+        (x, p1, tabs, grad_top), flops=10**10, sent=10**7,
     )
 
 
@@ -992,17 +984,15 @@
     return jnp.concatenate([ok] * 4, axis=0)
 
 
-def attend_kernel(q, kv, starts, out, lse):
-    block = pl.program_id(1)
-    first_query = 1024 + block * QUERIES
-    query = stack_low(q[0].astype(f32)).astype(bf16)
+def attend_block(q, kv, starts, first_query):
+    query = stack_low(q.astype(f32)).astype(bf16)
 
     def body(step, carry):
-        tile = block // 2 + step
+        tile = (first_query - 1024) // KEYS + step
         top, total, acc = carry
-        both = kv[0, pl.ds(pl.multiple_of(tile * KEYS, KEYS), KEYS), :]
+        both = kv[pl.ds(pl.multiple_of(tile * KEYS, KEYS), KEYS), :]
         scores = contract_last(query, both) * 0.125
-        ok = allowed_tile(starts[0], tile, first_query)
+        ok = allowed_tile(starts, tile, first_query)
         scores = jnp.where(ok, scores, masked_score)
         new_top = jnp.maximum(top, jnp.max(scores, axis=1, keepdims=True))
         shrink = jnp.exp(top - new_top)
@@ -1020,37 +1010,8 @@
         ),
         unroll=True,
     )
-    out[0] = unstack(acc / total, False).astype(bf16)
-    lse[0, 0] = jnp.broadcast_to(top + jnp.log(total), (4 * QUERIES, 128))
-
-
-def attend_specs():
-    return [
-        pl.BlockSpec((1, QUERIES, 256), lambda i, j: (i, j, 0)),
-        pl.BlockSpec((1, 1536, 128), lambda i, j: (i, 0, 0)),
-        pl.BlockSpec((1, QUERIES, 128), lambda i, j: (i, j, 2)),
-    ]
-
-
-def attend(q, kv, tabs):
-    return pl.pallas_call(
-        attend_kernel,
-        out_shape=(
-            jax.ShapeDtypeStruct((2, 512, 256), bf16),
-            jax.ShapeDtypeStruct((2, 4, 4 * QUERIES, 128), f32),
-        ),
-        grid_spec=pl.GridSpec(
-            grid=(2, 4),
-            in_specs=attend_specs(),
-            out_specs=[
-                pl.BlockSpec((1, QUERIES, 256), lambda i, j: (i, j, 0)),
-                pl.BlockSpec((1, 1, 4 * QUERIES, 128), lambda i, j: (i, j, 0, 0)),
-            ],
-        ),
-        compiler_params=pltpu.CompilerParams(vmem_limit_bytes=VMEM_LIMIT),
-        cost_estimate=pl.CostEstimate(flops=2 * 10**10, bytes_accessed=10**7, transcendentals=10**7),
-        name="attend",
-    )(q, kv, tabs)
+    logsum = jnp.broadcast_to(top + jnp.log(total), (4 * QUERIES, 128))
+    return unstack(acc / total, False).astype(bf16), logsum
 
 
 def out_block(p1, nn, half):
@@ -1058,9 +1019,10 @@
 
 
 def middle_kernel(
-    att, p1, hidden, gain, gate_own, up_own, mid_out, ffn_out, gate_out, up_out,
+    q, kv, tabs, p1, hidden, gain, gate_own, up_own, down_own,
+    att, lse, mid_out, ffn_out, gate_out, up_out, down_out,
     theirs, mine, from_pt, from_up, from_dn, s0, s1, s2, s3, s4, s5, fbuf, h0, h1, h2, h3, out_s,
-    gate_s, gate_g, up_s, up_g,
+    gate_s, gate_g, up_s, up_g, down_s, down_g,
 ):
     me = spot()
     r, n, w = me
@@ -1069,6 +1031,8 @@
     up = Square(up_own, up_out, (up_s, up_g), me)
     gate.start()
     up.start()
+    down = Square(down_own.at[256:512], down_out, (down_s, down_g), me)
+    down.start()
     scatter = Scatter(
         mine, theirs, (from_pt, from_up, from_dn), (s0, s1, s2, s3, s4, s5), me, 4
     )
@@ -1076,6 +1040,15 @@
     def shard(i, carry):
         s = scatter.order(i)
         rows = pl.ds(pl.multiple_of(s * 128, 128), 128)
+        for row in range(2):
+            att[row, rows, :], lse[row, s] = attend_block(
+                q[row, rows, :], kv.at[row], tabs[row, rows, 256:384], 1024 + s * 128
+            )
+
+        @pl.when((i >= 1) & ((w == 0) | (w == 3)))
+        def _():
+            scatter.step(scatter.order(i - 1))
+
         left = jnp.concatenate([att[1 - r, rows, :], att[r, rows, :]], axis=0)
         for nn in range(4):
             for half in range(2):
@@ -1087,7 +1060,7 @@
         return carry
 
     lax.fori_loop(0, 4, shard, 0)
-    scatter.advance((0, 1, 2, 3), (0, 1, 2, 3))
+    scatter.advance((3,), (0, 1, 2, 3))
     scatter.total(mid_out)
 
     def body(rows):
@@ -1099,8 +1072,10 @@
     ffn.own()
     gate.turn()
     up.turn()
-    for k in (1, 2, 3):
-        ffn.step(k)
+    ffn.step(1)
+    down.turn()
+    ffn.step(2)
+    ffn.step(3)
     ffn.rest()
     out_f = pltpu.make_async_copy(fbuf, ffn_out, out_s)
     out_f.start()
@@ -1108,23 +1083,30 @@
     ffn.sent()
     gate.finish()
     up.finish()
+    down.finish()
     out_f.wait()
 
 
-def middle_stage(att, p1, hidden, gain, gate_own, up_own):
+def middle_stage(q, kv, tabs, p1, hidden, gain, *weights):
     shard, width = hidden.shape
     rows = jax.ShapeDtypeStruct((2, 4, shard, width), bf16)
     return comm_call(
         middle_kernel, "middle", 3,
-        (jax.ShapeDtypeStruct((shard, width), f32), rows)
-        + (jax.ShapeDtypeStruct((4, 512, 1024), bf16),) * 2,
-        [vmem()] * 4 + [hbm()] * 2, [vmem()] + [hbm()] * 3,
+        (
+            jax.ShapeDtypeStruct((2, 512, 256), bf16),
+            jax.ShapeDtypeStruct((2, 4, 4 * QUERIES, 128), f32),
+            jax.ShapeDtypeStruct((shard, width), f32),
+            rows,
+        )
+        + (jax.ShapeDtypeStruct((4, 512, 1024), bf16),) * 2
+        + (jax.ShapeDtypeStruct((4, 256, 1024), bf16),),
+        [vmem()] * 6 + [hbm()] * 3, [vmem()] * 3 + [hbm()] * 4,
         [pltpu.VMEM((4, shard, width), bf16)] * 2
         + scatter_bufs(shard, width) + scatter_sems()
         + gather_scratch(shard, width)
         + [pltpu.SemaphoreType.DMA(())]
-        + square_sems() * 2,
-        (att, p1, hidden, gain, gate_own, up_own), flops=10**10, sent=2 * 10**8,
+        + square_sems() * 3,
+        (q, kv, tabs, p1, hidden, gain, *weights), flops=10**10, sent=2 * 10**8,
     )
 
 
@@ -1958,10 +1940,11 @@
 
     rows, tabs, p1, down_a = enter(hidden, gain_a, tab, p1_shard, down_own)
     rows3, rows2 = rows.reshape(2, 512, 2048), rows.reshape(1024, 2048)
-    q, kv, tops, down_b = project(rows3, p1, tabs, grad_top, down_own)
+    q, kv, tops = project(rows3, p1, tabs, grad_top)
     kv_flat = kv.reshape(2, 1536, 128)
-    att, lse = attend(q, kv_flat, tabs)
-    mid, ffn_rows, gate_all, up_all = middle_stage(att, p1, hidden, gain_f, gate_own, up_own)
+    att, lse, mid, ffn_rows, gate_all, up_all, down_b = middle_stage(
+        q, kv_flat, tabs, p1, hidden, gain_f, gate_own, up_own, down_own
+    )
     parts, total, gain_f_part, a_send, a_keep, b_send, b_keep, ra_dg, rb_dg = ffn_stage(
         ffn_rows.reshape(1024, 2048), tops, grad_top,
         gate_own, gate_all, up_own, up_all, down_own, down_a, down_b, gain_f,

time: 489 us -> 474 us (0.969)
  Pallas kernels: 452 us -> 437 us
    pallas_call x1 -> x0, Pallas kernels: 14.2 us -> none  [attend(): pl.pallas_call(attend_kernel, out_shape=(jax.ShapeDtypeStruct((2, 512, 25...]
where the time goes in v9:
time: 474 us; the launch traced here: 471 us
  Pallas kernels  437 us (92%)
  local copies, waits for them, and re-layouts  16.7 us (4%)
  other arithmetic  15.8 us (3%)
    pallas_call x7, Pallas kernels, comm_call(): pl.pallas_call(kernel, out_shape=out_shape, in_specs=in_specs, out_specs=...  437 us
    unnamed x49, local copies, waits for them, and re-layouts  10.1 us

profile of v9, /device:TPU:0, one launch (start us, length us, event | category | flops | bytes accessed | tf_op | source)
XLA Modules:
  0.0 470.8 jit_solution(15091215423089265953)
XLA Ops:
  0.6 0.0 copy-start
  0.7 0.0 copy-start.20
  0.7 0.9 reduce-window.4
  1.6 0.7 fusion.1
  2.2 0.1 select_reduce_fusion
  2.3 0.1 broadcast_in_dim.22
  2.5 1.1 constant_dynamic-slice_fusion.4
  3.6 1.0 constant_dynamic-slice_fusion
  4.6 0.0 copy-done
  4.6 1.0 maximum_maximum_fusion.p1_own
  5.6 0.0 copy-done.20
  5.6 1.0 multiply_sine_fusion
  6.6 1.5 concatenate.24.tab
  8.1 0.0 copy-done.15
  8.1 0.1 constant_dynamic-slice_fusion.7
  8.2 1.1 pad_maximum_fusion.2.down_own
  9.3 0.8 copy-done.6
  10.1 0.6 copy-done.7
  10.7 1.5 constant_dynamic-slice_fusion.1
  12.2 46.3 %enter.1 = (bf16[2,4,128,2048]{3,2,1,0:T(8,128)(2,1)}, f32[2,512,384]{2,1,0:T(8,128)}, bf16[4,512,640]{2,1,0:T(8,128)(2,1)}, bf16[4,256,1024]{2,1,0:T(8,128)(2,1)}) custom-call(bf16[128,2048]{1,0:T(8,128)(2,1)} %bitcast.65, f32[1,2048]{1,0:T(1,128)} %bitcast.71, f32[512,384]{1,0:T(8,128)} %concatenate.24.tab, bf16[512,640]{1,0:T(8,128)(2,1)} %maximum_maximum_fusion.p1_own, ...), custom_call_target="tpu_custom_call" | custom-call | flops 10000000000 | bytes 100000000 | tf_op jit(solution)/shard_map/enter/pallas_call | solution.py:732
  58.5 29.9 %project.1 = (bf16[2,512,256]{2,1,0:T(8,128)(2,1)}, bf16[2,3,512,128]{3,2,1,0:T(8,128)(2,1)}, bf16[2,4,64,2048]{3,2,1,0:T(8,128)(2,1)}) custom-call(bf16[2,512,2048]{2,1,0:T(8,128)(2,1)} %bitcast.75, bf16[4,512,640]{2,1,0:T(8,128)(2,1)} %get-tuple-element.62.p1, f32[2,512,384]{2,1,0:T(8,128)} %get-tuple-element.63.tabs, bf16[128,2048]{1,0:T(8,128)(2,1)} %bitcast.62), custom_call_target="tpu_custom_call" | custom-call | flops 10000000000 | bytes 10000000 | tf_op jit(solution)/shard_map/project/pallas_call | solution.py:732
  88.4 96.2 %middle.1 = (bf16[2,512,256]{2,1,0:T(8,128)(2,1)}, f32[2,4,512,128]{3,2,1,0:T(8,128)}, f32[128,2048]{1,0:T(8,128)}, bf16[2,4,128,2048]{3,2,1,0:T(8,128)(2,1)}, b...) custom-call(bf16[2,512,256]{2,1,0:T(8,128)(2,1)} %get-tuple-element.64.q, ...), custom_call_target="tpu_custom_call" | custom-call | flops 10000000000 | bytes 200000000 | tf_op jit(solution)/shard_map/middle/pallas_call | solution.py:732
  184.7 92.3 %ffn.1 = (bf16[2,4,128,2048]{3,2,1,0:T(8,128)(2,1)}, f32[128,2048]{1,0:T(8,128)}, f32[8,2048]{1,0:T(8,128)}, bf16[2,3,128,2048]{3,2,1,0:T(8,128)(2,1)}, bf16[2,3...) custom-call(bf16[1024,2048]{1,0:T(8,128)(2,1)} %bitcast.77, ...), custom_call_target="tpu_custom_call" | custom-call | flops 40000000000 | bytes 100000000 | tf_op jit(solution)/shard_map/ffn/pallas_call | solution.py:732
  276.9 54.9 %branch.1 = (f32[128,2048]{1,0:T(8,128)}, bf16[2,512,256]{2,1,0:T(8,128)(2,1)}, bf16[2,128,512]{2,1,0:T(8,128)(2,1)}, bf16[2,128,512]{2,1,0:T(8,128)(2,1)}, bf16...) custom-call(f32[128,2048]{1,0:T(8,128)} %get-tuple-element.73.total,, ...), custom_call_target="tpu_custom_call" | custom-call | flops 10000000000 | bytes 100000000 | tf_op jit(solution)/shard_map/branch/pallas_call | solution.py:732
  331.9 0.0 copy-start.9
  331.9 54.6 %unproject.1 = (bf16[2,4,128,2048]{3,2,1,0:T(8,128)(2,1)}, f32[8,2048]{1,0:T(8,128)}, bf16[2,128,768]{2,1,0:T(8,128)(2,1)}, bf16[2,128,768]{2,1,0:T(8,128)(2,1)}...) custom-call(bf16[2,512,256]{2,1,0:T(8,128)(2,1)} %get-tuple-element., ...), custom_call_target="tpu_custom_call" | custom-call | flops 10000000000 | bytes 10000000 | tf_op jit(solution)/shard_map/unproject/pallas_call | solution.py:732
  386.5 0.0 copy-done.9
  386.5 0.0 copy-start.4
  386.5 0.0 copy-start.5
  386.5 0.0 copy-start.8
  386.5 0.0 copy-start.16
  386.5 0.0 copy-start.17
  386.5 3.9 bitcast_add_fusion
  390.5 0.0 copy-done.4
  390.5 0.0 copy-done.5
  390.5 0.0 copy-done.8
  390.5 0.3 copy-done.16
  390.8 0.5 copy-done.17
  391.2 2.1 bitcast_add_fusion.1
  393.3 0.1 maximum_bitcast_fusion
  393.5 0.0 copy-start.19
  393.5 0.0 copy-start.18
  393.5 1.8 copy.30
  395.3 0.0 copy-done.19
  395.3 0.0 copy-done.18
  395.4 0.6 pad_maximum_fusion.3.gains
  396.0 63.2 %leave.1 = (bf16[128,2048]{1,0:T(8,128)(2,1)}, f32[8,256]{1,0:T(8,128)}, f32[256,512]{1,0:T(8,128)}, f32[256,512]{1,0:T(8,128)}, f32[256,512]{1,0:T(8,128)}, /*index=5*/f32[256,512]{1,0:T(8,128)}) custom-call(bf16[2,4,128,2048]{3,2,1,0:T(8,128)(2,1)} %get-tuple-element.89.parts, bf16[128,2048]{1,0:T(8,128)(2,1)} %bitcast.67, f32[1,2048]{1,0:T(1,128)} %bitcast.73, ...), custom_call_target="tpu_custom_call" | custom-call | flops 10000000000 | bytes 100000000 | tf_op jit(solution)/shard_map/leave/pallas_call | solution.py:732
  459.2 1.3 fusion.2
  460.5 2.0 copy.29
  462.5 0.0 copy-done.2
  462.5 2.8 pad_maximum_fusion
  465.3 0.0 copy-done.3
  465.3 1.5 pad_maximum_fusion.1
  466.8 0.0 copy-done.10
  466.8 0.0 copy-start.1
  466.8 0.8 copy.36
  467.6 0.0 copy-done.14
  467.6 0.8 copy.37
  468.4 0.0 copy-done.13
  468.4 0.8 copy.38
  469.2 0.0 copy-done.12
  469.2 0.8 copy.39
  470.0 0.0 copy-done.11
  470.0 0.8 copy.40
  (18 shorter events, 0.1 us)
Async XLA Ops:
  0.6 3.9 copy-start
  0.7 5.0 %copy-start.20 = (f32[32]{0:T(128)S(1)}, f32[32]{0:T(128)}, u32[]{:S(2)}) copy-start(f32[32]{0:T(128)} %constant.36.clone) | copy-start | bytes 388
  5.6 2.5 copy-start.15
  8.1 2.0 copy-start.6
  8.1 2.6 copy-start.7
  331.9 54.6 %copy-start.9 = (bf16[2,2,128,2048]{3,2,1,0:T(8,128)(2,1)S(1)}, bf16[2,2,128,2048]{3,2,1,0:T(8,128)(2,1)}, u32[]{:S(2)}) copy-start(bf16[2,2,128,2048]{3,2,1,0:T(8,128)(2,1)} %get-tuple-element.80.b_came.b_gate) | copy-start | bytes 6291460
  386.5 4.0 copy-start.4
  386.5 4.0 copy-start.5
  386.5 4.0 copy-start.8
  386.5 4.2 copy-start.16
  386.5 4.7 copy-start.17
  393.5 1.8 copy-start.19
  393.5 1.9 copy-start.18
  396.0 66.5 %copy-start.2 = (f32[128,2048]{1,0:T(8,128)S(1)}, f32[128,2048]{1,0:T(8,128)}, u32[]{:S(2)}) copy-start(f32[128,2048]{1,0:T(8,128)} %get-tuple-element.147) | copy-start | bytes 3145732
  462.5 2.8 copy-start.3
  465.3 1.5 copy-start.10
  465.3 2.3 copy-start.14
  466.8 1.6 copy-start.13
  466.8 2.4 copy-start.12
  466.8 3.2 copy-start.11
  466.8 4.0 copy-start.1

commit v10 on v9

--- a/solution.py
+++ b/solution.py
@@ -754,90 +754,20 @@
     return x * cosine + swapped * sine
 
 
+def nar_device(r, n, w, by):
+    return (r, jnp.clip(n + by, 0, 3), w)
+
+
 def enter_kernel(
-    hidden, gain, tab, p1_own, down_own, rows_out, tabs_out, p1_out, down_out,
-    buf, up_s, dn_s, pt_s, got, tabs, tab_s, tab_g, out_s, p1_s, p1_g, down_s, down_g, p1_here, here_s,
+    hidden, gain, tab, grad_top, p1_own, down_own,
+    q_out, rows_out, tabs_out, p1_out, down_out, kv_out, tops_out,
+    buf, up_s, dn_s, pt_s, got, tbuf, h0, h1, h2, h3, tabs, p1, kv,
+    tab_s, tab_g, out_s, p1_s, p1_g, down_s, down_g, s_s, s_g,
 ):
     me = spot()
     r, n, w = me
-    bring = pltpu.make_async_copy(p1_own, p1_here, here_s.at[0])
+    bring = pltpu.make_async_copy(p1_own, p1.at[n], out_s.at[0])
     bring.start()
-    greet(line_partners(r, n, w, 4) + square_partners(r, n, w))
-    p1 = Square(p1_own, p1_out, (p1_s, p1_g), me)
-    down = Square(down_own.at[0:256], down_out, (down_s, down_g), me)
-    p1.start()
-    down.start()
-    gather = Gather(buf, (up_s, dn_s, pt_s, got), me, 4)
-    tab_copy = pltpu.make_async_remote_copy(
-        tab, tabs.at[r], tab_s, tab_g, device_id=(1 - r, n, w), device_id_type=MESH
-    )
-
-    def body(rows):
-        buf[r, w, rows, :] = norm_rows(hidden[rows, :].astype(f32), gain[...]).astype(bf16)
-
-    each_rows(hidden.shape[0], 16, body)
-    gather.own()
-    tab_copy.start()
-
-    def keep(rows):
-        tabs[r, rows, :] = tab[rows, :]
-
-    each_rows(tab.shape[0], 16, keep)
-    bring.wait()
-    settle = pltpu.make_async_copy(p1_here, p1_out.at[n], here_s.at[1])
-    settle.start()
-    gather.step(1)
-    p1.turn()
-    gather.step(2)
-    down.turn()
-    gather.step(3)
-    gather.rest()
-    out = pltpu.make_async_copy(buf, rows_out, out_s.at[0])
-    out.start()
-    tab_copy.wait_recv()
-    out_tab = pltpu.make_async_copy(tabs, tabs_out, out_s.at[1])
-    out_tab.start()
-    gather.sent()
-    p1.finish()
-    down.finish()
-    settle.wait()
-    tab_copy.wait_send()
-    out.wait()
-    out_tab.wait()
-
-
-def enter(hidden, gain, tab, p1_own, down_own):
-    shard, width = hidden.shape
-    return comm_call(
-        enter_kernel, "enter", 1,
-        (
-            jax.ShapeDtypeStruct((2, 4, shard, width), bf16),
-            jax.ShapeDtypeStruct((2,) + tab.shape, f32),
-            jax.ShapeDtypeStruct((4,) + p1_own.shape, bf16),
-            jax.ShapeDtypeStruct((4, 256, 1024), bf16),
-        ),
-        [vmem()] * 3 + [hbm()] * 2, [hbm()] * 4,
-        gather_scratch(shard, width)
-        + [
-            pltpu.VMEM((2,) + tab.shape, f32),
-            pltpu.SemaphoreType.DMA(()),
-            pltpu.SemaphoreType.DMA(()),
-            pltpu.SemaphoreType.DMA((2,)),
-        ]
-        + square_sems() * 2
-        + [pltpu.VMEM(p1_own.shape, bf16), pltpu.SemaphoreType.DMA((2,))],
-        (hidden, gain, tab, p1_own, down_own), flops=10**10, sent=10**8,
-    )
-
-
-def nar_device(r, n, w, by):
-    return (r, jnp.clip(n + by, 0, 3), w)
-
-
-def project_kernel(
-    x, p1, tabs, grad_top, q_out, kv_out, tops_out, kv, s_s, s_g, out_s, buf, g0, g1, g2, g3, tops_s
-):
-    r, n, w = spot()
     greet(
         line_partners(r, n, w, 4)
         + [
@@ -847,13 +777,50 @@
             (n <= 1, nar_device(r, n, w, 2)),
         ]
     )
-    gather = Gather(buf, (g0, g1, g2, g3), (r, n, w), 4)
+    p1_square = Square(p1_own, p1, (p1_s, p1_g), me)
+    down = Square(down_own.at[0:256], down_out, (down_s, down_g), me)
+    p1_square.start()
+    down.start()
+    gather = Gather(buf, (up_s, dn_s, pt_s, got), me, 4)
+    tops = Gather(tbuf, (h0, h1, h2, h3), me, 4)
+    tab_copy = pltpu.make_async_remote_copy(
+        tab, tabs.at[r], tab_s, tab_g, device_id=(1 - r, n, w), device_id_type=MESH
+    )
+
+    def body(rows):
+        buf[r, w, rows, :] = norm_rows(hidden[rows, :].astype(f32), gain[...]).astype(bf16)
+
+    each_rows(hidden.shape[0], 16, body)
+    gather.own()
+    tab_copy.start()
 
     def keep(rows):
-        buf[r, w, rows, :] = grad_top[rows, :]
-
-    each_rows(64, 16, keep)
-    gather.own()
+        tabs[r, rows, :] = tab[rows, :]
+
+    each_rows(tab.shape[0], 16, keep)
+
+    def keep_top(rows):
+        tbuf[r, w, rows, :] = grad_top[rows, :]
+
+    each_rows(64, 16, keep_top)
+    gather.step(1)
+    p1_square.turn()
+    gather.step(2)
+    tops.own()
+    down.turn()
+    gather.step(3)
+    gather.rest()
+    tab_copy.wait_recv()
+    p1_square.finish()
+    bring.wait()
+    outs = [
+        pltpu.make_async_copy(buf, rows_out, out_s.at[1]),
+        pltpu.make_async_copy(tabs, tabs_out, out_s.at[2]),
+        pltpu.make_async_copy(p1, p1_out, out_s.at[3]),
+    ]
+    for out in outs:
+        out.start()
+    tops.step(1)
 
     def copy(row, slot, by):
         return pltpu.make_async_remote_copy(
@@ -867,7 +834,8 @@
         def tile(i, carry):
             rows = pl.ds(pl.multiple_of(i * 256, 256), 256)
             cosine, sine = tabs[row, rows, 0:128], tabs[row, rows, 128:256]
-            pre = jnp.dot(x[row, rows, :], weight, preferred_element_type=f32)
+            left = buf[row, pl.ds(i * 2, 2)].reshape(256, 2048)
+            pre = jnp.dot(left, weight, preferred_element_type=f32)
             q_out[row, rows, 0:128] = turn(pre[:, 0:128], cosine, sine).astype(bf16)
             q_out[row, rows, 128:256] = turn(pre[:, 128:256], cosine, sine).astype(bf16)
             both = pre[:, 256:384]
@@ -889,19 +857,19 @@
             def _():
                 kv[row, slot] = jnp.zeros((512, 128), bf16)
 
-    for k in (1, 2, 3):
-        gather.step(k)
-    gather.rest()
-    tops_copy = pltpu.make_async_copy(buf, tops_out, tops_s)
-    tops_copy.start()
+    tops.step(2)
     for row in range(2):
         for slot, least, by in ((1, 1, 1), (0, 2, 2)):
             @pl.when(n >= least)
             def _():
                 copy(row, slot, by).wait_recv()
 
-    out = pltpu.make_async_copy(kv, kv_out, out_s)
-    out.start()
+    outs.append(pltpu.make_async_copy(kv, kv_out, out_s.at[4]))
+    outs[3].start()
+    tops.step(3)
+    tops.rest()
+    outs.append(pltpu.make_async_copy(tbuf, tops_out, out_s.at[5]))
+    outs[4].start()
     for row in range(2):
         @pl.when(n <= 2)
         def _():
@@ -912,28 +880,40 @@
             copy(row, 0, 2).wait_send()
 
     gather.sent()
-    out.wait()
-    tops_copy.wait()
-
-
-def project(x, p1, tabs, grad_top):
+    tops.sent()
+    tab_copy.wait_send()
+    down.finish()
+    for out in outs:
+        out.wait()
+
+
+def enter(hidden, gain, tab, grad_top, p1_own, down_own):
+    shard, width = hidden.shape
     return comm_call(
-        project_kernel, "project", 2,
+        enter_kernel, "enter", 1,
         (
             jax.ShapeDtypeStruct((2, 512, 256), bf16),
+            jax.ShapeDtypeStruct((2, 4, shard, width), bf16),
+            jax.ShapeDtypeStruct((2,) + tab.shape, f32),
+            jax.ShapeDtypeStruct((4,) + p1_own.shape, bf16),
+            jax.ShapeDtypeStruct((4, 256, 1024), bf16),
             jax.ShapeDtypeStruct((2, 3, 512, 128), bf16),
-            jax.ShapeDtypeStruct((2, 4, 64, 2048), bf16),
+            jax.ShapeDtypeStruct((2, 4, 64, width), bf16),
         ),
-        [vmem()] * 4, [vmem(), hbm(), hbm()],
-        [
+        [vmem()] * 4 + [hbm()] * 2, [vmem()] + [hbm()] * 6,
+        gather_scratch(shard, width)
+        + gather_scratch(64, width)
+        + [
+            pltpu.VMEM((2,) + tab.shape, f32),
+            pltpu.VMEM((4,) + p1_own.shape, bf16),
             pltpu.VMEM((2, 3, 512, 128), bf16),
-            pltpu.SemaphoreType.DMA((2, 3)),
-            pltpu.SemaphoreType.DMA((2, 3)),
             pltpu.SemaphoreType.DMA(()),
+            pltpu.SemaphoreType.DMA(()),
+            pltpu.SemaphoreType.DMA((6,)),
         ]
-        + gather_scratch(64, 2048)
-        + [pltpu.SemaphoreType.DMA(())],
-        (x, p1, tabs, grad_top), flops=10**10, sent=10**7,
+        + square_sems() * 2
+        + [pltpu.SemaphoreType.DMA((2, 3))] * 2,
+        (hidden, gain, tab, grad_top, p1_own, down_own), flops=10**10, sent=10**8,
     )
 
 
@@ -1938,9 +1918,10 @@
         axis=1,
     )
 
-    rows, tabs, p1, down_a = enter(hidden, gain_a, tab, p1_shard, down_own)
-    rows3, rows2 = rows.reshape(2, 512, 2048), rows.reshape(1024, 2048)
-    q, kv, tops = project(rows3, p1, tabs, grad_top)
+    q, rows, tabs, p1, down_a, kv, tops = enter(
+        hidden, gain_a, tab, grad_top, p1_shard, down_own
+    )
+    rows2 = rows.reshape(1024, 2048)
     kv_flat = kv.reshape(2, 1536, 128)
     att, lse, mid, ffn_rows, gate_all, up_all, down_b = middle_stage(
         q, kv_flat, tabs, p1, hidden, gain_f, gate_own, up_own, down_own

time: 474 us -> 462 us (0.975)
  Pallas kernels: 437 us -> 425 us
    pallas_call x7 -> x6, Pallas kernels: 437 us -> 425 us  [comm_call(): pl.pallas_call(kernel, out_shape=out_shape, in_specs=in_specs, out_specs=...]
where the time goes in v10:
time: 462 us; the launch traced here: 459 us
  Pallas kernels  425 us (92%)
  local copies, waits for them, and re-layouts  16.8 us (4%)
  other arithmetic  15.8 us (3%)
    pallas_call x6, Pallas kernels, comm_call(): pl.pallas_call(kernel, out_shape=out_shape, in_specs=in_specs, out_specs=...  425 us
    unnamed x49, local copies, waits for them, and re-layouts  10.1 us

profile of v10, /device:TPU:0, one launch (start us, length us, event | category | flops | bytes accessed | tf_op | source)
XLA Modules:
  0.0 458.6 jit_solution(16351222990245979310)
XLA Ops:
  0.6 0.0 copy-start
  0.7 0.0 copy-start.20
  0.7 0.9 reduce-window.4
  1.6 0.7 fusion.1
  2.2 0.1 select_reduce_fusion
  2.3 0.1 broadcast_in_dim.22
  2.5 1.1 constant_dynamic-slice_fusion.4
  3.6 1.0 constant_dynamic-slice_fusion
  4.6 0.0 copy-done
  4.6 1.0 maximum_maximum_fusion.p1_own
  5.6 0.0 copy-done.20
  5.6 1.0 multiply_sine_fusion
  6.6 1.5 concatenate.24.tab
  8.1 0.0 copy-done.15
  8.1 0.1 constant_dynamic-slice_fusion.7
  8.2 1.1 pad_maximum_fusion.2.down_own
  9.3 0.8 copy-done.6
  10.1 0.6 copy-done.7
  10.7 1.5 constant_dynamic-slice_fusion.1
  12.2 63.7 %enter.1 = (bf16[2,512,256]{2,1,0:T(8,128)(2,1)}, bf16[2,4,128,2048]{3,2,1,0:T(8,128)(2,1)}, f32[2,512,384]{2,1,0:T(8,128)}, bf16[4,512,640]{2,1,0:T(8,128)(2,1)...) custom-call(bf16[128,2048]{1,0:T(8,128)(2,1)} %bitcast.64, ...), custom_call_target="tpu_custom_call" | custom-call | flops 10000000000 | bytes 100000000 | tf_op jit(solution)/shard_map/enter/pallas_call | solution.py:732
  76.0 96.8 %middle.1 = (bf16[2,512,256]{2,1,0:T(8,128)(2,1)}, f32[2,4,512,128]{3,2,1,0:T(8,128)}, f32[128,2048]{1,0:T(8,128)}, bf16[2,4,128,2048]{3,2,1,0:T(8,128)(2,1)}, b...) custom-call(bf16[2,512,256]{2,1,0:T(8,128)(2,1)} %get-tuple-element.61.q, ...), custom_call_target="tpu_custom_call" | custom-call | flops 10000000000 | bytes 200000000 | tf_op jit(solution)/shard_map/middle/pallas_call | solution.py:732
  172.8 93.0 %ffn.1 = (bf16[2,4,128,2048]{3,2,1,0:T(8,128)(2,1)}, f32[128,2048]{1,0:T(8,128)}, f32[8,2048]{1,0:T(8,128)}, bf16[2,3,128,2048]{3,2,1,0:T(8,128)(2,1)}, bf16[2,3...) custom-call(bf16[1024,2048]{1,0:T(8,128)(2,1)} %bitcast.75, ...), custom_call_target="tpu_custom_call" | custom-call | flops 40000000000 | bytes 100000000 | tf_op jit(solution)/shard_map/ffn/pallas_call | solution.py:732
  265.8 52.1 %branch.1 = (f32[128,2048]{1,0:T(8,128)}, bf16[2,512,256]{2,1,0:T(8,128)(2,1)}, bf16[2,128,512]{2,1,0:T(8,128)(2,1)}, bf16[2,128,512]{2,1,0:T(8,128)(2,1)}, bf16...) custom-call(f32[128,2048]{1,0:T(8,128)} %get-tuple-element.72.total,, ...), custom_call_target="tpu_custom_call" | custom-call | flops 10000000000 | bytes 100000000 | tf_op jit(solution)/shard_map/branch/pallas_call | solution.py:732
  317.9 0.0 copy-start.9
  317.9 56.0 %unproject.1 = (bf16[2,4,128,2048]{3,2,1,0:T(8,128)(2,1)}, f32[8,2048]{1,0:T(8,128)}, bf16[2,128,768]{2,1,0:T(8,128)(2,1)}, bf16[2,128,768]{2,1,0:T(8,128)(2,1)}...) custom-call(bf16[2,512,256]{2,1,0:T(8,128)(2,1)} %get-tuple-element., ...), custom_call_target="tpu_custom_call" | custom-call | flops 10000000000 | bytes 10000000 | tf_op jit(solution)/shard_map/unproject/pallas_call | solution.py:732
  374.0 0.0 copy-done.9
  374.0 0.0 copy-start.4
  374.0 0.0 copy-start.5
  374.0 0.0 copy-start.8
  374.0 0.0 copy-start.16
  374.0 0.0 copy-start.17
  374.1 3.9 bitcast_add_fusion
  378.0 0.0 copy-done.4
  378.0 0.0 copy-done.5
  378.0 0.0 copy-done.8
  378.0 0.3 copy-done.16
  378.3 0.5 copy-done.17
  378.7 2.1 bitcast_add_fusion.1
  380.8 0.1 maximum_bitcast_fusion
  381.0 0.0 copy-start.19
  381.0 0.0 copy-start.18
  381.0 1.8 copy.30
  382.8 0.0 copy-done.19
  382.8 0.0 copy-done.18
  382.9 0.6 pad_maximum_fusion.3.gains
  383.5 63.5 %leave.1 = (bf16[128,2048]{1,0:T(8,128)(2,1)}, f32[8,256]{1,0:T(8,128)}, f32[256,512]{1,0:T(8,128)}, f32[256,512]{1,0:T(8,128)}, f32[256,512]{1,0:T(8,128)}, /*index=5*/f32[256,512]{1,0:T(8,128)}) custom-call(bf16[2,4,128,2048]{3,2,1,0:T(8,128)(2,1)} %get-tuple-element.89.parts, bf16[128,2048]{1,0:T(8,128)(2,1)} %bitcast.66, f32[1,2048]{1,0:T(1,128)} %bitcast.72, ...), custom_call_target="tpu_custom_call" | custom-call | flops 10000000000 | bytes 100000000 | tf_op jit(solution)/shard_map/leave/pallas_call | solution.py:732
  447.0 1.3 fusion.2
  448.3 2.0 copy.29
  450.3 0.0 copy-done.2
  450.4 2.8 pad_maximum_fusion
  453.2 0.0 copy-done.3
  453.2 1.5 pad_maximum_fusion.1
  454.6 0.0 copy-done.10
  454.6 0.0 copy-start.1
  454.6 0.8 copy.36
  455.4 0.0 copy-done.14
  455.4 0.8 copy.37
  456.2 0.0 copy-done.13
  456.2 0.8 copy.38
  457.0 0.0 copy-done.12
  457.0 0.8 copy.39
  457.8 0.0 copy-done.11
  457.8 0.8 copy.40
  458.6 0.0 copy-done.1
  (17 shorter events, 0.1 us)
Async XLA Ops:
  0.6 3.9 copy-start
  0.7 5.0 %copy-start.20 = (f32[32]{0:T(128)S(1)}, f32[32]{0:T(128)}, u32[]{:S(2)}) copy-start(f32[32]{0:T(128)} %constant.36.clone) | copy-start | bytes 388
  5.6 2.5 copy-start.15
  8.1 2.0 copy-start.6
  8.1 2.6 copy-start.7
  317.9 56.1 %copy-start.9 = (bf16[2,2,128,2048]{3,2,1,0:T(8,128)(2,1)S(1)}, bf16[2,2,128,2048]{3,2,1,0:T(8,128)(2,1)}, u32[]{:S(2)}) copy-start(bf16[2,2,128,2048]{3,2,1,0:T(8,128)(2,1)} %get-tuple-element.79.b_came.b_gate) | copy-start | bytes 6291460
  374.0 4.0 copy-start.4
  374.0 4.0 copy-start.5
  374.0 4.0 copy-start.8
  374.0 4.2 copy-start.16
  374.0 4.7 %copy-start.17 = (bf16[2,128,2048]{2,1,0:T(8,128)(2,1)S(1)}, bf16[2,128,2048]{2,1,0:T(8,128)(2,1)}, u32[]{:S(2)}) copy-start(bf16[2,128,2048]{2,1,0:T(8,128)(2,1)} %get-tuple-element.84.a_up) | copy-start | bytes 3145732
  381.0 1.8 copy-start.19
  381.0 1.9 copy-start.18
  383.5 66.8 %copy-start.2 = (f32[128,2048]{1,0:T(8,128)S(1)}, f32[128,2048]{1,0:T(8,128)}, u32[]{:S(2)}) copy-start(f32[128,2048]{1,0:T(8,128)} %get-tuple-element.147) | copy-start | bytes 3145732
  450.4 2.8 copy-start.3
  453.2 1.5 copy-start.10
  453.2 2.3 copy-start.14
  454.6 1.6 copy-start.13
  454.6 2.4 copy-start.12
  454.6 3.2 copy-start.11
  454.6 4.0 copy-start.1

commit v11 on v10

--- a/solution.py
+++ b/solution.py
@@ -1369,123 +1369,26 @@
     return root * weighted - values * (root * root * root) * inner
 
 
-def branch_kernel(
-    total, mid, grad_top, gain, p1, att, a_in, b_in, a_keep, b_keep, a_came, b_came,
-    gmid_out, datt_out, o0, o1, o2, o3, ra_out, rb_out, la_out, lb_out,
-    buf, g0, g1, g2, g3, wide, give_s, give_g, keep_s, n_s, n_g, kept, came, in_s,
-):
-    me = spot()
-    r, n, w = me
-    greet(line_partners(r, n, w, 4) + square_partners(r, n, w))
-    gather = Gather(buf, (g0, g1, g2, g3), me, 4)
-    hops = [
-        push(a_in.at[:, 1], ra_out, n_s.at[0], n_g.at[0], over_x(r, n, w)),
-        push(b_in.at[:, 1], rb_out, n_s.at[1], n_g.at[1], over_y(r, n, w)),
-        push(kept.at[0], la_out, n_s.at[2], n_g.at[2], over_y(r, n, w)),
-        push(kept.at[1], lb_out, n_s.at[3], n_g.at[3], over_x(r, n, w)),
-    ]
-    loads = []
-    for j, (keep, first) in enumerate(((a_keep, a_came), (b_keep, b_came))):
-        loads += [
-            pltpu.make_async_copy(keep.at[1, 2], kept.at[j], in_s.at[j, 0]),
-            pltpu.make_async_copy(first.at[0, 1], came.at[j], in_s.at[j, 1]),
-        ]
-    for load in loads:
-        load.start()
-    hops[0].start()
-    hops[1].start()
-
-    def body(rows):
-        grad = norm_back(mid[rows, :], gain[...], total[rows, :]) + grad_top[rows, :].astype(f32)
-        gmid_out[rows, :] = grad
-        buf[r, w, rows, :] = grad.astype(bf16)
-
-    each_rows(mid.shape[0], 16, body)
-    gather.own()
-    for load in loads:
-        load.wait()
-    for j in range(2):
-        def join(rows):
-            kept[j, rows, :] = (kept[j, rows, :].astype(f32) + came[j, rows, :].astype(f32)).astype(bf16)
-
-        each_rows(128, 16, join)
-        hops[2 + j].start()
-    for k in (1, 2, 3):
-        gather.step(k)
-    gather.rest()
-    for row in range(2):
-        for pair in range(2):
-            left = jnp.concatenate([buf[row, 2 * pair], buf[row, 2 * pair + 1]], axis=0)
-            right = jnp.concatenate(
-                [out_block(p1, nn, half) for nn in range(4) for half in range(2)], axis=1
-            )
-            datt_out[row, pair * 256 : pair * 256 + 256, :] = contract_last(left, right).astype(bf16)
-
-    spread = Spread((o0, o1, o2, o3), (give_s, give_g, keep_s), me)
-
-    def moved(half):
-        def place(target):
-            return target.at[:, pl.ds(pl.multiple_of(r * 256, 256), 256)]
-
-        return wide.at[half], 0, place, half == 0
-
-    for half in range(2):
-        d_first = (jnp.where(half == 0, 1 - r, r)) * 1024
-
-        def weight_tile(i, carry):
-            columns = pl.ds(pl.multiple_of(d_first + i * 256, 256), 256)
-            left = buf[:, :, :, columns].reshape(1024, 256)
-            wide[half, i] = contract_first(left, att[...]).astype(bf16)
-            return carry
-
-        lax.fori_loop(0, 4, weight_tile, 0)
-        spread.start(*moved(half))
-    gather.sent()
-    spread.wait(*moved(0))
-    spread.wait(*moved(1))
-    for hop in hops:
-        hop.wait()
-
-
-def branch_stage(*args):
-    shard, width = 128, 2048
-    return comm_call(
-        branch_kernel, "branch", 5,
-        (
-            jax.ShapeDtypeStruct((shard, width), f32),
-            jax.ShapeDtypeStruct((2, 512, 256), bf16),
-        )
-        + spread_shapes(128, 512)
-        + (jax.ShapeDtypeStruct((2, 128, width), bf16),) * 2
-        + (jax.ShapeDtypeStruct((128, width), bf16),) * 2,
-        [vmem()] * 6 + [hbm()] * 6, [vmem(), vmem()] + [hbm()] * 8,
-        gather_scratch(shard, width)
-        + [pltpu.VMEM((2, 4, 256, 256), bf16)]
-        + spread_sems(1)
-        + [pltpu.SemaphoreType.DMA((4,))] * 2
-        + [pltpu.VMEM((2, 128, width), bf16)] * 2
-        + [pltpu.SemaphoreType.DMA((2, 2))],
-        args, flops=10**10, sent=10**8,
-    )
-
-
-def unproject_kernel(
-    q, kv, att, grad, lse, x, p1, tabs, gain, parts, mid, a_keep, b_keep, a_gate, b_gate, a_up, b_up, oa_in, ob_in,
-    part_out, gain_out, o0, o1, o2, o3, hid_out, ra_out, rb_out, roa_out, rob_out,
-    send, recv, both, wide_q, wide_kv, s_s, s_g, give_s, give_g, keep_s,
+def back_kernel(
+    total, mid, grad_top, gain_f, p1, att, q, kv, lse, x, tabs, gain,
+    parts, a_send, b_send, a_keep, b_keep, a_came, b_came,
+    gmid_out, part_out, gain_out, hid_out, o0, o1, o2, o3, oa_out, ob_out,
+    q0, q1, q2, q3, ua_out, ub_out, la_out, lb_out,
+    buf, g0, g1, g2, g3, grad, wide, give_s, give_g, keep_s,
+    send, recv, both, wide_q, wide_kv, s_s, s_g, qgive_s, qgive_g, qkeep_s,
     mine, from_pt, from_up, from_dn, s0, s1, s2, s3, s4, s5,
     kept, came, acc, in_s, n_s, n_g, m_s, dkv,
 ):
     me = spot()
     r, n, w = me
-    loads = []
-    for j, (keep, gate, up) in enumerate(((a_keep, a_gate, a_up), (b_keep, b_gate, b_up))):
+    x_side, y_side = over_x(r, n, w), over_y(r, n, w)
+    loads = [pltpu.make_async_copy(parts.at[r], mine, m_s)]
+    for j, (keep, first) in enumerate(((a_keep, a_came), (b_keep, b_came))):
         loads += [
-            pltpu.make_async_copy(keep.at[1, 0:2], kept.at[j], in_s.at[j, 0]),
-            pltpu.make_async_copy(gate.at[1, 1], came.at[j, 0], in_s.at[j, 1]),
-            pltpu.make_async_copy(up.at[1], came.at[j, 1], in_s.at[j, 2]),
+            pltpu.make_async_copy(keep.at[1], kept.at[j], in_s.at[j, 0]),
+            pltpu.make_async_copy(first.at[1, 1], came.at[j, 0], in_s.at[j, 1]),
+            pltpu.make_async_copy(first.at[0, 1], came.at[j, 2], in_s.at[j, 2]),
         ]
-    loads.append(pltpu.make_async_copy(parts.at[r], mine, m_s))
     for load in loads:
         load.start()
     greet(
@@ -1496,39 +1399,70 @@
             (n <= 2, nar_device(r, n, w, 1)),
             (n <= 1, nar_device(r, n, w, 2)),
         ]
-        + square_partners(r, n, w)
     )
     scatter = Scatter(
         mine, parts.at[1 - r], (from_pt, from_up, from_dn), (s0, s1, s2, s3, s4, s5), me, 4
     )
-    hops = [
-        push(kept.at[0], ra_out, n_s.at[0], n_g.at[0], over_y(r, n, w)),
-        push(kept.at[1], rb_out, n_s.at[1], n_g.at[1], over_x(r, n, w)),
-        push(oa_in, roa_out, n_s.at[2], n_g.at[2], over_x(r, n, w)),
-        push(ob_in, rob_out, n_s.at[3], n_g.at[3], over_y(r, n, w)),
+    gather = Gather(buf, (g0, g1, g2, g3), me, 4)
+
+    def hop(k, source, target, device):
+        return push(source, target, n_s.at[k], n_g.at[k], device)
+
+    up_hops = [
+        hop(0, a_send.at[:, 1], ua_out, x_side),
+        hop(1, b_send.at[:, 1], ub_out, y_side),
     ]
+    last_hops = [
+        [
+            hop(2 + which, kept.at[0, which], la_out.at[which], y_side),
+            hop(5 + which, kept.at[1, which], lb_out.at[which], x_side),
+        ]
+        for which in range(3)
+    ]
+    o_hops = [hop(8, o0, oa_out, x_side), hop(9, o2, ob_out, y_side)]
+    for one in up_hops:
+        one.start()
+
+    def body(rows):
+        got = norm_back(mid[rows, :], gain_f[...], total[rows, :]) + grad_top[rows, :].astype(f32)
+        gmid_out[rows, :] = got
+        buf[r, w, rows, :] = got.astype(bf16)
+
+    each_rows(mid.shape[0], 16, body)
+    gather.own()
+    for load in loads:
+        load.wait()
+
+    def join(which):
+        for j in range(2):
+            def add(rows):
+                one = kept[j, which, rows, :].astype(f32) + came[j, which, rows, :].astype(f32)
+                kept[j, which, rows, :] = one.astype(bf16)
+
+            each_rows(128, 16, add)
+            last_hops[which][j].start()
+
+    join(2)
+    join(0)
+    for i in range(4):
+        scatter.pair(scatter.order(i)).start()
+    for k in (1, 2, 3):
+        gather.step(k)
+    gather.rest()
+    scatter.advance((0, 1, 2, 3), ())
+    for row in range(2):
+        for pair in range(2):
+            left = jnp.concatenate([buf[row, 2 * pair], buf[row, 2 * pair + 1]], axis=0)
+            right = jnp.concatenate(
+                [out_block(p1, nn, half) for nn in range(4) for half in range(2)], axis=1
+            )
+            grad[row, pair * 256 : pair * 256 + 256, :] = contract_last(left, right).astype(bf16)
 
     def copy(row, slot, by):
         return pltpu.make_async_remote_copy(
             send.at[row, slot], recv.at[row, slot], s_s.at[row, slot], s_g.at[row, slot],
             device_id=nar_device(r, n, w, by), device_id_type=MESH,
         )
-
-    for i in range(4):
-        scatter.pair(scatter.order(i)).start()
-    for load in loads:
-        load.wait()
-    for j in range(2):
-        for which in range(2):
-            def join(rows):
-                total = kept[j, which, rows, :].astype(f32) + came[j, which, rows, :].astype(f32)
-                kept[j, which, rows, :] = total.astype(bf16)
-
-            each_rows(128, 16, join)
-        hops[j].start()
-    hops[2].start()
-    hops[3].start()
-    scatter.advance((0, 1, 2, 3), ())
 
     def attention(i, carry):
         row, block = i // 4, i % 4
@@ -1584,7 +1518,35 @@
     lax.fori_loop(0, 8, attention, 0)
     scatter.advance((), (1,))
 
-    spread = Spread((o0, o1, o2, o3), (give_s, give_g, keep_s), (r, n, w))
+    fresh = []
+    for j, first in enumerate((ua_out, ub_out)):
+        up_hops[j].wait_recv()
+        fresh.append(pltpu.make_async_copy(first.at[1], came.at[j, 1], in_s.at[j, 3]))
+        fresh[j].start()
+    for load in fresh:
+        load.wait()
+    join(1)
+
+    spread_o = Spread((o0, o1, o2, o3), (give_s, give_g, keep_s), me)
+    spread = Spread((q0, q1, q2, q3), (qgive_s, qgive_g, qkeep_s), me)
+
+    def moved_o(half):
+        def place(target):
+            return target.at[:, pl.ds(pl.multiple_of(r * 256, 256), 256)]
+
+        return wide.at[half], 0, place, half == 0
+
+    for half in range(2):
+        d_first = (jnp.where(half == 0, 1 - r, r)) * 1024
+
+        def weight_tile(i, carry):
+            columns = pl.ds(pl.multiple_of(d_first + i * 256, 256), 256)
+            left = buf[:, :, :, columns].reshape(1024, 256)
+            wide[half, i] = contract_first(left, att[...].reshape(1024, 256)).astype(bf16)
+            return carry
+
+        lax.fori_loop(0, 4, weight_tile, 0)
+        spread_o.start(*moved_o(half))
 
     def moved_q(half):
         def place(target):
@@ -1635,6 +1597,10 @@
         weight(half, slice(256, 384), wide_kv)
         spread.start(*moved_kv(half))
     scatter.advance((), (2,))
+    spread_o.wait_recv(*moved_o(0))
+    spread_o.wait(*moved_o(1))
+    for one in o_hops:
+        one.start()
     gain_out[...] = jnp.zeros_like(gain_out)
 
     def model_tile(dt, carry):
@@ -1671,24 +1637,34 @@
     for half in range(2):
         spread.wait(*moved_q(half))
         spread.wait(*moved_kv(half))
-    for hop in hops:
-        hop.wait()
-
-
-def unproject(*args):
+    spread_o.wait_send(*moved_o(0))
+    gather.sent()
+    for one in up_hops:
+        one.wait_send()
+    for one in last_hops[0] + last_hops[1] + last_hops[2] + o_hops:
+        one.wait()
+
+
+def back(*args):
+    shard, width = 128, 2048
     return comm_call(
-        unproject_kernel, "unproject", 6,
+        back_kernel, "back", 5,
         (
-            jax.ShapeDtypeStruct((2, 4, 128, 2048), bf16),
-            jax.ShapeDtypeStruct((8, 2048), f32),
+            jax.ShapeDtypeStruct((shard, width), f32),
+            jax.ShapeDtypeStruct((2, 4, shard, width), bf16),
+            jax.ShapeDtypeStruct((8, width), f32),
+            jax.ShapeDtypeStruct((shard, width), bf16),
         )
+        + spread_shapes(128, 512)
+        + (jax.ShapeDtypeStruct((2, 128, 512), bf16),) * 2
         + spread_shapes(128, 768)
-        + (jax.ShapeDtypeStruct((128, 2048), bf16),)
-        + (jax.ShapeDtypeStruct((2, 128, 2048), bf16),) * 2
-        + (jax.ShapeDtypeStruct((2, 128, 512), bf16),) * 2,
-        [vmem()] * 9 + [hbm(), vmem()] + [hbm()] * 8,
-        [vmem(), vmem()] + [hbm()] * 4 + [vmem()] + [hbm()] * 4,
-        [
+        + (jax.ShapeDtypeStruct((2, 128, width), bf16),) * 2
+        + (jax.ShapeDtypeStruct((3, 128, width), bf16),) * 2,
+        [vmem()] * 12 + [hbm()] * 7, [vmem()] * 4 + [hbm()] * 14,
+        gather_scratch(shard, width)
+        + [pltpu.VMEM((2, 512, 256), bf16), pltpu.VMEM((2, 4, 256, 256), bf16)]
+        + spread_sems(1)
+        + [
             pltpu.VMEM((2, 2, 512, 128), bf16),
             pltpu.VMEM((2, 2, 512, 128), bf16),
             pltpu.VMEM((1024, 384), bf16),
@@ -1698,19 +1674,19 @@
             pltpu.SemaphoreType.DMA((2, 2)),
         ]
         + spread_sems(2)
-        + [pltpu.VMEM((4, 128, 2048), bf16)]
-        + scatter_bufs(128, 2048) + scatter_sems()
+        + [pltpu.VMEM((4, shard, width), bf16)]
+        + scatter_bufs(shard, width) + scatter_sems()
         + [
-            pltpu.VMEM((2, 2, 128, 2048), bf16),
-            pltpu.VMEM((2, 2, 128, 2048), bf16),
-            pltpu.VMEM((128, 2048), f32),
-            pltpu.SemaphoreType.DMA((2, 3)),
-            pltpu.SemaphoreType.DMA((4,)),
-            pltpu.SemaphoreType.DMA((4,)),
+            pltpu.VMEM((2, 3, shard, width), bf16),
+            pltpu.VMEM((2, 3, shard, width), bf16),
+            pltpu.VMEM((shard, width), f32),
+            pltpu.SemaphoreType.DMA((2, 4)),
+            pltpu.SemaphoreType.DMA((10,)),
+            pltpu.SemaphoreType.DMA((10,)),
             pltpu.SemaphoreType.DMA(()),
             pltpu.VMEM((2, 1536, 128), f32),
         ],
-        args, flops=10**10, sent=10**7,
+        args, flops=10**10, sent=10**8,
     )
 
 
@@ -1930,16 +1906,12 @@
         ffn_rows.reshape(1024, 2048), tops, grad_top,
         gate_own, gate_all, up_own, up_all, down_own, down_a, down_b, gain_f,
     )
-    gmid, datt, oa_send, oa_keep, ob_send, ob_keep, ra_u, rb_u, la_d, lb_d = branch_stage(
-        total, mid, grad_top, gain_f, p1, att.reshape(1024, 256),
-        a_send, b_send, a_keep, b_keep, ra_dg, rb_dg,
-    )
     (
-        dparts, gain_a_part, qa_send, qa_keep, qb_send, qb_keep,
-        hidden_out, ra_last, rb_last, oa_came, ob_came,
-    ) = unproject(
-        q, kv_flat, att, datt, lse, rows2, p1, tabs, gain_a, parts, mid,
-        a_keep, b_keep, ra_dg, rb_dg, ra_u, rb_u, oa_send, ob_send,
+        gmid, dparts, gain_a_part, hidden_out, _, oa_keep, _, ob_keep, oa_came, ob_came,
+        qa_send, qa_keep, qb_send, qb_keep, ra_u, rb_u, a_last, b_last,
+    ) = back(
+        total, mid, grad_top, gain_f, p1, att, q, kv_flat, lse, rows2, tabs, gain_a,
+        parts, a_send, b_send, a_keep, b_keep, ra_dg, rb_dg,
     )
     gains = jnp.concatenate(
         [gain_f_part.sum(axis=0).reshape(8, 256), gain_a_part.sum(axis=0).reshape(8, 256)], axis=0
@@ -1953,13 +1925,11 @@
         def half_rows(keep, came, last):
             return keep[0, which].astype(f32) + came.astype(f32) + last.astype(f32)
 
-        a_came, b_came, a_last, b_last = (
-            (ra_dg[1, 0], rb_dg[1, 0], ra_last[0], rb_last[0]),
-            (ra_u[0], rb_u[0], ra_last[1], rb_last[1]),
-            (ra_dg[0, 0], rb_dg[0, 0], la_d, lb_d),
+        a_came, b_came = (
+            (ra_dg[1, 0], rb_dg[1, 0]), (ra_u[0], rb_u[0]), (ra_dg[0, 0], rb_dg[0, 0])
         )[which]
         return jnp.concatenate(
-            [half_rows(a_keep, a_came, a_last), half_rows(b_keep, b_came, b_last)], axis=0
+            [half_rows(a_keep, a_came, a_last[which]), half_rows(b_keep, b_came, b_last[which])], axis=0
         )
 
     return (

time: 462 us -> 443 us (0.959)
  Pallas kernels: 425 us -> 409 us
    pallas_call x6 -> x5, Pallas kernels: 425 us -> 409 us  [comm_call(): pl.pallas_call(kernel, out_shape=out_shape, in_specs=in_specs, out_specs=...]
    unnamed x49 -> x47, local copies, waits for them, and re-layouts: 10.1 us -> 10.1 us
where the time goes in v11:
time: 443 us
  Pallas kernels  409 us (92%)
  local copies, waits for them, and re-layouts  16.7 us (4%)
  other arithmetic  15.8 us (4%)
    pallas_call x5, Pallas kernels, comm_call(): pl.pallas_call(kernel, out_shape=out_shape, in_specs=in_specs, out_specs=...  409 us
    unnamed x47, local copies, waits for them, and re-layouts  10.1 us

profile of v11, /device:TPU:0, one launch (start us, length us, event | category | flops | bytes accessed | tf_op | source)
XLA Modules:
  0.0 442.7 jit_solution(14878772107848226784)
XLA Ops:
  0.6 0.0 copy-start
  0.7 0.0 copy-start.19
  0.7 0.9 reduce-window.4
  1.6 0.7 fusion.1
  2.2 0.1 select_reduce_fusion
  2.3 0.1 broadcast_in_dim.22
  2.5 1.1 constant_dynamic-slice_fusion.4
  3.6 1.0 constant_dynamic-slice_fusion
  4.6 0.0 copy-done
  4.6 1.0 maximum_maximum_fusion.p1_own
  5.6 0.0 copy-done.19
  5.7 0.0 copy-start.15
  5.7 1.0 multiply_sine_fusion
  6.7 1.5 concatenate.24.tab
  8.1 0.0 copy-done.15
  8.1 0.0 copy-start.6
  8.1 0.0 copy-start.7
  8.1 0.1 constant_dynamic-slice_fusion.7
  8.2 1.1 pad_maximum_fusion.2.down_own
  9.3 0.8 copy-done.6
  10.1 0.6 copy-done.7
  10.7 1.5 constant_dynamic-slice_fusion.1
  12.2 63.8 %enter.1 = (bf16[2,512,256]{2,1,0:T(8,128)(2,1)}, bf16[2,4,128,2048]{3,2,1,0:T(8,128)(2,1)}, f32[2,512,384]{2,1,0:T(8,128)}, bf16[4,512,640]{2,1,0:T(8,128)(2,1)...) custom-call(bf16[128,2048]{1,0:T(8,128)(2,1)} %bitcast.69, ...), custom_call_target="tpu_custom_call" | custom-call | flops 10000000000 | bytes 100000000 | tf_op jit(solution)/shard_map/enter/pallas_call | solution.py:732
  76.0 96.8 %middle.1 = (bf16[2,512,256]{2,1,0:T(8,128)(2,1)}, f32[2,4,512,128]{3,2,1,0:T(8,128)}, f32[128,2048]{1,0:T(8,128)}, bf16[2,4,128,2048]{3,2,1,0:T(8,128)(2,1)}, b...) custom-call(bf16[2,512,256]{2,1,0:T(8,128)(2,1)} %get-tuple-element.56.q, ...), custom_call_target="tpu_custom_call" | custom-call | flops 10000000000 | bytes 200000000 | tf_op jit(solution)/shard_map/middle/pallas_call | solution.py:732
  172.8 93.2 %ffn.1 = (bf16[2,4,128,2048]{3,2,1,0:T(8,128)(2,1)}, f32[128,2048]{1,0:T(8,128)}, f32[8,2048]{1,0:T(8,128)}, bf16[2,3,128,2048]{3,2,1,0:T(8,128)(2,1)}, bf16[2,3...) custom-call(bf16[1024,2048]{1,0:T(8,128)(2,1)} %bitcast.80, ...), custom_call_target="tpu_custom_call" | custom-call | flops 40000000000 | bytes 100000000 | tf_op jit(solution)/shard_map/ffn/pallas_call | solution.py:732
  266.0 0.0 copy-start.9
  266.0 98.0 %back.1 = (f32[128,2048]{1,0:T(8,128)}, bf16[2,4,128,2048]{3,2,1,0:T(8,128)(2,1)}, f32[8,2048]{1,0:T(8,128)}, bf16[128,2048]{1,0:T(8,128)(2,1)}, bf16[2,128,512]...) custom-call(f32[128,2048]{1,0:T(8,128)} %get-tuple-element.66.total,, ...), custom_call_target="tpu_custom_call" | custom-call | flops 10000000000 | bytes 100000000 | tf_op jit(solution)/shard_map/back/pallas_call | solution.py:732
  364.0 0.0 copy-done.9
  364.0 0.0 copy-start.4
  364.0 0.0 copy-start.5
  364.0 0.0 copy-start.8
  364.0 0.0 copy-start.16
  364.1 3.9 convert_add_fusion
  368.0 0.0 copy-done.4
  368.0 0.0 copy-done.5
  368.0 0.5 copy-done.8
  368.4 0.3 copy-done.16
  368.7 2.1 convert_add_fusion.1
  370.9 0.1 maximum_bitcast_fusion
  371.0 0.0 copy-start.18
  371.0 0.0 copy-start.17
  371.0 1.8 copy.30
  372.8 0.0 copy-done.18
  372.9 0.0 copy-done.17
  372.9 0.6 pad_maximum_fusion.3.gains
  373.5 57.5 %leave.1 = (bf16[128,2048]{1,0:T(8,128)(2,1)}, f32[8,256]{1,0:T(8,128)}, f32[256,512]{1,0:T(8,128)}, f32[256,512]{1,0:T(8,128)}, f32[256,512]{1,0:T(8,128)}, /*index=5*/f32[256,512]{1,0:T(8,128)}) custom-call(bf16[2,4,128,2048]{3,2,1,0:T(8,128)(2,1)} %get-tuple-element.79.parts, bf16[128,2048]{1,0:T(8,128)(2,1)} %bitcast.71, f32[1,2048]{1,0:T(1,128)} %bitcast.77, ...), custom_call_target="tpu_custom_call" | custom-call | flops 10000000000 | bytes 100000000 | tf_op jit(solution)/shard_map/leave/pallas_call | solution.py:732
  431.1 1.3 fusion.2
  432.4 2.0 copy.29
  434.4 0.0 copy-done.2
  434.5 2.8 pad_maximum_fusion
  437.3 0.0 copy-done.3
  437.3 1.5 pad_maximum_fusion.1
  438.7 0.0 copy-done.10
  438.7 0.0 copy-start.1
  438.7 0.8 copy.36
  439.5 0.0 copy-done.14
  439.5 0.8 copy.37
  440.3 0.0 copy-done.13
  440.3 0.8 copy.38
  441.1 0.0 copy-done.12
  441.1 0.8 copy.39
  441.9 0.0 copy-done.11
  441.9 0.8 copy.40
  442.7 0.0 copy-done.1
  (14 shorter events, 0.1 us)
Async XLA Ops:
  0.6 3.9 copy-start
  0.7 5.0 %copy-start.19 = (f32[32]{0:T(128)S(1)}, f32[32]{0:T(128)}, u32[]{:S(2)}) copy-start(f32[32]{0:T(128)} %constant.36.clone) | copy-start | bytes 388
  5.7 2.5 copy-start.15
  8.1 2.0 copy-start.6
  8.1 2.6 copy-start.7
  266.0 98.0 %copy-start.9 = (bf16[2,2,128,2048]{3,2,1,0:T(8,128)(2,1)S(1)}, bf16[2,2,128,2048]{3,2,1,0:T(8,128)(2,1)}, u32[]{:S(2)}) copy-start(bf16[2,2,128,2048]{3,2,1,0:T(8,128)(2,1)} %get-tuple-element.77.b_came) | copy-start | bytes 6291460
  364.0 4.0 copy-start.4
  364.0 4.0 copy-start.5
  364.0 4.4 copy-start.8
  364.0 4.7 %copy-start.16 = (bf16[2,128,2048]{2,1,0:T(8,128)(2,1)S(1)}, bf16[2,128,2048]{2,1,0:T(8,128)(2,1)}, u32[]{:S(2)}) copy-start(bf16[2,128,2048]{2,1,0:T(8,128)(2,1)} %get-tuple-element.98) | copy-start | bytes 3145732
  371.0 1.8 copy-start.18
  371.0 1.9 copy-start.17
  373.5 60.9 %copy-start.2 = (f32[128,2048]{1,0:T(8,128)S(1)}, f32[128,2048]{1,0:T(8,128)}, u32[]{:S(2)}) copy-start(f32[128,2048]{1,0:T(8,128)} %get-tuple-element.137) | copy-start | bytes 3145732
  434.4 2.8 copy-start.3
  437.3 1.5 copy-start.10
  437.3 2.3 copy-start.14
  438.7 1.6 copy-start.13
  438.7 2.4 copy-start.12
  438.7 3.2 copy-start.11
  438.7 4.0 copy-start.1

commit v12 on v11

--- a/solution.py
+++ b/solution.py
@@ -1007,8 +1007,9 @@
     me = spot()
     r, n, w = me
     greet(line_partners(r, n, w, 4) + square_partners(r, n, w))
-    gate = Square(gate_own, gate_out, (gate_s, gate_g), me)
-    up = Square(up_own, up_out, (up_s, up_g), me)
+    here = pl.ds(pl.multiple_of(r * 1024, 1024), 1024)
+    gate = Square(gate_own.at[:, here], gate_out, (gate_s, gate_g), me)
+    up = Square(up_own.at[:, here], up_out, (up_s, up_g), me)
     gate.start()
     up.start()
     down = Square(down_own.at[256:512], down_out, (down_s, down_g), me)
@@ -1145,9 +1146,10 @@
 ):
     me = spot()
     r, n, w = me
+    here = pl.ds(pl.multiple_of(r * 1024, 1024), 1024)
     loads = [
-        fetch(gate_own, gate_in, p2.at[0], in_s.at[0], n),
-        fetch(up_own, up_in, p2.at[1], in_s.at[1], n),
+        fetch(gate_own.at[:, here], gate_in, p2.at[0], in_s.at[0], n),
+        fetch(up_own.at[:, here], up_in, p2.at[1], in_s.at[1], n),
         fetch(down_own.at[0:256], down_a, p2.at[2, :, 0:256], in_s.at[2], n)
         + fetch(down_own.at[256:512], down_b, p2.at[2, :, 256:512], in_s.at[3], n),
         [pltpu.make_async_copy(tops_in, tops4.at[:, :, 0:64], tops_s)],
@@ -1275,8 +1277,10 @@
             push(o2.at[:, which], rb_out.at[at], n_s.at[1, at], n_g.at[1, at], over_y(r, n, w)),
         )
 
-    hops = hop(2, 0) + hop(0, 1)
-    weights(2)
+    hops = hop(2, 0) + (
+        push(o0.at[1, 0], ra_out.at[1, 1], n_s.at[0, 1], n_g.at[0, 1], over_x(r, n, w)),
+        push(o2.at[1, 0], rb_out.at[1, 1], n_s.at[1, 1], n_g.at[1, 1], over_y(r, n, w)),
+    )
     for i in range(4):
         s = scatter.order(i)
         rows_t = pl.ds(pl.multiple_of((1 - r) * 512 + s * 128, 128), 128)
@@ -1299,25 +1303,27 @@
 
         lax.fori_loop(0, 8, model_tile, 0)
         scatter.pair(s).start()
-        if i < 2:
-            which = (2, 0)[i]
+        if i == 0:
+            weights(2, lambda: scatter.advance((0,), ()))
+        elif i < 3:
+            which = (2, 0)[i - 1]
             spread.wait_recv(*moved(which, 0))
             spread.wait(*moved(which, 1))
-            hops[2 * i].start()
-            hops[2 * i + 1].start()
-        if i == 0:
-            weights(0)
-            scatter.advance((0,), ())
+            hops[2 * i - 2].start()
+            hops[2 * i - 1].start()
+        if i == 1:
+            weights(0, lambda: scatter.advance((1,), ()))
+            scatter.advance((), (0,))
         elif i > 1:
-            scatter.advance((i - 1,), (i - 2,))
+            scatter.advance((i,), (1,) if i == 3 else ())
 
     def scale(rows):
         gain_out[rows, :] = gain_out[rows, :] / gain[...]
 
     each_rows(8, 8, scale)
     spread.wait_send(*moved(2, 0))
-    weights(1, lambda: scatter.advance((3,), (2,)))
-    scatter.advance((), (3,))
+    weights(1)
+    scatter.advance((), (2, 3))
     scatter.total(sum_out)
     scatter.sent()
     gather.sent()
@@ -1373,7 +1379,7 @@
     total, mid, grad_top, gain_f, p1, att, q, kv, lse, x, tabs, gain,
     parts, a_send, b_send, a_keep, b_keep, a_came, b_came,
     gmid_out, part_out, gain_out, hid_out, o0, o1, o2, o3, oa_out, ob_out,
-    q0, q1, q2, q3, ua_out, ub_out, la_out, lb_out,
+    q0, q1, q2, q3, ua_out, ub_out, ga_out, gb_out, la_out, lb_out,
     buf, g0, g1, g2, g3, grad, wide, give_s, give_g, keep_s,
     send, recv, both, wide_q, wide_kv, s_s, s_g, qgive_s, qgive_g, qkeep_s,
     mine, from_pt, from_up, from_dn, s0, s1, s2, s3, s4, s5,
@@ -1419,6 +1425,7 @@
         ]
         for which in range(3)
     ]
+    gate_hops = [hop(10, a_send.at[0, 0], ga_out, x_side), hop(11, b_send.at[0, 0], gb_out, y_side)]
     o_hops = [hop(8, o0, oa_out, x_side), hop(9, o2, ob_out, y_side)]
     for one in up_hops:
         one.start()
@@ -1444,6 +1451,8 @@
 
     join(2)
     join(0)
+    for one in gate_hops:
+        one.start()
     for i in range(4):
         scatter.pair(scatter.order(i)).start()
     for k in (1, 2, 3):
@@ -1641,7 +1650,7 @@
     gather.sent()
     for one in up_hops:
         one.wait_send()
-    for one in last_hops[0] + last_hops[1] + last_hops[2] + o_hops:
+    for one in last_hops[0] + last_hops[1] + last_hops[2] + gate_hops + o_hops:
         one.wait()
 
 
@@ -1659,8 +1668,9 @@
         + (jax.ShapeDtypeStruct((2, 128, 512), bf16),) * 2
         + spread_shapes(128, 768)
         + (jax.ShapeDtypeStruct((2, 128, width), bf16),) * 2
+        + (jax.ShapeDtypeStruct((128, width), bf16),) * 2
         + (jax.ShapeDtypeStruct((3, 128, width), bf16),) * 2,
-        [vmem()] * 12 + [hbm()] * 7, [vmem()] * 4 + [hbm()] * 14,
+        [vmem()] * 12 + [hbm()] * 7, [vmem()] * 4 + [hbm()] * 16,
         gather_scratch(shard, width)
         + [pltpu.VMEM((2, 512, 256), bf16), pltpu.VMEM((2, 4, 256, 256), bf16)]
         + spread_sems(1)
@@ -1681,8 +1691,8 @@
             pltpu.VMEM((2, 3, shard, width), bf16),
             pltpu.VMEM((shard, width), f32),
             pltpu.SemaphoreType.DMA((2, 4)),
-            pltpu.SemaphoreType.DMA((10,)),
-            pltpu.SemaphoreType.DMA((10,)),
+            pltpu.SemaphoreType.DMA((12,)),
+            pltpu.SemaphoreType.DMA((12,)),
             pltpu.SemaphoreType.DMA(()),
             pltpu.VMEM((2, 1536, 128), f32),
         ],
@@ -1780,9 +1790,9 @@
     kv_gather.advance((), (2,))
     for j, (keep, came) in enumerate(((oa_keep, oa_in), (ob_keep, ob_in))):
         o_hops[j].wait_recv()
-        output_out[j * 128 : j * 128 + 128, :] = (
+        output_out[:, j * 128 : j * 128 + 128] = (
             keep[0].astype(f32) + came[0].astype(f32) + then_o[j].astype(f32)
-        )
+        ).T
     mine_block = r * 4 + n
     ga_out[0:1] = summed[pl.ds(mine_block, 1), :]
     ga_out[1:2] = summed[pl.ds(mine_block + 8, 1), :]
@@ -1831,7 +1841,8 @@
     return comm_call(
         leave_kernel, "leave", 7,
         (jax.ShapeDtypeStruct((shard, width), bf16), jax.ShapeDtypeStruct((8, 256), f32))
-        + (grad,) * 4,
+        + (grad,) * 3
+        + (jax.ShapeDtypeStruct((512, 256), f32),),
         [hbm()] + [vmem()] * 12, [vmem()] * 6,
         [pltpu.VMEM((4, shard, width), bf16)]
         + scatter_bufs(shard, width) + scatter_sems()
@@ -1881,7 +1892,6 @@
         axis=1,
     )
     down_half = half(w_down, 0)
-    gate_own, up_own = half(w_gate, 1), half(w_up, 1)
     down_own = jnp.concatenate([down_half[:512], down_half[512:]], axis=1)
 
     token_ids = n * 512 + jnp.arange(512, dtype=jnp.int32)
@@ -1900,15 +1910,15 @@
     rows2 = rows.reshape(1024, 2048)
     kv_flat = kv.reshape(2, 1536, 128)
     att, lse, mid, ffn_rows, gate_all, up_all, down_b = middle_stage(
-        q, kv_flat, tabs, p1, hidden, gain_f, gate_own, up_own, down_own
+        q, kv_flat, tabs, p1, hidden, gain_f, w_gate, w_up, down_own
     )
     parts, total, gain_f_part, a_send, a_keep, b_send, b_keep, ra_dg, rb_dg = ffn_stage(
         ffn_rows.reshape(1024, 2048), tops, grad_top,
-        gate_own, gate_all, up_own, up_all, down_own, down_a, down_b, gain_f,
+        w_gate, gate_all, w_up, up_all, down_own, down_a, down_b, gain_f,
     )
     (
         gmid, dparts, gain_a_part, hidden_out, _, oa_keep, _, ob_keep, oa_came, ob_came,
-        qa_send, qa_keep, qb_send, qb_keep, ra_u, rb_u, a_last, b_last,
+        qa_send, qa_keep, qb_send, qb_keep, ra_u, rb_u, ra_g, rb_g, a_last, b_last,
     ) = back(
         total, mid, grad_top, gain_f, p1, att, q, kv_flat, lse, rows2, tabs, gain_a,
         parts, a_send, b_send, a_keep, b_keep, ra_dg, rb_dg,
@@ -1926,7 +1936,7 @@
             return keep[0, which].astype(f32) + came.astype(f32) + last.astype(f32)
 
         a_came, b_came = (
-            (ra_dg[1, 0], rb_dg[1, 0]), (ra_u[0], rb_u[0]), (ra_dg[0, 0], rb_dg[0, 0])
+            (ra_g, rb_g), (ra_u[0], rb_u[0]), (ra_dg[0, 0], rb_dg[0, 0])
         )[which]
         return jnp.concatenate(
             [half_rows(a_keep, a_came, a_last[which]), half_rows(b_keep, b_came, b_last[which])], axis=0
@@ -1938,7 +1948,7 @@
         grad_query,
         grad_key,
         grad_value,
-        output_sum.T,
+        output_sum,
         joined(0),
         joined(1),
         joined(2).T,

time: 443 us -> 433 us (0.977)
  Pallas kernels: 409 us -> 402 us
  local copies, waits for them, and re-layouts: 16.7 us -> 11.8 us
    pallas_call x5, Pallas kernels: 409 us -> 402 us  [comm_call(): pl.pallas_call(kernel, out_shape=out_shape, in_specs=in_specs, out_specs=...]
    unnamed x47 -> x43, local copies, waits for them, and re-layouts: 10.1 us -> 6.66 us
where the time goes in v12:
time: 433 us; the launch traced here: 432 us
  Pallas kernels  402 us (93%)
  other arithmetic  17.2 us (4%)
  local copies, waits for them, and re-layouts  11.8 us (3%)
    pallas_call x5, Pallas kernels, comm_call(): pl.pallas_call(kernel, out_shape=out_shape, in_specs=in_specs, out_specs=...  402 us

profile of v12, /device:TPU:0, one launch (start us, length us, event | category | flops | bytes accessed | tf_op | source)
XLA Modules:
  0.0 432.2 jit_solution(11867744281448798165)
XLA Ops:
  0.6 0.0 copy-start
  0.7 0.0 copy-start.17
  0.7 0.9 reduce-window.4
  1.6 0.7 fusion.1
  2.2 0.1 select_reduce_fusion
  2.3 0.1 broadcast_in_dim.22
  2.5 1.1 constant_dynamic-slice_fusion.2
  3.6 1.0 constant_dynamic-slice_fusion
  4.6 0.0 copy-done
  4.6 1.0 maximum_maximum_fusion.p1_own
  5.6 0.0 copy-done.17
  5.6 0.0 copy-start.12
  5.6 1.0 multiply_sine_fusion
  6.6 1.5 concatenate.24.tab
  8.1 0.0 copy-done.12
  8.1 0.1 constant_dynamic-slice_fusion.5
  8.2 1.1 pad_maximum_fusion.2.down_own
  9.3 63.7 %enter.1 = (bf16[2,512,256]{2,1,0:T(8,128)(2,1)}, bf16[2,4,128,2048]{3,2,1,0:T(8,128)(2,1)}, f32[2,512,384]{2,1,0:T(8,128)}, bf16[4,512,640]{2,1,0:T(8,128)(2,1)...) custom-call(bf16[128,2048]{1,0:T(8,128)(2,1)} %bitcast.69, ...), custom_call_target="tpu_custom_call" | custom-call | flops 10000000000 | bytes 100000000 | tf_op jit(solution)/shard_map/enter/pallas_call | solution.py:732
  73.0 96.8 %middle.1 = (bf16[2,512,256]{2,1,0:T(8,128)(2,1)}, f32[2,4,512,128]{3,2,1,0:T(8,128)}, f32[128,2048]{1,0:T(8,128)}, bf16[2,4,128,2048]{3,2,1,0:T(8,128)(2,1)}, b...) custom-call(bf16[2,512,256]{2,1,0:T(8,128)(2,1)} %get-tuple-element.58.q, ...), custom_call_target="tpu_custom_call" | custom-call | flops 10000000000 | bytes 200000000 | tf_op jit(solution)/shard_map/middle/pallas_call | solution.py:732
  169.8 85.9 %ffn.1 = (bf16[2,4,128,2048]{3,2,1,0:T(8,128)(2,1)}, f32[128,2048]{1,0:T(8,128)}, f32[8,2048]{1,0:T(8,128)}, bf16[2,3,128,2048]{3,2,1,0:T(8,128)(2,1)}, bf16[2,3...) custom-call(bf16[1024,2048]{1,0:T(8,128)(2,1)} %bitcast.80, ...), custom_call_target="tpu_custom_call" | custom-call | flops 40000000000 | bytes 100000000 | tf_op jit(solution)/shard_map/ffn/pallas_call | solution.py:732
  255.8 98.9 %back.1 = (f32[128,2048]{1,0:T(8,128)}, bf16[2,4,128,2048]{3,2,1,0:T(8,128)(2,1)}, f32[8,2048]{1,0:T(8,128)}, bf16[128,2048]{1,0:T(8,128)(2,1)}, bf16[2,128,512]...) custom-call(f32[128,2048]{1,0:T(8,128)} %get-tuple-element.68.total,, ...), custom_call_target="tpu_custom_call" | custom-call | flops 10000000000 | bytes 100000000 | tf_op jit(solution)/shard_map/back/pallas_call | solution.py:732
  354.7 0.0 copy-start.4
  354.7 0.0 copy-start.5
  354.7 0.0 copy-start.13
  354.7 0.0 copy-start.14
  354.7 4.2 convert_add_fusion
  359.0 0.0 copy-done.4
  359.0 0.0 copy-done.5
  359.0 0.0 copy-done.13
  359.0 0.0 copy-done.14
  359.0 3.1 convert_add_fusion.1
  362.1 0.1 maximum_bitcast_fusion
  362.3 0.0 copy-start.16
  362.3 0.0 copy-start.15
  362.3 1.8 copy.27
  364.1 0.0 copy-done.16
  364.1 0.0 copy-done.15
  364.2 0.6 pad_maximum_fusion.3.gains
  364.8 0.0 copy-start.2
  364.8 56.8 %leave.1 = (bf16[128,2048]{1,0:T(8,128)(2,1)}, f32[8,256]{1,0:T(8,128)}, f32[256,512]{1,0:T(8,128)}, f32[256,512]{1,0:T(8,128)}, f32[256,512]{1,0:T(8,128)}, /*index=5*/f32[512,256]{1,0:T(8,128)}) custom-call(bf16[2,4,128,2048]{3,2,1,0:T(8,128)(2,1)} %get-tuple-element.81.parts, bf16[128,2048]{1,0:T(8,128)(2,1)} %bitcast.71, f32[1,2048]{1,0:T(1,128)} %bitcast.77, ...), custom_call_target="tpu_custom_call" | custom-call | flops 10000000000 | bytes 100000000 | tf_op jit(solution)/shard_map/leave/pallas_call | solution.py:732
  421.7 1.3 fusion.2
  423.0 0.0 copy-done.2
  423.0 0.0 copy-start.3
  423.0 2.9 pad_maximum_fusion.1
  425.9 0.0 copy-done.3
  425.9 0.0 copy-start.6
  425.9 0.0 copy-start.11
  425.9 1.5 pad_maximum_fusion
  427.4 0.0 copy-done.6
  427.4 0.0 copy-start.10
  427.4 0.0 copy-start.9
  427.4 0.0 copy-start.8
  427.4 0.8 copy.34
  428.2 0.0 copy-done.11
  428.2 0.8 copy.35
  429.0 0.0 copy-done.10
  429.0 0.8 copy.36
  429.8 0.0 copy-done.9
  429.8 0.8 copy.37
  430.6 0.0 copy-done.8
  430.6 0.8 copy.38
  431.4 0.0 copy-done.7
  431.4 0.8 copy.39
  432.2 0.0 copy-done.1
  (9 shorter events, 0.1 us)
Async XLA Ops:
  0.6 3.9 copy-start
  0.7 5.0 %copy-start.17 = (f32[32]{0:T(128)S(1)}, f32[32]{0:T(128)}, u32[]{:S(2)}) copy-start(f32[32]{0:T(128)} %constant.36.clone) | copy-start | bytes 388
  5.6 2.5 copy-start.12
  354.7 4.3 copy-start.4
  354.7 4.3 copy-start.5
  354.7 4.3 copy-start.13
  354.7 4.3 copy-start.14
  362.3 1.8 copy-start.16
  362.3 1.9 copy-start.15
  364.8 58.2 %copy-start.2 = (f32[128,2048]{1,0:T(8,128)S(1)}, f32[128,2048]{1,0:T(8,128)}, u32[]{:S(2)}) copy-start(f32[128,2048]{1,0:T(8,128)} %get-tuple-element.142) | copy-start | bytes 3145732
  423.0 2.9 copy-start.3
  425.9 1.5 copy-start.6
  425.9 2.3 copy-start.11
  427.4 1.6 copy-start.10
  427.4 2.4 copy-start.9
  427.4 3.2 copy-start.8
  428.2 3.2 copy-start.7
  428.2 4.0 copy-start.1

commit v13 on v12

--- a/solution.py
+++ b/solution.py
@@ -1702,15 +1702,27 @@
 
 def leave_kernel(
     parts, hidden, gain, gmid, gains, qa_send, qa_keep, qb_send, qb_keep, oa_keep, ob_keep, oa_in, ob_in,
-    grad_out, ga_out, query_out, key_out, value_out, output_out,
+    a_keep, b_keep, a_gate, b_gate, a_up, b_up, a_down, b_down, a_last, b_last,
+    grad_out, ga_out, query_out, key_out, value_out, output_out, gate_out, up_out, down_out,
     mine, from_pt, from_up, from_dn, s0, s1, s2, s3, s4, s5,
     acc, over_wid, summed, over_rest, w_s, w_g, t_s, t_g,
     first_q, next_q, then_q, next_o, then_o, kv, n_s, n_g, k0, k1, k2, k3, m_s,
+    terms, joined, t_in, t_out,
 ):
     me = spot()
     r, n, w = me
     own_parts = pltpu.make_async_copy(parts.at[r], mine, m_s)
     own_parts.start()
+    loads, puts = [], []
+    for j, (keep, gate, up, down, last_hop) in enumerate(
+        ((a_keep, a_gate, a_up, a_down, a_last), (b_keep, b_gate, b_up, b_down, b_last))
+    ):
+        for which, first in enumerate((gate, up.at[0], down.at[0, 0])):
+            at = 2 * which + j
+            for k, source in enumerate((keep.at[0, which], first, last_hop.at[which])):
+                loads.append(pltpu.make_async_copy(source, terms.at[k, at], t_in.at[k, at]))
+            place = (gate_out, up_out, down_out)[which].at[j * 128 : j * 128 + 128]
+            puts.append(pltpu.make_async_copy(joined.at[at], place, t_out.at[at]))
     partners = [(w != j, (r, n, jnp.int32(j))) for j in range(4)]
     partners += [
         ((r != a) | (n != b), (jnp.int32(a), jnp.int32(b), w)) for a in range(2) for b in range(4)
@@ -1732,6 +1744,8 @@
     ]
     for hop in q_hops:
         hop.start()
+    for load in loads:
+        load.start()
     scatter = Scatter(
         mine, parts.at[1 - r], (from_pt, from_up, from_dn), (s0, s1, s2, s3, s4, s5), me, 4
     )
@@ -1786,6 +1800,21 @@
     kv_gather.own()
     scatter.advance((3,), (1, 2))
     kv_gather.advance((), (1,))
+    for load in loads:
+        load.wait()
+
+    def add_terms(at, carry):
+        def body(rows):
+            joined[at, rows, :] = (
+                terms[0, at, rows, :].astype(f32) + terms[1, at, rows, :].astype(f32)
+            ) + terms[2, at, rows, :].astype(f32)
+
+        each_rows(128, 16, body)
+        return carry
+
+    lax.fori_loop(0, 6, add_terms, 0)
+    for put in puts:
+        put.start()
     scatter.advance((), (3,))
     kv_gather.advance((), (2,))
     for j, (keep, came) in enumerate(((oa_keep, oa_in), (ob_keep, ob_in))):
@@ -1821,6 +1850,8 @@
         value_out[:, here] = jnp.where(lane < 64, pltpu.roll(even, 64, 1), odd)
     scatter.sent()
     kv_gather.sent()
+    for put in puts:
+        put.wait()
     for hop in q_hops + q_later + o_hops:
         hop.wait_send()
     for j in range(4):
@@ -1842,8 +1873,9 @@
         leave_kernel, "leave", 7,
         (jax.ShapeDtypeStruct((shard, width), bf16), jax.ShapeDtypeStruct((8, 256), f32))
         + (grad,) * 3
-        + (jax.ShapeDtypeStruct((512, 256), f32),),
-        [hbm()] + [vmem()] * 12, [vmem()] * 6,
+        + (jax.ShapeDtypeStruct((512, 256), f32),)
+        + (jax.ShapeDtypeStruct((256, 2048), f32),) * 3,
+        [hbm()] + [vmem()] * 12 + [hbm()] * 10, [vmem()] * 6 + [hbm()] * 3,
         [pltpu.VMEM((4, shard, width), bf16)]
         + scatter_bufs(shard, width) + scatter_sems()
         + [
@@ -1865,7 +1897,13 @@
             pltpu.SemaphoreType.DMA((6,)),
         ]
         + gather_sems()
-        + [pltpu.SemaphoreType.DMA(())],
+        + [
+            pltpu.SemaphoreType.DMA(()),
+            pltpu.VMEM((3, 6, shard, width), bf16),
+            pltpu.VMEM((6, shard, width), f32),
+            pltpu.SemaphoreType.DMA((3, 6)),
+            pltpu.SemaphoreType.DMA((6,)),
+        ],
         args, flops=10**10, sent=10**8,
     )
 
@@ -1926,21 +1964,14 @@
     gains = jnp.concatenate(
         [gain_f_part.sum(axis=0).reshape(8, 256), gain_a_part.sum(axis=0).reshape(8, 256)], axis=0
     )
-    grad_in, gain_sums, grad_query, grad_key, grad_value, output_sum = leave(
+    (
+        grad_in, gain_sums, grad_query, grad_key, grad_value, output_sum,
+        grad_gate, grad_up, down_sum,
+    ) = leave(
         dparts, hidden, gain_a, gmid, gains,
         qa_send, qa_keep, qb_send, qb_keep, oa_keep, ob_keep, oa_came, ob_came,
-    )
-
-    def joined(which):
-        def half_rows(keep, came, last):
-            return keep[0, which].astype(f32) + came.astype(f32) + last.astype(f32)
-
-        a_came, b_came = (
-            (ra_g, rb_g), (ra_u[0], rb_u[0]), (ra_dg[0, 0], rb_dg[0, 0])
-        )[which]
-        return jnp.concatenate(
-            [half_rows(a_keep, a_came, a_last[which]), half_rows(b_keep, b_came, b_last[which])], axis=0
-        )
+        a_keep, b_keep, ra_g, rb_g, ra_u, rb_u, ra_dg, rb_dg, a_last, b_last,
+    )
 
     return (
         hidden_out[None],
@@ -1949,9 +1980,9 @@
         grad_key,
         grad_value,
         output_sum,
-        joined(0),
-        joined(1),
-        joined(2).T,
+        grad_gate,
+        grad_up,
+        down_sum.T,
         gain_sums[1],
         gain_sums[0],
     )

time: 433 us -> 427 us (0.986)
  other arithmetic: 17.2 us -> 6.22 us
  local copies, waits for them, and re-layouts: 11.8 us -> 16.6 us
    add x2 -> x0, other arithmetic: 7.38 us -> none  [half_rows(): return keep[0, which].astype(f32) + came.astype(f32) + last.astype(f32)]
    unnamed x43 -> x35, local copies, waits for them, and re-layouts: 6.66 us -> 11.4 us
    concatenate x2 -> x0, other arithmetic: 4.35 us -> none  [joined(): jnp.concatenate([half_rows(a_keep, a_came, a_last[which]), half_rows(b_ke...]
where the time goes in v13:
time: 427 us; the launch traced here: 426 us
  Pallas kernels  403 us (94%)
  local copies, waits for them, and re-layouts  16.6 us (4%)
  other arithmetic  6.22 us (1%)
    pallas_call x5, Pallas kernels, comm_call(): pl.pallas_call(kernel, out_shape=out_shape, in_specs=in_specs, out_specs=...  403 us
    unnamed x35, local copies, waits for them, and re-layouts  11.4 us

profile of v13, /device:TPU:0, one launch (start us, length us, event | category | flops | bytes accessed | tf_op | source)
XLA Modules:
  0.0 426.2 jit_solution(7918524642196754392)
XLA Ops:
  0.6 0.0 copy-start
  0.7 0.0 copy-start.12
  0.7 0.9 reduce-window.4
  1.6 0.7 fusion.1
  2.2 0.1 select_reduce_fusion
  2.3 0.1 broadcast_in_dim.22
  2.5 1.1 constant_dynamic-slice_fusion.2
  3.6 1.0 constant_dynamic-slice_fusion
  4.6 0.0 copy-done
  4.6 1.0 maximum_maximum_fusion.p1_own
  5.6 0.0 copy-done.12
  5.6 0.0 copy-start.10
  5.6 1.0 multiply_sine_fusion
  6.6 1.5 concatenate.15.tab
  8.1 0.0 copy-done.10
  8.1 0.1 constant_dynamic-slice_fusion.5
  8.2 1.1 pad_maximum_fusion.down_own
  9.3 63.7 %enter.1 = (bf16[2,512,256]{2,1,0:T(8,128)(2,1)}, bf16[2,4,128,2048]{3,2,1,0:T(8,128)(2,1)}, f32[2,512,384]{2,1,0:T(8,128)}, bf16[4,512,640]{2,1,0:T(8,128)(2,1)...) custom-call(bf16[128,2048]{1,0:T(8,128)(2,1)} %bitcast.29, ...), custom_call_target="tpu_custom_call" | custom-call | flops 10000000000 | bytes 100000000 | tf_op jit(solution)/shard_map/enter/pallas_call | solution.py:732
  73.0 96.6 %middle.1 = (bf16[2,512,256]{2,1,0:T(8,128)(2,1)}, f32[2,4,512,128]{3,2,1,0:T(8,128)}, f32[128,2048]{1,0:T(8,128)}, bf16[2,4,128,2048]{3,2,1,0:T(8,128)(2,1)}, b...) custom-call(bf16[2,512,256]{2,1,0:T(8,128)(2,1)} %get-tuple-element.61.q, ...), custom_call_target="tpu_custom_call" | custom-call | flops 10000000000 | bytes 200000000 | tf_op jit(solution)/shard_map/middle/pallas_call | solution.py:732
  169.6 86.0 %ffn.1 = (bf16[2,4,128,2048]{3,2,1,0:T(8,128)(2,1)}, f32[128,2048]{1,0:T(8,128)}, f32[8,2048]{1,0:T(8,128)}, bf16[2,3,128,2048]{3,2,1,0:T(8,128)(2,1)}, bf16[2,3...) custom-call(bf16[1024,2048]{1,0:T(8,128)(2,1)} %bitcast.40, ...), custom_call_target="tpu_custom_call" | custom-call | flops 40000000000 | bytes 100000000 | tf_op jit(solution)/shard_map/ffn/pallas_call | solution.py:732
  255.7 0.0 copy-start.11
  255.7 98.9 %back.1 = (f32[128,2048]{1,0:T(8,128)}, bf16[2,4,128,2048]{3,2,1,0:T(8,128)(2,1)}, f32[8,2048]{1,0:T(8,128)}, bf16[128,2048]{1,0:T(8,128)(2,1)}, bf16[2,128,512]...) custom-call(f32[128,2048]{1,0:T(8,128)} %get-tuple-element.71.total,, ...), custom_call_target="tpu_custom_call" | custom-call | flops 10000000000 | bytes 100000000 | tf_op jit(solution)/shard_map/back/pallas_call | solution.py:732
  354.6 0.9 reduce_sum.29
  355.5 0.0 copy-done.11
  355.6 0.6 pad_maximum_fusion.1.gains
  356.2 57.2 %leave.1 = (bf16[128,2048]{1,0:T(8,128)(2,1)}, f32[8,256]{1,0:T(8,128)}, f32[256,512]{1,0:T(8,128)}, f32[256,512]{1,0:T(8,128)}, f32[256,512]{1,0:T(8,128)}, /*i...) custom-call(bf16[2,4,128,2048]{3,2,1,0:T(8,128)(2,1)} %get-tuple-element.84.parts, ...), custom_call_target="tpu_custom_call" | custom-call | flops 10000000000 | bytes 100000000 | tf_op jit(solution)/shard_map/leave/pallas_call | solution.py:732
  413.4 1.3 fusion.2
  414.7 0.0 copy-start.4
  414.7 0.0 copy-start.9
  414.7 3.0 copy.27
  417.7 0.0 copy-done.4
  417.7 0.0 copy-start.8
  417.7 0.0 copy-start.7
  417.7 0.0 copy-start.6
  417.7 0.8 copy.36
  418.5 0.0 copy-done.9
  418.5 0.0 copy-start.5
  418.5 0.8 copy.37
  419.3 0.0 copy-done.8
  419.3 0.0 copy-start.3
  419.3 0.8 copy.38
  420.1 0.0 copy-done.7
  420.1 0.8 copy.39
  420.9 0.0 copy-done.6
  420.9 0.8 copy.40
  421.7 0.0 copy-done.5
  421.7 0.8 copy.41
  422.5 0.0 copy-done.3
  422.5 0.0 copy-start.2
  422.5 0.0 copy-start.1
  422.5 1.3 copy.42
  423.8 1.0 copy-done.2
  424.8 1.3 copy.43
  426.2 0.0 copy-done.1
  (6 shorter events, 0.1 us)
Async XLA Ops:
  0.6 3.9 copy-start
  0.7 5.0 %copy-start.12 = (f32[32]{0:T(128)S(1)}, f32[32]{0:T(128)}, u32[]{:S(2)}) copy-start(f32[32]{0:T(128)} %constant.36.clone) | copy-start | bytes 388
  5.6 2.5 copy-start.10
  255.7 99.8 %copy-start.11 = (f32[8,2048]{1,0:T(8,128)S(1)}, f32[8,2048]{1,0:T(8,128)}, u32[]{:S(2)}) copy-start(f32[8,2048]{1,0:T(8,128)} %get-tuple-element.86) | copy-start | bytes 196612
  414.7 3.0 copy-start.4
  414.7 3.8 copy-start.9
  417.7 1.6 copy-start.8
  417.7 2.4 copy-start.7
  417.7 3.2 copy-start.6
  418.5 3.2 copy-start.5
  419.3 3.2 copy-start.3
  422.5 2.3 copy-start.2
  422.5 3.7 copy-start.1
